TPU v7x, 32 devices: a whole 2x2x4 slice. The times are simulated.
32 devices in a mesh: seq: 8 (over z, x), tp: 4 (over y, core).
Axes of the slice: x: 2, y: 2, z: 4, core: 2. Of those that a mesh axis runs over, the one named last changes fastest.
Arguments:
- x_tokens: bfloat16 [2048, 1536], P('seq'), may hold values from -6 to 6
- caption: bfloat16 [2048, 4096], P('seq'), may hold values from -6 to 6
- timesteps: float32 [8], replicated, may hold values from 0 to 1, as said below
- segment_ids: int32 [2048], P('seq'), may hold values from 0 to 7, never falling along the last dimension, each value on 1 to 1792 neighbouring positions
- out_grad: bfloat16 [2048, 1536], P('seq'), may hold values from -6 to 6
- mod_weight: float32 [1024, 9216], P('seq'), may hold values from -0.1875 to 0.1875
- mod_first: float32 [1024, 9216], P('seq'), may hold values from -9.1552734e-05 to 9.1552734e-05
- mod_second: float32 [1024, 9216], P('seq'), may hold values from 9.934108e-10 to 7.947286e-09
- norm_gains: float32 [2, 1536], P(None, 'seq'), may hold values from 0.5 to 1.5
- gains_first: float32 [2, 1536], P(None, 'seq'), may hold values from -0.00024414062 to 0.00024414062
- gains_second: float32 [2, 1536], P(None, 'seq'), may hold values from 8.940697e-09 to 7.152558e-08
- qkv_weight: float32 [3, 1536, 1536], P(None, 'seq', 'tp'), may hold values from -0.15625 to 0.15625
- qkv_first: float32 [3, 1536, 1536], P(None, 'seq', 'tp'), may hold values from -9.1552734e-05 to 9.1552734e-05
- qkv_second: float32 [3, 1536, 1536], P(None, 'seq', 'tp'), may hold values from 9.934108e-10 to 7.947286e-09
- out_weight: float32 [1536, 1536], P('tp', 'seq'), may hold values from -0.625 to 0.625
- out_first: float32 [1536, 1536], P('tp', 'seq'), may hold values from -9.1552734e-05 to 9.1552734e-05
- out_second: float32 [1536, 1536], P('tp', 'seq'), may hold values from 9.934108e-10 to 7.947286e-09
- text_weight: float32 [2, 4096, 1536], P(None, 'seq', 'tp'), may hold values from -0.09375 to 0.09375
- text_first: float32 [2, 4096, 1536], P(None, 'seq', 'tp'), may hold values from -9.1552734e-05 to 9.1552734e-05
- text_second: float32 [2, 4096, 1536], P(None, 'seq', 'tp'), may hold values from 9.934108e-10 to 7.947286e-09
- cross_gates: float32 [24], P('tp'), may hold values from 0.4 to 1.6
- cross_first: float32 [24], P('tp'), may hold values from -0.00048828125 to 0.00048828125
- cross_second: float32 [24], P('tp'), may hold values from 2.4835268e-08 to 1.9868214e-07
- updown_weight: float32 [2, 1536, 4096], P(None, 'seq', 'tp'), may hold values from -0.15625 to 0.15625
- updown_first: float32 [2, 1536, 4096], P(None, 'seq', 'tp'), may hold values from -9.1552734e-05 to 9.1552734e-05
- updown_second: float32 [2, 1536, 4096], P(None, 'seq', 'tp'), may hold values from 9.934108e-10 to 7.947286e-09
- down_weight: float32 [4096, 1536], P('tp', 'seq'), may hold values from -0.09375 to 0.09375
- down_first: float32 [4096, 1536], P('tp', 'seq'), may hold values from -9.1552734e-05 to 9.1552734e-05
- down_second: float32 [4096, 1536], P('tp', 'seq'), may hold values from 9.934108e-10 to 7.947286e-09
Outputs:
- block_out: float32 [2048, 1536], P('seq')
- input_grad: float32 [2048, 1536], P('seq')
- grad_norm: float32 [], replicated
- mod_weight_new: float32 [1024, 9216], P('seq')
- mod_first_new: float32 [1024, 9216], P('seq')
- mod_second_new: float32 [1024, 9216], P('seq')
- gains_new: float32 [2, 1536], P(None, 'seq')
- gains_first_new: float32 [2, 1536], P(None, 'seq')
- gains_second_new: float32 [2, 1536], P(None, 'seq')
- qkv_weight_new: float32 [3, 1536, 1536], P(None, 'seq', 'tp')
- qkv_first_new: float32 [3, 1536, 1536], P(None, 'seq', 'tp')
- qkv_second_new: float32 [3, 1536, 1536], P(None, 'seq', 'tp')
- out_weight_new: float32 [1536, 1536], P('tp', 'seq')
- out_first_new: float32 [1536, 1536], P('tp', 'seq')
- out_second_new: float32 [1536, 1536], P('tp', 'seq')
- text_weight_new: float32 [2, 4096, 1536], P(None, 'seq', 'tp')
- text_first_new: float32 [2, 4096, 1536], P(None, 'seq', 'tp')
- text_second_new: float32 [2, 4096, 1536], P(None, 'seq', 'tp')
- cross_gates_new: float32 [24], P('tp')
- cross_first_new: float32 [24], P('tp')
- cross_second_new: float32 [24], P('tp')
- updown_weight_new: float32 [2, 1536, 4096], P(None, 'seq', 'tp')
- updown_first_new: float32 [2, 1536, 4096], P(None, 'seq', 'tp')
- updown_second_new: float32 [2, 1536, 4096], P(None, 'seq', 'tp')
- down_weight_new: float32 [4096, 1536], P('tp', 'seq')
- down_first_new: float32 [4096, 1536], P('tp', 'seq')
- down_second_new: float32 [4096, 1536], P('tp', 'seq')
Inputs may be any that keep to these rules, and one draw needn't show every extreme that they name: `segment_ids`: never falling along the tokens; every one of the 8 images has 1 to 1792 tokens and one has exactly 1792. `timesteps`: logistic function of a random draw.
All inputs are finite; a program needn't handle non-finite values.
Results may differ from a plain program's by a relative error of at most 0.015.
Values may be sent and summed in bfloat16 or wider, within the bound.
No kernel may reach another device: no remote copies, remote signals or barrier semaphores. Data moves between devices by JAX's collectives and lax.ppermute only.
A program may use at most 320 MiB of HBM per device.

v0:
```python
import math

import jax
import jax.numpy as jnp
from jax import lax
from jax.sharding import PartitionSpec as P

HD = 64
TE = 1024
TEXT = 256
ITEMS = 8
ADAM_STEP = 10


highest = lax.Precision.HIGHEST
eps_norm = 1e-06
key_span = 2048
huge_negative = -1e30
clip_limit = 1.0
beta_first = 0.9
beta_second = 0.95
adam_eps = 1e-08
rate_matrix = 0.05
rate_small = 0.5
decay_matrix = 0.1


def time_embed(timesteps):
    half_width = TE // 2
    frequency = jnp.exp(-math.log(10000.0) * jnp.arange(half_width, dtype=jnp.float32) / half_width)
    angles = 1000.0 * timesteps[:, None] * frequency[None, :]
    return jnp.concatenate([jnp.cos(angles), jnp.sin(angles)], axis=1)


def rms_parts(values):
    inverse = lax.rsqrt(jnp.mean(values * values, axis=-1, keepdims=True) + eps_norm)
    return (values * inverse, inverse)


def rms_back(normed, inverse, normed_grad):
    return inverse * (normed_grad - normed * jnp.mean(normed_grad * normed, axis=-1, keepdims=True))


def online_update(
    state, query_heads, segment_value, key_block, value_block, segment_block, score_scale
):
    running_max, running_sum, running_out = state
    head_count = query_heads.shape[1]
    key_heads = key_block.reshape(-1, head_count, HD)
    value_heads = value_block.reshape(-1, head_count, HD)
    scores = (
        jnp.einsum("qhd,khd->hqk", query_heads, key_heads, preferred_element_type=jnp.float32)
        * score_scale
    )
    allowed = (segment_value[:, None] == segment_block[None, :])[None]
    scores = jnp.where(allowed, scores, huge_negative)
    new_max = jnp.maximum(running_max, jnp.max(scores, axis=-1))
    weights = jnp.where(allowed, jnp.exp(scores - new_max[..., None]), 0.0)
    correction = jnp.exp(running_max - new_max)
    new_sum = running_sum * correction + jnp.sum(weights, axis=-1)
    new_out = running_out * correction[..., None] + jnp.einsum(
        "hqk,khd->hqd",
        weights.astype(jnp.bfloat16),
        value_heads,
        preferred_element_type=jnp.float32,
    )
    return (new_max, new_sum, new_out)


def attend_rows(state, query_heads, segment_value, key_rows, value_rows, segment_rows, score_scale):
    row_count = key_rows.shape[0]
    span_rows = math.gcd(row_count, key_span)
    block_count = row_count // span_rows
    row_width = key_rows.shape[1]
    block_data = (
        key_rows.reshape(block_count, span_rows, row_width),
        value_rows.reshape(block_count, span_rows, row_width),
        segment_rows.reshape(block_count, span_rows),
    )
    lowest_item = segment_value[0]
    highest_item = segment_value[-1]

    def attend_scan_step(carried, one_block):
        key_block, value_block, segment_block = one_block
        intersection = jnp.logical_and(
            segment_block[0] <= highest_item, segment_block[-1] >= lowest_item
        )

        def attend_active_branch(inner_state):
            return online_update(
                inner_state,
                query_heads,
                segment_value,
                key_block,
                value_block,
                segment_block,
                score_scale,
            )

        def attend_skip_branch(inner_state):
            return inner_state

        return (lax.cond(intersection, attend_active_branch, attend_skip_branch, carried), None)

    final_state, unused_out = lax.scan(attend_scan_step, state, block_data)
    return final_state


def self_backward(
    query_heads,
    grad_heads,
    log_total,
    delta_rows,
    segment_value,
    key_rows,
    value_rows,
    segment_rows,
    score_scale,
):
    row_count = key_rows.shape[0]
    span_rows = math.gcd(row_count, key_span)
    block_count = row_count // span_rows
    row_width = key_rows.shape[1]
    head_count = query_heads.shape[1]
    block_data = (
        key_rows.reshape(block_count, span_rows, row_width),
        value_rows.reshape(block_count, span_rows, row_width),
        segment_rows.reshape(block_count, span_rows),
    )
    lowest_item = segment_value[0]
    highest_item = segment_value[-1]

    def self_scan_step(query_total, one_block):
        key_block, value_block, segment_block = one_block
        intersection = jnp.logical_and(
            segment_block[0] <= highest_item, segment_block[-1] >= lowest_item
        )

        def self_active_branch(total_in):
            key_heads = key_block.reshape(-1, head_count, HD)
            value_heads = value_block.reshape(-1, head_count, HD)
            scores = (
                jnp.einsum(
                    "qhd,khd->hqk", query_heads, key_heads, preferred_element_type=jnp.float32
                )
                * score_scale
            )
            allowed = (segment_value[:, None] == segment_block[None, :])[None]
            probs = jnp.where(allowed, jnp.exp(scores - log_total[..., None]), 0.0)
            prob_grad = jnp.einsum(
                "qhd,khd->hqk", grad_heads, value_heads, preferred_element_type=jnp.float32
            )
            score_grad = (probs * (prob_grad - delta_rows[..., None])).astype(jnp.bfloat16)
            query_part = (
                jnp.einsum(
                    "hqk,khd->qhd", score_grad, key_heads, preferred_element_type=jnp.float32
                )
                * score_scale
            )
            key_part = (
                jnp.einsum(
                    "hqk,qhd->khd", score_grad, query_heads, preferred_element_type=jnp.float32
                )
                * score_scale
            )
            value_part = jnp.einsum(
                "hqk,qhd->khd",
                probs.astype(jnp.bfloat16),
                grad_heads,
                preferred_element_type=jnp.float32,
            )
            return (
                total_in + query_part,
                (key_part.reshape(span_rows, row_width), value_part.reshape(span_rows, row_width)),
            )

        def self_skip_branch(total_in):
            zero_rows = jnp.zeros((span_rows, row_width), jnp.float32)
            return (total_in, (zero_rows, zero_rows))

        new_total, parts = lax.cond(intersection, self_active_branch, self_skip_branch, query_total)
        return (new_total, parts)

    query_total, grad_parts = lax.scan(
        self_scan_step, jnp.zeros(query_heads.shape, jnp.float32), block_data
    )
    return (
        query_total,
        grad_parts[0].reshape(row_count, row_width),
        grad_parts[1].reshape(row_count, row_width),
    )


def adam_update(weight, first, second, grad, clip, rate, decay):
    clipped = grad * clip
    first_new = beta_first * first + (1.0 - beta_first) * clipped
    second_new = beta_second * second + (1.0 - beta_second) * clipped * clipped
    first_hat = first_new / (1.0 - beta_first**ADAM_STEP)
    second_hat = second_new / (1.0 - beta_second**ADAM_STEP)
    weight_new = weight - rate * (first_hat / (jnp.sqrt(second_hat) + adam_eps) + decay * weight)
    return (weight_new, first_new, second_new)


def square_sum(values):
    return jnp.sum(values * values)


def per_device(
    x_tokens,
    caption,
    timesteps,
    segment_ids,
    out_grad,
    mod_weight,
    mod_first,
    mod_second,
    norm_gains,
    gains_first,
    gains_second,
    qkv_weight,
    qkv_first,
    qkv_second,
    out_weight,
    out_first,
    out_second,
    text_weight,
    text_first,
    text_second,
    cross_gates,
    cross_first,
    cross_second,
    updown_weight,
    updown_first,
    updown_second,
    down_weight,
    down_first,
    down_second,
):
    seq_index = lax.axis_index("seq")
    tp_index = lax.axis_index("tp")
    tokens_here = x_tokens.shape[0]
    local_heads = cross_gates.shape[0]
    local_width = local_heads * HD
    score_scale = HD ** (-0.5)
    qkv_all, out_all, text_all, updown_all, down_all, gains_all, mod_all = (
        lax.all_gather(qkv_weight.astype(jnp.bfloat16), "seq", axis=1, tiled=True),
        lax.all_gather(out_weight.astype(jnp.bfloat16), "seq", axis=1, tiled=True),
        lax.all_gather(text_weight.astype(jnp.bfloat16), "seq", axis=1, tiled=True),
        lax.all_gather(updown_weight.astype(jnp.bfloat16), "seq", axis=1, tiled=True),
        lax.all_gather(down_weight.astype(jnp.bfloat16), "seq", axis=1, tiled=True),
        lax.all_gather(norm_gains.astype(jnp.bfloat16), "seq", axis=1, tiled=True),
        lax.all_gather(mod_weight.astype(jnp.bfloat16), "seq", axis=0, tiled=True),
    )
    gains_value = gains_all.astype(jnp.float32)
    silu_embed = jax.nn.silu(time_embed(timesteps)).astype(jnp.bfloat16)
    mod_rows = mod_weight.shape[0]
    embed_rows = lax.dynamic_slice_in_dim(silu_embed, seq_index * mod_rows, mod_rows, 1)
    modulation = jnp.dot(silu_embed, mod_all, preferred_element_type=jnp.float32)
    item_range = jnp.arange(ITEMS, dtype=jnp.int32)
    item_onehot = (segment_ids[:, None] == item_range[None, :]).astype(jnp.float32)
    per_token = jnp.dot(
        item_onehot, modulation, precision=highest, preferred_element_type=jnp.float32
    )
    shift_attn, scale_attn, gate_attn, shift_ffn, scale_ffn, gate_ffn = jnp.split(
        per_token, 6, axis=1
    )
    x_value = x_tokens.astype(jnp.float32)
    normed_attn, inverse_attn = rms_parts(x_value)
    hidden_attn = (normed_attn * gains_value[0] * (1.0 + scale_attn) + shift_attn).astype(
        jnp.bfloat16
    )
    projected = jnp.einsum(
        "nd,jdc->jnc", hidden_attn, qkv_all, preferred_element_type=jnp.float32
    ).astype(jnp.bfloat16)
    queries = projected[0]
    keys = projected[1]
    values = projected[2]
    text_local = jnp.einsum(
        "rt,jtc->jrc", caption, text_all, preferred_element_type=jnp.float32
    ).astype(jnp.bfloat16)
    text_kv = lax.all_gather(text_local, "seq", axis=1, tiled=True)
    text_rows = text_kv.shape[1]
    text_keys = text_kv[0].reshape(text_rows, local_heads, HD)
    text_values = text_kv[1].reshape(text_rows, local_heads, HD)
    text_items = jnp.arange(text_rows, dtype=jnp.int32) // TEXT
    segment_value = segment_ids.astype(jnp.bfloat16)
    query_heads = queries.reshape(tokens_here, local_heads, HD)
    start_state = (
        jnp.full((local_heads, tokens_here), huge_negative, jnp.float32),
        jnp.zeros((local_heads, tokens_here), jnp.float32),
        jnp.zeros((local_heads, tokens_here, HD), jnp.float32),
    )
    final_state = attend_rows(
        start_state,
        query_heads,
        segment_value,
        lax.all_gather(keys, "seq", axis=0, tiled=True),
        lax.all_gather(values, "seq", axis=0, tiled=True),
        lax.all_gather(segment_value, "seq", axis=0, tiled=True),
        score_scale,
    )
    running_max, running_sum, running_out = final_state
    log_total = running_max + jnp.log(running_sum)
    self_out = jnp.transpose(running_out / running_sum[..., None], (1, 0, 2))
    text_scores = (
        jnp.einsum("qhd,khd->hqk", query_heads, text_keys, preferred_element_type=jnp.float32)
        * score_scale
    )
    text_allowed = (segment_ids[:, None] == text_items[None, :])[None]
    text_masked = jnp.where(text_allowed, text_scores, huge_negative)
    text_top = jnp.max(text_masked, axis=-1, keepdims=True)
    text_weights = jnp.where(text_allowed, jnp.exp(text_masked - text_top), 0.0)
    text_probs = text_weights / jnp.sum(text_weights, axis=-1, keepdims=True)
    text_probs_low = text_probs.astype(jnp.bfloat16)
    text_out = jnp.einsum(
        "hqk,khd->qhd", text_probs_low, text_values, preferred_element_type=jnp.float32
    )
    tanh_cross = jnp.tanh(cross_gates)
    mixed = (
        (self_out + tanh_cross[None, :, None] * text_out)
        .reshape(tokens_here, local_width)
        .astype(jnp.bfloat16)
    )
    attn_part = jnp.dot(mixed, out_all, preferred_element_type=jnp.float32)
    attn = lax.psum(attn_part.astype(jnp.bfloat16), "tp").astype(jnp.float32)
    tanh_attn = jnp.tanh(gate_attn)
    x_mid = x_value + tanh_attn * attn
    normed_ffn, inverse_ffn = rms_parts(x_mid)
    hidden_ffn = (normed_ffn * gains_value[1] * (1.0 + scale_ffn) + shift_ffn).astype(jnp.bfloat16)
    gate_pre = jnp.dot(hidden_ffn, updown_all[0], preferred_element_type=jnp.float32)
    up_pre = jnp.dot(hidden_ffn, updown_all[1], preferred_element_type=jnp.float32)
    silu_gate = jax.nn.silu(gate_pre)
    inner = (silu_gate * up_pre).astype(jnp.bfloat16)
    ffn_part = jnp.dot(inner, down_all, preferred_element_type=jnp.float32)
    ffn_out = lax.psum(ffn_part.astype(jnp.bfloat16), "tp").astype(jnp.float32)
    tanh_ffn = jnp.tanh(gate_ffn)
    block_out = x_mid + tanh_ffn * ffn_out
    grad_value = out_grad.astype(jnp.float32)
    ffn_grad = (grad_value * tanh_ffn).astype(jnp.bfloat16)
    gate_ffn_grad = grad_value * ffn_out * (1.0 - tanh_ffn * tanh_ffn)
    inner_grad = jnp.dot(ffn_grad, down_all.T, preferred_element_type=jnp.float32)
    down_grad = jnp.dot(inner.T, ffn_grad, preferred_element_type=jnp.float32)
    sigmoid_gate = jax.nn.sigmoid(gate_pre)
    gate_grad = (
        inner_grad * up_pre * sigmoid_gate * (1.0 + gate_pre * (1.0 - sigmoid_gate))
    ).astype(jnp.bfloat16)
    up_grad = (inner_grad * silu_gate).astype(jnp.bfloat16)
    both_grads = jnp.stack([gate_grad, up_grad])
    updown_grad = jnp.einsum(
        "nd,jnf->jdf", hidden_ffn, both_grads, preferred_element_type=jnp.float32
    )
    hidden_ffn_part = jnp.einsum(
        "jnf,jdf->nd", both_grads, updown_all, preferred_element_type=jnp.float32
    )
    hidden_ffn_grad = lax.psum(hidden_ffn_part.astype(jnp.bfloat16), "tp").astype(jnp.float32)
    scale_ffn_grad = hidden_ffn_grad * normed_ffn * gains_value[1]
    gain_ffn_grad = jnp.sum(hidden_ffn_grad * normed_ffn * (1.0 + scale_ffn), axis=0)
    mid_grad = grad_value + rms_back(
        normed_ffn, inverse_ffn, hidden_ffn_grad * gains_value[1] * (1.0 + scale_ffn)
    )
    attn_grad = (mid_grad * tanh_attn).astype(jnp.bfloat16)
    gate_attn_grad = mid_grad * attn * (1.0 - tanh_attn * tanh_attn)
    mixed_grad = jnp.dot(attn_grad, out_all.T, preferred_element_type=jnp.float32).astype(
        jnp.bfloat16
    )
    out_weight_grad = jnp.dot(mixed.T, attn_grad, preferred_element_type=jnp.float32)
    grad_heads = mixed_grad.reshape(tokens_here, local_heads, HD)
    grad_heads_value = grad_heads.astype(jnp.float32)
    cross_gate_grad = jnp.einsum("qhd,qhd->h", grad_heads_value, text_out) * (
        1.0 - tanh_cross * tanh_cross
    )
    text_out_grad = (grad_heads_value * tanh_cross[None, :, None]).astype(jnp.bfloat16)
    text_prob_grad = jnp.einsum(
        "qhd,khd->hqk", text_out_grad, text_values, preferred_element_type=jnp.float32
    )
    text_score_grad = (
        text_probs * (text_prob_grad - jnp.sum(text_probs * text_prob_grad, axis=-1, keepdims=True))
    ).astype(jnp.bfloat16)
    text_query_grad = (
        jnp.einsum("hqk,khd->qhd", text_score_grad, text_keys, preferred_element_type=jnp.float32)
        * score_scale
    )
    text_key_part = (
        jnp.einsum("hqk,qhd->khd", text_score_grad, query_heads, preferred_element_type=jnp.float32)
        * score_scale
    )
    text_value_part = jnp.einsum(
        "hqk,qhd->khd", text_probs_low, text_out_grad, preferred_element_type=jnp.float32
    )
    text_kv_part = jnp.stack(
        [
            text_key_part.reshape(text_rows, local_width),
            text_value_part.reshape(text_rows, local_width),
        ]
    )
    delta_rows = jnp.einsum("qhd,qhd->hq", grad_heads_value, self_out)
    back_keys, back_values, back_segments = (
        lax.all_gather(keys, "seq", axis=0, tiled=True),
        lax.all_gather(values, "seq", axis=0, tiled=True),
        lax.all_gather(segment_value, "seq", axis=0, tiled=True),
    )
    self_query_grad, key_grad_all, value_grad_all = self_backward(
        query_heads,
        grad_heads,
        log_total,
        delta_rows,
        segment_value,
        back_keys,
        back_values,
        back_segments,
        score_scale,
    )
    self_kv_part = jnp.stack([key_grad_all, value_grad_all])
    self_kv_grad, text_kv_grad = (
        lax.psum_scatter(self_kv_part, "seq", scatter_dimension=1, tiled=True),
        lax.psum_scatter(text_kv_part, "seq", scatter_dimension=1, tiled=True),
    )
    text_kv_low = text_kv_grad.astype(jnp.bfloat16)
    text_weight_grad = jnp.einsum(
        "rt,jrc->jtc", caption, text_kv_low, preferred_element_type=jnp.float32
    )
    query_grad = (
        (self_query_grad + text_query_grad).reshape(tokens_here, local_width).astype(jnp.bfloat16)
    )
    qkv_grads = jnp.stack(
        [query_grad, self_kv_grad[0].astype(jnp.bfloat16), self_kv_grad[1].astype(jnp.bfloat16)]
    )
    qkv_weight_grad = jnp.einsum(
        "nd,jnc->jdc", hidden_attn, qkv_grads, preferred_element_type=jnp.float32
    )
    hidden_attn_part = jnp.einsum(
        "jnc,jdc->nd", qkv_grads, qkv_all, preferred_element_type=jnp.float32
    )
    hidden_attn_grad = lax.psum(hidden_attn_part.astype(jnp.bfloat16), "tp").astype(jnp.float32)
    scale_attn_grad = hidden_attn_grad * normed_attn * gains_value[0]
    gain_attn_grad = jnp.sum(hidden_attn_grad * normed_attn * (1.0 + scale_attn), axis=0)
    input_grad = mid_grad + rms_back(
        normed_attn, inverse_attn, hidden_attn_grad * gains_value[0] * (1.0 + scale_attn)
    )
    token_mod_grad = jnp.concatenate(
        [
            hidden_attn_grad,
            scale_attn_grad,
            gate_attn_grad,
            hidden_ffn_grad,
            scale_ffn_grad,
            gate_ffn_grad,
        ],
        axis=1,
    )
    item_mod_part = jnp.dot(
        item_onehot.T, token_mod_grad, precision=highest, preferred_element_type=jnp.float32
    )
    item_mod_grad, cross_total = lax.psum((item_mod_part, cross_gate_grad), "seq")
    mod_weight_grad = jnp.dot(
        embed_rows.T, item_mod_grad.astype(jnp.bfloat16), preferred_element_type=jnp.float32
    )
    gain_grads = jnp.stack([gain_attn_grad, gain_ffn_grad])
    qkv_owned, out_owned, text_owned, updown_owned, down_owned, gains_owned = (
        lax.psum_scatter(qkv_weight_grad, "seq", scatter_dimension=1, tiled=True),
        lax.psum_scatter(out_weight_grad, "seq", scatter_dimension=1, tiled=True),
        lax.psum_scatter(text_weight_grad, "seq", scatter_dimension=1, tiled=True),
        lax.psum_scatter(updown_grad, "seq", scatter_dimension=1, tiled=True),
        lax.psum_scatter(down_grad, "seq", scatter_dimension=1, tiled=True),
        lax.psum_scatter(gain_grads, "seq", scatter_dimension=1, tiled=True),
    )
    owned_square = (
        square_sum(qkv_owned)
        + square_sum(out_owned)
        + square_sum(text_owned)
        + square_sum(updown_owned)
        + square_sum(down_owned)
    )
    owned_square = owned_square + jnp.where(
        tp_index == 0, square_sum(gains_owned) + square_sum(mod_weight_grad), 0.0
    )
    owned_square = owned_square + jnp.where(seq_index == 0, square_sum(cross_total), 0.0)
    total_square = lax.psum(owned_square, ("seq", "tp"))
    grad_norm = jnp.sqrt(total_square)
    clip = jnp.minimum(1.0, clip_limit / (grad_norm + 1e-06))
    mod_new = adam_update(
        mod_weight, mod_first, mod_second, mod_weight_grad, clip, rate_matrix, decay_matrix
    )
    gains_new = adam_update(
        norm_gains, gains_first, gains_second, gains_owned, clip, rate_small, 0.0
    )
    qkv_new = adam_update(
        qkv_weight, qkv_first, qkv_second, qkv_owned, clip, rate_matrix, decay_matrix
    )
    out_new = adam_update(
        out_weight, out_first, out_second, out_owned, clip, rate_matrix, decay_matrix
    )
    text_new = adam_update(
        text_weight, text_first, text_second, text_owned, clip, rate_matrix, decay_matrix
    )
    cross_new = adam_update(
        cross_gates, cross_first, cross_second, cross_total, clip, rate_small, 0.0
    )
    updown_new = adam_update(
        updown_weight, updown_first, updown_second, updown_owned, clip, rate_matrix, decay_matrix
    )
    down_new = adam_update(
        down_weight, down_first, down_second, down_owned, clip, rate_matrix, decay_matrix
    )
    return (
        block_out,
        input_grad,
        grad_norm,
        mod_new[0],
        mod_new[1],
        mod_new[2],
        gains_new[0],
        gains_new[1],
        gains_new[2],
        qkv_new[0],
        qkv_new[1],
        qkv_new[2],
        out_new[0],
        out_new[1],
        out_new[2],
        text_new[0],
        text_new[1],
        text_new[2],
        cross_new[0],
        cross_new[1],
        cross_new[2],
        updown_new[0],
        updown_new[1],
        updown_new[2],
        down_new[0],
        down_new[1],
        down_new[2],
    )


def solution(mesh):
    in_specs = (
        P("seq", None),
        P("seq", None),
        P(),
        P("seq"),
        P("seq", None),
        P("seq", None),
        P("seq", None),
        P("seq", None),
        P(None, "seq"),
        P(None, "seq"),
        P(None, "seq"),
        P(None, "seq", "tp"),
        P(None, "seq", "tp"),
        P(None, "seq", "tp"),
        P("tp", "seq"),
        P("tp", "seq"),
        P("tp", "seq"),
        P(None, "seq", "tp"),
        P(None, "seq", "tp"),
        P(None, "seq", "tp"),
        P("tp"),
        P("tp"),
        P("tp"),
        P(None, "seq", "tp"),
        P(None, "seq", "tp"),
        P(None, "seq", "tp"),
        P("tp", "seq"),
        P("tp", "seq"),
        P("tp", "seq"),
    )
    out_specs = (
        P("seq", None),
        P("seq", None),
        P(),
        P("seq", None),
        P("seq", None),
        P("seq", None),
        P(None, "seq"),
        P(None, "seq"),
        P(None, "seq"),
        P(None, "seq", "tp"),
        P(None, "seq", "tp"),
        P(None, "seq", "tp"),
        P("tp", "seq"),
        P("tp", "seq"),
        P("tp", "seq"),
        P(None, "seq", "tp"),
        P(None, "seq", "tp"),
        P(None, "seq", "tp"),
        P("tp"),
        P("tp"),
        P("tp"),
        P(None, "seq", "tp"),
        P(None, "seq", "tp"),
        P(None, "seq", "tp"),
        P("tp", "seq"),
        P("tp", "seq"),
        P("tp", "seq"),
    )
    return jax.shard_map(
        per_device, mesh=mesh, in_specs=in_specs, out_specs=out_specs, check_vma=False
    )
```

profile of v0, /device:TPU:0, one launch (start us, length us, event | category | flops | bytes accessed | tf_op | source)
XLA Modules:
  0.0 2433.1 jit_solution(3155377845071003227)
XLA Ops:
  12.9 4.0 convert_element_type.158
  19.0 96.6 %all-gather.18.cloned.1.call-done = bf16[2,4096,384]{1,2,0:T(8,128)(2,1)} async-done(((bf16[2,512,384]{1,2,0:T(8,128)(2,1)}), bf16[2,4096,384]{1,2,0:T(8,128)(2,1)}) %all-gather.18.cloned.1.call-update) | async-done | bytes 6291472 | tf_op jit(solution)/shard_map/all_gather | solution.py:248
  115.6 5.4 fusion.65
  121.1 39.2 %all-gather.3 = bf16[8,192,2]{1,2,0:T(2,128)(2,1)S(1)} all-gather(bf16[1,192,2]{1,2,0:T(2,128)(2,1)S(1)} %convert_bitcast_fusion), channel_id=1, replica_groups=mesh['seq'=8,'tp'=4] {'seq'}, dimensions={0}, use_global_device_ids=true | all-gather | bytes 6912 | tf_op jit(solution)/shard_map/all_gather | solution.py:251
  160.9 317.7 %all-gather.14.cloned.1.call-done = bf16[1024,9216]{1,0:T(8,128)(2,1)} async-done(((bf16[128,9216]{1,0:T(8,128)(2,1)}), bf16[1024,9216]{1,0:T(8,128)(2,1)}) %all-gather.14.cloned.1.call-update) | async-done | bytes 18874384 | tf_op jit(solution)/shard_map/all_gather | solution.py:252
  478.6 7.7 fusion.123
  486.3 3.9 fusion.86
  495.1 51.4 %all-gather.16.cloned.1.call-done = bf16[3,1536,384]{2,1,0:T(8,128)(2,1)} async-done(((bf16[3,192,384]{2,1,0:T(8,128)(2,1)}), bf16[3,1536,384]{2,1,0:T(8,128)(2,1)}) %all-gather.16.cloned.1.call-update) | async-done | bytes 3538960 | tf_op jit(solution)/shard_map/all_gather | solution.py:246
  552.8 18.8 all-gather.2
  576.7 33.9 %all-gather.20.cloned.1.call-done = bf16[2,2048,384]{1,2,0:T(8,128)(2,1)} async-done(((bf16[2,256,384]{1,2,0:T(8,128)(2,1)}), bf16[2,2048,384]{1,2,0:T(8,128)(2,1)}) %all-gather.20.cloned.1.call-update) | async-done | bytes 3145744 | tf_op jit(solution)/shard_map/all_gather | solution.py:281
  610.6 4.0 fusion.115
  614.8 11.3 fusion.119
  626.1 29.6 %all-gather.28.cloned.1.call-done = bf16[1,2048,384]{2,1,0:T(8,128)(2,1)} async-done(((bf16[1,256,384]{2,1,0:T(8,128)(2,1)}), bf16[1,2048,384]{2,1,0:T(8,128)(2,1)}) %all-gather.28.cloned.1.call-update) | async-done | bytes 1572880 | tf_op jit(solution)/shard_map/all_gather | solution.py:297
  655.6 45.6 %all-gather.30.cloned.1.call-done = bf16[1,2048,384]{2,1,0:T(8,128)(2,1)} async-done(((bf16[1,256,384]{2,1,0:T(8,128)(2,1)}), bf16[1,2048,384]{2,1,0:T(8,128)(2,1)}) %all-gather.30.cloned.1.call-update) | async-done | bytes 1572880 | tf_op jit(solution)/shard_map/all_gather | solution.py:298
  701.3 22.4 conditional.2
  705.2 4.0 fusion
  709.2 4.2 fusion.2
  716.3 7.3 fusion.6
  724.4 8.0 fusion.78
  732.5 11.5 all-gather.22.cloned.1.call-done
  751.5 28.8 %all-reduce.9.cloned.1.call-done = bf16[256,1536]{1,0:T(8,128)(2,1)} async-done(((bf16[256,1536]{1,0:T(8,128)(2,1)}), bf16[256,1536]{1,0:T(8,128)(2,1)}) %all-reduce.9.cloned.1.call-update) | async-done | bytes 786448 | tf_op jit(solution)/shard_map/psum | solution.py:325
  786.7 95.5 %all-gather.24.cloned.1.call-done = bf16[2,1536,1024]{2,1,0:T(8,128)(2,1)} async-done(((bf16[2,192,1024]{2,1,0:T(8,128)(2,1)}), bf16[2,1536,1024]{2,1,0:T(8,128)(2,1)}) %all-gather.24.cloned.1.call-update) | async-done | bytes 6291472 | tf_op jit(solution)/shard_map/all_gather | solution.py:249
  882.2 4.1 fusion.27
  886.3 3.9 fusion.26
  890.3 53.2 %all-gather.26.cloned.1.call-done = bf16[1024,1536]{0,1:T(8,128)(2,1)} async-done(((bf16[1024,192]{0,1:T(8,128)(2,1)}), bf16[1024,1536]{0,1:T(8,128)(2,1)}) %all-gather.26.cloned.1.call-update) | async-done | bytes 3145744 | tf_op jit(solution)/shard_map/all_gather | solution.py:250
  943.5 5.3 fusion.75
  949.7 5.5 fusion.33
  955.3 33.3 %all-reduce.11.cloned.1.call-done = bf16[256,1536]{1,0:T(8,128)(2,1)} async-done(((bf16[256,1536]{1,0:T(8,128)(2,1)}), bf16[256,1536]{1,0:T(8,128)(2,1)}) %all-reduce.11.cloned.1.call-update) | async-done | bytes 786448 | tf_op jit(solution)/shard_map/psum | solution.py:355
  991.6 3.8 multiply_convert_fusion.2
  997.9 44.1 %conditional.3 = (f32[256,6,64]{0,2,1:T(8,128)S(1)}, f32[1,2048,384]{2,1,0:T(8,128)}, f32[1,2048,384]{2,1,0:T(8,128)}) conditional(s32[]{:T(128)} %bitcast.13, f32[256,6,64]{0,2,1:T(8,128)S(1)} %broadcast_in_dim.101, (bf16[256]{0:T(256)(128)(2,1)S(1)}, bf16[2048]{0:T(1024)(128)(2,1)S(1)}, bf16[2048,384]{1,0:T(8,128)(2,1)}, ...), branch_computations={%region_12.13_spmd, %region_13.14_spmd} | conditional | flops 2046427136 | bytes 99924592 | solution.py:181
  1001.0 7.8 fusion.122
  1012.6 8.4 multiply_convert_fusion
  1029.4 9.0 fusion.13
  1042.0 5.9 pad_maximum_fusion
  1048.2 4.1 convolution_convert_fusion
  1052.3 11.4 multiply_reduce_fusion.1
  1064.8 6.1 multiply_convert_fusion.1
  1075.4 7.9 fusion.28
  1083.3 82.8 %reduce-scatter.12.cloned.1.call-done = f32[2,256,384]{2,1,0:T(8,128)} async-done(((f32[2,2048,384]{2,1,0:T(8,128)}), f32[2,256,384]{2,1,0:T(8,128)}) %reduce-scatter.12.cloned.1.call-update) | async-done | bytes 786448 | tf_op jit(solution)/shard_map/reduce_scatter | solution.py:415
  1167.3 4.2 fusion.32
  1171.6 4.1 convolution_multiply_fusion.2
  1183.0 5.5 fusion.103
  1188.5 7.9 convolution_bitcast_fusion.1
  1196.4 19.5 copy.174
  1223.9 5.4 convolution_bitcast_fusion.2
  1229.3 10.9 copy.202
  1240.2 7.3 copy.214
  1247.6 88.2 %reduce-scatter.16.cloned.1.call-done = f32[2,256,384]{1,2,0:T(8,128)} async-done(((f32[2,2048,384]{1,2,0:T(8,128)}), f32[2,256,384]{1,2,0:T(8,128)}) %reduce-scatter.16.cloned.1.call-update) | async-done | bytes 786448 | tf_op jit(solution)/shard_map/reduce_scatter | solution.py:416
  1335.8 7.5 convolution_bitcast_fusion
  1347.9 60.0 %reduce-scatter.14.cloned.1.call-done = f32[384,192]{0,1:T(8,128)} async-done(((f32[384,1536]{0,1:T(8,128)}), f32[384,192]{0,1:T(8,128)}) %reduce-scatter.14.cloned.1.call-update) | async-done | bytes 294928 | tf_op jit(solution)/shard_map/reduce_scatter | solution.py:461
  1409.5 118.8 %reduce-scatter.20.cloned.1.call-done = f32[1024,192]{0,1:T(8,128)} async-done(((f32[1024,1536]{0,1:T(8,128)}), f32[1024,192]{0,1:T(8,128)}) %reduce-scatter.20.cloned.1.call-update) | async-done | bytes 786448 | tf_op jit(solution)/shard_map/reduce_scatter | solution.py:464
  1530.3 398.8 %all-reduce.13.cloned.1.call-done = f32[2,1536,1024]{2,0,1:T(2,128)} async-done(((f32[2,1536,1024]{2,0,1:T(2,128)}), f32[2,1536,1024]{2,0,1:T(2,128)}) %all-reduce.13.cloned.1.call-update) | async-done | bytes 12582928
  1929.1 4.9 multiply_reduce_fusion.5
  1934.0 4.6 fusion.41
  1942.4 3.8 fusion.53
  1946.2 6.8 fusion.85
  1953.0 38.4 %all-reduce.16 = (bf16[8,9216]{1,0:T(8,128)(2,1)S(1)}, f32[6]{0:T(128)S(1)}) all-reduce(f32[8,9216]{1,0:T(8,128)S(1)} %fusion.85, f32[6]{0:T(128)S(1)} %subtract_multiply_fusion), channel_id=1, replica_groups=mesh['seq'=8,'tp'=4] {'seq'}, use_global_device_ids=true, to_apply=%region_33.34 | all-reduce | flops 73734 | bytes 442416 | tf_op jit(solution)/shard_map/psum | solution.py:454
  1992.6 4.3 multiply_reduce_fusion.2
  1999.8 127.0 %reduce-scatter.22.cloned.1.call-done = f32[192,1152]{1,0:T(8,128)} async-done(((f32[1536,1152]{1,0:T(8,128)}), f32[192,1152]{1,0:T(8,128)}) %reduce-scatter.22.cloned.1.call-update) | async-done | bytes 884752
  2133.2 204.3 %reduce-scatter.18.cloned.1.call-done = f32[2,512,384]{1,2,0:T(8,128)} async-done(((f32[2,4096,384]{1,2,0:T(8,128)}), f32[2,512,384]{1,2,0:T(8,128)}) %reduce-scatter.18.cloned.1.call-update) | async-done | bytes 1572880 | tf_op jit(solution)/shard_map/reduce_scatter | solution.py:462
  2344.9 39.3 %psum.55 = f32[]{:T(128)} all-reduce(f32[]{:T(128)S(6)} %add.280), channel_id=1, replica_groups=mesh['seq'=8,'tp'=4] {'seq','tp'}, use_global_device_ids=true, to_apply=%region_37.38 | all-reduce | flops 1 | bytes 8 | tf_op jit(solution)/shard_map/psum | solution.py:478
  2385.0 5.9 multiply_subtract_fusion.2
  2400.6 3.7 multiply_subtract_fusion.3
  2404.8 13.0 multiply_subtract_fusion
  (279 shorter events, 131.7 us)
Async XLA Ops:
  7.2 108.4 %copy-start = (bf16[256,4096]{1,0:T(8,128)(2,1)S(1)}, bf16[256,4096]{1,0:T(8,128)(2,1)}, u32[]{:S(2)}) copy-start(bf16[256,4096]{1,0:T(8,128)(2,1)} %param.34) | copy-start | bytes 6291460
  7.2 108.4 %all-gather.18.cloned.1.call-start = ((), (), s32[]{:S(2)}) async-start(), calls=%async_computation.9 | async-start | bytes 7077888 | tf_op jit(solution)/shard_map/all_gather | solution.py:248
  12.8 465.7 %all-gather.14.cloned.1.call-start = ((), (), s32[]{:S(2)}) async-start(), calls=%async_computation.7 | async-start | bytes 21233664 | tf_op jit(solution)/shard_map/all_gather | solution.py:252
  16.9 529.6 %all-gather.16.cloned.1.call-start = ((), (), s32[]{:S(2)}) async-start(), calls=%async_computation.8 | async-start | bytes 3981312 | tf_op jit(solution)/shard_map/all_gather | solution.py:246
  18.9 102.1 %copy-start.58 = (f32[2,192]{1,0:T(2,128)S(1)}, f32[2,192]{1,0:T(2,128)}, u32[]{:S(2)}) copy-start(f32[2,192]{1,0:T(2,128)} %param.41) | copy-start | bytes 4612
  18.9 141.4 %copy-start.66 = (f32[8]{0:T(128)S(1)}, f32[8]{0:T(128)}, u32[]{:S(2)}) copy-start(f32[8]{0:T(128)} %param.35) | copy-start | bytes 100
  18.9 141.7 %copy-start.8 = (bf16[256,1536]{1,0:T(8,128)(2,1)S(1)}, bf16[256,1536]{1,0:T(8,128)(2,1)}, u32[]{:S(2)}) copy-start(bf16[256,1536]{1,0:T(8,128)(2,1)} %param.33) | copy-start | bytes 2359300
  19.0 591.7 %all-gather.20.cloned.1.call-start = ((), (), s32[]{:S(2)}) async-start(), calls=%async_computation.10 | async-start | bytes 3538944 | tf_op jit(solution)/shard_map/all_gather | solution.py:281
  121.0 534.6 %all-gather.28.cloned.1.call-start = ((), (), s32[]{:S(2)}) async-start(), calls=%async_computation.21 | async-start | bytes 1769472 | tf_op jit(solution)/shard_map/all_gather | solution.py:297
  160.6 325.7 %copy-start.53 = (bf16[8,1024]{1,0:T(8,128)(2,1)}, bf16[8,1024]{1,0:T(8,128)(2,1)S(1)}, u32[]{:S(2)}) copy-start(bf16[8,1024]{1,0:T(8,128)(2,1)S(1)} %multiply_convert_fusion.9) | copy-start | bytes 49156
  160.6 329.5 %copy-start.51 = (f32[1536]{0:T(1024)}, f32[1536]{0:T(1024)S(1)}, u32[]{:S(2)}) copy-start(f32[1536]{0:T(1024)S(1)} %get-tuple-element.390) | copy-start | bytes 18436
  160.9 329.3 %copy-start.56 = (f32[256]{0:T(256)}, f32[256]{0:T(256)S(1)}, u32[]{:S(2)}) copy-start(f32[256]{0:T(256)S(1)} %add_rsqrt_fusion.1) | copy-start | bytes 3076
  160.9 325.4 %copy-start.54 = (s32[256]{0:T(256)S(1)}, s32[256]{0:T(256)}, u32[]{:S(2)}) copy-start(s32[256]{0:T(256)} %param.36) | copy-start | bytes 3076
  490.1 3.6 copy-start.1
  495.1 56.3 %copy-start.33 = (f32[384,192]{0,1:T(8,128)S(1)}, f32[384,192]{0,1:T(8,128)}, u32[]{:S(2)}) copy-start(f32[384,192]{0,1:T(8,128)} %param.47) | copy-start | bytes 884740
  550.8 150.5 %all-gather.30.cloned.1.call-start = ((), (), s32[]{:S(2)}) async-start(), calls=%async_computation.22 | async-start | bytes 1769472 | tf_op jit(solution)/shard_map/all_gather | solution.py:298
  551.4 192.6 %all-gather.22.cloned.1.call-start = ((), (), s32[]{:S(2)}) async-start(), calls=%async_computation.11 | async-start | bytes 1327104 | tf_op jit(solution)/shard_map/all_gather | solution.py:247
  552.1 228.2 %all-reduce.9.cloned.1.call-start = ((), (), s32[]{:S(2)}) async-start(), calls=%async_computation.12 | async-start | bytes 1572864 | tf_op jit(solution)/shard_map/psum | solution.py:325
  614.7 86.5 %copy-start.46 = (f32[6,256,64]{1,2,0:T(8,128)S(1)}, f32[6,256,64]{1,2,0:T(8,128)}, u32[]{:S(2)}) copy-start(f32[6,256,64]{1,2,0:T(8,128)} %broadcast_in_dim.97) | copy-start | bytes 1179652
  705.2 4.0 copy-start.19
  709.2 4.6 copy-start.6
  732.5 16.7 copy-start.37
  746.7 135.5 %all-gather.24.cloned.1.call-start = ((), (), s32[]{:S(2)}) async-start(), calls=%async_computation.13 | async-start | bytes 7077888 | tf_op jit(solution)/shard_map/all_gather | solution.py:249
  749.2 194.2 %all-gather.26.cloned.1.call-start = ((), (), s32[]{:S(2)}) async-start(), calls=%async_computation.14 | async-start | bytes 3538944 | tf_op jit(solution)/shard_map/all_gather | solution.py:250
  751.2 237.4 %all-reduce.11.cloned.1.call-start = ((), (), s32[]{:S(2)}) async-start(), calls=%async_computation.15 | async-start | bytes 1572864 | tf_op jit(solution)/shard_map/psum | solution.py:355
  882.2 4.2 copy-start.21
  955.2 210.9 %reduce-scatter.12.cloned.1.call-start = ((), (), s32[]{:S(2)}) async-start(), calls=%async_computation.16 | async-start | bytes 7077888 | tf_op jit(solution)/shard_map/reduce_scatter | solution.py:415
  991.6 4.7 copy-start.36
  1000.9 7.9 copy-start.30
  1000.9 7.9 copy-start.45
  1012.6 8.4 copy-start.7
  1048.0 168.5 %all-reduce.15.cloned.1.call-start = ((), (), s32[]{:S(2)}) async-start(), calls=%async_computation.26 | async-start | bytes 3145728 | tf_op jit(solution)/shard_map/psum | solution.py:335
  1048.2 4.1 copy-start.28
  1048.2 15.5 slice-start
  1052.3 11.4 slice-start.1
  1052.3 12.4 slice-start.2
  1064.8 6.1 copy-start.15
  1171.5 164.3 %reduce-scatter.16.cloned.1.call-start = ((), (), s32[]{:S(2)}) async-start(), calls=%async_computation.18 | async-start | bytes 7077888 | tf_op jit(solution)/shard_map/reduce_scatter | solution.py:416
  1171.6 4.2 copy-start.23
  1178.8 229.0 %reduce-scatter.14.cloned.1.call-start = ((), (), s32[]{:S(2)}) async-start(), calls=%async_computation.17 | async-start | bytes 2654208 | tf_op jit(solution)/shard_map/reduce_scatter | solution.py:461
  1182.9 345.4 %reduce-scatter.20.cloned.1.call-start = ((), (), s32[]{:S(2)}) async-start(), calls=%async_computation.20 | async-start | bytes 7077888 | tf_op jit(solution)/shard_map/reduce_scatter | solution.py:464
  1188.5 740.6 %all-reduce.13.cloned.1.call-start = ((), (), s32[]{:S(2)}) async-start(), calls=%async_computation.25 | async-start | bytes 25165824
  1216.0 780.9 %reduce-scatter.24.cloned.1.call-start = ((), (), s32[]{:S(2)}) async-start(), calls=%async_computation.24 | async-start | bytes 884736
  1219.1 4.8 copy-start.41
  1223.8 903.0 %reduce-scatter.22.cloned.1.call-start = ((), (), s32[]{:S(2)}) async-start(), calls=%async_computation.23 | async-start | bytes 7962624
  1247.6 1089.9 %reduce-scatter.18.cloned.1.call-start = ((), (), s32[]{:S(2)}) async-start(), calls=%async_computation.19 | async-start | bytes 14155776 | tf_op jit(solution)/shard_map/reduce_scatter | solution.py:462
  1343.3 4.4 copy-start.29
  1343.3 4.4 copy-start.48
  1343.3 4.5 copy-start.63
  1929.1 4.9 copy-start.12
  1929.1 4.9 copy-start.16
  1929.1 4.9 copy-start.22
  1934.0 4.6 copy-start.10
  1942.4 3.8 copy-start.55
  2400.6 3.7 copy-start.64
  2400.6 3.7 copy-start.65
  2404.8 13.0 copy-start.17
  2404.8 13.0 copy-start.18
  2404.8 13.0 copy-start.31
  2404.8 13.0 copy-start.32
  2417.9 3.5 copy-start.34
  2417.9 3.5 copy-start.35
  2417.9 4.6 copy-start.39
  2417.9 4.5 copy-start.40
  (27 other events, 58.8 us)
Sparse Core Ops, SparseCore 0:
  13.0 102.6 all-gather.17
  117.7 360.7 all-gather.13
  481.3 65.1 all-gather.15
  549.0 61.6 all-gather.19
  613.2 42.3 all-gather.27
  658.3 42.9 all-gather.29
  704.0 39.8 all-gather.21
  746.9 33.3 all-reduce.8
  783.1 99.0 all-gather.23
  884.8 58.6 all-gather.25
  955.3 33.2 all-reduce.10
  1048.1 117.9 reduce-scatter.11
  1171.6 42.2 all-reduce.14
  1217.4 118.3 reduce-scatter.15
  1339.7 68.1 reduce-scatter.13
  1411.3 116.9 reduce-scatter.19
  1532.3 396.7 all-reduce.12
  1933.2 61.9 reduce-scatter.23
  1998.8 127.9 reduce-scatter.21
  2130.7 206.7 reduce-scatter.17
where the time goes:
time: 2440 us; the launch traced here: 2430 us
  waiting for transfers between devices  1880 us (77%)
  matrix products  178 us (7%)
  blocking collectives  136 us (6%)
  other arithmetic  113 us (5%)
  local copies, waits for them, and re-layouts  101 us (4%)
  between operations  25.6 us (1%)
    unnamed x23, waiting for transfers between devices  527 us
    all_gather x1, waiting for transfers between devices, per_device(): lax.all_gather(mod_weight.astype(jnp.bfloat16), 'seq', axis=0, tiled=True)  318 us
    reduce_scatter x1, waiting for transfers between devices, per_device(): lax.psum_scatter(text_weight_grad, 'seq', scatter_dimension=1, tiled=True)  204 us
    reduce_scatter x1, waiting for transfers between devices, per_device(): lax.psum_scatter(down_grad, 'seq', scatter_dimension=1, tiled=True)  119 us
    all_gather x1, waiting for transfers between devices, per_device(): lax.all_gather(text_weight.astype(jnp.bfloat16), 'seq', axis=1, tiled=True)  96.6 us
    all_gather x1, waiting for transfers between devices, per_device(): lax.all_gather(updown_weight.astype(jnp.bfloat16), 'seq', axis=1, tiled=T...  95.5 us
    reduce_scatter x1, waiting for transfers between devices, per_device(): lax.psum_scatter(text_kv_part, 'seq', scatter_dimension=1, tiled=True)  88.2 us
    reduce_scatter x1, waiting for transfers between devices, per_device(): lax.psum_scatter(self_kv_part, 'seq', scatter_dimension=1, tiled=True)  82.8 us
  transfers between devices with their start and end apart: 20, of which 18 were waited for; matrix products, arithmetic and copies ran while one was open for 10% of the time, Pallas kernels for 0%

commit v1 on v0

v1 whole, which is shorter than its diff:
```python
import functools
import math

import jax
import jax.numpy as jnp
from jax import lax
from jax.experimental import pallas as pl
from jax.experimental.pallas import tpu as pltpu
from jax.sharding import PartitionSpec as P

HD = 64
TE = 1024
TEXT = 256
ITEMS = 8
ADAM_STEP = 10

bf16 = jnp.bfloat16
f32 = jnp.float32
highest = lax.Precision.HIGHEST
eps_norm = 1e-06
masked_score = -1e30
lowest_max = -1e20
clip_limit = 1.0
beta_first = 0.9
beta_second = 0.95
adam_eps = 1e-08
rate_matrix = 0.05
rate_small = 0.5
decay_matrix = 0.1
score_scale = HD ** (-0.5)

CORE_SWAP = [(0, 1), (1, 0), (2, 3), (3, 2)]
Y_SWAP = [(0, 2), (2, 0), (1, 3), (3, 1)]
CYCLE = (0, 2, 4, 6, 7, 5, 3, 1)


def time_embed(timesteps):
    half_width = TE // 2
    frequency = jnp.exp(-math.log(10000.0) * jnp.arange(half_width, dtype=f32) / half_width)
    angles = 1000.0 * timesteps[:, None] * frequency[None, :]
    return jnp.concatenate([jnp.cos(angles), jnp.sin(angles)], axis=1)


def rms_parts(values):
    inverse = lax.rsqrt(jnp.mean(values * values, axis=-1, keepdims=True) + eps_norm)
    return (values * inverse, inverse)


def rms_back(normed, inverse, normed_grad):
    return inverse * (normed_grad - normed * jnp.mean(normed_grad * normed, axis=-1, keepdims=True))


def adam_update(weight, first, second, grad, clip, rate, decay):
    clipped = grad * clip
    first_new = beta_first * first + (1.0 - beta_first) * clipped
    second_new = beta_second * second + (1.0 - beta_second) * clipped * clipped
    first_hat = first_new / (1.0 - beta_first**ADAM_STEP)
    second_hat = second_new / (1.0 - beta_second**ADAM_STEP)
    weight_new = weight - rate * (first_hat / (jnp.sqrt(second_hat) + adam_eps) + decay * weight)
    return (weight_new, first_new, second_new)


def square_sum(values):
    return jnp.sum(values * values)


def dot(a, b, dims):
    return lax.dot_general(a, b, (dims, ((), ())), preferred_element_type=f32)


class Ring:
    def __init__(self, size):
        self.size = size
        self.ring = size == len(CYCLE)
        self.seq = lax.axis_index("seq")
        if self.ring:
            place_of = [CYCLE.index(s) for s in range(size)]
            self.place = jnp.asarray(place_of, jnp.int32)[self.seq]
            self.cycle = jnp.asarray(CYCLE + CYCLE, jnp.int32)

    def at(self, offset):
        return self.cycle[self.place + offset % self.size]

    def pairs(self, step, sends=None):
        n = self.size
        return [
            (CYCLE[p], CYCLE[(p + step) % n]) for p in range(n) if sends is None or sends(p)
        ]

    def hop(self, value, step, sends=None):
        return lax.ppermute(value, "seq", self.pairs(step, sends))

    def gather_rows(self, own):
        if not self.ring:
            return lax.all_gather(own, "seq", axis=0, tiled=True)
        rows = own.shape[0]
        half = rows // 2
        whole = jnp.zeros((self.size * rows, own.shape[1]), own.dtype)

        def put(whole, part, offset, start):
            return lax.dynamic_update_slice(whole, part, (self.at(offset) * rows + start, 0))

        whole = put(whole, own, 0, 0)
        ahead = behind = own
        for k in range(1, 4):
            ahead = self.hop(ahead, 1)
            behind = self.hop(behind, -1)
            whole = put(whole, ahead, -k, 0)
            whole = put(whole, behind, k, 0)
        whole = put(whole, self.hop(ahead[:half], 1), 4, 0)
        return put(whole, self.hop(behind[half:], -1), 4, half)

    def reduce_rows(self, chunk_of, active=None):
        if not self.ring:
            chunks = jnp.concatenate([chunk_of(s).astype(bf16) for s in range(self.size)], 0)
            return lax.psum_scatter(chunks, "seq", scatter_dimension=0, tiled=True).astype(f32)

        def sends(k):
            if active is None:
                return None
            return lambda p: CYCLE[(p + k) % self.size] in active

        ahead = chunk_of(self.at(4)).astype(bf16)
        behind = chunk_of(self.at(-3)).astype(bf16)
        for k in (3, 2, 1):
            moved = self.hop(ahead, 1, sends(k + 1))
            ahead = (moved.astype(f32) + chunk_of(self.at(k))).astype(bf16)
            if k > 1:
                moved = self.hop(behind, -1, sends(-k))
                behind = (moved.astype(f32) + chunk_of(self.at(1 - k))).astype(bf16)
        ahead = self.hop(ahead, 1, sends(1))
        behind = self.hop(behind, -1, sends(-1))
        return chunk_of(self.at(0)) + ahead.astype(f32) + behind.astype(f32)


def butterfly(value, axis, size):
    step = 1
    while step < size:
        value = value + lax.ppermute(value, axis, [(i, i ^ step) for i in range(size)])
        step *= 2
    return value


def join_pair(second, mine, other, axis):
    low = jnp.where(second, other, mine)
    high = jnp.where(second, mine, other)
    return jnp.concatenate([low, high], axis)


def gather_tp(value, axis):
    tp = lax.axis_index("tp")
    pair = join_pair(tp % 2 == 1, value, lax.ppermute(value, "tp", CORE_SWAP), axis)
    return join_pair(tp >= 2, pair, lax.ppermute(pair, "tp", Y_SWAP), axis)


def psum_tp(part):
    second = lax.axis_index("tp") % 2
    part = part.astype(bf16)
    half = part.shape[0] // 2
    mine = lax.dynamic_slice_in_dim(part, second * half, half, 0)
    other = lax.dynamic_slice_in_dim(part, (1 - second) * half, half, 0)
    mine = (mine.astype(f32) + lax.ppermute(other, "tp", CORE_SWAP).astype(f32)).astype(bf16)
    mine = (mine.astype(f32) + lax.ppermute(mine, "tp", Y_SWAP).astype(f32)).astype(bf16)
    return join_pair(second == 1, mine, lax.ppermute(mine, "tp", CORE_SWAP), 0).astype(f32)


def attend_kernel(
    table, gate, q_ref, k_ref, vt_ref, tk_ref, tvt_ref, sq_ref, sk_ref,
    mixed_ref, self_ref, text_ref, stats_ref, *, block_k,
):
    i = pl.program_id(0)
    q = q_ref[...]
    item_of_q = sq_ref[...]
    width = q.shape[0]

    def self_step(j, carry):
        top, total, out = carry
        at = pl.ds(pl.multiple_of(j * block_k, block_k), block_k)
        scores = dot(k_ref[at, :], q, ((1,), (1,)))
        scores = jnp.where(sk_ref[at, :] == item_of_q, scores, masked_score)
        new_top = jnp.maximum(top, jnp.max(scores, axis=0, keepdims=True))
        weights = jnp.exp(scores - new_top)
        shrink = jnp.exp(top - new_top)
        total = total * shrink + jnp.sum(weights, axis=0, keepdims=True)
        out = out * shrink + dot(vt_ref[:, at], weights.astype(bf16), ((1,), (0,)))
        return (new_top, total, out)

    start = (
        jnp.full((1, width), lowest_max, f32),
        jnp.zeros((1, width), f32),
        jnp.zeros((HD, width), f32),
    )
    top, total, out = lax.fori_loop(table[0, i], table[1, i], self_step, start)
    self_out = out / total
    self_ref[...] = self_out
    stats_ref[0:1, :] = top + jnp.log(total)

    def text_step(item, carry):
        out, stat = carry
        at = pl.ds(pl.multiple_of(item * TEXT, TEXT), TEXT)
        scores = dot(tk_ref[at, :], q, ((1,), (1,)))
        top = jnp.max(scores, axis=0, keepdims=True)
        weights = jnp.exp(scores - top)
        total = jnp.sum(weights, axis=0, keepdims=True)
        probs = (weights / total).astype(bf16)
        part = dot(tvt_ref[:, at], probs, ((1,), (0,)))
        here = item_of_q == item
        return (jnp.where(here, part, out), jnp.where(here, top + jnp.log(total), stat))

    start = (jnp.zeros((HD, width), f32), jnp.zeros((1, width), f32))
    text_out, text_stat = lax.fori_loop(table[2, i], table[3, i], text_step, start)
    text_ref[...] = text_out
    stats_ref[1:2, :] = text_stat
    mixed_ref[...] = jnp.transpose(self_out + gate[0] * text_out).astype(bf16)


def attend_back_kernel(
    table, gate, q_ref, g_ref, k_ref, v_ref, kt_ref, tk_ref, tv_ref, tkt_ref,
    self_ref, text_ref, stats_ref, sq_ref, sk_ref,
    dq_ref, dk_ref, dv_ref, tdk_ref, tdv_ref, cross_ref,
    dk_sum, dv_sum, tdk_sum, tdv_sum, *, block_k,
):
    i = pl.program_id(0)

    @pl.when(i == 0)
    def _():
        dk_sum[...] = jnp.zeros_like(dk_sum)
        dv_sum[...] = jnp.zeros_like(dv_sum)
        tdk_sum[...] = jnp.zeros_like(tdk_sum)
        tdv_sum[...] = jnp.zeros_like(tdv_sum)

    q = q_ref[...]
    g = g_ref[...]
    item_of_q = sq_ref[...]
    g_value = g.astype(f32)
    gt_value = (g_value * gate[0]).astype(bf16)
    g_turned = jnp.transpose(g_value)
    gt_turned = jnp.transpose(gt_value.astype(f32))
    text_out = text_ref[...]
    cross_ref[...] = jnp.sum(g_turned * text_out, axis=0, keepdims=True)
    delta = jnp.sum(g_turned * self_ref[...], axis=0, keepdims=True)
    text_delta = jnp.sum(gt_turned * text_out, axis=0, keepdims=True)
    stat = stats_ref[0:1, :]
    text_stat = stats_ref[1:2, :]

    def self_step(j, total):
        at = pl.ds(pl.multiple_of(j * block_k, block_k), block_k)
        scores = dot(k_ref[at, :], q, ((1,), (1,)))
        allowed = sk_ref[at, :] == item_of_q
        probs = jnp.exp(jnp.where(allowed, scores - stat, masked_score))
        prob_grad = dot(v_ref[at, :], g, ((1,), (1,)))
        score_grad = (probs * (prob_grad - delta)).astype(bf16)
        dk_sum[at, :] += dot(score_grad, q, ((1,), (0,)))
        dv_sum[at, :] += dot(probs.astype(bf16), g, ((1,), (0,)))
        return total + dot(kt_ref[:, at], score_grad, ((1,), (0,)))

    total = lax.fori_loop(
        table[0, i], table[1, i], self_step, jnp.zeros((HD, q.shape[0]), f32)
    )

    def text_step(item, total):
        at = pl.ds(pl.multiple_of(item * TEXT, TEXT), TEXT)
        scores = dot(tk_ref[at, :], q, ((1,), (1,)))
        probs = jnp.exp(jnp.where(item_of_q == item, scores - text_stat, masked_score))
        prob_grad = dot(tv_ref[at, :], gt_value, ((1,), (1,)))
        score_grad = (probs * (prob_grad - text_delta)).astype(bf16)
        tdk_sum[at, :] += dot(score_grad, q, ((1,), (0,)))
        tdv_sum[at, :] += dot(probs.astype(bf16), gt_value, ((1,), (0,)))
        return total + dot(tkt_ref[:, at], score_grad, ((1,), (0,)))

    total = lax.fori_loop(table[2, i], table[3, i], text_step, total)
    dq_ref[...] = jnp.transpose(total * score_scale).astype(bf16)

    @pl.when(i == pl.num_programs(0) - 1)
    def _():
        dk_ref[...] = dk_sum[...].astype(bf16)
        dv_ref[...] = dv_sum[...].astype(bf16)
        tdk_ref[...] = tdk_sum[...].astype(bf16)
        tdv_ref[...] = tdv_sum[...].astype(bf16)


def whole(shape):
    return pl.BlockSpec(shape, lambda i, *_: (0, 0), pipeline_mode=pl.Buffered(1))


def rows_block(block, width):
    return pl.BlockSpec((block, width), lambda i, *_: (i, 0))


def lanes_block(rows, block):
    return pl.BlockSpec((rows, block), lambda i, *_: (0, i))


def attention_table(segments, block_q, block_k):
    by_block = segments.reshape(-1, block_q)
    low_item, high_item = by_block[:, 0], by_block[:, -1]
    first_key = jnp.sum(segments[None, :] < low_item[:, None], axis=1)
    end_key = jnp.sum(segments[None, :] <= high_item[:, None], axis=1)
    return jnp.stack(
        [first_key // block_k, (end_key + block_k - 1) // block_k, low_item, high_item + 1]
    ).astype(jnp.int32)


def attend(table, gate, q, k, vt, tk, tvt, segments, block_q, block_k):
    count, rows = q.shape[0], tk.shape[0]
    return pl.pallas_call(
        functools.partial(attend_kernel, block_k=block_k),
        out_shape=(
            jax.ShapeDtypeStruct((count, HD), bf16),
            jax.ShapeDtypeStruct((HD, count), f32),
            jax.ShapeDtypeStruct((HD, count), f32),
            jax.ShapeDtypeStruct((2, count), f32),
        ),
        grid_spec=pltpu.PrefetchScalarGridSpec(
            num_scalar_prefetch=2,
            grid=(count // block_q,),
            in_specs=[
                rows_block(block_q, HD),
                whole((count, HD)),
                whole((HD, count)),
                whole((rows, HD)),
                whole((HD, rows)),
                lanes_block(1, block_q),
                whole((count, 1)),
            ],
            out_specs=(
                rows_block(block_q, HD),
                lanes_block(HD, block_q),
                lanes_block(HD, block_q),
                lanes_block(2, block_q),
            ),
        ),
        cost_estimate=pl.CostEstimate(
            flops=4 * count * count * HD, bytes_accessed=8 * count * HD, transcendentals=count * count
        ),
        name="attend",
    )(table, gate, q, k, vt, tk, tvt, segments[None, :], segments[:, None])


def attend_back(
    table, gate, q, g, k, v, kt, tk, tv, tkt, self_out, text_out, stats, segments, block_q, block_k
):
    count, rows = q.shape[0], tk.shape[0]
    return pl.pallas_call(
        functools.partial(attend_back_kernel, block_k=block_k),
        out_shape=(
            jax.ShapeDtypeStruct((count, HD), bf16),
            jax.ShapeDtypeStruct((count, HD), bf16),
            jax.ShapeDtypeStruct((count, HD), bf16),
            jax.ShapeDtypeStruct((rows, HD), bf16),
            jax.ShapeDtypeStruct((rows, HD), bf16),
            jax.ShapeDtypeStruct((1, count), f32),
        ),
        grid_spec=pltpu.PrefetchScalarGridSpec(
            num_scalar_prefetch=2,
            grid=(count // block_q,),
            in_specs=[
                rows_block(block_q, HD),
                rows_block(block_q, HD),
                whole((count, HD)),
                whole((count, HD)),
                whole((HD, count)),
                whole((rows, HD)),
                whole((rows, HD)),
                whole((HD, rows)),
                lanes_block(HD, block_q),
                lanes_block(HD, block_q),
                lanes_block(2, block_q),
                lanes_block(1, block_q),
                whole((count, 1)),
            ],
            out_specs=(
                rows_block(block_q, HD),
                whole((count, HD)),
                whole((count, HD)),
                whole((rows, HD)),
                whole((rows, HD)),
                lanes_block(1, block_q),
            ),
            scratch_shapes=[
                pltpu.VMEM((count, HD), f32),
                pltpu.VMEM((count, HD), f32),
                pltpu.VMEM((rows, HD), f32),
                pltpu.VMEM((rows, HD), f32),
            ],
        ),
        cost_estimate=pl.CostEstimate(
            flops=10 * count * count * HD, bytes_accessed=24 * count * HD, transcendentals=count * count
        ),
        name="attend_back",
    )(
        table, gate, q, g, k, v, kt, tk, tv, tkt, self_out, text_out, stats,
        segments[None, :], segments[:, None],
    )


def per_device(
    x_tokens, caption, timesteps, segment_ids, out_grad,
    mod_weight, mod_first, mod_second,
    norm_gains, gains_first, gains_second,
    qkv_weight, qkv_first, qkv_second,
    out_weight, out_first, out_second,
    text_weight, text_first, text_second,
    cross_gates, cross_first, cross_second,
    updown_weight, updown_first, updown_second,
    down_weight, down_first, down_second,
    *, seq_size, tp_size,
):
    seq_index = lax.axis_index("seq")
    tp_index = lax.axis_index("tp")
    ring = Ring(seq_size)
    here, width = x_tokens.shape
    heads = cross_gates.shape[0]
    local_width = heads * HD
    count = here * seq_size
    first_owner = 1 if seq_size >= heads + 2 else 0
    owners = range(first_owner, first_owner + heads)
    my_head = jnp.clip(seq_index - first_owner, 0, heads - 1)
    is_owner = (seq_index >= first_owner) & (seq_index < first_owner + heads)

    def to_owners(by_head):
        spare = ((first_owner, seq_size - heads - first_owner), (0, 0), (0, 0))
        out = lax.all_to_all(jnp.pad(by_head, spare), "seq", 0, 0, tiled=True)
        return out.reshape(count, by_head.shape[2])

    def from_owner(rows):
        out = lax.all_to_all(rows.reshape(seq_size, here, -1), "seq", 0, 0, tiled=True)
        return out[first_owner : first_owner + heads]

    slots = jnp.zeros((seq_size, here), f32)
    slots = lax.dynamic_update_slice(slots, segment_ids.astype(f32)[None], (seq_index, 0))
    gain_cols = norm_gains.shape[1]
    gain_slots = jnp.zeros((2, width), f32)
    gain_slots = lax.dynamic_update_slice(gain_slots, norm_gains, (0, seq_index * gain_cols))

    silu_embed = jax.nn.silu(time_embed(timesteps)).astype(bf16)
    mod_rows = mod_weight.shape[0]
    quarter = width // tp_size
    embed_rows = lax.dynamic_slice_in_dim(silu_embed, seq_index * mod_rows, mod_rows, 1)
    mod_quarter = lax.dynamic_slice_in_dim(
        mod_weight.reshape(mod_rows, 6, width), tp_index * quarter, quarter, 2
    ).astype(bf16)
    mod_part = dot(embed_rows, mod_quarter.reshape(mod_rows, 6 * quarter), ((1,), (0,)))
    packed = jnp.concatenate(
        [mod_part.reshape(-1), slots.reshape(-1), gain_slots.reshape(-1)]
    ).reshape(-1, 128)
    packed = butterfly(packed, "seq", seq_size).reshape(-1)
    mod_end = mod_part.size
    modulation = gather_tp(packed[:mod_end].reshape(ITEMS, 6, quarter), 2)
    modulation = modulation.reshape(ITEMS, 6 * width)
    segments = packed[mod_end : mod_end + count].astype(jnp.int32)
    gains_value = packed[mod_end + count :].reshape(2, width).astype(bf16).astype(f32)

    def turned(shard):
        return jnp.transpose(shard.astype(bf16), (1, 0, 2)).reshape(shard.shape[1], -1)

    qkv_all = ring.gather_rows(turned(qkv_weight))

    cap_cols = caption.shape[1] // seq_size
    cap_part = cap_cols // tp_size
    cap_own = lax.dynamic_index_in_dim(
        caption.reshape(here_rows := caption.shape[0], seq_size, tp_size, cap_part),
        tp_index, 2, keepdims=False,
    )
    cap_own = lax.all_to_all(cap_own, "seq", 1, 0, tiled=True)
    text_rows = here_rows * seq_size
    caption_cols = gather_tp(cap_own.reshape(text_rows, cap_part), 1)
    text_by_head = jnp.transpose(
        text_weight.astype(bf16).reshape(2, cap_cols, heads, HD), (2, 1, 0, 3)
    ).reshape(heads, cap_cols, 2 * HD)

    def text_chunk(s):
        head = jnp.clip(s - first_owner, 0, heads - 1)
        return dot(
            caption_cols,
            lax.dynamic_index_in_dim(text_by_head, head, 0, keepdims=False),
            ((1,), (0,)),
        )

    text_kv = ring.reduce_rows(text_chunk, owners).astype(bf16)
    text_keys = text_kv[:, :HD]
    text_values = text_kv[:, HD:]

    out_all = ring.gather_rows(out_weight.astype(bf16).T)
    updown_all = ring.gather_rows(turned(updown_weight))
    down_all = ring.gather_rows(down_weight.astype(bf16).T)
    hidden_units = down_weight.shape[0]

    item_onehot = (segment_ids[:, None] == jnp.arange(ITEMS, dtype=jnp.int32)[None, :]).astype(f32)
    per_token = jnp.dot(item_onehot, modulation, precision=highest, preferred_element_type=f32)
    shift_attn, scale_attn, gate_attn, shift_ffn, scale_ffn, gate_ffn = jnp.split(
        per_token, 6, axis=1
    )
    x_value = x_tokens.astype(f32)
    normed_attn, inverse_attn = rms_parts(x_value)
    hidden_attn = (normed_attn * gains_value[0] * (1.0 + scale_attn) + shift_attn).astype(bf16)
    projected = dot(hidden_attn, qkv_all, ((1,), (0,))).astype(bf16)
    by_head = jnp.transpose(projected.reshape(here, 3, heads, HD), (2, 0, 1, 3))
    head_qkv = to_owners(by_head.reshape(heads, here, 3 * HD))
    queries = head_qkv[:, :HD] * jnp.asarray(score_scale, bf16)
    keys = head_qkv[:, HD : 2 * HD]
    values = head_qkv[:, 2 * HD :]

    block_q = math.gcd(count, 512)
    block_k = math.gcd(count, 512)
    table = attention_table(segments, block_q, block_k)
    tanh_cross = jnp.tanh(cross_gates)
    my_gate = lax.dynamic_slice_in_dim(tanh_cross, my_head, 1)
    mixed_head, self_out, text_out, stats = attend(
        table, my_gate, queries, keys, values.T, text_keys, text_values.T, segments,
        block_q, block_k,
    )
    mixed = jnp.transpose(from_owner(mixed_head), (1, 0, 2)).reshape(here, local_width)
    attn = psum_tp(dot(mixed, out_all, ((1,), (1,))))
    tanh_attn = jnp.tanh(gate_attn)
    x_mid = x_value + tanh_attn * attn
    normed_ffn, inverse_ffn = rms_parts(x_mid)
    hidden_ffn = (normed_ffn * gains_value[1] * (1.0 + scale_ffn) + shift_ffn).astype(bf16)
    both_pre = dot(hidden_ffn, updown_all, ((1,), (0,)))
    gate_pre = both_pre[:, :hidden_units]
    up_pre = both_pre[:, hidden_units:]
    silu_gate = jax.nn.silu(gate_pre)
    inner = (silu_gate * up_pre).astype(bf16)
    ffn_out = psum_tp(dot(inner, down_all, ((1,), (1,))))
    tanh_ffn = jnp.tanh(gate_ffn)
    block_out = x_mid + tanh_ffn * ffn_out

    grad_value = out_grad.astype(f32)
    ffn_grad = (grad_value * tanh_ffn).astype(bf16)
    inner_grad = dot(ffn_grad, down_all, ((1,), (0,)))
    sigmoid_gate = jax.nn.sigmoid(gate_pre)
    gate_grad = (
        inner_grad * up_pre * sigmoid_gate * (1.0 + gate_pre * (1.0 - sigmoid_gate))
    ).astype(bf16)
    up_grad = (inner_grad * silu_gate).astype(bf16)
    both_grads = jnp.concatenate([gate_grad, up_grad], axis=1)
    hidden_ffn_grad = psum_tp(dot(both_grads, updown_all, ((1,), (1,))))

    def slabs(value):
        return jnp.transpose(value.reshape(here, seq_size, -1), (1, 0, 2))

    def slab_product(left_slabs, right):
        return lambda s: dot(
            lax.dynamic_index_in_dim(left_slabs, s, 0, keepdims=False), right, ((0,), (0,))
        )

    down_owned = ring.reduce_rows(slab_product(slabs(ffn_grad), inner)).T
    updown_rows = ring.reduce_rows(slab_product(slabs(hidden_ffn), both_grads))
    mid_grad = grad_value + rms_back(
        normed_ffn, inverse_ffn, hidden_ffn_grad * gains_value[1] * (1.0 + scale_ffn)
    )
    attn_grad = (mid_grad * tanh_attn).astype(bf16)
    mixed_grad = dot(attn_grad, out_all, ((1,), (0,))).astype(bf16)
    out_owned = ring.reduce_rows(slab_product(slabs(attn_grad), mixed)).T
    head_grad = to_owners(jnp.transpose(mixed_grad.reshape(here, heads, HD), (1, 0, 2)))
    query_grad, key_grad, value_grad, text_key_grad, text_value_grad, cross_rows = attend_back(
        table, my_gate, queries, head_grad, keys, values, keys.T, text_keys, text_values,
        text_keys.T, self_out, text_out, stats, segments, block_q, block_k,
    )
    back = from_owner(jnp.concatenate([query_grad, key_grad, value_grad], axis=1))
    qkv_grads = jnp.transpose(back.reshape(heads, here, 3, HD), (1, 2, 0, 3))
    qkv_grads = qkv_grads.reshape(here, 3 * local_width)
    hidden_attn_grad = psum_tp(dot(qkv_grads, qkv_all, ((1,), (1,))))
    qkv_rows = ring.reduce_rows(slab_product(slabs(hidden_attn), qkv_grads))
    text_grads = ring.gather_rows(jnp.concatenate([text_key_grad, text_value_grad], axis=1))
    text_grads = text_grads.reshape(seq_size, text_rows, 2, HD)
    text_grads = text_grads[first_owner : first_owner + heads]
    text_grads = jnp.transpose(text_grads, (1, 2, 0, 3)).reshape(text_rows, 2 * local_width)
    text_cols = dot(caption_cols, text_grads, ((0,), (0,)))

    input_grad = mid_grad + rms_back(
        normed_attn, inverse_attn, hidden_attn_grad * gains_value[0] * (1.0 + scale_attn)
    )

    def part(value):
        return lax.dynamic_slice_in_dim(value, tp_index * quarter, quarter, 1)

    hidden_attn_part = part(hidden_attn_grad)
    hidden_ffn_part = part(hidden_ffn_grad)
    tanh_attn_part = part(tanh_attn)
    tanh_ffn_part = part(tanh_ffn)
    token_mod = jnp.concatenate(
        [
            hidden_attn_part,
            hidden_attn_part * part(normed_attn) * part(gains_value[0:1]),
            part(mid_grad) * part(attn) * (1.0 - tanh_attn_part * tanh_attn_part),
            hidden_ffn_part,
            hidden_ffn_part * part(normed_ffn) * part(gains_value[1:2]),
            part(grad_value) * part(ffn_out) * (1.0 - tanh_ffn_part * tanh_ffn_part),
        ],
        axis=1,
    )
    item_mod_part = lax.dot_general(
        item_onehot, token_mod, (((0,), (0,)), ((), ())),
        precision=highest, preferred_element_type=f32,
    )
    gain_attn_grad = jnp.sum(hidden_attn_grad * normed_attn * (1.0 + scale_attn), axis=0)
    gain_ffn_grad = jnp.sum(hidden_ffn_grad * normed_ffn * (1.0 + scale_ffn), axis=0)
    cross_here = jnp.where(
        is_owner & (jnp.arange(128) == my_head), jnp.sum(cross_rows), 0.0
    )
    packed = jnp.concatenate(
        [item_mod_part.reshape(-1), gain_attn_grad, gain_ffn_grad, cross_here]
    ).reshape(-1, 128)
    packed = butterfly(packed, "seq", seq_size).reshape(-1)
    item_mod_low = packed[:mod_end].reshape(ITEMS, 6 * quarter).astype(bf16)
    gain_grads = packed[mod_end : mod_end + 2 * width].reshape(2, width)
    gains_owned = lax.dynamic_slice_in_dim(gain_grads, seq_index * gain_cols, gain_cols, 1)
    cross_total = packed[mod_end + 2 * width :][:heads] * (1.0 - tanh_cross * tanh_cross)
    item_mod_all = gather_tp(item_mod_low.reshape(ITEMS, 6, quarter), 2).reshape(ITEMS, -1)
    mod_weight_grad = dot(embed_rows, item_mod_all, ((0,), (0,)))
    mod_quarter_grad = dot(embed_rows, item_mod_low, ((0,), (0,)))

    owned_square = (
        square_sum(qkv_rows)
        + square_sum(out_owned)
        + square_sum(text_cols)
        + square_sum(updown_rows)
        + square_sum(down_owned)
        + square_sum(mod_quarter_grad)
    )
    owned_square = owned_square + jnp.where(tp_index == 0, square_sum(gains_owned), 0.0)
    owned_square = owned_square + jnp.where(seq_index == 0, square_sum(cross_total), 0.0)
    total_square = jnp.full((8, 128), owned_square)
    total_square = butterfly(butterfly(total_square, "tp", tp_size), "seq", seq_size)[0, 0]
    grad_norm = jnp.sqrt(total_square)
    clip = jnp.minimum(1.0, clip_limit / (grad_norm + 1e-06))

    def unturned(rows, blocks):
        return jnp.transpose(rows.reshape(rows.shape[0], blocks, -1), (1, 0, 2))

    matrix = functools.partial(adam_update, clip=clip, rate=rate_matrix, decay=decay_matrix)
    small = functools.partial(adam_update, clip=clip, rate=rate_small, decay=0.0)
    return (
        block_out,
        input_grad,
        grad_norm,
        *matrix(mod_weight, mod_first, mod_second, mod_weight_grad),
        *small(norm_gains, gains_first, gains_second, gains_owned),
        *matrix(qkv_weight, qkv_first, qkv_second, unturned(qkv_rows, 3)),
        *matrix(out_weight, out_first, out_second, out_owned),
        *matrix(text_weight, text_first, text_second, unturned(text_cols, 2)),
        *small(cross_gates, cross_first, cross_second, cross_total),
        *matrix(updown_weight, updown_first, updown_second, unturned(updown_rows, 2)),
        *matrix(down_weight, down_first, down_second, down_owned),
    )


def solution(mesh):
    rows = P("seq", None)
    cols = P(None, "seq")
    split = P(None, "seq", "tp")
    turned = P("tp", "seq")
    heads = P("tp")
    weights = (rows,) * 3 + (cols,) * 3 + (split,) * 3 + (turned,) * 3 + (split,) * 3
    weights = weights + (heads,) * 3 + (split,) * 3 + (turned,) * 3
    return jax.shard_map(
        functools.partial(per_device, seq_size=mesh.shape["seq"], tp_size=mesh.shape["tp"]),
        mesh=mesh,
        in_specs=(rows, rows, P(), P("seq"), rows) + weights,
        out_specs=(rows, rows, P()) + weights,
        check_vma=False,
    )
```

time: 2440 us -> 785 us (0.32)
  waiting for transfers between devices: 1880 us -> 166 us
  starting transfers between devices: 1.63 us -> 160 us
  blocking collectives: 136 us -> 0 us
  matrix products: 178 us -> 106 us
  local copies, waits for them, and re-layouts: 101 us -> 149 us
  Pallas kernels: 0 us -> 46.6 us
  between operations: 25.6 us -> 52.4 us
    all_gather x9 -> x0, waiting for transfers between devices: 735 us -> none  [the longest x1 318 us: per_device(): lax.all_gather(mod_weight.astype(jnp.bfloat16), 'seq', axis=0, tiled=True)]
    reduce_scatter x5 -> x0, waiting for transfers between devices: 554 us -> none  [the longest x1 204 us: per_device(): lax.psum_scatter(text_weight_grad, 'seq', scatter_dimension=1, tiled=True)]
    unnamed x23 -> x0, waiting for transfers between devices: 527 us -> none
    ppermute x0 -> x104, waiting for transfers between devices: none -> 163 us  [the longest x75 113 us: hop(): return lax.ppermute(value, 'seq', self.pairs(step, sends))]
    ppermute x0 -> x104, starting transfers between devices: none -> 134 us  [the longest x75 106 us: hop(): return lax.ppermute(value, 'seq', self.pairs(step, sends))]
    psum x2 -> x0, blocking collectives: 77.7 us -> none  [the longest x1 39.3 us: per_device(): total_square = lax.psum(owned_square, ('seq', 'tp'))]
    dot_general x30 -> x53, matrix products: 163 us -> 100 us  [the longest x52 99.2 us: dot(): return lax.dot_general(a, b, (dims, ((), ())), preferred_element_type=f32)]
    psum x3 -> x0, waiting for transfers between devices: 62.2 us -> none  [the longest x1 33.3 us: per_device(): lax.psum(hidden_ffn_part.astype(jnp.bfloat16), 'tp').astype(jnp.float32)]
  transfers between devices with their start and end apart: 20 -> 109, of which waited for: 18 -> 33; matrix products, arithmetic and copies ran while one was open for 10% -> 35% of each run, Pallas kernels for 0% -> 6%
where the time goes in v1:
time: 785 us; the launch traced here: 771 us
  waiting for transfers between devices  166 us (21%)
  starting transfers between devices  160 us (20%)
  local copies, waits for them, and re-layouts  149 us (19%)
  matrix products  106 us (14%)
  other arithmetic  91.1 us (12%)
  between operations  52.4 us (7%)
  Pallas kernels  46.6 us (6%)
    ppermute x75, waiting for transfers between devices, hop(): return lax.ppermute(value, 'seq', self.pairs(step, sends))  113 us
    ppermute x75, starting transfers between devices, hop(): return lax.ppermute(value, 'seq', self.pairs(step, sends))  106 us
    dot_general x52, matrix products, dot(): return lax.dot_general(a, b, (dims, ((), ())), preferred_element_type=f32)  99.2 us
    dynamic_update_slice x43, local copies, waits for them, and re-layouts, put(): lax.dynamic_update_slice(whole, part, (self.at(offset) * rows + start, 0))  49.2 us
    ppermute x11, waiting for transfers between devices, butterfly(): lax.ppermute(value, axis, [(i, i ^ step) for i in range(size)])  36.8 us
    pallas_call x1, Pallas kernels, attend_back(): pl.pallas_call(functools.partial(attend_back_kernel, block_k=block_k), ou...  25.9 us
    pallas_call x1, Pallas kernels, attend(): pl.pallas_call(functools.partial(attend_kernel, block_k=block_k), out_sha...  20.7 us
    unnamed x227, local copies, waits for them, and re-layouts  19 us
  transfers between devices with their start and end apart: 109, of which 33 were waited for; matrix products, arithmetic and copies ran while one was open for 35% of the time, Pallas kernels for 6%

profile of v1, /device:TPU:0, one launch (start us, length us, event | category | flops | bytes accessed | tf_op | source)
XLA Modules:
  0.0 771.5 jit_solution(3282705078603112193)
XLA Ops:
  2.8 3.0 collective-permute-start.5
  23.0 3.6 copy.298
  29.8 3.3 copy.303
  34.2 4.9 all-to-all-start.1
  42.6 3.5 broadcast_in_dim.54
  93.2 13.0 %collective-permute-done.1 = f32[184,128]{1,0:T(8,128)S(1)} collective-permute-done((f32[184,128]{1,0:T(8,128)S(1)}, f32[184,128]{1,0:T(8,128)S(1)}, u32[]{:S(2)}, u32[]{:S(2)}) %collective-permute-start.1) | collective-permute-done | bytes 94240 | tf_op jit(solution)/shard_map/ppermute | solution.py:139
  113.7 3.5 collective-permute-done.2
  125.0 3.8 collective-permute-done.41
  131.1 5.9 collective-permute-done.42
  146.6 9.5 %collective-permute-done.27 = bf16[192,384]{1,0:T(8,128)(2,1)S(1)} collective-permute-done((bf16[192,384]{1,0:T(8,128)(2,1)S(1)}, bf16[192,384]{1,0:T(8,128)(2,1)S(1)}, u32[]{:S(2)}, u32[]{:S(2)}) %collective-permute-start.27) | collective-permute-done | bytes 147488 | tf_op jit(solution)/shard_map/ppermute | solution.py:91
  157.1 6.3 fusion.53
  163.4 3.5 convert_multiply_fusion
  179.4 5.7 collective-permute-done.7
  187.6 8.7 %collective-permute-done.9 = bf16[192,1152]{1,0:T(8,128)(2,1)S(1)} collective-permute-done((bf16[192,1152]{1,0:T(8,128)(2,1)S(1)}, bf16[192,1152]{1,0:T(8,128)(2,1)S(1)}, u32[]{:S(2)}, u32[]{:S(2)}) %collective-permute-start.9) | collective-permute-done | bytes 442400 | tf_op jit(solution)/shard_map/ppermute | solution.py:91
  206.0 4.5 collective-permute-done.12
  212.5 3.0 collective-permute-start.19
  215.5 2.8 collective-permute-done.15
  226.2 4.7 all-to-all-start
  235.2 2.8 collective-permute-done.16
  241.8 3.9 collective-permute-start.17
  251.7 5.6 collective-permute-done.20
  258.9 3.5 collective-permute-start.21
  262.4 11.8 %collective-permute-done.17 = bf16[2048,128]{0,1:T(8,128)(2,1)S(1)} collective-permute-done((bf16[2048,128]{0,1:T(8,128)(2,1)S(1)}, bf16[2048,128]{0,1:T(8,128)(2,1)S(1)}, u32[]{:S(2)}, u32[]{:S(2)}) %collective-permute-start.17) | collective-permute-done | bytes 524320 | tf_op jit(solution)/shard_map/ppermute | solution.py:91
  275.8 6.3 collective-permute-start.18
  290.8 3.4 collective-permute-start.48
  298.2 20.7 %attend.1 = (bf16[2048,64]{1,0:T(8,128)(2,1)}, f32[64,2048]{1,0:T(8,128)}, f32[64,2048]{1,0:T(8,128)}, f32[2,2048]{1,0:T(2,128)}) custom-call(s32[4,4]{1,0:T(4,128)} %pad_add_fusion.table, f32[1]{0:T(128)} %dynamic_slice.240.gate, bf16[2048,64]{1,0:T(8,128)(2,1)} %copy.315.q_ref, bf16[2048,64]{1,0:T(8,128)(2,1)} %copy.316.k_ref, ...), custom_call_target="tpu_custom_call" | custom-call | flops 1073741824 | bytes 1048576 | tf_op jit(solution)/shard_map/attend/pallas_call | solution.py:306
  321.0 6.3 all-to-all-start.2
  334.2 3.2 all-to-all-done.2
  343.6 5.5 collective-permute-done.37
  355.5 4.3 collective-permute-done.31
  365.8 5.0 fusion.10
  373.0 6.2 fusion.226
  381.4 4.2 multiply_convert_fusion.3
  386.7 4.7 convolution_convert_fusion.1
  408.1 19.1 %collective-permute-done.91 = bf16[192,1024]{1,0:T(8,128)(2,1)S(1)} collective-permute-done((bf16[192,1024]{1,0:T(8,128)(2,1)S(1)}, bf16[192,1024]{1,0:T(8,128)(2,1)S(1)}, u32[]{:S(2)}, u32[]{:S(2)}) %collective-permute-start.91) | collective-permute-done | bytes 393248 | tf_op jit(solution)/shard_map/ppermute | solution.py:91
  431.5 6.5 collective-permute-done.50
  449.2 2.8 multiply_convert_fusion
  468.4 5.8 all-to-all-start.3
  494.3 3.8 collective-permute-done.66
  505.6 3.0 multiply_reduce_fusion.8
  512.5 25.9 %attend_back.1 = (bf16[2048,64]{1,0:T(8,128)(2,1)}, bf16[2048,64]{1,0:T(8,128)(2,1)}, bf16[2048,64]{1,0:T(8,128)(2,1)}, bf16[2048,64]{1,0:T(8,128)(2,1)}, bf16[2048,64]{1,0:T(8,128)(2,1)}, /*index=5*/f32[1,2048]{1,0:T(1,128)}) custom-call(s32[4,4]{1,0:T(4,128)} %pad_add_fusion.table, f32[1]{0:T(128)} %dynamic_slice.240.gate, bf16[2048,64]{1,0:T(8,128)(2,1)} %copy.315.q_ref, ...), custom_call_target="tpu_custom_call" | custom-call | flops 2684354560 | bytes 3145728 | tf_op jit(solution)/shard_map/attend_back/pallas_call | solution.py:344
  543.1 2.8 pad_maximum_fusion.3
  548.2 4.6 all-to-all-start.4
  559.4 2.6 multiply_reduce_fusion.9
  572.5 6.8 collective-permute-done.74
  580.5 2.9 collective-permute-start.76
  583.3 11.5 %collective-permute-done.75 = bf16[2048,128]{1,0:T(8,128)(2,1)} collective-permute-done((bf16[2048,128]{1,0:T(8,128)(2,1)}, bf16[2048,128]{1,0:T(8,128)(2,1)}, u32[]{:S(2)}, u32[]{:S(2)}) %collective-permute-start.75) | collective-permute-done | bytes 524320 | tf_op jit(solution)/shard_map/ppermute | solution.py:91
  600.7 3.3 convolution_convert_fusion.4
  610.9 3.9 collective-permute-start.62
  615.7 3.7 multiply_reduce_fusion.2
  649.6 3.8 slice.179
  653.4 7.7 slice.145
  661.1 4.1 copy.342
  665.2 3.6 multiply_reduce_fusion.3
  691.5 7.7 collective-permute-done.95
  699.2 2.5 collective-permute-start.96
  701.8 3.7 collective-permute-done.96
  709.4 3.1 multiply_reduce_fusion.7
  722.7 5.0 multiply_add_fusion.1
  732.1 3.8 collective-permute-done.101
  739.4 10.5 %multiply_subtract_fusion = (f32[128,9216]{1,0:T(8,128)}, f32[128,9216]{1,0:T(8,128)}, f32[128,9216]{1,0:T(8,128)}) fusion(f32[128,9216]{1,0:T(8,128)} %param.36, f32[128,9216]{1,0:T(8,128)} %param.37, f32[128,9216]{1,0:T(8,128)} %param.38, f32[]{:T(128)S(6)} %min.40, bf16[8,128]{1,0:T(8,128)(2,1)S(1)} %copy-done.91, bf16[8,9216]{1,0:T(8,128)(2,1)S(1)} %bitcast.500), kind=kOutput, calls=%fused_computation.3 | convolution fusion | flops 37748736 | bytes 28461060 | tf_op jit(solution)/shard_map/dot_general | solution.py:68
  755.2 2.9 multiply_subtract_fusion.2
  761.6 3.1 multiply_subtract_fusion.1
  767.0 3.0 multiply_subtract_fusion.4
  (665 shorter events, 355.0 us)
Async XLA Ops:
  2.8 136.0 %collective-permute-start.5 = (bf16[192,1152]{1,0:T(8,128)(2,1)}, bf16[192,1152]{1,0:T(8,128)(2,1)}, u32[]{:S(2)}, u32[]{:S(2)}) collective-permute-start(bf16[192,1152]{1,0:T(8,128)(2,1)} %bitcast.119), channel_id=1, source_target_pairs={{0,8},{8,16},{16,24},{24,28},{28,20},{20,12},{12,4},{4,0},{1,9},{9... | collective-permute-start | bytes 1327112 | tf_op jit(solution)/shard_map/ppermute | solution.py:91
  5.8 136.8 %collective-permute-start.6 = (bf16[192,1152]{1,0:T(8,128)(2,1)}, bf16[192,1152]{1,0:T(8,128)(2,1)}, u32[]{:S(2)}, u32[]{:S(2)}) collective-permute-start(bf16[192,1152]{1,0:T(8,128)(2,1)} %bitcast.119), channel_id=1, source_target_pairs={{0,4},{8,0},{16,8},{24,16},{28,24},{20,28},{12,20},{4,12},{1,5},{9... | collective-permute-start | bytes 1327112 | tf_op jit(solution)/shard_map/ppermute | solution.py:91
  20.6 69.4 %collective-permute-start.22 = (bf16[192,384]{1,0:T(8,128)(2,1)}, bf16[192,384]{1,0:T(8,128)(2,1)}, u32[]{:S(2)}, u32[]{:S(2)}) collective-permute-start(bf16[192,384]{1,0:T(8,128)(2,1)} %get-tuple-element.197), channel_id=1, source_target_pairs={{0,8},{8,16},{16,24},{24,28},{28,20},{20,12},{12,4},{4,0},{1,9},{9... | collective-permute-start | bytes 442376 | tf_op jit(solution)/shard_map/ppermute | solution.py:91
  22.6 87.0 %collective-permute-start.23 = (bf16[192,384]{1,0:T(8,128)(2,1)}, bf16[192,384]{1,0:T(8,128)(2,1)}, u32[]{:S(2)}, u32[]{:S(2)}) collective-permute-start(bf16[192,384]{1,0:T(8,128)(2,1)} %get-tuple-element.197), channel_id=1, source_target_pairs={{0,4},{8,0},{16,8},{24,16},{28,24},{20,28},{12,20},{4,12},{1,5},{9... | collective-permute-start | bytes 442376 | tf_op jit(solution)/shard_map/ppermute | solution.py:91
  27.8 59.3 %collective-permute-start = (f32[184,128]{1,0:T(8,128)}, f32[184,128]{1,0:T(8,128)}, u32[]{:S(2)}, u32[]{:S(2)}) collective-permute-start(f32[184,128]{1,0:T(8,128)} %maximum_bitcast_fusion.2), channel_id=1, source_target_pairs={{0,4},{4,0},{8,12},{12,8},{16,20},{20,16},{24,28},{28,24},{1,5},{5... | collective-permute-start | bytes 282632 | tf_op jit(solution)/shard_map/ppermute | solution.py:139
  34.2 129.2 %all-to-all-start.1 = ((bf16[256,8,128]{2,0,1:T(8,128)(2,1)}), bf16[256,8,128]{2,0,1:T(8,128)(2,1)}, u32[]{:S(2)}, u32[]{:S(2)}) async-start(bf16[256,8,128]{2,0,1:T(8,128)(2,1)} %copy.305), calls=%async_computation.1 | async-start | bytes 1048576 | tf_op jit(solution)/shard_map/all_to_all | solution.py:465
  87.1 89.8 %collective-permute-start.33 = (bf16[192,2048]{1,0:T(8,128)(2,1)S(1)}, bf16[192,2048]{1,0:T(8,128)(2,1)S(1)}, u32[]{:S(2)}, u32[]{:S(2)}) collective-permute-start(bf16[192,2048]{1,0:T(8,128)(2,1)S(1)} %bitcast.463), channel_id=1, source_target_pairs={{0,8},{8,16},{16,24},{24,28},{28,20},{20,12},{12,4},{4,0},{1,9},{9... | collective-permute-start | bytes 2359304 | tf_op jit(solution)/shard_map/ppermute | solution.py:91
  90.1 16.1 %collective-permute-start.1 = (f32[184,128]{1,0:T(8,128)S(1)}, f32[184,128]{1,0:T(8,128)S(1)}, u32[]{:S(2)}, u32[]{:S(2)}) collective-permute-start(f32[184,128]{1,0:T(8,128)S(1)} %fusion.208), channel_id=1, source_target_pairs={{0,8},{4,12},{8,0},{12,4},{16,24},{20,28},{24,16},{28,20},{1,9},{5... | collective-permute-start | bytes 282632 | tf_op jit(solution)/shard_map/ppermute | solution.py:139
  128.8 118.7 %collective-permute-start.34 = (bf16[192,2048]{1,0:T(8,128)(2,1)S(1)}, bf16[192,2048]{1,0:T(8,128)(2,1)}, u32[]{:S(2)}, u32[]{:S(2)}) collective-permute-start(bf16[192,2048]{1,0:T(8,128)(2,1)S(1)} %bitcast.464), channel_id=1, source_target_pairs={{0,4},{8,0},{16,8},{24,16},{28,24},{20,28},{12,20},{4,12},{1,5},{9... | collective-permute-start | bytes 2359304 | tf_op jit(solution)/shard_map/ppermute | solution.py:91
  138.8 17.3 %collective-permute-start.27 = (bf16[192,384]{1,0:T(8,128)(2,1)S(1)}, bf16[192,384]{1,0:T(8,128)(2,1)S(1)}, u32[]{:S(2)}, u32[]{:S(2)}) collective-permute-start(bf16[192,384]{1,0:T(8,128)(2,1)S(1)} %collective-permute-done.25), channel_id=1, source_target_pairs={{0,4},{8,0},{16,8},{24,16},{28,24},{20,28},{12,20},{4,12},{1,5},{9... | collective-permute-start | bytes 442376 | tf_op jit(solution)/shard_map/ppermute | solution.py:91
  145.9 95.9 %collective-permute-start.43 = (bf16[192,1024]{1,0:T(8,128)(2,1)}, bf16[192,1024]{1,0:T(8,128)(2,1)}, u32[]{:S(2)}, u32[]{:S(2)}) collective-permute-start(bf16[192,1024]{1,0:T(8,128)(2,1)} %collective-permute-done.41), channel_id=1, source_target_pairs={{0,8},{8,16},{16,24},{24,28},{28,20},{20,12},{12,4},{4,0},{1,9},{9... | collective-permute-start | bytes 1179656 | tf_op jit(solution)/shard_map/ppermute | solution.py:91
  176.9 24.6 %collective-permute-start.14 = (bf16[2048,256]{1,0:T(8,128)(2,1)S(1)}, bf16[2048,256]{1,0:T(8,128)(2,1)S(1)}, u32[]{:S(2)}, u32[]{:S(2)}) collective-permute-start(bf16[2048,256]{1,0:T(8,128)(2,1)S(1)} %pad_maximum_fusion.1), channel_id=1, source_target_pairs={{0,2},{2,0},{1,3},{3,1},{4,6},{6,4},{5,7},{7,5},{8,10},{10,8},{9,1... | collective-permute-start | bytes 3145736 | tf_op jit(solution)/shard_map/ppermute | solution.py:153
  196.3 51.5 %collective-permute-start.44 = (bf16[192,1024]{1,0:T(8,128)(2,1)}, bf16[192,1024]{1,0:T(8,128)(2,1)}, u32[]{:S(2)}, u32[]{:S(2)}) collective-permute-start(bf16[192,1024]{1,0:T(8,128)(2,1)} %collective-permute-done.42), channel_id=1, source_target_pairs={{0,4},{8,0},{16,8},{24,16},{28,24},{20,28},{12,20},{4,12},{1,5},{9... | collective-permute-start | bytes 1179656 | tf_op jit(solution)/shard_map/ppermute | solution.py:91
  212.5 18.4 %collective-permute-start.19 = (bf16[2048,128]{0,1:T(8,128)(2,1)}, bf16[2048,128]{0,1:T(8,128)(2,1)}, u32[]{:S(2)}, u32[]{:S(2)}) collective-permute-start(bf16[2048,128]{0,1:T(8,128)(2,1)} %convolution_convert_fusion.9), channel_id=1, source_target_pairs={{0,4},{8,0},{16,8},{28,24},{20,28},{12,20},{1,5},{9,1},{17,9},{29,... | collective-permute-start | bytes 1572872 | tf_op jit(solution)/shard_map/ppermute | solution.py:91
  219.9 18.0 %collective-permute-start.16 = (bf16[2048,128]{0,1:T(8,128)(2,1)}, bf16[2048,128]{0,1:T(8,128)(2,1)}, u32[]{:S(2)}, u32[]{:S(2)}) collective-permute-start(bf16[2048,128]{0,1:T(8,128)(2,1)} %add_convert_fusion.9), channel_id=1, source_target_pairs={{0,8},{16,24},{24,28},{28,20},{12,4},{4,0},{1,9},{17,25},{25,29},{... | collective-permute-start | bytes 1572872 | tf_op jit(solution)/shard_map/ppermute | solution.py:91
  226.2 61.6 %all-to-all-start = ((bf16[8,256,192]{1,2,0:T(8,128)(2,1)}), bf16[8,256,192]{1,2,0:T(8,128)(2,1)S(1)}, u32[]{:S(2)}, u32[]{:S(2)}) async-start(bf16[8,256,192]{1,2,0:T(8,128)(2,1)} %pad.8), calls=%async_computation | async-start | bytes 1572864 | tf_op jit(solution)/shard_map/all_to_all | solution.py:423
  230.8 101.3 %collective-permute-start.35 = (bf16[192,2048]{1,0:T(8,128)(2,1)}, bf16[192,2048]{1,0:T(8,128)(2,1)}, u32[]{:S(2)}, u32[]{:S(2)}) collective-permute-start(bf16[192,2048]{1,0:T(8,128)(2,1)} %copy-done.78), channel_id=1, source_target_pairs={{0,8},{8,16},{16,24},{24,28},{28,20},{20,12},{12,4},{4,0},{1,9},{9... | collective-permute-start | bytes 2359304 | tf_op jit(solution)/shard_map/ppermute | solution.py:91
  238.0 19.3 %collective-permute-start.20 = (bf16[2048,128]{0,1:T(8,128)(2,1)S(1)}, bf16[2048,128]{0,1:T(8,128)(2,1)S(1)}, u32[]{:S(2)}, u32[]{:S(2)}) collective-permute-start(bf16[2048,128]{0,1:T(8,128)(2,1)S(1)} %add_convert_fusion.6), channel_id=1, source_target_pairs={{0,4},{8,0},{24,16},{28,24},{20,28},{4,12},{1,5},{9,1},{25,17},{29... | collective-permute-start | bytes 1572872 | tf_op jit(solution)/shard_map/ppermute | solution.py:91
  241.8 32.4 %collective-permute-start.17 = (bf16[2048,128]{0,1:T(8,128)(2,1)S(1)}, bf16[2048,128]{0,1:T(8,128)(2,1)S(1)}, u32[]{:S(2)}, u32[]{:S(2)}) collective-permute-start(bf16[2048,128]{0,1:T(8,128)(2,1)S(1)} %add_convert_fusion.8), channel_id=1, source_target_pairs={{0,8},{8,16},{24,28},{28,20},{20,12},{4,0},{1,9},{9,17},{25,29},{2... | collective-permute-start | bytes 1572872 | tf_op jit(solution)/shard_map/ppermute | solution.py:91
  247.5 36.4 %collective-permute-start.45 = (bf16[192,1024]{1,0:T(8,128)(2,1)}, bf16[192,1024]{1,0:T(8,128)(2,1)S(1)}, u32[]{:S(2)}, u32[]{:S(2)}) collective-permute-start(bf16[192,1024]{1,0:T(8,128)(2,1)} %collective-permute-done.43), channel_id=1, source_target_pairs={{0,8},{8,16},{16,24},{24,28},{28,20},{20,12},{12,4},{4,0},{1,9},{9... | collective-permute-start | bytes 1179656 | tf_op jit(solution)/shard_map/ppermute | solution.py:91
  247.8 36.8 %collective-permute-start.46 = (bf16[192,1024]{1,0:T(8,128)(2,1)}, bf16[192,1024]{1,0:T(8,128)(2,1)S(1)}, u32[]{:S(2)}, u32[]{:S(2)}) collective-permute-start(bf16[192,1024]{1,0:T(8,128)(2,1)} %collective-permute-done.44), channel_id=1, source_target_pairs={{0,4},{8,0},{16,8},{24,16},{28,24},{20,28},{12,20},{4,12},{1,5},{9... | collective-permute-start | bytes 1179656 | tf_op jit(solution)/shard_map/ppermute | solution.py:91
  258.9 32.0 %collective-permute-start.21 = (bf16[2048,128]{0,1:T(8,128)(2,1)}, bf16[2048,128]{0,1:T(8,128)(2,1)}, u32[]{:S(2)}, u32[]{:S(2)}) collective-permute-start(bf16[2048,128]{0,1:T(8,128)(2,1)} %add_convert_fusion.5), channel_id=1, source_target_pairs={{0,4},{16,8},{24,16},{28,24},{12,20},{4,12},{1,5},{17,9},{25,17},{... | collective-permute-start | bytes 1572872 | tf_op jit(solution)/shard_map/ppermute | solution.py:91
  275.8 18.4 %collective-permute-start.18 = (bf16[2048,128]{0,1:T(8,128)(2,1)}, bf16[2048,128]{0,1:T(8,128)(2,1)}, u32[]{:S(2)}, u32[]{:S(2)}) collective-permute-start(bf16[2048,128]{0,1:T(8,128)(2,1)} %add_convert_fusion.7), channel_id=1, source_target_pairs={{0,8},{8,16},{16,24},{28,20},{20,12},{12,4},{1,9},{9,17},{17,25},{... | collective-permute-start | bytes 1572872 | tf_op jit(solution)/shard_map/ppermute | solution.py:91
  283.9 50.2 %collective-permute-start.36 = (bf16[192,2048]{1,0:T(8,128)(2,1)}, bf16[192,2048]{1,0:T(8,128)(2,1)}, u32[]{:S(2)}, u32[]{:S(2)}) collective-permute-start(bf16[192,2048]{1,0:T(8,128)(2,1)} %collective-permute-done.34), channel_id=1, source_target_pairs={{0,4},{8,0},{16,8},{24,16},{28,24},{20,28},{12,20},{4,12},{1,5},{9... | collective-permute-start | bytes 2359304 | tf_op jit(solution)/shard_map/ppermute | solution.py:91
  284.6 44.2 %collective-permute-start.47 = (bf16[96,1024]{1,0:T(8,128)(2,1)}, bf16[96,1024]{1,0:T(8,128)(2,1)}, u32[]{:S(2)}, u32[]{:S(2)}) collective-permute-start(bf16[96,1024]{1,0:T(8,128)(2,1)} %slice.174), channel_id=1, source_target_pairs={{0,8},{8,16},{16,24},{24,28},{28,20},{20,12},{12,4},{4,0},{1,9},{9... | collective-permute-start | bytes 589832 | tf_op jit(solution)/shard_map/ppermute | solution.py:91
  290.8 39.6 %collective-permute-start.48 = (bf16[96,1024]{1,0:T(8,128)(2,1)}, bf16[96,1024]{1,0:T(8,128)(2,1)}, u32[]{:S(2)}, u32[]{:S(2)}) collective-permute-start(bf16[96,1024]{1,0:T(8,128)(2,1)} %slice.175), channel_id=1, source_target_pairs={{0,4},{8,0},{16,8},{24,16},{28,24},{20,28},{12,20},{4,12},{1,5},{9... | collective-permute-start | bytes 589832 | tf_op jit(solution)/shard_map/ppermute | solution.py:91
  321.0 16.4 %all-to-all-start.2 = ((bf16[8,256,64]{1,2,0:T(8,128)(2,1)}), bf16[8,256,64]{1,2,0:T(8,128)(2,1)S(1)}, u32[]{:S(2)}, u32[]{:S(2)}) async-start(bf16[8,256,64]{1,2,0:T(8,128)(2,1)} %copy.319), calls=%async_computation.2 | async-start | bytes 524288 | tf_op jit(solution)/shard_map/all_to_all | solution.py:427
  332.1 17.0 %collective-permute-start.37 = (bf16[192,2048]{1,0:T(8,128)(2,1)}, bf16[192,2048]{1,0:T(8,128)(2,1)S(1)}, u32[]{:S(2)}, u32[]{:S(2)}) collective-permute-start(bf16[192,2048]{1,0:T(8,128)(2,1)} %collective-permute-done.35), channel_id=1, source_target_pairs={{0,8},{8,16},{16,24},{24,28},{28,20},{20,12},{12,4},{4,0},{1,9},{9... | collective-permute-start | bytes 2359304 | tf_op jit(solution)/shard_map/ppermute | solution.py:91
  334.1 17.4 %collective-permute-start.38 = (bf16[192,2048]{1,0:T(8,128)(2,1)}, bf16[192,2048]{1,0:T(8,128)(2,1)S(1)}, u32[]{:S(2)}, u32[]{:S(2)}) collective-permute-start(bf16[192,2048]{1,0:T(8,128)(2,1)} %collective-permute-done.36), channel_id=1, source_target_pairs={{0,4},{8,0},{16,8},{24,16},{28,24},{20,28},{12,20},{4,12},{1,5},{9... | collective-permute-start | bytes 2359304 | tf_op jit(solution)/shard_map/ppermute | solution.py:91
  398.7 40.2 %collective-permute-start.84 = (bf16[192,2048]{1,0:T(8,128)(2,1)S(1)}, bf16[192,2048]{1,0:T(8,128)(2,1)S(1)}, u32[]{:S(2)}, u32[]{:S(2)}) collective-permute-start(bf16[192,2048]{1,0:T(8,128)(2,1)S(1)} %convolution_convert_fusion.5), channel_id=1, source_target_pairs={{0,4},{8,0},{16,8},{24,16},{28,24},{20,28},{12,20},{4,12},{1,5},{9... | collective-permute-start | bytes 2359304 | tf_op jit(solution)/shard_map/ppermute | solution.py:91
  400.7 40.0 %collective-permute-start.80 = (bf16[192,2048]{1,0:T(8,128)(2,1)S(1)}, bf16[192,2048]{1,0:T(8,128)(2,1)S(1)}, u32[]{:S(2)}, u32[]{:S(2)}) collective-permute-start(bf16[192,2048]{1,0:T(8,128)(2,1)S(1)} %convolution_convert_fusion.6), channel_id=1, source_target_pairs={{0,8},{8,16},{16,24},{24,28},{28,20},{20,12},{12,4},{4,0},{1,9},{9... | collective-permute-start | bytes 2359304 | tf_op jit(solution)/shard_map/ppermute | solution.py:91
  400.7 26.5 %collective-permute-start.91 = (bf16[192,1024]{1,0:T(8,128)(2,1)S(1)}, bf16[192,1024]{1,0:T(8,128)(2,1)S(1)}, u32[]{:S(2)}, u32[]{:S(2)}) collective-permute-start(bf16[192,1024]{1,0:T(8,128)(2,1)S(1)} %convolution_convert_fusion.11), channel_id=1, source_target_pairs={{0,4},{8,0},{16,8},{24,16},{28,24},{20,28},{12,20},{4,12},{1,5},{9... | collective-permute-start | bytes 1179656 | tf_op jit(solution)/shard_map/ppermute | solution.py:91
  405.8 23.2 %collective-permute-start.87 = (bf16[192,1024]{1,0:T(8,128)(2,1)S(1)}, bf16[192,1024]{1,0:T(8,128)(2,1)S(1)}, u32[]{:S(2)}, u32[]{:S(2)}) collective-permute-start(bf16[192,1024]{1,0:T(8,128)(2,1)S(1)} %convolution_convert_fusion.12), channel_id=1, source_target_pairs={{0,8},{8,16},{16,24},{24,28},{28,20},{20,12},{12,4},{4,0},{1,9},{9... | collective-permute-start | bytes 1179656 | tf_op jit(solution)/shard_map/ppermute | solution.py:91
  406.4 24.7 %collective-permute-start.53 = (bf16[128,1536]{1,0:T(8,128)(2,1)S(1)}, bf16[128,1536]{1,0:T(8,128)(2,1)S(1)}, u32[]{:S(2)}, u32[]{:S(2)}) collective-permute-start(bf16[128,1536]{1,0:T(8,128)(2,1)S(1)} %add_convert_fusion.23), channel_id=1, source_target_pairs={{0,2},{2,0},{1,3},{3,1},{4,6},{6,4},{5,7},{7,5},{8,10},{10,8},{9,1... | collective-permute-start | bytes 1179656 | tf_op jit(solution)/shard_map/ppermute | solution.py:163
  438.9 37.8 %collective-permute-start.51 = (bf16[128,1536]{1,0:T(8,128)(2,1)}, bf16[128,1536]{1,0:T(8,128)(2,1)}, u32[]{:S(2)}, u32[]{:S(2)}) collective-permute-start(bf16[128,1536]{1,0:T(8,128)(2,1)} %add_convert_fusion.24), channel_id=1, source_target_pairs={{0,1},{1,0},{2,3},{3,2},{4,5},{5,4},{6,7},{7,6},{8,9},{9,8},{10,11... | collective-permute-start | bytes 1179656 | tf_op jit(solution)/shard_map/ppermute | solution.py:164
  440.7 61.8 %collective-permute-start.85 = (bf16[192,2048]{1,0:T(8,128)(2,1)}, bf16[192,2048]{1,0:T(8,128)(2,1)}, u32[]{:S(2)}, u32[]{:S(2)}) collective-permute-start(bf16[192,2048]{1,0:T(8,128)(2,1)} %add_convert_fusion.1), channel_id=1, source_target_pairs={{0,4},{8,0},{16,8},{24,16},{28,24},{20,28},{12,20},{4,12},{1,5},{9... | collective-permute-start | bytes 2359304 | tf_op jit(solution)/shard_map/ppermute | solution.py:91
  443.6 56.3 %collective-permute-start.81 = (bf16[192,2048]{1,0:T(8,128)(2,1)}, bf16[192,2048]{1,0:T(8,128)(2,1)}, u32[]{:S(2)}, u32[]{:S(2)}) collective-permute-start(bf16[192,2048]{1,0:T(8,128)(2,1)} %add_convert_fusion.4), channel_id=1, source_target_pairs={{0,8},{8,16},{16,24},{24,28},{28,20},{20,12},{12,4},{4,0},{1,9},{9... | collective-permute-start | bytes 2359304 | tf_op jit(solution)/shard_map/ppermute | solution.py:91
  444.9 60.7 %collective-permute-start.93 = (bf16[192,1024]{1,0:T(8,128)(2,1)}, bf16[192,1024]{1,0:T(8,128)(2,1)}, u32[]{:S(2)}, u32[]{:S(2)}) collective-permute-start(bf16[192,1024]{1,0:T(8,128)(2,1)} %add_convert_fusion.15), channel_id=1, source_target_pairs={{0,4},{8,0},{16,8},{24,16},{28,24},{20,28},{12,20},{4,12},{1,5},{9... | collective-permute-start | bytes 1179656 | tf_op jit(solution)/shard_map/ppermute | solution.py:91
  447.3 34.0 %collective-permute-start.89 = (bf16[192,1024]{1,0:T(8,128)(2,1)}, bf16[192,1024]{1,0:T(8,128)(2,1)}, u32[]{:S(2)}, u32[]{:S(2)}) collective-permute-start(bf16[192,1024]{1,0:T(8,128)(2,1)} %add_convert_fusion.18), channel_id=1, source_target_pairs={{0,8},{8,16},{16,24},{24,28},{28,20},{20,12},{12,4},{4,0},{1,9},{9... | collective-permute-start | bytes 1179656 | tf_op jit(solution)/shard_map/ppermute | solution.py:91
  468.4 42.1 %all-to-all-start.3 = ((bf16[8,256,64]{1,2,0:T(8,128)(2,1)}), bf16[8,256,64]{1,2,0:T(8,128)(2,1)}, u32[]{:S(2)}, u32[]{:S(2)}) async-start(bf16[8,256,64]{1,2,0:T(8,128)(2,1)} %pad.9), calls=%async_computation.3 | async-start | bytes 524288 | tf_op jit(solution)/shard_map/all_to_all | solution.py:423
  484.3 21.3 %collective-permute-start.90 = (bf16[192,1024]{1,0:T(8,128)(2,1)S(1)}, bf16[192,1024]{1,0:T(8,128)(2,1)S(1)}, u32[]{:S(2)}, u32[]{:S(2)}) collective-permute-start(bf16[192,1024]{1,0:T(8,128)(2,1)S(1)} %add_convert_fusion.17), channel_id=1, source_target_pairs={{0,8},{8,16},{16,24},{24,28},{28,20},{20,12},{12,4},{4,0},{1,9},{9... | collective-permute-start | bytes 1179656 | tf_op jit(solution)/shard_map/ppermute | solution.py:91
  498.1 59.3 %collective-permute-start.71 = (bf16[192,384]{1,0:T(8,128)(2,1)}, bf16[192,384]{1,0:T(8,128)(2,1)}, u32[]{:S(2)}, u32[]{:S(2)}) collective-permute-start(bf16[192,384]{1,0:T(8,128)(2,1)} %add_convert_fusion.28), channel_id=1, source_target_pairs={{0,4},{8,0},{16,8},{24,16},{28,24},{20,28},{12,20},{4,12},{1,5},{9... | collective-permute-start | bytes 442376 | tf_op jit(solution)/shard_map/ppermute | solution.py:91
  502.5 67.6 %collective-permute-start.82 = (bf16[192,2048]{1,0:T(8,128)(2,1)}, bf16[192,2048]{1,0:T(8,128)(2,1)}, u32[]{:S(2)}, u32[]{:S(2)}) collective-permute-start(bf16[192,2048]{1,0:T(8,128)(2,1)} %add_convert_fusion.3), channel_id=1, source_target_pairs={{0,8},{8,16},{16,24},{24,28},{28,20},{20,12},{12,4},{4,0},{1,9},{9... | collective-permute-start | bytes 2359304 | tf_op jit(solution)/shard_map/ppermute | solution.py:91
  509.3 50.2 %collective-permute-start.68 = (bf16[192,384]{1,0:T(8,128)(2,1)}, bf16[192,384]{1,0:T(8,128)(2,1)}, u32[]{:S(2)}, u32[]{:S(2)}) collective-permute-start(bf16[192,384]{1,0:T(8,128)(2,1)} %add_convert_fusion.30), channel_id=1, source_target_pairs={{0,8},{8,16},{16,24},{24,28},{28,20},{20,12},{12,4},{4,0},{1,9},{9... | collective-permute-start | bytes 442376 | tf_op jit(solution)/shard_map/ppermute | solution.py:91
  541.0 21.1 %collective-permute-start.72 = (bf16[2048,128]{1,0:T(8,128)(2,1)S(1)}, bf16[2048,128]{1,0:T(8,128)(2,1)}, u32[]{:S(2)}, u32[]{:S(2)}) collective-permute-start(bf16[2048,128]{1,0:T(8,128)(2,1)S(1)} %pad_maximum_fusion.4), channel_id=1, source_target_pairs={{0,8},{8,16},{16,24},{24,28},{28,20},{20,12},{12,4},{4,0},{1,9},{9... | collective-permute-start | bytes 1572872 | tf_op jit(solution)/shard_map/ppermute | solution.py:91
  542.4 21.7 %collective-permute-start.73 = (bf16[2048,128]{1,0:T(8,128)(2,1)S(1)}, bf16[2048,128]{1,0:T(8,128)(2,1)}, u32[]{:S(2)}, u32[]{:S(2)}) collective-permute-start(bf16[2048,128]{1,0:T(8,128)(2,1)S(1)} %pad_maximum_fusion.4), channel_id=1, source_target_pairs={{0,4},{8,0},{16,8},{24,16},{28,24},{20,28},{12,20},{4,12},{1,5},{9... | collective-permute-start | bytes 1572872 | tf_op jit(solution)/shard_map/ppermute | solution.py:91
  548.2 51.4 %all-to-all-start.4 = ((bf16[8,256,192]{1,2,0:T(8,128)(2,1)}), bf16[8,256,192]{1,2,0:T(8,128)(2,1)}, u32[]{:S(2)}, u32[]{:S(2)}) async-start(bf16[8,256,192]{1,2,0:T(8,128)(2,1)} %copy.329), calls=%async_computation.4 | async-start | bytes 1572864 | tf_op jit(solution)/shard_map/all_to_all | solution.py:427
  557.4 53.5 %collective-permute-start.86 = (bf16[192,2048]{1,0:T(8,128)(2,1)}, bf16[192,2048]{1,0:T(8,128)(2,1)}, u32[]{:S(2)}, u32[]{:S(2)}) collective-permute-start(bf16[192,2048]{1,0:T(8,128)(2,1)} %add_convert_fusion), channel_id=1, source_target_pairs={{0,4},{8,0},{16,8},{24,16},{28,24},{20,28},{12,20},{4,12},{1,5},{9... | collective-permute-start | bytes 2359304 | tf_op jit(solution)/shard_map/ppermute | solution.py:91
  564.1 15.2 %collective-permute-start.74 = (bf16[2048,128]{1,0:T(8,128)(2,1)}, bf16[2048,128]{1,0:T(8,128)(2,1)}, u32[]{:S(2)}, u32[]{:S(2)}) collective-permute-start(bf16[2048,128]{1,0:T(8,128)(2,1)} %collective-permute-done.72), channel_id=1, source_target_pairs={{0,8},{8,16},{16,24},{24,28},{28,20},{20,12},{12,4},{4,0},{1,9},{9... | collective-permute-start | bytes 1572872 | tf_op jit(solution)/shard_map/ppermute | solution.py:91
  565.4 29.4 %collective-permute-start.75 = (bf16[2048,128]{1,0:T(8,128)(2,1)}, bf16[2048,128]{1,0:T(8,128)(2,1)}, u32[]{:S(2)}, u32[]{:S(2)}) collective-permute-start(bf16[2048,128]{1,0:T(8,128)(2,1)} %collective-permute-done.73), channel_id=1, source_target_pairs={{0,4},{8,0},{16,8},{24,16},{28,24},{20,28},{12,20},{4,12},{1,5},{9... | collective-permute-start | bytes 1572872 | tf_op jit(solution)/shard_map/ppermute | solution.py:91
  572.3 42.5 %collective-permute-start.83 = (bf16[192,2048]{1,0:T(8,128)(2,1)}, bf16[192,2048]{1,0:T(8,128)(2,1)}, u32[]{:S(2)}, u32[]{:S(2)}) collective-permute-start(bf16[192,2048]{1,0:T(8,128)(2,1)} %add_convert_fusion.2), channel_id=1, source_target_pairs={{0,8},{8,16},{16,24},{24,28},{28,20},{20,12},{12,4},{4,0},{1,9},{9... | collective-permute-start | bytes 2359304 | tf_op jit(solution)/shard_map/ppermute | solution.py:91
  580.5 38.9 %collective-permute-start.76 = (bf16[2048,128]{1,0:T(8,128)(2,1)}, bf16[2048,128]{1,0:T(8,128)(2,1)}, u32[]{:S(2)}, u32[]{:S(2)}) collective-permute-start(bf16[2048,128]{1,0:T(8,128)(2,1)} %collective-permute-done.74), channel_id=1, source_target_pairs={{0,8},{8,16},{16,24},{24,28},{28,20},{20,12},{12,4},{4,0},{1,9},{9... | collective-permute-start | bytes 1572872 | tf_op jit(solution)/shard_map/ppermute | solution.py:91
  596.8 26.3 %collective-permute-start.77 = (bf16[2048,128]{1,0:T(8,128)(2,1)}, bf16[2048,128]{1,0:T(8,128)(2,1)}, u32[]{:S(2)}, u32[]{:S(2)}) collective-permute-start(bf16[2048,128]{1,0:T(8,128)(2,1)} %collective-permute-done.75), channel_id=1, source_target_pairs={{0,4},{8,0},{16,8},{24,16},{28,24},{20,28},{12,20},{4,12},{1,5},{9... | collective-permute-start | bytes 1572872 | tf_op jit(solution)/shard_map/ppermute | solution.py:91
  607.2 25.5 %collective-permute-start.55 = (bf16[128,1536]{1,0:T(8,128)(2,1)}, bf16[128,1536]{1,0:T(8,128)(2,1)}, u32[]{:S(2)}, u32[]{:S(2)}) collective-permute-start(bf16[128,1536]{1,0:T(8,128)(2,1)} %constant_dynamic-slice_fusion.3), channel_id=1, source_target_pairs={{0,1},{1,0},{2,3},{3,2},{4,5},{5,4},{6,7},{7,6},{8,9},{9,8},{10,11... | collective-permute-start | bytes 1179656 | tf_op jit(solution)/shard_map/ppermute | solution.py:162
  610.9 25.2 %collective-permute-start.62 = (bf16[192,1152]{1,0:T(8,128)(2,1)}, bf16[192,1152]{1,0:T(8,128)(2,1)}, u32[]{:S(2)}, u32[]{:S(2)}) collective-permute-start(bf16[192,1152]{1,0:T(8,128)(2,1)} %convolution_convert_fusion.7), channel_id=1, source_target_pairs={{0,4},{8,0},{16,8},{24,16},{28,24},{20,28},{12,20},{4,12},{1,5},{9... | collective-permute-start | bytes 1327112 | tf_op jit(solution)/shard_map/ppermute | solution.py:91
  614.8 25.0 %collective-permute-start.58 = (bf16[192,1152]{1,0:T(8,128)(2,1)}, bf16[192,1152]{1,0:T(8,128)(2,1)}, u32[]{:S(2)}, u32[]{:S(2)}) collective-permute-start(bf16[192,1152]{1,0:T(8,128)(2,1)} %convolution_convert_fusion.8), channel_id=1, source_target_pairs={{0,8},{8,16},{16,24},{24,28},{28,20},{20,12},{12,4},{4,0},{1,9},{9... | collective-permute-start | bytes 1327112 | tf_op jit(solution)/shard_map/ppermute | solution.py:91
  621.1 21.6 %collective-permute-start.78 = (bf16[1024,128]{1,0:T(8,128)(2,1)}, bf16[1024,128]{1,0:T(8,128)(2,1)}, u32[]{:S(2)}, u32[]{:S(2)}) collective-permute-start(bf16[1024,128]{1,0:T(8,128)(2,1)} %slice.177), channel_id=1, source_target_pairs={{0,8},{8,16},{16,24},{24,28},{28,20},{20,12},{12,4},{4,0},{1,9},{9... | collective-permute-start | bytes 786440 | tf_op jit(solution)/shard_map/ppermute | solution.py:91
  624.8 21.3 %collective-permute-start.79 = (bf16[1024,128]{1,0:T(8,128)(2,1)}, bf16[1024,128]{1,0:T(8,128)(2,1)}, u32[]{:S(2)}, u32[]{:S(2)}) collective-permute-start(bf16[1024,128]{1,0:T(8,128)(2,1)} %slice.178), channel_id=1, source_target_pairs={{0,4},{8,0},{16,8},{24,16},{28,24},{20,28},{12,20},{4,12},{1,5},{9... | collective-permute-start | bytes 786440 | tf_op jit(solution)/shard_map/ppermute | solution.py:91
  634.5 34.3 %collective-permute-start.56 = (bf16[128,1536]{1,0:T(8,128)(2,1)}, bf16[128,1536]{1,0:T(8,128)(2,1)}, u32[]{:S(2)}, u32[]{:S(2)}) collective-permute-start(bf16[128,1536]{1,0:T(8,128)(2,1)} %add_convert_fusion.21), channel_id=1, source_target_pairs={{0,2},{2,0},{1,3},{3,1},{4,6},{6,4},{5,7},{7,5},{8,10},{10,8},{9,1... | collective-permute-start | bytes 1179656 | tf_op jit(solution)/shard_map/ppermute | solution.py:163
  638.2 44.4 %collective-permute-start.63 = (bf16[192,1152]{1,0:T(8,128)(2,1)}, bf16[192,1152]{1,0:T(8,128)(2,1)}, u32[]{:S(2)}, u32[]{:S(2)}) collective-permute-start(bf16[192,1152]{1,0:T(8,128)(2,1)} %add_convert_fusion.11), channel_id=1, source_target_pairs={{0,4},{8,0},{16,8},{24,16},{28,24},{20,28},{12,20},{4,12},{1,5},{9... | collective-permute-start | bytes 1327112 | tf_op jit(solution)/shard_map/ppermute | solution.py:91
  642.0 28.1 %collective-permute-start.59 = (bf16[192,1152]{1,0:T(8,128)(2,1)}, bf16[192,1152]{1,0:T(8,128)(2,1)}, u32[]{:S(2)}, u32[]{:S(2)}) collective-permute-start(bf16[192,1152]{1,0:T(8,128)(2,1)} %add_convert_fusion.14), channel_id=1, source_target_pairs={{0,8},{8,16},{16,24},{24,28},{28,20},{20,12},{12,4},{4,0},{1,9},{9... | collective-permute-start | bytes 1327112 | tf_op jit(solution)/shard_map/ppermute | solution.py:91
  672.0 17.3 %collective-permute-start.60 = (bf16[192,1152]{1,0:T(8,128)(2,1)}, bf16[192,1152]{1,0:T(8,128)(2,1)}, u32[]{:S(2)}, u32[]{:S(2)}) collective-permute-start(bf16[192,1152]{1,0:T(8,128)(2,1)} %add_convert_fusion.13), channel_id=1, source_target_pairs={{0,8},{8,16},{16,24},{24,28},{28,20},{20,12},{12,4},{4,0},{1,9},{9... | collective-permute-start | bytes 1327112 | tf_op jit(solution)/shard_map/ppermute | solution.py:91
  684.5 24.9 %collective-permute-start.64 = (bf16[192,1152]{1,0:T(8,128)(2,1)}, bf16[192,1152]{1,0:T(8,128)(2,1)}, u32[]{:S(2)}, u32[]{:S(2)}) collective-permute-start(bf16[192,1152]{1,0:T(8,128)(2,1)} %add_convert_fusion.10), channel_id=1, source_target_pairs={{0,4},{8,0},{16,8},{24,16},{28,24},{20,28},{12,20},{4,12},{1,5},{9... | collective-permute-start | bytes 1327112 | tf_op jit(solution)/shard_map/ppermute | solution.py:91
  691.2 18.2 %collective-permute-start.61 = (bf16[192,1152]{1,0:T(8,128)(2,1)}, bf16[192,1152]{1,0:T(8,128)(2,1)}, u32[]{:S(2)}, u32[]{:S(2)}) collective-permute-start(bf16[192,1152]{1,0:T(8,128)(2,1)} %add_convert_fusion.12), channel_id=1, source_target_pairs={{0,8},{8,16},{16,24},{24,28},{28,20},{20,12},{12,4},{4,0},{1,9},{9... | collective-permute-start | bytes 1327112 | tf_op jit(solution)/shard_map/ppermute | solution.py:91
  (153 other events, 1326.1 us)

commit v2 on v1

v2 whole, which is shorter than its diff:
```python
import functools
import math

import jax
import jax.numpy as jnp
from jax import lax
from jax.experimental import pallas as pl
from jax.experimental.pallas import tpu as pltpu
from jax.sharding import PartitionSpec as P

HD = 64
TE = 1024
TEXT = 256
ITEMS = 8
ADAM_STEP = 10

bf16 = jnp.bfloat16
f32 = jnp.float32
highest = lax.Precision.HIGHEST
eps_norm = 1e-06
masked_score = -1e30
lowest_max = -1e20
clip_limit = 1.0
beta_first = 0.9
beta_second = 0.95
adam_eps = 1e-08
rate_matrix = 0.05
rate_small = 0.5
decay_matrix = 0.1
score_scale = HD ** (-0.5)

WIDE = 256
ROWS = 64

CORE_SWAP = [(0, 1), (1, 0), (2, 3), (3, 2)]
Y_SWAP = [(0, 2), (2, 0), (1, 3), (3, 1)]
CYCLE = (0, 2, 4, 6, 7, 5, 3, 1)


def time_embed(timesteps):
    half_width = TE // 2
    frequency = jnp.exp(-math.log(10000.0) * jnp.arange(half_width, dtype=f32) / half_width)
    angles = 1000.0 * timesteps[:, None] * frequency[None, :]
    return jnp.concatenate([jnp.cos(angles), jnp.sin(angles)], axis=1)


def rms_parts(values):
    inverse = lax.rsqrt(jnp.mean(values * values, axis=-1, keepdims=True) + eps_norm)
    return (values * inverse, inverse)


def rms_back(normed, inverse, normed_grad):
    return inverse * (normed_grad - normed * jnp.mean(normed_grad * normed, axis=-1, keepdims=True))


def adam_update(weight, first, second, grad, clip, rate, decay):
    clipped = grad * clip
    first_new = beta_first * first + (1.0 - beta_first) * clipped
    second_new = beta_second * second + (1.0 - beta_second) * clipped * clipped
    first_hat = first_new / (1.0 - beta_first**ADAM_STEP)
    second_hat = second_new / (1.0 - beta_second**ADAM_STEP)
    weight_new = weight - rate * (first_hat / (jnp.sqrt(second_hat) + adam_eps) + decay * weight)
    return (weight_new, first_new, second_new)


def square_sum(values):
    return jnp.sum(values * values)


def dot(a, b, dims):
    return lax.dot_general(a, b, (dims, ((), ())), preferred_element_type=f32)


class Ring:
    def __init__(self, size):
        self.size = size
        self.ring = size == len(CYCLE)

    def hop(self, value, step, sends=None):
        n = self.size
        pairs = [(CYCLE[p], CYCLE[(p + step) % n]) for p in range(n) if sends is None or sends(p)]
        return lax.ppermute(value, "seq", pairs)

    def gather(self, own):
        if not self.ring:
            return [lax.all_gather(own, "seq", axis=0, tiled=True)]
        half = own.shape[0] // 2
        ahead, behind = [own], [own]
        for _ in range(3):
            ahead.append(self.hop(ahead[-1], 1))
            behind.append(self.hop(behind[-1], -1))
        far = [self.hop(behind[-1][:half], -1), self.hop(ahead[-1][half:], 1)]
        return behind + far + ahead[:0:-1]

    def reduce(self, step, first, active=None):
        def sends(k):
            if active is None:
                return None
            return lambda p: CYCLE[(p + k) % self.size] in active

        ahead, behind = first(4), first(5)
        for k in (3, 2, 1):
            ahead = step(k, self.hop(ahead, 1, sends(k + 1)))
            if k > 1:
                behind = step(9 - k, self.hop(behind, -1, sends(-k)))
        return step(0, self.hop(ahead, 1, sends(1)), self.hop(behind, -1, sends(-1)))

    def reduce_product(self, left, right):
        slab = left.shape[1] // self.size

        def block(k):
            return dot(left[:, k * slab : (k + 1) * slab], right, ((0,), (0,)))

        if not self.ring:
            blocks = jnp.concatenate([block(k).astype(bf16) for k in range(self.size)], 0)
            return lax.psum_scatter(blocks, "seq", scatter_dimension=0, tiled=True).astype(f32)

        def step(k, *moved):
            total = block(k)
            for one in moved:
                total = total + one.astype(f32)
            return total.astype(bf16) if k else total

        return self.reduce(step, step)


def butterfly(value, axis, size):
    step = 1
    while step < size:
        value = value + lax.ppermute(value, axis, [(i, i ^ step) for i in range(size)])
        step *= 2
    return value


def gather_tp(value, axis):
    tp = lax.axis_index("tp")

    def join(second, mine, other):
        low = jnp.where(second, other, mine)
        high = jnp.where(second, mine, other)
        return jnp.concatenate([low, high], axis)

    pair = join(tp % 2 == 1, value, lax.ppermute(value, "tp", CORE_SWAP))
    return join(tp >= 2, pair, lax.ppermute(pair, "tp", Y_SWAP))


def psum_tp(halves):
    mine, other = halves
    mine = (mine.astype(f32) + lax.ppermute(other, "tp", CORE_SWAP).astype(f32)).astype(bf16)
    mine = (mine.astype(f32) + lax.ppermute(mine, "tp", Y_SWAP).astype(f32)).astype(bf16)
    return (mine, lax.ppermute(mine, "tp", CORE_SWAP))


def exact_dot(a, b):
    return lax.dot_general(
        a, b, (((1,), (0,)), ((), ())), precision=highest, preferred_element_type=f32
    )


def anywhere():
    return pl.BlockSpec(memory_space=pl.ANY)


def whole(shape):
    return pl.BlockSpec(
        shape, lambda i, *_: (0,) * len(shape), pipeline_mode=pl.Buffered(1)
    )


def rows_block(block, width):
    return pl.BlockSpec((block, width), lambda i, *_: (i, 0))


def lanes_block(rows, block):
    return pl.BlockSpec((rows, block), lambda i, *_: (0, i))


def shape_of(shape, dtype):
    return jax.ShapeDtypeStruct(shape, dtype)


def call(kernel, name, grid, scalars, ins, outs, scratch=(), flops=0, moved=0, exps=0):
    return pl.pallas_call(
        kernel,
        out_shape=tuple(shape_of(shape, dtype) for shape, dtype, _ in outs),
        grid_spec=pltpu.PrefetchScalarGridSpec(
            num_scalar_prefetch=len(scalars),
            grid=(grid,),
            in_specs=[spec for _, spec in ins],
            out_specs=tuple(spec for _, _, spec in outs),
            scratch_shapes=list(scratch),
        ),
        cost_estimate=pl.CostEstimate(flops=flops, bytes_accessed=moved, transcendentals=exps),
        name=name,
    )(*scalars, *[array for array, _ in ins])


def starts_of(chunks):
    at = 0
    for chunk in chunks:
        yield at
        at += chunk.shape[0]


def chunk_copies(chunks, low, high, held, sems):
    return [
        pltpu.make_async_copy(
            chunk.at[:, low:high], held.at[start : start + chunk.shape[0], :], sems.at[j]
        )
        for j, (chunk, start) in enumerate(zip(chunks, starts_of(chunks)))
    ]


def relative_store(ring_size, ring, place, out_ref, value):
    slab = value.shape[1] // ring_size
    if not ring:
        out_ref[...] = value
        return
    for p in range(ring_size):

        @pl.when(place == p)
        def _(p=p):
            for k in range(ring_size):
                s = CYCLE[(p + k) % ring_size]
                out_ref[:, k * slab : (k + 1) * slab] = value[:, s * slab : (s + 1) * slab]


def absolute_store(ring_size, ring, place, out_ref, value):
    slab = value.shape[1] // ring_size
    if not ring:
        out_ref[...] = value
        return
    for p in range(ring_size):

        @pl.when(place == p)
        def _(p=p):
            for k in range(ring_size):
                s = CYCLE[(p + k) % ring_size]
                out_ref[:, s * slab : (s + 1) * slab] = value[:, k * slab : (k + 1) * slab]


def onehot_rows(segment_col):
    items = lax.broadcasted_iota(jnp.int32, (segment_col.shape[0], ITEMS), 1)
    return (segment_col == items).astype(f32)


def onehot_cols(segment_row):
    items = lax.broadcasted_iota(jnp.int32, (ITEMS, segment_row.shape[1]), 0)
    return (segment_row == items).astype(f32)


def modulate(onehot, mod_ref, block):
    return exact_dot(onehot, mod_ref[block * ITEMS : (block + 1) * ITEMS, :])


def enter_kernel(scal, x_ref, g_ref, mod_ref, gain_ref, sc_ref,
                 xr_ref, gr_ref, modr_ref, gainr_ref, hidden_ref, *, size, ring):
    place = scal[0]

    @pl.when(pl.program_id(0) == 0)
    def _():
        relative_store(size, ring, place, modr_ref, mod_ref[...])
        relative_store(size, ring, place, gainr_ref, gain_ref[...])

    relative_store(size, ring, place, xr_ref, x_ref[...])
    relative_store(size, ring, place, gr_ref, g_ref[...])
    x = xr_ref[...].astype(f32)
    normed, _ = rms_parts(x)
    onehot = onehot_rows(sc_ref[...])
    scale = modulate(onehot, modr_ref, 1)
    shift = modulate(onehot, modr_ref, 0)
    hidden_ref[...] = (normed * gainr_ref[0:1, :] * (1.0 + scale) + shift).astype(bf16)


def project_kernel(hidden_ref, *refs, heads, first_owner, count):
    chunks, (slab_ref, held, sems) = refs[:count], refs[count:]
    width = heads * HD
    copies = chunk_copies(chunks, 0, 3 * width, held, sems)
    for one in copies:
        one.start()
    for s in range(slab_ref.shape[0]):
        if not first_owner <= s < first_owner + heads:
            slab_ref[s] = jnp.zeros(slab_ref.shape[1:], bf16)
    for one in copies:
        one.wait()
    hidden = hidden_ref[...]
    for j in range(3):
        part = dot(hidden, held[:, j * width : (j + 1) * width], ((1,), (0,))).astype(bf16)
        if j == 0:
            part = part * jnp.asarray(score_scale, bf16)
        for h in range(heads):
            slab_ref[first_owner + h, :, j * HD : (j + 1) * HD] = part[:, h * HD : (h + 1) * HD]


def split_halves(core, full_ref, mine_ref, other_ref):
    half = mine_ref.shape[0]
    mine_ref[...] = full_ref[pl.ds(pl.multiple_of(core * half, half), half), :]
    other_ref[...] = full_ref[pl.ds(pl.multiple_of((1 - core) * half, half), half), :]


def join_halves(core, mine_ref, other_ref, full_ref):
    half = mine_ref.shape[0]
    full_ref[pl.ds(pl.multiple_of(core * half, half), half), :] = mine_ref[...]
    full_ref[pl.ds(pl.multiple_of((1 - core) * half, half), half), :] = other_ref[...]


def times_turned(value_ref, held, full_ref):
    tiles = held.shape[0] // WIDE

    def one(i, _):
        at = pl.ds(pl.multiple_of(i * WIDE, WIDE), WIDE)
        full_ref[:, at] = dot(value_ref[...], held[at, :], ((1,), (1,))).astype(bf16)
        return 0

    lax.fori_loop(0, tiles, one, 0)


def out_kernel(scal, slab_ref, *refs, heads, first_owner, count, low, high):
    chunks, (mixed_ref, mine_ref, other_ref, held, full, sems) = refs[:count], refs[count:]
    copies = chunk_copies(chunks, low, high, held, sems)
    for one in copies:
        one.start()
    for h in range(heads):
        mixed_ref[:, h * HD : (h + 1) * HD] = slab_ref[first_owner + h]
    for one in copies:
        one.wait()
    times_turned(mixed_ref, held, full)
    split_halves(scal[1], full, mine_ref, other_ref)


def qkv_back_kernel(scal, slab_ref, *refs, heads, first_owner, count):
    chunks, (grads_ref, mine_ref, other_ref, held, full, sems) = refs[:count], refs[count:]
    width = heads * HD
    copies = chunk_copies(chunks, 0, 3 * width, held, sems)
    for one in copies:
        one.start()
    for j in range(3):
        for h in range(heads):
            at = j * width + h * HD
            grads_ref[:, at : at + HD] = slab_ref[first_owner + h, :, j * HD : (j + 1) * HD]
    for one in copies:
        one.wait()
    times_turned(grads_ref, held, full)
    split_halves(scal[1], full, mine_ref, other_ref)


def ffn_kernel(scal, x_ref, g_ref, am_ref, ao_ref, modr_ref, gainr_ref, sc_ref, *refs,
               count, units):
    chunks = refs[:count]
    (mid_ref, hidden_ref, fgrad_ref, inner_ref, both_ref, hm_ref, ho_ref, fm_ref, fo_ref,
     held, attn, full, sems) = refs[count:]
    core = scal[1]
    copies = chunk_copies(chunks, 0, held.shape[1], held, sems)
    for one in copies:
        one.start()
    join_halves(core, am_ref, ao_ref, attn)

    def prepare(i, _):
        at = pl.ds(pl.multiple_of(i * ROWS, ROWS), ROWS)
        onehot = onehot_rows(sc_ref[at, :])
        x_mid = x_ref[at, :].astype(f32) + jnp.tanh(modulate(onehot, modr_ref, 2)) * attn[
            at, :
        ].astype(f32)
        mid_ref[at, :] = x_mid
        normed, _ = rms_parts(x_mid)
        scale = modulate(onehot, modr_ref, 4)
        shift = modulate(onehot, modr_ref, 3)
        hidden_ref[at, :] = (normed * gainr_ref[1:2, :] * (1.0 + scale) + shift).astype(bf16)
        tanh_ffn = jnp.tanh(modulate(onehot, modr_ref, 5))
        fgrad_ref[at, :] = (g_ref[at, :].astype(f32) * tanh_ffn).astype(bf16)
        return 0

    lax.fori_loop(0, x_ref.shape[0] // ROWS, prepare, 0)
    for one in copies:
        one.wait()

    def tile(i, _):
        def at(base):
            return pl.ds(pl.multiple_of(base + i * WIDE, WIDE), WIDE)

        gate_pre = dot(hidden_ref[...], held[:, at(0)], ((1,), (0,)))
        up_pre = dot(hidden_ref[...], held[:, at(units)], ((1,), (0,)))
        inner_grad = dot(fgrad_ref[...], held[:, at(2 * units)], ((1,), (0,)))
        sigmoid = jax.nn.sigmoid(gate_pre)
        silu = gate_pre * sigmoid
        inner_ref[:, at(0)] = (silu * up_pre).astype(bf16)
        both_ref[:, at(0)] = (
            inner_grad * up_pre * sigmoid * (1.0 + gate_pre * (1.0 - sigmoid))
        ).astype(bf16)
        both_ref[:, at(units)] = (inner_grad * silu).astype(bf16)
        return 0

    lax.fori_loop(0, units // WIDE, tile, 0)
    times_turned(both_ref, held.at[:, 0 : 2 * units], full)
    split_halves(core, full, hm_ref, ho_ref)
    times_turned(inner_ref, held.at[:, 2 * units : 3 * units], full)
    split_halves(core, full, fm_ref, fo_ref)


def mid_kernel(scal, mid_ref, g_ref, hm_ref, ho_ref, modr_ref, gainr_ref, sc_ref, *refs,
               heads, first_owner, count, low, high):
    chunks = refs[:count]
    grad_ref, agrad_ref, slab_ref, held, hgrad, sems = refs[count:]
    copies = chunk_copies(chunks, low, high, held, sems)
    for one in copies:
        one.start()
    join_halves(scal[1], hm_ref, ho_ref, hgrad)
    for s in range(slab_ref.shape[0]):
        if not first_owner <= s < first_owner + heads:
            slab_ref[s] = jnp.zeros(slab_ref.shape[1:], bf16)

    def prepare(i, _):
        at = pl.ds(pl.multiple_of(i * ROWS, ROWS), ROWS)
        onehot = onehot_rows(sc_ref[at, :])
        normed, inverse = rms_parts(mid_ref[at, :])
        scale = modulate(onehot, modr_ref, 4)
        normed_grad = hgrad[at, :].astype(f32) * gainr_ref[1:2, :] * (1.0 + scale)
        grad = g_ref[at, :].astype(f32) + rms_back(normed, inverse, normed_grad)
        grad_ref[at, :] = grad
        agrad_ref[at, :] = (grad * jnp.tanh(modulate(onehot, modr_ref, 2))).astype(bf16)
        return 0

    lax.fori_loop(0, mid_ref.shape[0] // ROWS, prepare, 0)
    for one in copies:
        one.wait()
    mixed = dot(agrad_ref[...], held[...], ((1,), (0,))).astype(bf16)
    for h in range(heads):
        slab_ref[first_owner + h] = mixed[:, h * HD : (h + 1) * HD]


def own_rows(core, mine_ref, other_ref):
    first = pl.program_id(0) < pl.num_programs(0) // 2
    mine = jnp.logical_xor(first, core == 1)
    return jnp.where(mine, mine_ref[...].astype(f32), other_ref[...].astype(f32))


def side_kernel(scal, mid_ref, grad_ref, g_ref, am_ref, ao_ref, fm_ref, fo_ref, hm_ref, ho_ref,
                modr_ref, gainr_ref, sc_ref, sr_ref,
                block_ref, sums_ref, gain_ref, *, size, ring):
    place, core = scal[0], scal[1]

    @pl.when(pl.program_id(0) == 0)
    def _():
        sums_ref[...] = jnp.zeros_like(sums_ref)
        gain_ref[...] = jnp.zeros_like(gain_ref)

    attn = own_rows(core, am_ref, ao_ref)
    ffn_out = own_rows(core, fm_ref, fo_ref)
    hgrad = own_rows(core, hm_ref, ho_ref)
    onehot = onehot_rows(sc_ref[...])
    by_item = onehot_cols(sr_ref[0])
    tanh_attn = jnp.tanh(modulate(onehot, modr_ref, 2))
    tanh_ffn = jnp.tanh(modulate(onehot, modr_ref, 5))
    scale = modulate(onehot, modr_ref, 4)
    x_mid = mid_ref[...]
    absolute_store(size, ring, place, block_ref, x_mid + tanh_ffn * ffn_out)
    normed, _ = rms_parts(x_mid)

    def add(block, value):
        sums_ref[block * ITEMS : (block + 1) * ITEMS, :] += exact_dot(by_item, value)

    add(0, grad_ref[...] * attn * (1.0 - tanh_attn * tanh_attn))
    add(1, hgrad)
    add(2, hgrad * normed * gainr_ref[1:2, :])
    add(3, g_ref[...].astype(f32) * ffn_out * (1.0 - tanh_ffn * tanh_ffn))
    gain_ref[0:1, :] += jnp.sum(hgrad * normed * (1.0 + scale), axis=0, keepdims=True)


def leave_kernel(scal, x_ref, grad_ref, hm_ref, ho_ref, modr_ref, gainr_ref, sc_ref, sr_ref,
                 early_ref, egain_ref, input_ref, sums_ref, gain_ref, total, turned, *, size, ring):
    place, core = scal[0], scal[1]

    @pl.when(pl.program_id(0) == 0)
    def _():
        total[...] = jnp.zeros_like(total)
        total[2 * ITEMS : 6 * ITEMS, :] = early_ref[...]
        total[6 * ITEMS + 1 : 6 * ITEMS + 2, :] = egain_ref[0:1, :]

    hgrad = own_rows(core, hm_ref, ho_ref)
    onehot = onehot_rows(sc_ref[...])
    by_item = onehot_cols(sr_ref[0])
    scale = modulate(onehot, modr_ref, 1)
    normed, inverse = rms_parts(x_ref[...].astype(f32))
    normed_grad = hgrad * gainr_ref[0:1, :] * (1.0 + scale)
    absolute_store(
        size, ring, place, input_ref, grad_ref[...] + rms_back(normed, inverse, normed_grad)
    )
    total[0:ITEMS, :] += exact_dot(by_item, hgrad)
    total[ITEMS : 2 * ITEMS, :] += exact_dot(by_item, hgrad * normed * gainr_ref[0:1, :])
    total[6 * ITEMS : 6 * ITEMS + 1, :] += jnp.sum(
        hgrad * normed * (1.0 + scale), axis=0, keepdims=True
    )

    @pl.when(pl.program_id(0) == pl.num_programs(0) - 1)
    def _():
        absolute_store(size, ring, place, turned, total[...])
        quarter = sums_ref.shape[1]
        at = pl.ds(pl.multiple_of(scal[2] * quarter, quarter), quarter)
        sums_ref[...] = turned[0 : 6 * ITEMS, at]
        gain_ref[...] = turned[6 * ITEMS : 6 * ITEMS + 8, :]


def text_heads_kernel(w_ref, out_ref):
    for h in range(out_ref.shape[0]):
        for j in range(2):
            out_ref[h, :, j * HD : (j + 1) * HD] = w_ref[j, :, h * HD : (h + 1) * HD].astype(bf16)


def text_step_kernel(head_of, cap_ref, w_ref, *refs):
    total = dot(cap_ref[...], w_ref[0], ((1,), (0,)))
    for moved in refs[:-1]:
        total = total + moved[...].astype(f32)
    refs[-1][...] = total.astype(refs[-1].dtype)


def mod_kernel(scal, embed_ref, w_ref, out_ref):
    out_ref[...] = dot(embed_ref[...], w_ref[...].astype(bf16), ((1,), (0,)))


def text_join_kernel(head_at, low_ref, high_ref, k_ref, v_ref):
    for j, ref in enumerate((low_ref, high_ref)):
        k_ref[:, j * HD : (j + 1) * HD] = ref[0, :, :HD]
        v_ref[:, j * HD : (j + 1) * HD] = ref[0, :, HD:]


def turned_copy(source_ref, low, out_ref, block):
    def one(j, _):
        at = pl.ds(pl.multiple_of(j * block, block), block)
        out_ref[:, at] = jnp.transpose(source_ref[at, low : low + HD].astype(f32)).astype(bf16)
        return 0

    lax.fori_loop(0, source_ref.shape[0] // block, one, 0)


def self_kernel(table, q_ref, all_ref, sq_ref, sk_ref, out_ref, stat_ref, k_ref, vt_ref, *, block_k):
    i = pl.program_id(0)

    @pl.when(i == 0)
    def _():
        k_ref[...] = all_ref[:, HD : 2 * HD]
        turned_copy(all_ref, 2 * HD, vt_ref, block_k)

    q = q_ref[:, :HD]
    item_of_q = sq_ref[...]
    width = q.shape[0]

    def step(j, carry):
        top, total, out = carry
        at = pl.ds(pl.multiple_of(j * block_k, block_k), block_k)
        scores = dot(k_ref[at, :], q, ((1,), (1,)))
        scores = jnp.where(sk_ref[at, :] == item_of_q, scores, masked_score)
        new_top = jnp.maximum(top, jnp.max(scores, axis=0, keepdims=True))
        weights = jnp.exp(scores - new_top)
        shrink = jnp.exp(top - new_top)
        total = total * shrink + jnp.sum(weights, axis=0, keepdims=True)
        out = out * shrink + dot(vt_ref[:, at], weights.astype(bf16), ((1,), (0,)))
        return (new_top, total, out)

    start = (
        jnp.full((1, width), lowest_max, f32),
        jnp.zeros((1, width), f32),
        jnp.zeros((HD, width), f32),
    )
    top, total, out = lax.fori_loop(table[0, i], table[1, i], step, start)
    out_ref[...] = out / total
    stat_ref[...] = top + jnp.log(total)


def text_kernel(table, gate, q_ref, kv_ref, self_ref, sq_ref,
                mixed_ref, out_ref, stat_ref, k_ref, vt_ref):
    i = pl.program_id(0)

    @pl.when(i == 0)
    def _():
        k_ref[...] = kv_ref[:, :HD]
        turned_copy(kv_ref, HD, vt_ref, TEXT)

    q = q_ref[:, :HD]
    item_of_q = sq_ref[...]

    def step(item, carry):
        out, stat = carry
        at = pl.ds(pl.multiple_of(item * TEXT, TEXT), TEXT)
        scores = dot(k_ref[at, :], q, ((1,), (1,)))
        top = jnp.max(scores, axis=0, keepdims=True)
        weights = jnp.exp(scores - top)
        total = jnp.sum(weights, axis=0, keepdims=True)
        probs = (weights / total).astype(bf16)
        part = dot(vt_ref[:, at], probs, ((1,), (0,)))
        here = item_of_q == item
        return (jnp.where(here, part, out), jnp.where(here, top + jnp.log(total), stat))

    start = (jnp.zeros((HD, q.shape[0]), f32), jnp.zeros((1, q.shape[0]), f32))
    text_out, stat = lax.fori_loop(table[2, i], table[3, i], step, start)
    out_ref[...] = text_out
    stat_ref[...] = stat
    mixed_ref[...] = jnp.transpose(self_ref[...] + gate[0] * text_out).astype(bf16)


def text_back_kernel(table, gate, q_ref, g_ref, kv_ref, text_ref, stat_ref, sq_ref,
                     dkv_ref, dq_ref, cross_ref, k_ref, v_ref, kt_ref, dk_sum, dv_sum):
    i = pl.program_id(0)

    @pl.when(i == 0)
    def _():
        k_ref[...] = kv_ref[:, :HD]
        v_ref[...] = kv_ref[:, HD:]
        turned_copy(kv_ref, 0, kt_ref, TEXT)
        dk_sum[...] = jnp.zeros_like(dk_sum)
        dv_sum[...] = jnp.zeros_like(dv_sum)

    q = q_ref[:, :HD]
    item_of_q = sq_ref[...]
    g_value = g_ref[...].astype(f32)
    g = (g_value * gate[0]).astype(bf16)
    text_out = text_ref[...]
    cross_ref[...] = jnp.sum(jnp.transpose(g_value) * text_out, axis=0, keepdims=True)
    delta = jnp.sum(jnp.transpose(g.astype(f32)) * text_out, axis=0, keepdims=True)
    stat = stat_ref[...]

    def step(item, total):
        at = pl.ds(pl.multiple_of(item * TEXT, TEXT), TEXT)
        scores = dot(k_ref[at, :], q, ((1,), (1,)))
        probs = jnp.exp(jnp.where(item_of_q == item, scores - stat, masked_score))
        prob_grad = dot(v_ref[at, :], g, ((1,), (1,)))
        score_grad = (probs * (prob_grad - delta)).astype(bf16)
        dk_sum[at, :] += dot(score_grad, q, ((1,), (0,)))
        dv_sum[at, :] += dot(probs.astype(bf16), g, ((1,), (0,)))
        return total + dot(kt_ref[:, at], score_grad, ((1,), (0,)))

    start = jnp.zeros((HD, q.shape[0]), f32)
    dq_ref[...] = lax.fori_loop(table[2, i], table[3, i], step, start)

    @pl.when(i == pl.num_programs(0) - 1)
    def _():
        dkv_ref[:, :HD] = dk_sum[...].astype(bf16)
        dkv_ref[:, HD:] = dv_sum[...].astype(bf16)


def self_back_kernel(table, q_ref, g_ref, all_ref, self_ref, stat_ref, start_ref, sq_ref, sk_ref,
                     dqkv_ref, k_ref, v_ref, kt_ref, dk_sum, dv_sum, *, block_k):
    i = pl.program_id(0)

    @pl.when(i == 0)
    def _():
        k_ref[...] = all_ref[:, HD : 2 * HD]
        v_ref[...] = all_ref[:, 2 * HD :]
        turned_copy(all_ref, HD, kt_ref, block_k)
        dk_sum[...] = jnp.zeros_like(dk_sum)
        dv_sum[...] = jnp.zeros_like(dv_sum)

    q = q_ref[:, :HD]
    g = g_ref[...]
    item_of_q = sq_ref[...]
    delta = jnp.sum(jnp.transpose(g.astype(f32)) * self_ref[...], axis=0, keepdims=True)
    stat = stat_ref[...]

    def step(j, total):
        at = pl.ds(pl.multiple_of(j * block_k, block_k), block_k)
        scores = dot(k_ref[at, :], q, ((1,), (1,)))
        allowed = sk_ref[at, :] == item_of_q
        probs = jnp.exp(jnp.where(allowed, scores - stat, masked_score))
        prob_grad = dot(v_ref[at, :], g, ((1,), (1,)))
        score_grad = (probs * (prob_grad - delta)).astype(bf16)
        dk_sum[at, :] += dot(score_grad, q, ((1,), (0,)))
        dv_sum[at, :] += dot(probs.astype(bf16), g, ((1,), (0,)))
        return total + dot(kt_ref[:, at], score_grad, ((1,), (0,)))

    total = lax.fori_loop(table[0, i], table[1, i], step, start_ref[...])
    rows = q.shape[0]
    dqkv_ref[pl.ds(pl.multiple_of(i * rows, rows), rows), :HD] = jnp.transpose(
        total * score_scale
    ).astype(bf16)

    @pl.when(i == pl.num_programs(0) - 1)
    def _():
        dqkv_ref[:, HD : 2 * HD] = dk_sum[...].astype(bf16)
        dqkv_ref[:, 2 * HD :] = dv_sum[...].astype(bf16)


def attention_table(segments, block_q, block_k):
    by_block = segments.reshape(-1, block_q)
    low_item, high_item = by_block[:, 0], by_block[:, -1]
    first_key = jnp.sum(segments[None, :] < low_item[:, None], axis=1)
    end_key = jnp.sum(segments[None, :] <= high_item[:, None], axis=1)
    return jnp.stack(
        [first_key // block_k, (end_key + block_k - 1) // block_k, low_item, high_item + 1]
    ).astype(jnp.int32)


def per_device(
    x_tokens, caption, timesteps, segment_ids, out_grad,
    mod_weight, mod_first, mod_second,
    norm_gains, gains_first, gains_second,
    qkv_weight, qkv_first, qkv_second,
    out_weight, out_first, out_second,
    text_weight, text_first, text_second,
    cross_gates, cross_first, cross_second,
    updown_weight, updown_first, updown_second,
    down_weight, down_first, down_second,
    *, seq_size, tp_size,
):
    seq_index = lax.axis_index("seq")
    tp_index = lax.axis_index("tp")
    ring = Ring(seq_size)
    here, width = x_tokens.shape
    heads = cross_gates.shape[0]
    local_width = heads * HD
    count = here * seq_size
    units = down_weight.shape[0]
    quarter = width // tp_size
    first_owner = 1 if seq_size >= heads + 2 else 0
    owners = range(first_owner, first_owner + heads)
    seqs = jnp.full((seq_size,), seq_index)
    place = jnp.where(seqs % 2 == 0, seqs // 2, (15 - seqs) // 2)
    places = (place + jnp.arange(seq_size)) % seq_size
    slab_owner = jnp.where(places < 4, 2 * places, 15 - 2 * places)
    slab_head = jnp.clip(slab_owner - first_owner, 0, heads - 1)
    my_head = jnp.clip(seq_index - first_owner, 0, heads - 1)
    is_owner = (seq_index >= first_owner) & (seq_index < first_owner + heads)
    tps = jnp.full((1,), tp_index)
    scal = jnp.concatenate([place[:1], tps % 2, tps]).astype(jnp.int32)
    which = {"size": seq_size, "ring": ring.ring}

    def exchange(slabs):
        return lax.all_to_all(slabs, "seq", 0, 0, tiled=True)

    silu_embed = jax.nn.silu(time_embed(timesteps)).astype(bf16)
    mod_rows = mod_weight.shape[0]
    embed_rows = lax.dynamic_slice_in_dim(silu_embed, seq_index * mod_rows, mod_rows, 1)
    mod_part = call(
        mod_kernel, "modulation", 6, [scal],
        [
            (embed_rows, whole((ITEMS, mod_rows))),
            (mod_weight, pl.BlockSpec((mod_rows, quarter), lambda i, s: (0, i * tp_size + s[2]))),
        ],
        [((6 * ITEMS, quarter), f32, rows_block(ITEMS, quarter))],
        moved=mod_rows * 6 * quarter * 4, flops=2 * ITEMS * mod_rows * 6 * quarter,
    )[0]
    is_here = jnp.arange(seq_size) == seq_index
    slots = jnp.where(is_here[:, None], segment_ids.astype(f32)[None, :], 0.0).reshape(-1)
    gain_cols = norm_gains.shape[1]
    gain_slots = jnp.where(is_here[None, :, None], norm_gains[:, None, :], 0.0).reshape(-1)
    spare = -(slots.size + gain_slots.size) % (8 * quarter)
    packed = jnp.concatenate([slots, gain_slots, jnp.zeros((spare,), f32)]).reshape(-1, quarter)
    packed = butterfly(jnp.concatenate([mod_part, packed]), "seq", seq_size)
    modulation = gather_tp(packed[: 6 * ITEMS], 1)
    packed = packed[6 * ITEMS :].reshape(-1)
    segments = packed[:count].astype(jnp.int32)
    gains_value = packed[count : count + 2 * width].reshape(2, width).astype(bf16).astype(f32)
    gains_value = jnp.concatenate([gains_value] * 4)

    def turned(shard):
        return jnp.transpose(shard.astype(bf16), (1, 0, 2)).reshape(shard.shape[1], -1)

    attn_chunks = ring.gather(
        jnp.concatenate([turned(qkv_weight), out_weight.astype(bf16).T], axis=1)
    )
    pieces = len(attn_chunks)
    piece_sems = pltpu.SemaphoreType.DMA((pieces,))
    attn_ins = [(chunk, anywhere()) for chunk in attn_chunks]
    qkv_width = 3 * local_width

    cap_rows = caption.shape[0]
    cap_cols = caption.shape[1] // seq_size
    cap_part = cap_cols // tp_size
    text_rows = cap_rows * seq_size
    if cap_part % 128 == 0:
        cap_own = call(
            lambda scal, in_ref, out_ref: out_ref.__setitem__(0, in_ref[...]),
            "caption_slabs", seq_size, [scal],
            [(caption, pl.BlockSpec((cap_rows, cap_part), lambda i, s: (0, i * tp_size + s[2])))],
            [
                (
                    (seq_size, cap_rows, cap_part), bf16,
                    pl.BlockSpec((1, cap_rows, cap_part), lambda i, s: (i, 0, 0)),
                )
            ],
            moved=2 * cap_rows * cap_cols * 4,
        )[0]
    else:
        cap_own = lax.dynamic_index_in_dim(
            caption.reshape(cap_rows, seq_size, tp_size, cap_part), tp_index, 2, keepdims=False
        )
        cap_own = jnp.transpose(cap_own, (1, 0, 2))
    caption_cols = gather_tp(exchange(cap_own).reshape(text_rows, cap_part), 1)
    text_by_head = call(
        text_heads_kernel, "text_heads", 1, [],
        [(text_weight, whole(text_weight.shape))],
        [((heads, cap_cols, 2 * HD), bf16, whole((heads, cap_cols, 2 * HD)))],
        moved=text_weight.size * 6,
    )[0]
    text_block = math.gcd(text_rows, 512)

    def text_step(k, *moved):
        block = rows_block(text_block, 2 * HD)
        return call(
            text_step_kernel, "text_step", text_rows // text_block, [slab_head],
            [
                (caption_cols, rows_block(text_block, cap_cols)),
                (
                    text_by_head,
                    pl.BlockSpec((1, cap_cols, 2 * HD), lambda i, head_of: (head_of[k], 0, 0)),
                ),
            ]
            + [(one, block) for one in moved],
            [((text_rows, 2 * HD), bf16, block)],
            moved=text_rows * cap_cols * 2, flops=4 * text_rows * cap_cols * HD,
        )[0]

    if ring.ring:
        text_kv = ring.reduce(text_step, text_step, owners)
    else:
        parts = jnp.einsum("rc,hcw->hrw", caption_cols, text_by_head, preferred_element_type=f32)
        after = seq_size - heads - first_owner
        parts = jnp.pad(parts.astype(bf16), ((first_owner, after), (0, 0), (0, 0)))
        text_kv = lax.psum_scatter(parts, "seq", scatter_dimension=0, tiled=False)

    ffn_chunks = ring.gather(
        jnp.concatenate([turned(updown_weight), down_weight.astype(bf16).T], axis=1)
    )
    ffn_ins = [(chunk, anywhere()) for chunk in ffn_chunks]

    segment_col = segment_ids[:, None]
    steps = here // ROWS
    segment_row = segment_ids.reshape(steps, 1, ROWS)
    row_ins = [
        (segment_col, rows_block(ROWS, 1)),
        (segment_row, pl.BlockSpec((1, 1, ROWS), lambda i, *_: (i, 0, 0))),
    ]
    block = rows_block(ROWS, width)
    mod_shape, gain_shape = modulation.shape, gains_value.shape
    x_rel, g_rel, mod_rel, gain_rel, hidden_attn = call(
        functools.partial(enter_kernel, **which), "enter", steps, [scal],
        [
            (x_tokens, block), (out_grad, block), (modulation, whole(mod_shape)),
            (gains_value, whole(gain_shape)), row_ins[0],
        ],
        [
            ((here, width), bf16, block), ((here, width), bf16, block),
            (mod_shape, f32, whole(mod_shape)), (gain_shape, f32, whole(gain_shape)),
            ((here, width), bf16, block),
        ],
        moved=here * width * 10,
    )
    mod_ins = [(mod_rel, whole(mod_shape)), (gain_rel, whole(gain_shape))]
    full_ins = mod_ins + [(segment_col, whole((here, 1)))]
    slab_shape = (seq_size, here, 3 * HD)
    slabs = call(
        functools.partial(
            project_kernel, heads=heads, first_owner=first_owner, count=pieces
        ),
        "project", 1, [],
        [(hidden_attn, whole((here, width)))] + attn_ins,
        [(slab_shape, bf16, whole(slab_shape))],
        [pltpu.VMEM((width, qkv_width), bf16), piece_sems],
        moved=width * qkv_width * 2, flops=2 * here * width * qkv_width,
    )[0]
    qkv_head = exchange(slabs).reshape(count, 3 * HD)

    block_q = math.gcd(count, 512)
    block_k = math.gcd(count, 512)
    table = attention_table(segments, block_q, block_k)
    tanh_cross = jnp.tanh(cross_gates)
    my_gate = jnp.sum(jnp.where(jnp.arange(heads) == my_head, tanh_cross, 0.0)).reshape(1)
    blocks = count // block_q
    q_ins = [(qkv_head, rows_block(block_q, 3 * HD))]
    seg_row = (segments[None, :], lanes_block(1, block_q))
    seg_col = (segments[:, None], whole((count, 1)))
    turned_out = ((HD, count), f32, lanes_block(HD, block_q))
    stat_out = ((1, count), f32, lanes_block(1, block_q))
    area = count * count * HD
    self_out, stat = call(
        functools.partial(self_kernel, block_k=block_k), "attend", blocks, [table],
        q_ins + [(qkv_head, whole(qkv_head.shape)), seg_row, seg_col],
        [turned_out, stat_out],
        [pltpu.VMEM((count, HD), bf16), pltpu.VMEM((HD, count), bf16)],
        flops=4 * area, moved=count * HD * 20, exps=count * count,
    )
    mixed_head, text_out, text_stat = call(
        text_kernel, "attend_text", blocks, [table, my_gate],
        q_ins
        + [(text_kv, whole(text_kv.shape)), (self_out, lanes_block(HD, block_q)), seg_row],
        [((count, HD), bf16, rows_block(block_q, HD)), turned_out, stat_out],
        [pltpu.VMEM((text_rows, HD), bf16), pltpu.VMEM((HD, text_rows), bf16)],
        flops=4 * count * TEXT * HD, moved=count * HD * 20, exps=count * TEXT,
    )
    mixed_slabs = exchange(mixed_head.reshape(seq_size, here, HD))
    low, high = qkv_width, qkv_width + local_width
    head_args = {"heads": heads, "first_owner": first_owner, "count": pieces}
    half_shape = (here // 2, width)
    half_out = (half_shape, bf16, whole(half_shape))
    slab64 = (seq_size, here, HD)
    held_out = [pltpu.VMEM((width, local_width), bf16)]
    full_sum = [pltpu.VMEM((here, width), bf16), piece_sems]
    mixed, *attn = call(
        functools.partial(out_kernel, low=low, high=high, **head_args), "out", 1, [scal],
        [(mixed_slabs, whole(slab64))] + attn_ins,
        [((here, local_width), bf16, whole((here, local_width))), half_out, half_out],
        held_out + full_sum,
        moved=width * local_width * 2, flops=2 * here * width * local_width,
    )
    attn = psum_tp(attn)

    def halves(pair, spec=None):
        return [(one, spec or whole(half_shape)) for one in pair]

    tokens = (here, width)
    x_mid, hidden_ffn, ffn_grad, inner, both_grads, hm, ho, fm, fo = call(
        functools.partial(ffn_kernel, count=pieces, units=units), "ffn", 1, [scal],
        [(x_rel, whole(tokens)), (g_rel, whole(tokens))] + halves(attn) + full_ins + ffn_ins,
        [
            (tokens, f32, whole(tokens)), (tokens, bf16, whole(tokens)),
            (tokens, bf16, whole(tokens)), ((here, units), bf16, whole((here, units))),
            ((here, 2 * units), bf16, whole((here, 2 * units))),
            half_out, half_out, half_out, half_out,
        ],
        [pltpu.VMEM((width, 3 * units), bf16), pltpu.VMEM(tokens, bf16)] + full_sum,
        moved=width * 3 * units * 2, flops=12 * here * width * units,
    )
    hgrad = psum_tp((hm, ho))
    ffn_out = psum_tp((fm, fo))
    down_owned = ring.reduce_product(ffn_grad, inner)
    updown_rows = ring.reduce_product(hidden_ffn, both_grads)

    mid_grad, attn_grad, grad_slabs = call(
        functools.partial(mid_kernel, low=low, high=high, **head_args), "mid", 1, [scal],
        [(x_mid, whole(tokens)), (g_rel, whole(tokens))] + halves(hgrad) + full_ins + attn_ins,
        [(tokens, f32, whole(tokens)), (tokens, bf16, whole(tokens)), (slab64, bf16, whole(slab64))],
        held_out + full_sum,
        moved=width * local_width * 2, flops=2 * here * width * local_width,
    )
    head_grad = exchange(grad_slabs).reshape(count, HD)
    out_owned = ring.reduce_product(attn_grad, mixed)
    half_block = pl.BlockSpec((ROWS, width), lambda i, *_: (i % (steps // 2), 0))
    sums_shape, one_gain = (4 * ITEMS, width), (8, width)
    block_out, early_sums, early_gain = call(
        functools.partial(side_kernel, **which), "side", steps, [scal],
        [(x_mid, block), (mid_grad, block), (g_rel, block)]
        + halves(attn, half_block) + halves(ffn_out, half_block) + halves(hgrad, half_block)
        + mod_ins + row_ins,
        [(tokens, f32, block), (sums_shape, f32, whole(sums_shape)), (one_gain, f32, whole(one_gain))],
        moved=here * width * 24,
    )

    g_ins = [(head_grad, rows_block(block_q, HD))]
    kv64 = pltpu.VMEM((text_rows, HD), bf16)
    text_dkv, text_dq, cross_rows = call(
        text_back_kernel, "attend_text_back", blocks, [table, my_gate],
        q_ins + g_ins
        + [
            (text_kv, whole(text_kv.shape)), (text_out, lanes_block(HD, block_q)),
            (text_stat, lanes_block(1, block_q)), seg_row,
        ],
        [((text_rows, 2 * HD), bf16, whole((text_rows, 2 * HD))), turned_out, stat_out],
        [kv64, kv64, pltpu.VMEM((HD, text_rows), bf16)] + [pltpu.VMEM((text_rows, HD), f32)] * 2,
        flops=10 * count * TEXT * HD, moved=count * HD * 20, exps=count * TEXT,
    )
    head64 = pltpu.VMEM((count, HD), bf16)
    dqkv = call(
        functools.partial(self_back_kernel, block_k=block_k), "attend_back", blocks, [table],
        q_ins + g_ins
        + [
            (qkv_head, whole(qkv_head.shape)), (self_out, lanes_block(HD, block_q)),
            (stat, lanes_block(1, block_q)), (text_dq, lanes_block(HD, block_q)), seg_row, seg_col,
        ],
        [(qkv_head.shape, bf16, whole(qkv_head.shape))],
        [head64, head64, pltpu.VMEM((HD, count), bf16)] + [pltpu.VMEM((count, HD), f32)] * 2,
        flops=10 * area, moved=count * HD * 20, exps=count * count,
    )[0]

    text_grads = ring.gather(text_dkv)
    text_grads = jnp.concatenate(text_grads, axis=0).reshape(seq_size, text_rows, 2 * HD)
    head_at = jnp.argmax(
        (slab_owner if ring.ring else jnp.arange(seq_size))[None, :]
        == jnp.arange(first_owner, first_owner + heads)[:, None], axis=1,
    ).astype(jnp.int32)
    pair_block = pl.BlockSpec((text_rows, 2 * HD), lambda i, at: (0, i))
    text_grad_keys, text_grad_values = call(
        text_join_kernel, "text_join", heads // 2, [head_at],
        [
            (text_grads, pl.BlockSpec((1, text_rows, 2 * HD), lambda i, at: (at[2 * i], 0, 0))),
            (text_grads, pl.BlockSpec((1, text_rows, 2 * HD), lambda i, at: (at[2 * i + 1], 0, 0))),
        ],
        [((text_rows, local_width), bf16, pair_block)] * 2,
        moved=text_rows * local_width * 8,
    )
    text_owned = jnp.stack(
        [dot(caption_cols, one, ((0,), (0,))) for one in (text_grad_keys, text_grad_values)]
    )

    back_slabs = exchange(dqkv.reshape(slab_shape))
    qkv_grads, *hidden_grad = call(
        functools.partial(qkv_back_kernel, **head_args), "qkv_back", 1, [scal],
        [(back_slabs, whole(slab_shape))] + attn_ins,
        [((here, qkv_width), bf16, whole((here, qkv_width))), half_out, half_out],
        [pltpu.VMEM((width, qkv_width), bf16)] + full_sum,
        moved=width * qkv_width * 2, flops=2 * here * width * qkv_width,
    )
    qkv_rows = ring.reduce_product(hidden_attn, qkv_grads)
    hidden_grad = psum_tp(hidden_grad)
    all_sums = (6 * ITEMS, quarter)
    input_grad, item_sums, gain_sums = call(
        functools.partial(leave_kernel, **which), "leave", steps, [scal],
        [(x_rel, block), (mid_grad, block)] + halves(hidden_grad, half_block) + mod_ins + row_ins
        + [(early_sums, whole(sums_shape)), (early_gain, whole(one_gain))],
        [(tokens, f32, block), (all_sums, f32, whole(all_sums)), (one_gain, f32, whole(one_gain))],
        [pltpu.VMEM((6 * ITEMS + 8, width), f32)] * 2,
        moved=here * width * 16,
    )

    cross_here = jnp.where(
        is_owner & (jnp.arange(quarter) == my_head), jnp.sum(cross_rows), 0.0
    )
    packed = jnp.concatenate(
        [
            item_sums, gain_sums[:2].reshape(-1, quarter), cross_here[None],
            jnp.zeros((-(2 * tp_size + 1) % 8, quarter), f32),
        ]
    )
    packed = butterfly(packed, "seq", seq_size)
    item_mod_low = packed[: 6 * ITEMS].astype(bf16)
    gain_grads = packed[6 * ITEMS : 6 * ITEMS + 2 * tp_size].reshape(2, seq_size, gain_cols)
    gains_owned = jnp.sum(jnp.where(is_here[None, :, None], gain_grads, 0.0), axis=1)
    cross_total = packed[6 * ITEMS + 2 * tp_size, :heads] * (1.0 - tanh_cross * tanh_cross)

    def by_block(sums):
        return jnp.transpose(sums.reshape(6, ITEMS, -1), (1, 0, 2)).reshape(ITEMS, -1)

    mod_weight_grad = dot(embed_rows, by_block(gather_tp(item_mod_low, 1)), ((0,), (0,)))
    mod_quarter_grad = dot(embed_rows, by_block(item_mod_low), ((0,), (0,)))

    owned_square = (
        square_sum(qkv_rows)
        + square_sum(out_owned)
        + square_sum(text_owned)
        + square_sum(updown_rows)
        + square_sum(down_owned)
        + square_sum(mod_quarter_grad)
    )
    owned_square = owned_square + jnp.where(tp_index == 0, square_sum(gains_owned), 0.0)
    owned_square = owned_square + jnp.where(seq_index == 0, square_sum(cross_total), 0.0)
    total_square = jnp.full((8, 128), owned_square)
    total_square = butterfly(butterfly(total_square, "tp", tp_size), "seq", seq_size)[0, 0]
    grad_norm = jnp.sqrt(total_square)
    clip = jnp.minimum(1.0, clip_limit / (grad_norm + 1e-06))

    def unturned(rows, blocks):
        return jnp.transpose(rows.reshape(rows.shape[0], blocks, -1), (1, 0, 2))

    matrix = functools.partial(adam_update, clip=clip, rate=rate_matrix, decay=decay_matrix)
    small = functools.partial(adam_update, clip=clip, rate=rate_small, decay=0.0)
    return (
        block_out,
        input_grad,
        grad_norm,
        *matrix(mod_weight, mod_first, mod_second, mod_weight_grad),
        *small(norm_gains, gains_first, gains_second, gains_owned),
        *matrix(qkv_weight, qkv_first, qkv_second, unturned(qkv_rows, 3)),
        *matrix(out_weight, out_first, out_second, out_owned.T),
        *matrix(text_weight, text_first, text_second, text_owned),
        *small(cross_gates, cross_first, cross_second, cross_total),
        *matrix(updown_weight, updown_first, updown_second, unturned(updown_rows, 2)),
        *matrix(down_weight, down_first, down_second, down_owned.T),
    )


def solution(mesh):
    rows = P("seq", None)
    cols = P(None, "seq")
    split = P(None, "seq", "tp")
    turned = P("tp", "seq")
    heads = P("tp")
    weights = (rows,) * 3 + (cols,) * 3 + (split,) * 3 + (turned,) * 3 + (split,) * 3
    weights = weights + (heads,) * 3 + (split,) * 3 + (turned,) * 3
    return jax.shard_map(
        functools.partial(per_device, seq_size=mesh.shape["seq"], tp_size=mesh.shape["tp"]),
        mesh=mesh,
        in_specs=(rows, rows, P(), P("seq"), rows) + weights,
        out_specs=(rows, rows, P()) + weights,
        check_vma=False,
    )
```

time: 785 us -> 689 us (0.88)
  Pallas kernels: 46.6 us -> 188 us
  local copies, waits for them, and re-layouts: 149 us -> 49.3 us
  other arithmetic: 91.1 us -> 43.7 us
  matrix products: 106 us -> 58.8 us
  between operations: 52.4 us -> 9.76 us
  starting transfers between devices: 160 us -> 126 us
  waiting for transfers between devices: 166 us -> 187 us
  blocking collectives: 0 us -> 14.7 us
    pallas_call x2 -> x24, Pallas kernels: 46.6 us -> 188 us  [call(): pl.pallas_call(kernel, out_shape=tuple((shape_of(shape, dtype) for shape,...]
    dynamic_update_slice x45 -> x0, local copies, waits for them, and re-layouts: 49.4 us -> none  [the longest x43 49.2 us: put(): lax.dynamic_update_slice(whole, part, (self.at(offset) * rows + start, 0))]
    dot_general x52 -> x36, matrix products: 99.2 us -> 58.8 us  [dot(): return lax.dot_general(a, b, (dims, ((), ())), preferred_element_type=f32)]
    convert_element_type x22 -> x3, other arithmetic: 31 us -> 0.73 us  [the longest x2 0.72 us: per_device(): segments = packed[:count].astype(jnp.int32)]
    ppermute x85 -> x69, waiting for transfers between devices: 115 us -> 141 us  [the longest x59 141 us: hop(): return lax.ppermute(value, 'seq', pairs)]
    ppermute x85 -> x69, starting transfers between devices: 111 us -> 94.1 us  [the longest x59 88.8 us: hop(): return lax.ppermute(value, 'seq', pairs)]
    slice x21 -> x14, local copies, waits for them, and re-layouts: 21.5 us -> 6.08 us  [the longest x6 3.99 us: gather(): far = [self.hop(behind[-1][:half], -1), self.hop(ahead[-1][half:], 1)]]
    all_to_all x0 -> x1, blocking collectives: none -> 14.7 us  [exchange(): return lax.all_to_all(slabs, 'seq', 0, 0, tiled=True)]
  transfers between devices with their start and end apart: 109 -> 92, of which waited for: 33 -> 34; matrix products, arithmetic and copies ran while one was open for 35% -> 16% of each run, Pallas kernels for 6% -> 25%
where the time goes in v2:
time: 689 us; the launch traced here: 677 us
  Pallas kernels  188 us (27%)
  waiting for transfers between devices  187 us (27%)
  starting transfers between devices  126 us (18%)
  matrix products  58.8 us (9%)
  local copies, waits for them, and re-layouts  49.3 us (7%)
  other arithmetic  43.7 us (6%)
  blocking collectives  14.7 us (2%)
  between operations  9.76 us (1%)
    pallas_call x24, Pallas kernels, call(): pl.pallas_call(kernel, out_shape=tuple((shape_of(shape, dtype) for shape,...  188 us
    ppermute x59, waiting for transfers between devices, hop(): return lax.ppermute(value, 'seq', pairs)  141 us
    ppermute x59, starting transfers between devices, hop(): return lax.ppermute(value, 'seq', pairs)  88.8 us
    dot_general x36, matrix products, dot(): return lax.dot_general(a, b, (dims, ((), ())), preferred_element_type=f32)  58.8 us
    ppermute x11, waiting for transfers between devices, butterfly(): lax.ppermute(value, axis, [(i, i ^ step) for i in range(size)])  26.2 us
    unnamed x210, local copies, waits for them, and re-layouts  25.2 us
    all_to_all x4, starting transfers between devices, exchange(): return lax.all_to_all(slabs, 'seq', 0, 0, tiled=True)  19.2 us
    all_to_all x1, blocking collectives, exchange(): return lax.all_to_all(slabs, 'seq', 0, 0, tiled=True)  14.7 us
  transfers between devices with their start and end apart: 92, of which 34 were waited for; matrix products, arithmetic and copies ran while one was open for 16% of the time, Pallas kernels for 25%

profile of v2, /device:TPU:0, one launch (start us, length us, event | category | flops | bytes accessed | tf_op | source)
XLA Modules:
  0.0 677.5 jit_solution(9659267497948605106)
XLA Ops:
  3.0 3.1 collective-permute-start.9
  6.7 5.5 caption_slabs.1
  12.2 6.3 all-to-all-start.1
  18.9 14.3 %all-to-all-done.1 = bf16[8,256,128]{2,1,0:T(8,128)(2,1)} async-done(((bf16[8,256,128]{2,1,0:T(8,128)(2,1)}), bf16[8,256,128]{2,1,0:T(8,128)(2,1)}, u32[]{:S(2)}, u32[]{:S(2)}) %all-to-all-start.1) | async-done | bytes 524320 | tf_op jit(solution)/shard_map/all_to_all | solution.py:726
  33.9 5.2 modulation.1
  46.4 4.5 collective-permute-done.1
  57.1 2.8 text_heads.1.w_ref
  75.0 4.8 text_step.8
  82.4 23.4 %collective-permute-done.11.refs_6_ = bf16[192,1536]{1,0:T(8,128)(2,1)S(1)} collective-permute-done((bf16[192,1536]{1,0:T(8,128)(2,1)S(1)}, bf16[192,1536]{1,0:T(8,128)(2,1)S(1)}, u32[]{:S(2)}, u32[]{:S(2)}) %collective-permute-start.11) | collective-permute-done | bytes 589856 | tf_op jit(solution)/shard_map/ppermute | solution.py:82
  112.0 4.7 text_step.12
  117.0 4.5 collective-permute-start.19
  121.5 4.8 text_step.9
  128.9 7.3 %enter.1 = (bf16[256,1536]{1,0:T(8,128)(2,1)}, bf16[256,1536]{1,0:T(8,128)(2,1)}, f32[48,1536]{1,0:T(8,128)}, f32[8,1536]{1,0:T(8,128)}, bf16[256,1536]{1,0:T(8,128)(2,1)}) custom-call(s32[3]{0:T(128)} %pad_add_fusion.1.scal, bf16[256,1536]{1,0:T(8,128)(2,1)} %x_ref.1, bf16[256,1536]{1,0:T(8,128)(2,1)} %g_ref.1, f32[48,1536]{1,0:T(8,128)} %pad_maximum_fusion.5.mod_ref, ...), custom_call_target="tpu_custom_call" | custom-call | bytes 3932160 | tf_op jit(solution)/shard_map/enter/pallas_call | solution.py:183
  136.2 9.1 %collective-permute-done.8.refs_4_ = bf16[96,1536]{1,0:T(8,128)(2,1)S(1)} collective-permute-done((bf16[96,1536]{1,0:T(8,128)(2,1)S(1)}, bf16[96,1536]{1,0:T(8,128)(2,1)S(1)}, u32[]{:S(2)}, u32[]{:S(2)}) %collective-permute-start.8) | collective-permute-done | bytes 294944 | tf_op jit(solution)/shard_map/ppermute | solution.py:82
  146.0 5.6 project.1
  153.8 4.2 all-to-all-start
  158.8 4.8 text_step.13
  163.6 4.0 collective-permute-start.20
  168.5 4.8 text_step.10
  183.6 4.8 text_step.14
  191.0 4.8 text_step.11
  200.4 14.4 %attend.1 = (f32[64,2048]{1,0:T(8,128)}, f32[1,2048]{1,0:T(1,128)}) custom-call(s32[4,4]{1,0:T(4,128)} %pad_add_fusion.table, bf16[2048,192]{1,0:T(8,128)(2,1)} %bitcast.167, bf16[2048,192]{1,0:T(8,128)(2,1)} %bitcast.168, s32[1,2048]{1,0:T(1,128)} %bitcast.184, s32[2048,1]{1,0:T(8,128)} %copy.136.sk_ref), custom_call_target="tpu_custom_call" | custom-call | flops 1073741824 | bytes 2621440 | tf_op jit(solution)/shard_map/attend/pallas_call | solution.py:183
  214.9 3.0 collective-permute-done.18.refs_0_
  218.6 5.0 text_step.15.kv_ref
  223.6 11.3 %attend_text.1 = (bf16[2048,64]{1,0:T(8,128)(2,1)}, f32[64,2048]{1,0:T(8,128)}, f32[1,2048]{1,0:T(1,128)}) custom-call(s32[4,4]{1,0:T(4,128)} %pad_add_fusion.table, f32[1]{0:T(128)} %bitcast.9.gate, bf16[2048,192]{1,0:T(8,128)(2,1)} %bitcast.169, bf16[2048,128]{1,0:T(8,128)(2,1)} %text_step.15.kv_ref, f32[64,2048]{1,0:T(8,128)} %get-tuple-element.70.self_ref, ...), custom_call_target="tpu_custom_call" | custom-call | flops 134217728 | bytes 2621440 | tf_op jit(solution)/shard_map/attend_text/pallas_call | solution.py:183
  236.1 14.7 %all_to_all.25 = bf16[8,256,64]{1,2,0:T(8,128)(2,1)S(1)} all-to-all(bf16[8,256,64]{1,2,0:T(8,128)(2,1)S(1)} %copy.137), channel_id=1, replica_groups=mesh['seq'=8,'tp'=4] {'seq'}, dimensions={0} | all-to-all | bytes 524288 | tf_op jit(solution)/shard_map/all_to_all | solution.py:726
  251.8 5.8 out.1
  261.9 24.3 %collective-permute-done.31.refs_6_ = bf16[192,3072]{1,0:T(8,128)(2,1)S(1)} collective-permute-done((bf16[192,3072]{1,0:T(8,128)(2,1)}, bf16[192,3072]{1,0:T(8,128)(2,1)S(1)}, u32[]{:S(2)}, u32[]{:S(2)}) %collective-permute-start.31) | collective-permute-done | bytes 1179680 | tf_op jit(solution)/shard_map/ppermute | solution.py:82
  290.5 10.9 %collective-permute-done.32.refs_5_ = bf16[96,3072]{1,0:T(8,128)(2,1)S(1)} collective-permute-done((bf16[96,3072]{1,0:T(8,128)(2,1)S(1)}, bf16[96,3072]{1,0:T(8,128)(2,1)S(1)}, u32[]{:S(2)}, u32[]{:S(2)}) %collective-permute-start.32) | collective-permute-done | bytes 589856 | tf_op jit(solution)/shard_map/ppermute | solution.py:82
  303.8 19.0 %ffn.1 = (f32[256,1536]{1,0:T(8,128)}, bf16[256,1536]{1,0:T(8,128)(2,1)}, bf16[256,1536]{1,0:T(8,128)(2,1)}, bf16[256,1024]{1,0:T(8,128)(2,1)}, bf16[256,2048]{1...) custom-call(s32[3]{0:T(128)} %pad_add_fusion.1.scal, ...), custom_call_target="tpu_custom_call" | custom-call | flops 4831838208 | bytes 9437184 | tf_op jit(solution)/shard_map/ffn/pallas_call | solution.py:183
  330.0 8.0 %collective-permute-done.71 = bf16[192,1024]{1,0:T(8,128)(2,1)S(1)} collective-permute-done((bf16[192,1024]{1,0:T(8,128)(2,1)S(1)}, bf16[192,1024]{1,0:T(8,128)(2,1)S(1)}, u32[]{:S(2)}, u32[]{:S(2)}) %collective-permute-start.71) | collective-permute-done | bytes 393248 | tf_op jit(solution)/shard_map/ppermute | solution.py:82
  342.7 18.3 %collective-permute-done.72 = bf16[192,1024]{1,0:T(8,128)(2,1)S(1)} collective-permute-done((bf16[192,1024]{1,0:T(8,128)(2,1)S(1)}, bf16[192,1024]{1,0:T(8,128)(2,1)S(1)}, u32[]{:S(2)}, u32[]{:S(2)}) %collective-permute-start.72) | collective-permute-done | bytes 393248 | tf_op jit(solution)/shard_map/ppermute | solution.py:82
  364.9 5.1 collective-permute-done.37
  377.3 8.0 %mid.1 = (f32[256,1536]{1,0:T(8,128)}, bf16[256,1536]{1,0:T(8,128)(2,1)}, bf16[8,256,64]{2,1,0:T(8,128)(2,1)}) custom-call(s32[3]{0:T(128)} %pad_add_fusion.1.scal, f32[256,1536]{1,0:T(8,128)} %get-tuple-element.76.mid_ref, bf16[256,1536]{1,0:T(8,128)(2,1)} %get-tuple-element.68.g_ref, bf16[128,1536]{1,0:T(8,128)(2,1)} %copy-done.21, ...), custom_call_target="tpu_custom_call" | custom-call | flops 301989888 | bytes 1179648 | tf_op jit(solution)/shard_map/mid/pallas_call | solution.py:183
  387.2 3.4 all-to-all-start.3
  393.7 12.5 %side.1 = (f32[256,1536]{1,0:T(8,128)}, f32[32,1536]{1,0:T(8,128)}, f32[8,1536]{1,0:T(8,128)}) custom-call(s32[3]{0:T(128)} %pad_add_fusion.1.scal, f32[256,1536]{1,0:T(8,128)} %get-tuple-element.76.mid_ref, f32[256,1536]{1,0:T(8,128)} %get-tuple-element.79.grad_ref, bf16[256,1536]{1,0:T(8,128)(2,1)} %get-tuple-element.68.g_ref, ...), custom_call_target="tpu_custom_call" | custom-call | bytes 9437184 | tf_op jit(solution)/shard_map/side/pallas_call | solution.py:183
  408.7 3.1 collective-permute-done.53
  413.4 3.4 collective-permute-done.50
  429.0 3.0 multiply_reduce_fusion.3
  435.6 12.0 %attend_text_back.1 = (bf16[2048,128]{1,0:T(8,128)(2,1)}, f32[64,2048]{1,0:T(8,128)}, f32[1,2048]{1,0:T(1,128)}) custom-call(s32[4,4]{1,0:T(4,128)} %pad_add_fusion.table, f32[1]{0:T(128)} %bitcast.9.gate, bf16[2048,192]{1,0:T(8,128)(2,1)} %bitcast.170, bf16[2048,64]{1,0:T(8,128)(2,1)} %bitcast.178, bf16[2048,128]{1,0:T(8,128)(2,1)} %text_step.15.kv_ref, ...), custom_call_target="tpu_custom_call" | custom-call | flops 335544320 | bytes 2621440 | tf_op jit(solution)/shard_map/attend_text_back/pallas_call | solution.py:183
  447.6 19.2 %attend_back.1 = bf16[2048,192]{1,0:T(8,128)(2,1)} custom-call(s32[4,4]{1,0:T(4,128)} %pad_add_fusion.table, bf16[2048,192]{1,0:T(8,128)(2,1)} %bitcast.171, bf16[2048,64]{1,0:T(8,128)(2,1)} %bitcast.179, bf16[2048,192]{1,0:T(8,128)(2,1)} %bitcast.172, f32[64,2048]{1,0:T(8,128)} %get-tuple-element.70.self_ref, f32[1,2048]{1,0:T(1,128)} %get-tuple-element.84.stat_ref, ...), custom_call_target="tpu_custom_call" | custom-call | flops 2684354560 | bytes 2621440 | tf_op jit(solution)/shard_map/attend_back/pallas_call | solution.py:183
  469.0 5.3 all-to-all-start.4
  483.6 7.1 %collective-permute-done.52 = bf16[192,384]{1,0:T(8,128)(2,1)} collective-permute-done((bf16[192,384]{1,0:T(8,128)(2,1)}, bf16[192,384]{1,0:T(8,128)(2,1)}, u32[]{:S(2)}, u32[]{:S(2)}) %collective-permute-start.52) | collective-permute-done | bytes 147488 | tf_op jit(solution)/shard_map/ppermute | solution.py:82
  493.2 3.2 collective-permute-done.60
  496.3 5.6 collective-permute-start.61
  508.8 5.5 collective-permute-done.61
  514.3 2.8 collective-permute-start.62
  517.1 7.3 %collective-permute-done.57 = bf16[2048,128]{1,0:T(8,128)(2,1)} collective-permute-done((bf16[2048,128]{1,0:T(8,128)(2,1)}, bf16[2048,128]{1,0:T(8,128)(2,1)}, u32[]{:S(2)}, u32[]{:S(2)}) %collective-permute-start.57) | collective-permute-done | bytes 524320 | tf_op jit(solution)/shard_map/ppermute | solution.py:82
  527.6 7.3 %qkv_back.1 = (bf16[256,1152]{1,0:T(8,128)(2,1)}, bf16[128,1536]{1,0:T(8,128)(2,1)}, bf16[128,1536]{1,0:T(8,128)(2,1)}) custom-call(s32[3]{0:T(128)} %pad_add_fusion.1.scal, bf16[8,256,192]{2,1,0:T(8,128)(2,1)} %copy.147.slab_ref, bf16[192,1536]{1,0:T(8,128)(2,1)} %copy-done.3, bf16[192,1536]{1,0:T(8,128)(2,1)} %copy-done.8, bf16[192,1536]{1,0:T(8,128)(2,1)} %copy-done.10, ...), custom_call_target="tpu_custom_call" | custom-call | flops 905969664 | bytes 3538944 | tf_op jit(solution)/shard_map/qkv_back/pallas_call | solution.py:183
  537.8 5.0 collective-permute-start.42
  558.0 3.4 collective-permute-done.59
  567.4 5.6 text_join.1
  573.0 3.5 convolution_bitcast_fusion.1
  581.1 8.6 %leave.1 = (f32[256,1536]{1,0:T(8,128)}, f32[48,384]{1,0:T(8,128)}, f32[8,1536]{1,0:T(8,128)}) custom-call(s32[3]{0:T(128)} %pad_add_fusion.1.scal, bf16[256,1536]{1,0:T(8,128)(2,1)} %get-tuple-element.67.x_ref, f32[256,1536]{1,0:T(8,128)} %get-tuple-element.79.grad_ref, bf16[128,1536]{1,0:T(8,128)(2,1)} %copy-done.34, bf16[128,1536]{1,0:T(8,128)(2,1)} %copy-done.62, ...), custom_call_target="tpu_custom_call" | custom-call | bytes 6291456 | tf_op jit(solution)/shard_map/leave/pallas_call | solution.py:183
  600.7 6.5 collective-permute-done.79
  609.7 2.7 collective-permute-start.45
  612.4 3.4 collective-permute-done.80
  622.2 3.0 multiply_reduce_fusion.2
  634.0 3.5 collective-permute-start.83
  639.7 3.0 collective-permute-done.84
  644.5 2.7 collective-permute-done.85
  650.9 5.1 multiply_subtract_fusion.2
  662.4 3.1 multiply_subtract_fusion.1
  666.9 9.0 %multiply_subtract_fusion = (f32[128,9216]{1,0:T(8,128)}, f32[128,9216]{1,0:T(8,128)}, f32[128,9216]{1,0:T(8,128)}) fusion(f32[128,9216]{1,0:T(8,128)S(1)} %bitcast.175, f32[128,9216]{1,0:T(8,128)S(1)} %bitcast.193, f32[128,9216]{1,0:T(8,128)} %param.36, f32[]{:T(128)S(6)} %min.18, bf16[8,128]{1,0:T(8,128)(2,1)S(1)} %copy-done.78, ...), kind=kOutput, calls=%fused_computation.3 | convolution fusion | flops 37748736 | bytes 28461060 | tf_op jit(solution)/shard_map/dot_general | solution.py:71
  (508 shorter events, 218.1 us)
Async XLA Ops:
  3.0 48.5 %collective-permute-start.9 = (bf16[192,1536]{1,0:T(8,128)(2,1)S(1)}, bf16[192,1536]{1,0:T(8,128)(2,1)S(1)}, u32[]{:S(2)}, u32[]{:S(2)}) collective-permute-start(bf16[192,1536]{1,0:T(8,128)(2,1)S(1)} %pad_maximum_fusion.4.refs_0_), channel_id=1, source_target_pairs={{0,8},{8,16},{16,24},{24,28},{28,20},{20,12},{12,4},{4,0},{1,9},{9... | collective-permute-start | bytes 1769480 | tf_op jit(solution)/shard_map/ppermute | solution.py:82
  6.1 47.1 %collective-permute-start.5 = (bf16[192,1536]{1,0:T(8,128)(2,1)S(1)}, bf16[192,1536]{1,0:T(8,128)(2,1)S(1)}, u32[]{:S(2)}, u32[]{:S(2)}) collective-permute-start(bf16[192,1536]{1,0:T(8,128)(2,1)S(1)} %pad_maximum_fusion.4.refs_0_), channel_id=1, source_target_pairs={{0,4},{8,0},{16,8},{24,16},{28,24},{20,28},{12,20},{4,12},{1,5},{9... | collective-permute-start | bytes 1769480 | tf_op jit(solution)/shard_map/ppermute | solution.py:82
  12.2 21.0 %all-to-all-start.1 = ((bf16[8,256,128]{2,1,0:T(8,128)(2,1)}), bf16[8,256,128]{2,1,0:T(8,128)(2,1)}, u32[]{:S(2)}, u32[]{:S(2)}) async-start(bf16[8,256,128]{2,1,0:T(8,128)(2,1)} %caption_slabs.1), calls=%async_computation.1 | async-start | bytes 1048576 | tf_op jit(solution)/shard_map/all_to_all | solution.py:726
  43.3 27.2 %collective-permute-start.14 = (bf16[2048,256]{1,0:T(8,128)(2,1)}, bf16[2048,256]{1,0:T(8,128)(2,1)}, u32[]{:S(2)}, u32[]{:S(2)}) collective-permute-start(bf16[2048,256]{1,0:T(8,128)(2,1)} %pad_maximum_fusion.3), channel_id=1, source_target_pairs={{0,2},{2,0},{1,3},{3,1},{4,6},{6,4},{5,7},{7,5},{8,10},{10,8},{9,1... | collective-permute-start | bytes 3145736 | tf_op jit(solution)/shard_map/ppermute | solution.py:144
  51.5 16.3 %collective-permute-start.10 = (bf16[192,1536]{1,0:T(8,128)(2,1)S(1)}, bf16[192,1536]{1,0:T(8,128)(2,1)S(1)}, u32[]{:S(2)}, u32[]{:S(2)}) collective-permute-start(bf16[192,1536]{1,0:T(8,128)(2,1)S(1)} %collective-permute-done.9.refs_8_), channel_id=1, source_target_pairs={{0,8},{8,16},{16,24},{24,28},{28,20},{20,12},{12,4},{4,0},{1,9},{9... | collective-permute-start | bytes 1769480 | tf_op jit(solution)/shard_map/ppermute | solution.py:82
  53.2 16.9 %collective-permute-start.6 = (bf16[192,1536]{1,0:T(8,128)(2,1)S(1)}, bf16[192,1536]{1,0:T(8,128)(2,1)S(1)}, u32[]{:S(2)}, u32[]{:S(2)}) collective-permute-start(bf16[192,1536]{1,0:T(8,128)(2,1)S(1)} %collective-permute-done.5.refs_1_), channel_id=1, source_target_pairs={{0,4},{8,0},{16,8},{24,16},{28,24},{20,28},{12,20},{4,12},{1,5},{9... | collective-permute-start | bytes 1769480 | tf_op jit(solution)/shard_map/ppermute | solution.py:82
  54.7 123.5 %collective-permute-start.29 = (bf16[192,3072]{1,0:T(8,128)(2,1)}, bf16[192,3072]{1,0:T(8,128)(2,1)}, u32[]{:S(2)}, u32[]{:S(2)}) collective-permute-start(bf16[192,3072]{1,0:T(8,128)(2,1)} %pad_maximum_fusion.2.refs_0_), channel_id=1, source_target_pairs={{0,8},{8,16},{16,24},{24,28},{28,20},{20,12},{12,4},{4,0},{1,9},{9... | collective-permute-start | bytes 3538952 | tf_op jit(solution)/shard_map/ppermute | solution.py:82
  67.8 37.9 %collective-permute-start.11 = (bf16[192,1536]{1,0:T(8,128)(2,1)S(1)}, bf16[192,1536]{1,0:T(8,128)(2,1)S(1)}, u32[]{:S(2)}, u32[]{:S(2)}) collective-permute-start(bf16[192,1536]{1,0:T(8,128)(2,1)S(1)} %collective-permute-done.10.refs_7_), channel_id=1, source_target_pairs={{0,8},{8,16},{16,24},{24,28},{28,20},{20,12},{12,4},{4,0},{1,9},{9... | collective-permute-start | bytes 1769480 | tf_op jit(solution)/shard_map/ppermute | solution.py:82
  70.0 39.3 %collective-permute-start.7 = (bf16[192,1536]{1,0:T(8,128)(2,1)S(1)}, bf16[192,1536]{1,0:T(8,128)(2,1)S(1)}, u32[]{:S(2)}, u32[]{:S(2)}) collective-permute-start(bf16[192,1536]{1,0:T(8,128)(2,1)S(1)} %collective-permute-done.6.refs_2_), channel_id=1, source_target_pairs={{0,4},{8,0},{16,8},{24,16},{28,24},{20,28},{12,20},{4,12},{1,5},{9... | collective-permute-start | bytes 1769480 | tf_op jit(solution)/shard_map/ppermute | solution.py:82
  79.8 37.2 %collective-permute-start.15 = (bf16[2048,128]{1,0:T(8,128)(2,1)}, bf16[2048,128]{1,0:T(8,128)(2,1)S(1)}, u32[]{:S(2)}, u32[]{:S(2)}) collective-permute-start(bf16[2048,128]{1,0:T(8,128)(2,1)} %text_step.8), channel_id=1, source_target_pairs={{8,16},{16,24},{24,28},{20,12},{12,4},{4,0},{9,17},{17,25},{25,29}... | collective-permute-start | bytes 1572872 | tf_op jit(solution)/shard_map/ppermute | solution.py:82
  81.1 28.7 %collective-permute-start.4 = (f32[48,768]{1,0:T(8,128)S(1)}, f32[48,768]{1,0:T(8,128)S(1)}, u32[]{:S(2)}, u32[]{:S(2)}) collective-permute-start(f32[48,768]{1,0:T(8,128)S(1)} %pad_maximum_fusion.6), channel_id=1, source_target_pairs={{0,2},{2,0},{1,3},{3,1},{4,6},{6,4},{5,7},{7,5},{8,10},{10,8},{9,1... | collective-permute-start | bytes 442376 | tf_op jit(solution)/shard_map/ppermute | solution.py:144
  106.5 19.8 %collective-permute-start.12 = (bf16[96,1536]{1,0:T(8,128)(2,1)}, bf16[96,1536]{1,0:T(8,128)(2,1)S(1)}, u32[]{:S(2)}, u32[]{:S(2)}) collective-permute-start(bf16[96,1536]{1,0:T(8,128)(2,1)} %slice.217), channel_id=1, source_target_pairs={{0,8},{8,16},{16,24},{24,28},{28,20},{20,12},{12,4},{4,0},{1,9},{9... | collective-permute-start | bytes 884744 | tf_op jit(solution)/shard_map/ppermute | solution.py:82
  109.4 69.5 %collective-permute-start.25 = (bf16[192,3072]{1,0:T(8,128)(2,1)}, bf16[192,3072]{1,0:T(8,128)(2,1)}, u32[]{:S(2)}, u32[]{:S(2)}) collective-permute-start(bf16[192,3072]{1,0:T(8,128)(2,1)} %pad_maximum_fusion.2.refs_0_), channel_id=1, source_target_pairs={{0,4},{8,0},{16,8},{24,16},{28,24},{20,28},{12,20},{4,12},{1,5},{9... | collective-permute-start | bytes 3538952 | tf_op jit(solution)/shard_map/ppermute | solution.py:82
  109.8 35.5 %collective-permute-start.8 = (bf16[96,1536]{1,0:T(8,128)(2,1)S(1)}, bf16[96,1536]{1,0:T(8,128)(2,1)S(1)}, u32[]{:S(2)}, u32[]{:S(2)}) collective-permute-start(bf16[96,1536]{1,0:T(8,128)(2,1)S(1)} %slice.216), channel_id=1, source_target_pairs={{0,4},{8,0},{16,8},{24,16},{28,24},{20,28},{12,20},{4,12},{1,5},{9... | collective-permute-start | bytes 884744 | tf_op jit(solution)/shard_map/ppermute | solution.py:82
  117.0 41.1 %collective-permute-start.19 = (bf16[2048,128]{1,0:T(8,128)(2,1)}, bf16[2048,128]{1,0:T(8,128)(2,1)S(1)}, u32[]{:S(2)}, u32[]{:S(2)}) collective-permute-start(bf16[2048,128]{1,0:T(8,128)(2,1)} %text_step.12), channel_id=1, source_target_pairs={{0,4},{8,0},{16,8},{28,24},{20,28},{12,20},{1,5},{9,1},{17,9},{29,... | collective-permute-start | bytes 1572872 | tf_op jit(solution)/shard_map/ppermute | solution.py:82
  126.3 41.4 %collective-permute-start.16 = (bf16[2048,128]{1,0:T(8,128)(2,1)}, bf16[2048,128]{1,0:T(8,128)(2,1)S(1)}, u32[]{:S(2)}, u32[]{:S(2)}) collective-permute-start(bf16[2048,128]{1,0:T(8,128)(2,1)} %text_step.9), channel_id=1, source_target_pairs={{0,8},{16,24},{24,28},{28,20},{12,4},{4,0},{1,9},{17,25},{25,29},{... | collective-permute-start | bytes 1572872 | tf_op jit(solution)/shard_map/ppermute | solution.py:82
  153.8 45.3 %all-to-all-start = ((bf16[8,256,192]{1,2,0:T(8,128)(2,1)}), bf16[8,256,192]{1,2,0:T(8,128)(2,1)S(1)}, u32[]{:S(2)}, u32[]{:S(2)}) async-start(bf16[8,256,192]{1,2,0:T(8,128)(2,1)} %copy.134), calls=%async_computation | async-start | bytes 1572864 | tf_op jit(solution)/shard_map/all_to_all | solution.py:726
  163.6 19.1 %collective-permute-start.20 = (bf16[2048,128]{1,0:T(8,128)(2,1)}, bf16[2048,128]{1,0:T(8,128)(2,1)S(1)}, u32[]{:S(2)}, u32[]{:S(2)}) collective-permute-start(bf16[2048,128]{1,0:T(8,128)(2,1)} %text_step.13), channel_id=1, source_target_pairs={{0,4},{8,0},{24,16},{28,24},{20,28},{4,12},{1,5},{9,1},{25,17},{29... | collective-permute-start | bytes 1572872 | tf_op jit(solution)/shard_map/ppermute | solution.py:82
  173.3 17.0 %collective-permute-start.17 = (bf16[2048,128]{1,0:T(8,128)(2,1)}, bf16[2048,128]{1,0:T(8,128)(2,1)S(1)}, u32[]{:S(2)}, u32[]{:S(2)}) collective-permute-start(bf16[2048,128]{1,0:T(8,128)(2,1)} %text_step.10), channel_id=1, source_target_pairs={{0,8},{8,16},{24,28},{28,20},{20,12},{4,0},{1,9},{9,17},{25,29},{2... | collective-permute-start | bytes 1572872 | tf_op jit(solution)/shard_map/ppermute | solution.py:82
  178.1 79.6 %collective-permute-start.30 = (bf16[192,3072]{1,0:T(8,128)(2,1)}, bf16[192,3072]{1,0:T(8,128)(2,1)}, u32[]{:S(2)}, u32[]{:S(2)}) collective-permute-start(bf16[192,3072]{1,0:T(8,128)(2,1)} %collective-permute-done.29.refs_8_), channel_id=1, source_target_pairs={{0,8},{8,16},{16,24},{24,28},{28,20},{20,12},{12,4},{4,0},{1,9},{9... | collective-permute-start | bytes 3538952 | tf_op jit(solution)/shard_map/ppermute | solution.py:82
  178.9 78.8 %collective-permute-start.26 = (bf16[192,3072]{1,0:T(8,128)(2,1)}, bf16[192,3072]{1,0:T(8,128)(2,1)}, u32[]{:S(2)}, u32[]{:S(2)}) collective-permute-start(bf16[192,3072]{1,0:T(8,128)(2,1)} %collective-permute-done.25.refs_1_), channel_id=1, source_target_pairs={{0,4},{8,0},{16,8},{24,16},{28,24},{20,28},{12,20},{4,12},{1,5},{9... | collective-permute-start | bytes 3538952 | tf_op jit(solution)/shard_map/ppermute | solution.py:82
  188.3 26.5 %collective-permute-start.21 = (bf16[2048,128]{1,0:T(8,128)(2,1)}, bf16[2048,128]{1,0:T(8,128)(2,1)S(1)}, u32[]{:S(2)}, u32[]{:S(2)}) collective-permute-start(bf16[2048,128]{1,0:T(8,128)(2,1)} %text_step.14), channel_id=1, source_target_pairs={{0,4},{16,8},{24,16},{28,24},{12,20},{4,12},{1,5},{17,9},{25,17},{... | collective-permute-start | bytes 1572872 | tf_op jit(solution)/shard_map/ppermute | solution.py:82
  195.8 22.0 %collective-permute-start.18 = (bf16[2048,128]{1,0:T(8,128)(2,1)}, bf16[2048,128]{1,0:T(8,128)(2,1)S(1)}, u32[]{:S(2)}, u32[]{:S(2)}) collective-permute-start(bf16[2048,128]{1,0:T(8,128)(2,1)} %text_step.11), channel_id=1, source_target_pairs={{0,8},{8,16},{16,24},{28,20},{20,12},{12,4},{1,9},{9,17},{17,25},{... | collective-permute-start | bytes 1572872 | tf_op jit(solution)/shard_map/ppermute | solution.py:82
  257.7 28.6 %collective-permute-start.31 = (bf16[192,3072]{1,0:T(8,128)(2,1)}, bf16[192,3072]{1,0:T(8,128)(2,1)S(1)}, u32[]{:S(2)}, u32[]{:S(2)}) collective-permute-start(bf16[192,3072]{1,0:T(8,128)(2,1)} %collective-permute-done.30.refs_7_), channel_id=1, source_target_pairs={{0,8},{8,16},{16,24},{24,28},{28,20},{20,12},{12,4},{4,0},{1,9},{9... | collective-permute-start | bytes 3538952 | tf_op jit(solution)/shard_map/ppermute | solution.py:82
  257.8 28.9 %collective-permute-start.27 = (bf16[192,3072]{1,0:T(8,128)(2,1)}, bf16[192,3072]{1,0:T(8,128)(2,1)}, u32[]{:S(2)}, u32[]{:S(2)}) collective-permute-start(bf16[192,3072]{1,0:T(8,128)(2,1)} %collective-permute-done.26.refs_2_), channel_id=1, source_target_pairs={{0,4},{8,0},{16,8},{24,16},{28,24},{20,28},{12,20},{4,12},{1,5},{9... | collective-permute-start | bytes 3538952 | tf_op jit(solution)/shard_map/ppermute | solution.py:82
  260.9 28.7 %collective-permute-start.23 = (bf16[128,1536]{1,0:T(8,128)(2,1)S(1)}, bf16[128,1536]{1,0:T(8,128)(2,1)S(1)}, u32[]{:S(2)}, u32[]{:S(2)}) collective-permute-start(bf16[128,1536]{1,0:T(8,128)(2,1)S(1)} %add_convert_fusion.7), channel_id=1, source_target_pairs={{0,2},{2,0},{1,3},{3,1},{4,6},{6,4},{5,7},{7,5},{8,10},{10,8},{9,1... | collective-permute-start | bytes 1179656 | tf_op jit(solution)/shard_map/ppermute | solution.py:150
  286.3 15.0 %collective-permute-start.32 = (bf16[96,3072]{1,0:T(8,128)(2,1)S(1)}, bf16[96,3072]{1,0:T(8,128)(2,1)S(1)}, u32[]{:S(2)}, u32[]{:S(2)}) collective-permute-start(bf16[96,3072]{1,0:T(8,128)(2,1)S(1)} %slice.219), channel_id=1, source_target_pairs={{0,8},{8,16},{16,24},{24,28},{28,20},{20,12},{12,4},{4,0},{1,9},{9... | collective-permute-start | bytes 1769480 | tf_op jit(solution)/shard_map/ppermute | solution.py:82
  287.8 15.0 %collective-permute-start.28 = (bf16[96,3072]{1,0:T(8,128)(2,1)S(1)}, bf16[96,3072]{1,0:T(8,128)(2,1)S(1)}, u32[]{:S(2)}, u32[]{:S(2)}) collective-permute-start(bf16[96,3072]{1,0:T(8,128)(2,1)S(1)} %slice.218), channel_id=1, source_target_pairs={{0,4},{8,0},{16,8},{24,16},{28,24},{20,28},{12,20},{4,12},{1,5},{9... | collective-permute-start | bytes 1769480 | tf_op jit(solution)/shard_map/ppermute | solution.py:82
  326.4 13.3 %collective-permute-start.75 = (bf16[192,1024]{1,0:T(8,128)(2,1)S(1)}, bf16[192,1024]{1,0:T(8,128)(2,1)S(1)}, u32[]{:S(2)}, u32[]{:S(2)}) collective-permute-start(bf16[192,1024]{1,0:T(8,128)(2,1)S(1)} %convolution_convert_fusion.4), channel_id=1, source_target_pairs={{0,4},{8,0},{16,8},{24,16},{28,24},{20,28},{12,20},{4,12},{1,5},{9... | collective-permute-start | bytes 1179656 | tf_op jit(solution)/shard_map/ppermute | solution.py:82
  329.0 13.3 %collective-permute-start.36 = (bf16[128,1536]{1,0:T(8,128)(2,1)S(1)}, bf16[128,1536]{1,0:T(8,128)(2,1)S(1)}, u32[]{:S(2)}, u32[]{:S(2)}) collective-permute-start(bf16[128,1536]{1,0:T(8,128)(2,1)S(1)} %copy-done.93), channel_id=1, source_target_pairs={{0,1},{1,0},{2,3},{3,2},{4,5},{5,4},{6,7},{7,6},{8,9},{9,8},{10,11... | collective-permute-start | bytes 1179656 | tf_op jit(solution)/shard_map/ppermute | solution.py:149
  329.4 40.7 %collective-permute-start.64 = (bf16[192,2048]{1,0:T(8,128)(2,1)S(1)}, bf16[192,2048]{1,0:T(8,128)(2,1)S(1)}, u32[]{:S(2)}, u32[]{:S(2)}) collective-permute-start(bf16[192,2048]{1,0:T(8,128)(2,1)S(1)} %convolution_convert_fusion.1), channel_id=1, source_target_pairs={{0,8},{8,16},{16,24},{24,28},{28,20},{20,12},{12,4},{4,0},{1,9},{9... | collective-permute-start | bytes 2359304 | tf_op jit(solution)/shard_map/ppermute | solution.py:82
  337.9 34.2 %collective-permute-start.68 = (bf16[192,2048]{1,0:T(8,128)(2,1)S(1)}, bf16[192,2048]{1,0:T(8,128)(2,1)S(1)}, u32[]{:S(2)}, u32[]{:S(2)}) collective-permute-start(bf16[192,2048]{1,0:T(8,128)(2,1)S(1)} %convolution_convert_fusion), channel_id=1, source_target_pairs={{0,4},{8,0},{16,8},{24,16},{28,24},{20,28},{12,20},{4,12},{1,5},{9... | collective-permute-start | bytes 2359304 | tf_op jit(solution)/shard_map/ppermute | solution.py:82
  339.7 21.3 %collective-permute-start.72 = (bf16[192,1024]{1,0:T(8,128)(2,1)S(1)}, bf16[192,1024]{1,0:T(8,128)(2,1)S(1)}, u32[]{:S(2)}, u32[]{:S(2)}) collective-permute-start(bf16[192,1024]{1,0:T(8,128)(2,1)S(1)} %fusion.20), channel_id=1, source_target_pairs={{0,8},{8,16},{16,24},{24,28},{28,20},{20,12},{12,4},{4,0},{1,9},{9... | collective-permute-start | bytes 1179656 | tf_op jit(solution)/shard_map/ppermute | solution.py:82
  340.7 20.9 %collective-permute-start.76 = (bf16[192,1024]{1,0:T(8,128)(2,1)S(1)}, bf16[192,1024]{1,0:T(8,128)(2,1)S(1)}, u32[]{:S(2)}, u32[]{:S(2)}) collective-permute-start(bf16[192,1024]{1,0:T(8,128)(2,1)S(1)} %fusion.22), channel_id=1, source_target_pairs={{0,4},{8,0},{16,8},{24,16},{28,24},{20,28},{12,20},{4,12},{1,5},{9... | collective-permute-start | bytes 1179656 | tf_op jit(solution)/shard_map/ppermute | solution.py:82
  342.3 20.8 %collective-permute-start.34 = (bf16[128,1536]{1,0:T(8,128)(2,1)S(1)}, bf16[128,1536]{1,0:T(8,128)(2,1)S(1)}, u32[]{:S(2)}, u32[]{:S(2)}) collective-permute-start(bf16[128,1536]{1,0:T(8,128)(2,1)S(1)} %add_convert_fusion.5), channel_id=1, source_target_pairs={{0,2},{2,0},{1,3},{3,1},{4,6},{6,4},{5,7},{7,5},{8,10},{10,8},{9,1... | collective-permute-start | bytes 1179656 | tf_op jit(solution)/shard_map/ppermute | solution.py:150
  363.0 64.6 %collective-permute-start.77 = (bf16[192,1024]{1,0:T(8,128)(2,1)}, bf16[192,1024]{1,0:T(8,128)(2,1)}, u32[]{:S(2)}, u32[]{:S(2)}) collective-permute-start(bf16[192,1024]{1,0:T(8,128)(2,1)} %fusion.21), channel_id=1, source_target_pairs={{0,4},{8,0},{16,8},{24,16},{28,24},{20,28},{12,20},{4,12},{1,5},{9... | collective-permute-start | bytes 1179656 | tf_op jit(solution)/shard_map/ppermute | solution.py:82
  370.1 21.6 %collective-permute-start.38 = (bf16[128,1536]{1,0:T(8,128)(2,1)S(1)}, bf16[128,1536]{1,0:T(8,128)(2,1)S(1)}, u32[]{:S(2)}, u32[]{:S(2)}) collective-permute-start(bf16[128,1536]{1,0:T(8,128)(2,1)S(1)} %add_convert_fusion.2.fm_ref), channel_id=1, source_target_pairs={{0,1},{1,0},{2,3},{3,2},{4,5},{5,4},{6,7},{7,6},{8,9},{9,8},{10,11... | collective-permute-start | bytes 1179656 | tf_op jit(solution)/shard_map/ppermute | solution.py:151
  372.1 52.4 %collective-permute-start.65 = (bf16[192,2048]{1,0:T(8,128)(2,1)}, bf16[192,2048]{1,0:T(8,128)(2,1)}, u32[]{:S(2)}, u32[]{:S(2)}) collective-permute-start(bf16[192,2048]{1,0:T(8,128)(2,1)} %fusion.5), channel_id=1, source_target_pairs={{0,8},{8,16},{16,24},{24,28},{28,20},{20,12},{12,4},{4,0},{1,9},{9... | collective-permute-start | bytes 2359304 | tf_op jit(solution)/shard_map/ppermute | solution.py:82
  373.4 58.7 %collective-permute-start.69 = (bf16[192,2048]{1,0:T(8,128)(2,1)}, bf16[192,2048]{1,0:T(8,128)(2,1)}, u32[]{:S(2)}, u32[]{:S(2)}) collective-permute-start(bf16[192,2048]{1,0:T(8,128)(2,1)} %fusion.7), channel_id=1, source_target_pairs={{0,4},{8,0},{16,8},{24,16},{28,24},{20,28},{12,20},{4,12},{1,5},{9... | collective-permute-start | bytes 2359304 | tf_op jit(solution)/shard_map/ppermute | solution.py:82
  376.5 52.5 %collective-permute-start.74 = (bf16[192,1024]{1,0:T(8,128)(2,1)}, bf16[192,1024]{1,0:T(8,128)(2,1)}, u32[]{:S(2)}, u32[]{:S(2)}) collective-permute-start(bf16[192,1024]{1,0:T(8,128)(2,1)} %fusion.18), channel_id=1, source_target_pairs={{0,8},{8,16},{16,24},{24,28},{28,20},{20,12},{12,4},{4,0},{1,9},{9... | collective-permute-start | bytes 1179656 | tf_op jit(solution)/shard_map/ppermute | solution.py:82
  387.2 47.4 %all-to-all-start.3 = ((bf16[8,256,64]{1,2,0:T(8,128)(2,1)}), bf16[8,256,64]{1,2,0:T(8,128)(2,1)S(1)}, u32[]{:S(2)}, u32[]{:S(2)}) async-start(bf16[8,256,64]{1,2,0:T(8,128)(2,1)} %copy.143), calls=%async_computation.3 | async-start | bytes 524288 | tf_op jit(solution)/shard_map/all_to_all | solution.py:726
  391.8 14.8 %collective-permute-start.49 = (bf16[192,384]{1,0:T(8,128)(2,1)S(1)}, bf16[192,384]{1,0:T(8,128)(2,1)S(1)}, u32[]{:S(2)}, u32[]{:S(2)}) collective-permute-start(bf16[192,384]{1,0:T(8,128)(2,1)S(1)} %convolution_convert_fusion.7), channel_id=1, source_target_pairs={{0,8},{8,16},{16,24},{24,28},{28,20},{20,12},{12,4},{4,0},{1,9},{9... | collective-permute-start | bytes 442376 | tf_op jit(solution)/shard_map/ppermute | solution.py:82
  422.0 52.3 %collective-permute-start.51 = (bf16[192,384]{1,0:T(8,128)(2,1)}, bf16[192,384]{1,0:T(8,128)(2,1)}, u32[]{:S(2)}, u32[]{:S(2)}) collective-permute-start(bf16[192,384]{1,0:T(8,128)(2,1)} %fusion.25), channel_id=1, source_target_pairs={{0,8},{8,16},{16,24},{24,28},{28,20},{20,12},{12,4},{4,0},{1,9},{9... | collective-permute-start | bytes 442376 | tf_op jit(solution)/shard_map/ppermute | solution.py:82
  424.5 59.0 %collective-permute-start.55 = (bf16[192,384]{1,0:T(8,128)(2,1)}, bf16[192,384]{1,0:T(8,128)(2,1)S(1)}, u32[]{:S(2)}, u32[]{:S(2)}) collective-permute-start(bf16[192,384]{1,0:T(8,128)(2,1)} %fusion.27), channel_id=1, source_target_pairs={{0,4},{8,0},{16,8},{24,16},{28,24},{20,28},{12,20},{4,12},{1,5},{9... | collective-permute-start | bytes 442376 | tf_op jit(solution)/shard_map/ppermute | solution.py:82
  427.7 76.2 %collective-permute-start.66 = (bf16[192,2048]{1,0:T(8,128)(2,1)}, bf16[192,2048]{1,0:T(8,128)(2,1)}, u32[]{:S(2)}, u32[]{:S(2)}) collective-permute-start(bf16[192,2048]{1,0:T(8,128)(2,1)} %fusion.4), channel_id=1, source_target_pairs={{0,8},{8,16},{16,24},{24,28},{28,20},{20,12},{12,4},{4,0},{1,9},{9... | collective-permute-start | bytes 2359304 | tf_op jit(solution)/shard_map/ppermute | solution.py:82
  469.0 57.3 %all-to-all-start.4 = ((bf16[8,256,192]{1,2,0:T(8,128)(2,1)}), bf16[8,256,192]{1,2,0:T(8,128)(2,1)S(1)}, u32[]{:S(2)}, u32[]{:S(2)}) async-start(bf16[8,256,192]{1,2,0:T(8,128)(2,1)} %copy.146), calls=%async_computation.4 | async-start | bytes 1572864 | tf_op jit(solution)/shard_map/all_to_all | solution.py:726
  476.2 14.5 %collective-permute-start.52 = (bf16[192,384]{1,0:T(8,128)(2,1)}, bf16[192,384]{1,0:T(8,128)(2,1)}, u32[]{:S(2)}, u32[]{:S(2)}) collective-permute-start(bf16[192,384]{1,0:T(8,128)(2,1)} %fusion.24), channel_id=1, source_target_pairs={{0,8},{8,16},{16,24},{24,28},{28,20},{20,12},{12,4},{4,0},{1,9},{9... | collective-permute-start | bytes 442376 | tf_op jit(solution)/shard_map/ppermute | solution.py:82
  478.2 18.1 %collective-permute-start.60 = (bf16[2048,128]{1,0:T(8,128)(2,1)}, bf16[2048,128]{1,0:T(8,128)(2,1)S(1)}, u32[]{:S(2)}, u32[]{:S(2)}) collective-permute-start(bf16[2048,128]{1,0:T(8,128)(2,1)} %get-tuple-element.97), channel_id=1, source_target_pairs={{0,8},{8,16},{16,24},{24,28},{28,20},{20,12},{12,4},{4,0},{1,9},{9... | collective-permute-start | bytes 1572872 | tf_op jit(solution)/shard_map/ppermute | solution.py:82
  479.7 22.2 %collective-permute-start.56 = (bf16[2048,128]{1,0:T(8,128)(2,1)}, bf16[2048,128]{1,0:T(8,128)(2,1)}, u32[]{:S(2)}, u32[]{:S(2)}) collective-permute-start(bf16[2048,128]{1,0:T(8,128)(2,1)} %get-tuple-element.97), channel_id=1, source_target_pairs={{0,4},{8,0},{16,8},{24,16},{28,24},{20,28},{12,20},{4,12},{1,5},{9... | collective-permute-start | bytes 1572872 | tf_op jit(solution)/shard_map/ppermute | solution.py:82
  483.5 54.4 %collective-permute-start.70 = (bf16[192,2048]{1,0:T(8,128)(2,1)}, bf16[192,2048]{1,0:T(8,128)(2,1)}, u32[]{:S(2)}, u32[]{:S(2)}) collective-permute-start(bf16[192,2048]{1,0:T(8,128)(2,1)} %fusion.6), channel_id=1, source_target_pairs={{0,4},{8,0},{16,8},{24,16},{28,24},{20,28},{12,20},{4,12},{1,5},{9... | collective-permute-start | bytes 2359304 | tf_op jit(solution)/shard_map/ppermute | solution.py:82
  496.3 18.0 %collective-permute-start.61 = (bf16[2048,128]{1,0:T(8,128)(2,1)S(1)}, bf16[2048,128]{1,0:T(8,128)(2,1)}, u32[]{:S(2)}, u32[]{:S(2)}) collective-permute-start(bf16[2048,128]{1,0:T(8,128)(2,1)S(1)} %collective-permute-done.60), channel_id=1, source_target_pairs={{0,8},{8,16},{16,24},{24,28},{28,20},{20,12},{12,4},{4,0},{1,9},{9... | collective-permute-start | bytes 1572872 | tf_op jit(solution)/shard_map/ppermute | solution.py:82
  501.9 22.4 %collective-permute-start.57 = (bf16[2048,128]{1,0:T(8,128)(2,1)}, bf16[2048,128]{1,0:T(8,128)(2,1)}, u32[]{:S(2)}, u32[]{:S(2)}) collective-permute-start(bf16[2048,128]{1,0:T(8,128)(2,1)} %collective-permute-done.56), channel_id=1, source_target_pairs={{0,4},{8,0},{16,8},{24,16},{28,24},{20,28},{12,20},{4,12},{1,5},{9... | collective-permute-start | bytes 1572872 | tf_op jit(solution)/shard_map/ppermute | solution.py:82
  506.5 36.4 %collective-permute-start.67 = (bf16[192,2048]{1,0:T(8,128)(2,1)}, bf16[192,2048]{1,0:T(8,128)(2,1)}, u32[]{:S(2)}, u32[]{:S(2)}) collective-permute-start(bf16[192,2048]{1,0:T(8,128)(2,1)} %fusion.3), channel_id=1, source_target_pairs={{0,8},{8,16},{16,24},{24,28},{28,20},{20,12},{12,4},{4,0},{1,9},{9... | collective-permute-start | bytes 2359304 | tf_op jit(solution)/shard_map/ppermute | solution.py:82
  514.3 31.2 %collective-permute-start.62 = (bf16[2048,128]{1,0:T(8,128)(2,1)}, bf16[2048,128]{1,0:T(8,128)(2,1)}, u32[]{:S(2)}, u32[]{:S(2)}) collective-permute-start(bf16[2048,128]{1,0:T(8,128)(2,1)} %collective-permute-done.61), channel_id=1, source_target_pairs={{0,8},{8,16},{16,24},{24,28},{28,20},{20,12},{12,4},{4,0},{1,9},{9... | collective-permute-start | bytes 1572872 | tf_op jit(solution)/shard_map/ppermute | solution.py:82
  524.4 24.3 %collective-permute-start.58 = (bf16[2048,128]{1,0:T(8,128)(2,1)}, bf16[2048,128]{1,0:T(8,128)(2,1)}, u32[]{:S(2)}, u32[]{:S(2)}) collective-permute-start(bf16[2048,128]{1,0:T(8,128)(2,1)} %collective-permute-done.57), channel_id=1, source_target_pairs={{0,4},{8,0},{16,8},{24,16},{28,24},{20,28},{12,20},{4,12},{1,5},{9... | collective-permute-start | bytes 1572872 | tf_op jit(solution)/shard_map/ppermute | solution.py:82
  534.9 16.7 %collective-permute-start.39 = (bf16[128,1536]{1,0:T(8,128)(2,1)}, bf16[128,1536]{1,0:T(8,128)(2,1)S(1)}, u32[]{:S(2)}, u32[]{:S(2)}) collective-permute-start(bf16[128,1536]{1,0:T(8,128)(2,1)} %get-tuple-element.89), channel_id=1, source_target_pairs={{0,1},{1,0},{2,3},{3,2},{4,5},{5,4},{6,7},{7,6},{8,9},{9,8},{10,11... | collective-permute-start | bytes 1179656 | tf_op jit(solution)/shard_map/ppermute | solution.py:149
  537.8 15.5 %collective-permute-start.42 = (bf16[192,1152]{1,0:T(8,128)(2,1)S(1)}, bf16[192,1152]{1,0:T(8,128)(2,1)S(1)}, u32[]{:S(2)}, u32[]{:S(2)}) collective-permute-start(bf16[192,1152]{1,0:T(8,128)(2,1)S(1)} %convolution_convert_fusion.3), channel_id=1, source_target_pairs={{0,8},{8,16},{16,24},{24,28},{28,20},{20,12},{12,4},{4,0},{1,9},{9... | collective-permute-start | bytes 1327112 | tf_op jit(solution)/shard_map/ppermute | solution.py:82
  542.8 14.1 %collective-permute-start.46 = (bf16[192,1152]{1,0:T(8,128)(2,1)S(1)}, bf16[192,1152]{1,0:T(8,128)(2,1)S(1)}, u32[]{:S(2)}, u32[]{:S(2)}) collective-permute-start(bf16[192,1152]{1,0:T(8,128)(2,1)S(1)} %convolution_convert_fusion.2), channel_id=1, source_target_pairs={{0,4},{8,0},{16,8},{24,16},{28,24},{20,28},{12,20},{4,12},{1,5},{9... | collective-permute-start | bytes 1327112 | tf_op jit(solution)/shard_map/ppermute | solution.py:82
  546.6 15.6 %collective-permute-start.63 = (bf16[1024,128]{1,0:T(8,128)(2,1)S(1)}, bf16[1024,128]{1,0:T(8,128)(2,1)S(1)}, u32[]{:S(2)}, u32[]{:S(2)}) collective-permute-start(bf16[1024,128]{1,0:T(8,128)(2,1)S(1)} %slice.221), channel_id=1, source_target_pairs={{0,8},{8,16},{16,24},{24,28},{28,20},{20,12},{12,4},{4,0},{1,9},{9... | collective-permute-start | bytes 786440 | tf_op jit(solution)/shard_map/ppermute | solution.py:82
  551.7 24.8 %collective-permute-start.40 = (bf16[128,1536]{1,0:T(8,128)(2,1)S(1)}, bf16[128,1536]{1,0:T(8,128)(2,1)}, u32[]{:S(2)}, u32[]{:S(2)}) collective-permute-start(bf16[128,1536]{1,0:T(8,128)(2,1)S(1)} %add_convert_fusion.1), channel_id=1, source_target_pairs={{0,2},{2,0},{1,3},{3,1},{4,6},{6,4},{5,7},{7,5},{8,10},{10,8},{9,1... | collective-permute-start | bytes 1179656 | tf_op jit(solution)/shard_map/ppermute | solution.py:150
  554.5 37.1 %collective-permute-start.43 = (bf16[192,1152]{1,0:T(8,128)(2,1)}, bf16[192,1152]{1,0:T(8,128)(2,1)}, u32[]{:S(2)}, u32[]{:S(2)}) collective-permute-start(bf16[192,1152]{1,0:T(8,128)(2,1)} %fusion.10), channel_id=1, source_target_pairs={{0,8},{8,16},{16,24},{24,28},{28,20},{20,12},{12,4},{4,0},{1,9},{9... | collective-permute-start | bytes 1327112 | tf_op jit(solution)/shard_map/ppermute | solution.py:82
  558.0 40.9 %collective-permute-start.47 = (bf16[192,1152]{1,0:T(8,128)(2,1)}, bf16[192,1152]{1,0:T(8,128)(2,1)}, u32[]{:S(2)}, u32[]{:S(2)}) collective-permute-start(bf16[192,1152]{1,0:T(8,128)(2,1)} %fusion.12), channel_id=1, source_target_pairs={{0,4},{8,0},{16,8},{24,16},{28,24},{20,28},{12,20},{4,12},{1,5},{9... | collective-permute-start | bytes 1327112 | tf_op jit(solution)/shard_map/ppermute | solution.py:82
  592.9 15.6 %collective-permute-start.44 = (bf16[192,1152]{1,0:T(8,128)(2,1)S(1)}, bf16[192,1152]{1,0:T(8,128)(2,1)S(1)}, u32[]{:S(2)}, u32[]{:S(2)}) collective-permute-start(bf16[192,1152]{1,0:T(8,128)(2,1)S(1)} %fusion.9), channel_id=1, source_target_pairs={{0,8},{8,16},{16,24},{24,28},{28,20},{20,12},{12,4},{4,0},{1,9},{9... | collective-permute-start | bytes 1327112 | tf_op jit(solution)/shard_map/ppermute | solution.py:82
  600.4 21.1 %collective-permute-start.48 = (bf16[192,1152]{1,0:T(8,128)(2,1)S(1)}, bf16[192,1152]{1,0:T(8,128)(2,1)}, u32[]{:S(2)}, u32[]{:S(2)}) collective-permute-start(bf16[192,1152]{1,0:T(8,128)(2,1)S(1)} %fusion.11), channel_id=1, source_target_pairs={{0,4},{8,0},{16,8},{24,16},{28,24},{20,28},{12,20},{4,12},{1,5},{9... | collective-permute-start | bytes 1327112 | tf_op jit(solution)/shard_map/ppermute | solution.py:82
  (128 other events, 794.9 us)

commit v3 on v2

--- a/solution.py
+++ b/solution.py
@@ -81,47 +81,78 @@
         pairs = [(CYCLE[p], CYCLE[(p + step) % n]) for p in range(n) if sends is None or sends(p)]
         return lax.ppermute(value, "seq", pairs)
 
-    def gather(self, own):
+    def gather(self, own, held=((), (), ())):
         if not self.ring:
             return [lax.all_gather(own, "seq", axis=0, tiled=True)]
         half = own.shape[0] // 2
         ahead, behind = [own], [own]
-        for _ in range(3):
+        for i in range(3):
             ahead.append(self.hop(ahead[-1], 1))
             behind.append(self.hop(behind[-1], -1))
+            if held[i]:
+                ahead[-1], behind[-1] = lax.optimization_barrier(
+                    (ahead[-1], behind[-1], *held[i])
+                )[:2]
         far = [self.hop(behind[-1][:half], -1), self.hop(ahead[-1][half:], 1)]
         return behind + far + ahead[:0:-1]
 
-    def reduce(self, step, first, active=None):
+    def reduce(self, block, active=None):
+        rows = block(0).shape[0]
+        half = rows // 2
+
         def sends(k):
             if active is None:
                 return None
             return lambda p: CYCLE[(p + k) % self.size] in active
 
-        ahead, behind = first(4), first(5)
-        for k in (3, 2, 1):
-            ahead = step(k, self.hop(ahead, 1, sends(k + 1)))
-            if k > 1:
-                behind = step(9 - k, self.hop(behind, -1, sends(-k)))
-        return step(0, self.hop(ahead, 1, sends(1)), self.hop(behind, -1, sends(-1)))
-
-    def reduce_product(self, left, right):
-        slab = left.shape[1] // self.size
-
-        def block(k):
-            return dot(left[:, k * slab : (k + 1) * slab], right, ((0,), (0,)))
+        def wait(held, *values):
+            return lax.optimization_barrier((*values, *held))[: len(values)] if held else values
+
+        def plus(part, moved):
+            return (part.astype(f32) + moved.astype(f32)).astype(bf16)
+
+        ahead, behind = block(4)[:half], block(4)[half:]
+        for k in (3, 2, 1, 0):
+            sent = (ahead, behind)
+            ahead = self.hop(ahead, 1, sends(k + 1))
+            behind = self.hop(behind, -1, sends(-k - 1))
+            ahead, behind = wait((yield sent), ahead, behind)
+            if k == 3:
+                near, far = block(3), block(5)
+                ahead = jnp.concatenate([plus(near[:half], ahead), near[half:]])
+                behind = jnp.concatenate([far[:half], plus(far[half:], behind)])
+            elif k:
+                ahead, behind = plus(block(k), ahead), plus(block(8 - k), behind)
+        yield block(0).astype(f32) + ahead.astype(f32) + behind.astype(f32)
+
+    def reduce_products(self, pairs):
+        parts = [dot(left, right, ((0,), (0,))).astype(bf16) for left, right in pairs]
+        widths = [part.shape[1] for part in parts]
+        edges = [sum(widths[:i]) for i in range(len(widths) + 1)]
+        slab = parts[0].shape[0] // self.size
+
+        def split(rows):
+            return [rows[:, low:high] for low, high in zip(edges, edges[1:])]
 
         if not self.ring:
-            blocks = jnp.concatenate([block(k).astype(bf16) for k in range(self.size)], 0)
-            return lax.psum_scatter(blocks, "seq", scatter_dimension=0, tiled=True).astype(f32)
-
-        def step(k, *moved):
-            total = block(k)
-            for one in moved:
-                total = total + one.astype(f32)
-            return total.astype(bf16) if k else total
-
-        return self.reduce(step, step)
+            for _ in range(4):
+                yield ()
+            rows = jnp.concatenate(parts, 1)
+            rows = lax.psum_scatter(rows, "seq", scatter_dimension=0, tiled=True)
+            yield split(rows.astype(f32))
+            return
+
+        ring = self.reduce(
+            lambda k: jnp.concatenate([part[k * slab : (k + 1) * slab] for part in parts], axis=1)
+        )
+        held = yield next(ring)
+        for _ in range(3):
+            held = yield ring.send(held)
+        yield split(ring.send(held))
+
+
+def once(value, *others):
+    return lax.optimization_barrier((value, *others))[0]
 
 
 def butterfly(value, axis, size):
@@ -500,27 +531,31 @@
         gain_ref[...] = turned[6 * ITEMS : 6 * ITEMS + 8, :]
 
 
-def text_heads_kernel(w_ref, out_ref):
-    for h in range(out_ref.shape[0]):
+def text_heads_kernel(head_of, w_ref, out_ref, by_head):
+    for h in range(by_head.shape[0]):
         for j in range(2):
-            out_ref[h, :, j * HD : (j + 1) * HD] = w_ref[j, :, h * HD : (h + 1) * HD].astype(bf16)
-
-
-def text_step_kernel(head_of, cap_ref, w_ref, *refs):
-    total = dot(cap_ref[...], w_ref[0], ((1,), (0,)))
-    for moved in refs[:-1]:
-        total = total + moved[...].astype(f32)
-    refs[-1][...] = total.astype(refs[-1].dtype)
+            by_head[h, :, j * HD : (j + 1) * HD] = w_ref[j, :, h * HD : (h + 1) * HD].astype(bf16)
+    for k in range(out_ref.shape[1] // (2 * HD)):
+        out_ref[:, 2 * k * HD : 2 * (k + 1) * HD] = by_head[head_of[k]]
+
+
+def text_grad_kernel(slab_at, cap_ref, *refs):
+    chunks, (out_ref, held, sems) = refs[:-3], refs[-3:]
+    copies = chunk_copies(chunks, 0, 2 * HD, held, sems)
+    for one in copies:
+        one.start()
+    for one in copies:
+        one.wait()
+    rows = cap_ref.shape[1]
+    for h in range(out_ref.shape[2] // HD):
+        at = pl.ds(pl.multiple_of(slab_at[h] * rows, rows), rows)
+        part = dot(cap_ref[...], held[at, :], ((1,), (0,)))
+        out_ref[0, :, h * HD : (h + 1) * HD] = part[:, :HD]
+        out_ref[1, :, h * HD : (h + 1) * HD] = part[:, HD:]
 
 
 def mod_kernel(scal, embed_ref, w_ref, out_ref):
     out_ref[...] = dot(embed_ref[...], w_ref[...].astype(bf16), ((1,), (0,)))
-
-
-def text_join_kernel(head_at, low_ref, high_ref, k_ref, v_ref):
-    for j, ref in enumerate((low_ref, high_ref)):
-        k_ref[:, j * HD : (j + 1) * HD] = ref[0, :, :HD]
-        v_ref[:, j * HD : (j + 1) * HD] = ref[0, :, HD:]
 
 
 def turned_copy(source_ref, low, out_ref, block):
@@ -714,7 +749,7 @@
     seqs = jnp.full((seq_size,), seq_index)
     place = jnp.where(seqs % 2 == 0, seqs // 2, (15 - seqs) // 2)
     places = (place + jnp.arange(seq_size)) % seq_size
-    slab_owner = jnp.where(places < 4, 2 * places, 15 - 2 * places)
+    slab_owner = jnp.where(places < 4, 2 * places, 15 - 2 * places).astype(jnp.int32)
     slab_head = jnp.clip(slab_owner - first_owner, 0, heads - 1)
     my_head = jnp.clip(seq_index - first_owner, 0, heads - 1)
     is_owner = (seq_index >= first_owner) & (seq_index < first_owner + heads)
@@ -725,8 +760,31 @@
     def exchange(slabs):
         return lax.all_to_all(slabs, "seq", 0, 0, tiled=True)
 
+    cap_rows = caption.shape[0]
+    cap_cols = caption.shape[1] // seq_size
+    cap_part = cap_cols // tp_size
+    text_rows = cap_rows * seq_size
+    if cap_part % 128 == 0:
+        cap_own = call(
+            lambda scal, in_ref, out_ref: out_ref.__setitem__(0, in_ref[...]),
+            "caption_slabs", seq_size, [scal],
+            [(caption, pl.BlockSpec((cap_rows, cap_part), lambda i, s: (0, i * tp_size + s[2])))],
+            [
+                (
+                    (seq_size, cap_rows, cap_part), bf16,
+                    pl.BlockSpec((1, cap_rows, cap_part), lambda i, s: (i, 0, 0)),
+                )
+            ],
+            moved=2 * cap_rows * cap_cols * 4,
+        )[0]
+    else:
+        cap_own = lax.dynamic_index_in_dim(
+            caption.reshape(cap_rows, seq_size, tp_size, cap_part), tp_index, 2, keepdims=False
+        )
+        cap_own = jnp.transpose(cap_own, (1, 0, 2))
     silu_embed = jax.nn.silu(time_embed(timesteps)).astype(bf16)
     mod_rows = mod_weight.shape[0]
+    silu_embed = once(silu_embed, cap_own)
     embed_rows = lax.dynamic_slice_in_dim(silu_embed, seq_index * mod_rows, mod_rows, 1)
     mod_part = call(
         mod_kernel, "modulation", 6, [scal],
@@ -761,66 +819,15 @@
     attn_ins = [(chunk, anywhere()) for chunk in attn_chunks]
     qkv_width = 3 * local_width
 
-    cap_rows = caption.shape[0]
-    cap_cols = caption.shape[1] // seq_size
-    cap_part = cap_cols // tp_size
-    text_rows = cap_rows * seq_size
-    if cap_part % 128 == 0:
-        cap_own = call(
-            lambda scal, in_ref, out_ref: out_ref.__setitem__(0, in_ref[...]),
-            "caption_slabs", seq_size, [scal],
-            [(caption, pl.BlockSpec((cap_rows, cap_part), lambda i, s: (0, i * tp_size + s[2])))],
-            [
-                (
-                    (seq_size, cap_rows, cap_part), bf16,
-                    pl.BlockSpec((1, cap_rows, cap_part), lambda i, s: (i, 0, 0)),
-                )
-            ],
-            moved=2 * cap_rows * cap_cols * 4,
-        )[0]
-    else:
-        cap_own = lax.dynamic_index_in_dim(
-            caption.reshape(cap_rows, seq_size, tp_size, cap_part), tp_index, 2, keepdims=False
-        )
-        cap_own = jnp.transpose(cap_own, (1, 0, 2))
-    caption_cols = gather_tp(exchange(cap_own).reshape(text_rows, cap_part), 1)
-    text_by_head = call(
-        text_heads_kernel, "text_heads", 1, [],
-        [(text_weight, whole(text_weight.shape))],
-        [((heads, cap_cols, 2 * HD), bf16, whole((heads, cap_cols, 2 * HD)))],
-        moved=text_weight.size * 6,
-    )[0]
-    text_block = math.gcd(text_rows, 512)
-
-    def text_step(k, *moved):
-        block = rows_block(text_block, 2 * HD)
-        return call(
-            text_step_kernel, "text_step", text_rows // text_block, [slab_head],
-            [
-                (caption_cols, rows_block(text_block, cap_cols)),
-                (
-                    text_by_head,
-                    pl.BlockSpec((1, cap_cols, 2 * HD), lambda i, head_of: (head_of[k], 0, 0)),
-                ),
-            ]
-            + [(one, block) for one in moved],
-            [((text_rows, 2 * HD), bf16, block)],
-            moved=text_rows * cap_cols * 2, flops=4 * text_rows * cap_cols * HD,
-        )[0]
-
-    if ring.ring:
-        text_kv = ring.reduce(text_step, text_step, owners)
-    else:
-        parts = jnp.einsum("rc,hcw->hrw", caption_cols, text_by_head, preferred_element_type=f32)
-        after = seq_size - heads - first_owner
-        parts = jnp.pad(parts.astype(bf16), ((first_owner, after), (0, 0), (0, 0)))
-        text_kv = lax.psum_scatter(parts, "seq", scatter_dimension=0, tiled=False)
-
-    ffn_chunks = ring.gather(
-        jnp.concatenate([turned(updown_weight), down_weight.astype(bf16).T], axis=1)
-    )
+    def hop(chunks, k):
+        return (chunks[k], chunks[-k]) if ring.ring else ()
+
+    cap_own = once(exchange(cap_own), *hop(attn_chunks, 1))
+    caption_cols = gather_tp(cap_own.reshape(text_rows, cap_part), 1)
+    ffn_shard = jnp.concatenate([turned(updown_weight), down_weight.astype(bf16).T], axis=1)
+    ffn_chunks = ring.gather(once(ffn_shard, packed))
     ffn_ins = [(chunk, anywhere()) for chunk in ffn_chunks]
-
+    modulation = once(modulation, *hop(attn_chunks, 3), *hop(ffn_chunks, 1))
     segment_col = segment_ids[:, None]
     steps = here // ROWS
     segment_row = segment_ids.reshape(steps, 1, ROWS)
@@ -856,7 +863,33 @@
         [pltpu.VMEM((width, qkv_width), bf16), piece_sems],
         moved=width * qkv_width * 2, flops=2 * here * width * qkv_width,
     )[0]
-    qkv_head = exchange(slabs).reshape(count, 3 * HD)
+    if ring.ring:
+        text_slabs = call(
+            text_heads_kernel, "text_heads", 1, [slab_head],
+            [(text_weight, whole(text_weight.shape))],
+            [((cap_cols, seq_size * 2 * HD), bf16, whole((cap_cols, seq_size * 2 * HD)))],
+            [pltpu.VMEM((heads, cap_cols, 2 * HD), bf16)],
+            moved=text_weight.size * 6,
+        )[0]
+        text_parts = dot(caption_cols, text_slabs, ((1,), (0,))).astype(bf16)
+
+        text_sum = ring.reduce(
+            lambda k: text_parts[:, 2 * k * HD : 2 * (k + 1) * HD], owners
+        )
+        next(text_sum)
+        for held in ((slabs,), (), (), ()):
+            text_kv = text_sum.send(held)
+        text_kv = text_kv.astype(bf16)
+    else:
+        parts = jnp.einsum(
+            "rc,jchd->hrjd", caption_cols,
+            text_weight.astype(bf16).reshape(2, cap_cols, heads, HD), preferred_element_type=f32,
+        ).reshape(heads, text_rows, 2 * HD)
+        after = seq_size - heads - first_owner
+        parts = jnp.pad(parts.astype(bf16), ((first_owner, after), (0, 0), (0, 0)))
+        text_kv = lax.psum_scatter(parts, "seq", scatter_dimension=0, tiled=False)
+
+    qkv_head = once(exchange(slabs), *hop(ffn_chunks, 2)).reshape(count, 3 * HD)
 
     block_q = math.gcd(count, 512)
     block_k = math.gcd(count, 512)
@@ -885,7 +918,9 @@
         [pltpu.VMEM((text_rows, HD), bf16), pltpu.VMEM((HD, text_rows), bf16)],
         flops=4 * count * TEXT * HD, moved=count * HD * 20, exps=count * TEXT,
     )
+    mixed_head = once(mixed_head, *hop(ffn_chunks, 3))
     mixed_slabs = exchange(mixed_head.reshape(seq_size, here, HD))
+    mixed_slabs = once(mixed_slabs, *(ffn_chunks[4:6] if ring.ring else ()))
     low, high = qkv_width, qkv_width + local_width
     head_args = {"heads": heads, "first_owner": first_owner, "count": pieces}
     half_shape = (here // 2, width)
@@ -919,10 +954,7 @@
         moved=width * 3 * units * 2, flops=12 * here * width * units,
     )
     hgrad = psum_tp((hm, ho))
-    ffn_out = psum_tp((fm, fo))
-    down_owned = ring.reduce_product(ffn_grad, inner)
-    updown_rows = ring.reduce_product(hidden_ffn, both_grads)
-
+    ffn_out = psum_tp(lax.optimization_barrier((fm, fo, *hgrad))[:2])
     mid_grad, attn_grad, grad_slabs = call(
         functools.partial(mid_kernel, low=low, high=high, **head_args), "mid", 1, [scal],
         [(x_mid, whole(tokens)), (g_rel, whole(tokens))] + halves(hgrad) + full_ins + attn_ins,
@@ -931,7 +963,10 @@
         moved=width * local_width * 2, flops=2 * here * width * local_width,
     )
     head_grad = exchange(grad_slabs).reshape(count, HD)
-    out_owned = ring.reduce_product(attn_grad, mixed)
+    ffn_sum = ring.reduce_products([(hidden_ffn, both_grads), (ffn_grad, inner)])
+    next(ffn_sum)
+    ffn_sum.send((grad_slabs,))
+    head_grad = once(head_grad, *ffn_sum.send((head_grad,)))
     half_block = pl.BlockSpec((ROWS, width), lambda i, *_: (i % (steps // 2), 0))
     sums_shape, one_gain = (4 * ITEMS, width), (8, width)
     block_out, early_sums, early_gain = call(
@@ -969,26 +1004,6 @@
         flops=10 * area, moved=count * HD * 20, exps=count * count,
     )[0]
 
-    text_grads = ring.gather(text_dkv)
-    text_grads = jnp.concatenate(text_grads, axis=0).reshape(seq_size, text_rows, 2 * HD)
-    head_at = jnp.argmax(
-        (slab_owner if ring.ring else jnp.arange(seq_size))[None, :]
-        == jnp.arange(first_owner, first_owner + heads)[:, None], axis=1,
-    ).astype(jnp.int32)
-    pair_block = pl.BlockSpec((text_rows, 2 * HD), lambda i, at: (0, i))
-    text_grad_keys, text_grad_values = call(
-        text_join_kernel, "text_join", heads // 2, [head_at],
-        [
-            (text_grads, pl.BlockSpec((1, text_rows, 2 * HD), lambda i, at: (at[2 * i], 0, 0))),
-            (text_grads, pl.BlockSpec((1, text_rows, 2 * HD), lambda i, at: (at[2 * i + 1], 0, 0))),
-        ],
-        [((text_rows, local_width), bf16, pair_block)] * 2,
-        moved=text_rows * local_width * 8,
-    )
-    text_owned = jnp.stack(
-        [dot(caption_cols, one, ((0,), (0,))) for one in (text_grad_keys, text_grad_values)]
-    )
-
     back_slabs = exchange(dqkv.reshape(slab_shape))
     qkv_grads, *hidden_grad = call(
         functools.partial(qkv_back_kernel, **head_args), "qkv_back", 1, [scal],
@@ -997,7 +1012,36 @@
         [pltpu.VMEM((width, qkv_width), bf16)] + full_sum,
         moved=width * qkv_width * 2, flops=2 * here * width * qkv_width,
     )
-    qkv_rows = ring.reduce_product(hidden_attn, qkv_grads)
+    text_grads = ring.gather(text_dkv)
+    if ring.ring:
+        slab_at = jnp.argmax(
+            slab_owner[None, :] == jnp.arange(first_owner, first_owner + heads)[:, None], axis=1
+        ).astype(jnp.int32)
+        text_owned = call(
+            text_grad_kernel, "text_grad", 1, [slab_at],
+            [(caption_cols.T, whole((cap_cols, text_rows)))]
+            + [(one, anywhere()) for one in text_grads],
+            [(text_weight.shape, f32, whole(text_weight.shape))],
+            [
+                pltpu.VMEM((seq_size * text_rows, 2 * HD), bf16),
+                pltpu.SemaphoreType.DMA((len(text_grads),)),
+            ],
+            flops=4 * text_rows * cap_cols * local_width, moved=text_rows * cap_cols * 4,
+        )[0]
+    else:
+        text_grads = text_grads[0].reshape(seq_size, text_rows, 2, HD)
+        text_owned = jnp.einsum(
+            "rc,hrjd->jchd", caption_cols, text_grads[first_owner : first_owner + heads],
+            preferred_element_type=f32,
+        ).reshape(text_weight.shape)
+
+    attn_sum = ring.reduce_products([(hidden_attn, qkv_grads), (attn_grad, mixed)])
+    next(attn_sum)
+    ffn_sum.send((dqkv,))
+    updown_rows, down_owned = ffn_sum.send(())
+    for _ in range(4):
+        attn_grads = attn_sum.send(())
+    qkv_rows, out_owned = attn_grads
     hidden_grad = psum_tp(hidden_grad)
     all_sums = (6 * ITEMS, quarter)
     input_grad, item_sums, gain_sums = call(

time: 689 us -> 644 us (0.935)
  matrix products: 58.8 us -> 18.8 us
  other arithmetic: 43.7 us -> 82.6 us
  Pallas kernels: 188 us -> 154 us
  waiting for transfers between devices: 187 us -> 207 us
  blocking collectives: 14.7 us -> 0 us
  starting transfers between devices: 126 us -> 112 us
    dot_general x36 -> x7, matrix products: 58.8 us -> 18.8 us  [dot(): return lax.dot_general(a, b, (dims, ((), ())), preferred_element_type=f32)]
    pallas_call x24 -> x16, Pallas kernels: 188 us -> 154 us  [call(): pl.pallas_call(kernel, out_shape=tuple((shape_of(shape, dtype) for shape,...]
    convert_element_type x0 -> x17, other arithmetic: none -> 25.1 us  [the longest x16 23 us: plus(): return (part.astype(f32) + moved.astype(f32)).astype(bf16)]
    all_to_all x4 -> x5, waiting for transfers between devices: 14.3 us -> 36.9 us  [exchange(): return lax.all_to_all(slabs, 'seq', 0, 0, tiled=True)]
    ppermute x59 -> x48, waiting for transfers between devices: 141 us -> 121 us  [hop(): return lax.ppermute(value, 'seq', pairs)]
    ppermute x59 -> x48, starting transfers between devices: 88.8 us -> 69.5 us  [hop(): return lax.ppermute(value, 'seq', pairs)]
    all_to_all x1 -> x0, blocking collectives: 14.7 us -> none  [exchange(): return lax.all_to_all(slabs, 'seq', 0, 0, tiled=True)]
    unnamed x210 -> x214, local copies, waits for them, and re-layouts: 25.2 us -> 11.8 us
  transfers between devices with their start and end apart: 92 -> 82, of which waited for: 34 -> 32; matrix products, arithmetic and copies ran while one was open for 16% -> 17% of each run, Pallas kernels for 25% -> 21%
where the time goes in v3:
time: 644 us; the launch traced here: 632 us
  waiting for transfers between devices  207 us (32%)
  Pallas kernels  154 us (24%)
  starting transfers between devices  112 us (17%)
  other arithmetic  82.6 us (13%)
  local copies, waits for them, and re-layouts  47.3 us (7%)
  matrix products  18.8 us (3%)
  between operations  9.78 us (2%)
    pallas_call x16, Pallas kernels, call(): pl.pallas_call(kernel, out_shape=tuple((shape_of(shape, dtype) for shape,...  154 us
    ppermute x48, waiting for transfers between devices, hop(): return lax.ppermute(value, 'seq', pairs)  121 us
    ppermute x48, starting transfers between devices, hop(): return lax.ppermute(value, 'seq', pairs)  69.5 us
    all_to_all x5, waiting for transfers between devices, exchange(): return lax.all_to_all(slabs, 'seq', 0, 0, tiled=True)  36.9 us
    all_to_all x5, starting transfers between devices, exchange(): return lax.all_to_all(slabs, 'seq', 0, 0, tiled=True)  25.4 us
    convert_element_type x16, other arithmetic, plus(): return (part.astype(f32) + moved.astype(f32)).astype(bf16)  23 us
    ppermute x11, waiting for transfers between devices, butterfly(): lax.ppermute(value, axis, [(i, i ^ step) for i in range(size)])  21.1 us
    dot_general x7, matrix products, dot(): return lax.dot_general(a, b, (dims, ((), ())), preferred_element_type=f32)  18.8 us
  transfers between devices with their start and end apart: 82, of which 32 were waited for; matrix products, arithmetic and copies ran while one was open for 17% of the time, Pallas kernels for 21%

profile of v3, /device:TPU:0, one launch (start us, length us, event | category | flops | bytes accessed | tf_op | source)
XLA Modules:
  0.0 631.9 jit_solution(16734334777602580901)
XLA Ops:
  2.1 3.1 collective-permute-start.8
  5.8 5.5 caption_slabs.1
  11.3 6.3 all-to-all-start.1
  18.7 5.2 modulation.1
  26.9 5.5 all-to-all-done.1
  38.3 3.4 collective-permute-done.1
  52.2 3.8 text_heads.1
  64.9 9.1 %collective-permute-done.4 = f32[48,768]{1,0:T(8,128)S(1)} collective-permute-done((f32[48,768]{1,0:T(8,128)S(1)}, f32[48,768]{1,0:T(8,128)S(1)}, u32[]{:S(2)}, u32[]{:S(2)}) %collective-permute-start.4) | collective-permute-done | bytes 147488 | tf_op jit(solution)/shard_map/ppermute | solution.py:175
  75.2 22.7 %collective-permute-done.7.refs_3_ = bf16[192,1536]{1,0:T(8,128)(2,1)S(1)} collective-permute-done((bf16[192,1536]{1,0:T(8,128)(2,1)S(1)}, bf16[192,1536]{1,0:T(8,128)(2,1)S(1)}, u32[]{:S(2)}, u32[]{:S(2)}) %collective-permute-start.7) | collective-permute-done | bytes 589856 | tf_op jit(solution)/shard_map/ppermute | solution.py:82
  103.6 2.4 convolution_convert_fusion.3
  111.6 7.3 %enter.1 = (bf16[256,1536]{1,0:T(8,128)(2,1)}, bf16[256,1536]{1,0:T(8,128)(2,1)}, f32[48,1536]{1,0:T(8,128)}, f32[8,1536]{1,0:T(8,128)}, bf16[256,1536]{1,0:T(8,128)(2,1)}) custom-call(s32[3]{0:T(128)} %pad_add_fusion.1.scal, bf16[256,1536]{1,0:T(8,128)(2,1)} %x_ref.1, bf16[256,1536]{1,0:T(8,128)(2,1)} %g_ref.1, f32[48,1536]{1,0:T(8,128)} %pad_maximum_fusion.13.mod_ref, ...), custom_call_target="tpu_custom_call" | custom-call | bytes 3932160 | tf_op jit(solution)/shard_map/enter/pallas_call | solution.py:214
  119.7 5.6 project.1
  126.5 5.9 collective-permute-start.21
  134.6 8.9 %collective-permute-done.21 = bf16[2048,128]{1,0:T(8,128)(2,1)S(1)} collective-permute-done((bf16[2048,128]{1,0:T(8,128)(2,1)S(1)}, bf16[2048,128]{1,0:T(8,128)(2,1)S(1)}, u32[]{:S(2)}, u32[]{:S(2)}) %collective-permute-start.21) | collective-permute-done | bytes 524320 | tf_op jit(solution)/shard_map/ppermute | solution.py:82
  144.7 3.7 collective-permute-start.22
  150.9 10.7 %collective-permute-done.22 = bf16[2048,128]{1,0:T(8,128)(2,1)} collective-permute-done((bf16[2048,128]{1,0:T(8,128)(2,1)S(1)}, bf16[2048,128]{1,0:T(8,128)(2,1)}, u32[]{:S(2)}, u32[]{:S(2)}) %collective-permute-start.22) | collective-permute-done | bytes 524320 | tf_op jit(solution)/shard_map/ppermute | solution.py:82
  167.3 4.3 all-to-all-start
  173.6 6.2 collective-permute-done.15.refs_2_
  179.8 9.7 %collective-permute-done.16.refs_7_ = bf16[192,3072]{1,0:T(8,128)(2,1)} collective-permute-done((bf16[192,3072]{1,0:T(8,128)(2,1)}, bf16[192,3072]{1,0:T(8,128)(2,1)}, u32[]{:S(2)}, u32[]{:S(2)}) %collective-permute-start.16) | collective-permute-done | bytes 1179680 | tf_op jit(solution)/shard_map/ppermute | solution.py:82
  189.5 3.8 collective-permute-start.23
  193.3 3.9 collective-permute-done.25
  202.7 14.4 %attend.1 = (f32[64,2048]{1,0:T(8,128)}, f32[1,2048]{1,0:T(1,128)}) custom-call(s32[4,4]{1,0:T(4,128)} %pad_add_fusion.table, bf16[2048,192]{1,0:T(8,128)(2,1)} %bitcast.137, bf16[2048,192]{1,0:T(8,128)(2,1)} %bitcast.138, s32[1,2048]{1,0:T(1,128)} %bitcast.154, s32[2048,1]{1,0:T(8,128)} %copy.142.sk_ref), custom_call_target="tpu_custom_call" | custom-call | flops 1073741824 | bytes 2621440 | tf_op jit(solution)/shard_map/attend/pallas_call | solution.py:214
  217.1 6.5 %collective-permute-done.27.refs_3_ = bf16[192,3072]{1,0:T(8,128)(2,1)} collective-permute-done((bf16[192,3072]{1,0:T(8,128)(2,1)}, bf16[192,3072]{1,0:T(8,128)(2,1)}, u32[]{:S(2)}, u32[]{:S(2)}) %collective-permute-start.27) | collective-permute-done | bytes 1179680 | tf_op jit(solution)/shard_map/ppermute | solution.py:82
  229.4 5.8 collective-permute-done.23
  237.3 11.3 %attend_text.1 = (bf16[2048,64]{1,0:T(8,128)(2,1)}, f32[64,2048]{1,0:T(8,128)}, f32[1,2048]{1,0:T(1,128)}) custom-call(s32[4,4]{1,0:T(4,128)} %pad_add_fusion.table, f32[1]{0:T(128)} %bitcast.13.gate, bf16[2048,192]{1,0:T(8,128)(2,1)} %bitcast.139, bf16[2048,128]{1,0:T(8,128)(2,1)} %add_convert_fusion.10.kv_ref, f32[64,2048]{1,0:T(8,128)} %get-tuple-element.93.self_ref, ...), custom_call_target="tpu_custom_call" | custom-call | flops 134217728 | bytes 2621440 | tf_op jit(solution)/shard_map/attend_text/pallas_call | solution.py:214
  250.5 7.4 %all-to-all-start.2 = ((bf16[8,256,64]{1,2,0:T(8,128)(2,1)}), bf16[8,256,64]{1,2,0:T(8,128)(2,1)S(1)}, u32[]{:S(2)}, u32[]{:S(2)}) async-start(bf16[8,256,64]{1,2,0:T(8,128)(2,1)} %copy.143), calls=%async_computation.2 | async-start | bytes 524288 | tf_op jit(solution)/shard_map/all_to_all | solution.py:761
  257.9 8.2 %all-to-all-done.2 = bf16[8,256,64]{1,2,0:T(8,128)(2,1)S(1)} async-done(((bf16[8,256,64]{1,2,0:T(8,128)(2,1)}), bf16[8,256,64]{1,2,0:T(8,128)(2,1)S(1)}, u32[]{:S(2)}, u32[]{:S(2)}) %all-to-all-start.2) | async-done | bytes 262176 | tf_op jit(solution)/shard_map/all_to_all | solution.py:761
  267.1 5.7 out.1
  277.5 9.7 %collective-permute-done.32 = bf16[128,1536]{1,0:T(8,128)(2,1)S(1)} collective-permute-done((bf16[128,1536]{1,0:T(8,128)(2,1)S(1)}, bf16[128,1536]{1,0:T(8,128)(2,1)S(1)}, u32[]{:S(2)}, u32[]{:S(2)}) %collective-permute-start.32) | collective-permute-done | bytes 393248 | tf_op jit(solution)/shard_map/ppermute | solution.py:181
  289.8 19.0 %ffn.1 = (f32[256,1536]{1,0:T(8,128)}, bf16[256,1536]{1,0:T(8,128)(2,1)}, bf16[256,1536]{1,0:T(8,128)(2,1)}, bf16[256,1024]{1,0:T(8,128)(2,1)}, bf16[256,2048]{1...) custom-call(s32[3]{0:T(128)} %pad_add_fusion.1.scal, ...), custom_call_target="tpu_custom_call" | custom-call | flops 4831838208 | bytes 9437184 | tf_op jit(solution)/shard_map/ffn/pallas_call | solution.py:214
  309.0 3.3 convolution_convert_fusion
  321.8 5.3 collective-permute-done.35
  329.4 7.8 %mid.1 = (f32[256,1536]{1,0:T(8,128)}, bf16[256,1536]{1,0:T(8,128)(2,1)}, bf16[8,256,64]{2,1,0:T(8,128)(2,1)}) custom-call(s32[3]{0:T(128)} %pad_add_fusion.1.scal, f32[256,1536]{1,0:T(8,128)} %get-tuple-element.101.mid_ref, bf16[256,1536]{1,0:T(8,128)(2,1)} %get-tuple-element.87.g_ref, bf16[128,1536]{1,0:T(8,128)(2,1)} %copy-done.20, ...), custom_call_target="tpu_custom_call" | custom-call | flops 301989888 | bytes 1179648 | tf_op jit(solution)/shard_map/mid/pallas_call | solution.py:214
  347.3 3.4 all-to-all-start.3
  353.3 22.3 %all-to-all-done.3 = bf16[8,256,64]{1,2,0:T(8,128)(2,1)S(1)} async-done(((bf16[8,256,64]{1,2,0:T(8,128)(2,1)}), bf16[8,256,64]{1,2,0:T(8,128)(2,1)S(1)}, u32[]{:S(2)}, u32[]{:S(2)}) %all-to-all-start.3) | async-done | bytes 262176 | tf_op jit(solution)/shard_map/all_to_all | solution.py:761
  376.7 2.8 add_convert_fusion.2
  380.9 2.7 add_convert_fusion.3
  384.2 12.0 %attend_text_back.1 = (bf16[2048,128]{1,0:T(8,128)(2,1)}, f32[64,2048]{1,0:T(8,128)}, f32[1,2048]{1,0:T(1,128)}) custom-call(s32[4,4]{1,0:T(4,128)} %pad_add_fusion.table, f32[1]{0:T(128)} %bitcast.13.gate, bf16[2048,192]{1,0:T(8,128)(2,1)} %bitcast.140, bf16[2048,64]{1,0:T(8,128)(2,1)} %bitcast.148, bf16[2048,128]{1,0:T(8,128)(2,1)} %add_convert_fusion.10.kv_ref, ...), custom_call_target="tpu_custom_call" | custom-call | flops 335544320 | bytes 2621440 | tf_op jit(solution)/shard_map/attend_text_back/pallas_call | solution.py:214
  398.5 19.2 %attend_back.1 = bf16[2048,192]{1,0:T(8,128)(2,1)} custom-call(s32[4,4]{1,0:T(4,128)} %pad_add_fusion.table, bf16[2048,192]{1,0:T(8,128)(2,1)} %bitcast.141, bf16[2048,64]{1,0:T(8,128)(2,1)} %bitcast.149, bf16[2048,192]{1,0:T(8,128)(2,1)} %bitcast.142, f32[64,2048]{1,0:T(8,128)} %get-tuple-element.93.self_ref, f32[1,2048]{1,0:T(1,128)} %get-tuple-element.120.stat_ref, ...), custom_call_target="tpu_custom_call" | custom-call | flops 2684354560 | bytes 2621440 | tf_op jit(solution)/shard_map/attend_back/pallas_call | solution.py:214
  417.7 2.3 copy.151
  420.0 4.1 all-to-all-start.4
  429.8 12.5 %side.1 = (f32[256,1536]{1,0:T(8,128)}, f32[32,1536]{1,0:T(8,128)}, f32[8,1536]{1,0:T(8,128)}) custom-call(s32[3]{0:T(128)} %pad_add_fusion.1.scal, f32[256,1536]{1,0:T(8,128)} %get-tuple-element.101.mid_ref, f32[256,1536]{1,0:T(8,128)} %get-tuple-element.104.grad_ref, bf16[256,1536]{1,0:T(8,128)(2,1)} %get-tuple-element.87.g_ref, ...), custom_call_target="tpu_custom_call" | custom-call | bytes 9437184 | tf_op jit(solution)/shard_map/side/pallas_call | solution.py:214
  442.2 8.8 %collective-permute-done.56.refs_2_ = bf16[2048,128]{1,0:T(8,128)(2,1)} collective-permute-done((bf16[2048,128]{1,0:T(8,128)(2,1)}, bf16[2048,128]{1,0:T(8,128)(2,1)}, u32[]{:S(2)}, u32[]{:S(2)}) %collective-permute-start.56) | collective-permute-done | bytes 524320 | tf_op jit(solution)/shard_map/ppermute | solution.py:82
  451.1 5.9 collective-permute-start.61
  457.0 2.7 add_convert_fusion.1
  463.0 7.3 %qkv_back.1 = (bf16[256,1152]{1,0:T(8,128)(2,1)}, bf16[128,1536]{1,0:T(8,128)(2,1)}, bf16[128,1536]{1,0:T(8,128)(2,1)}) custom-call(s32[3]{0:T(128)} %pad_add_fusion.1.scal, bf16[8,256,192]{2,1,0:T(8,128)(2,1)} %copy.152.slab_ref, bf16[192,1536]{1,0:T(8,128)(2,1)} %copy-done, bf16[192,1536]{1,0:T(8,128)(2,1)} %copy-done.5, bf16[192,1536]{1,0:T(8,128)(2,1)} %copy-done.7, ...), custom_call_target="tpu_custom_call" | custom-call | flops 905969664 | bytes 3538944 | tf_op jit(solution)/shard_map/qkv_back/pallas_call | solution.py:214
  470.3 2.3 convolution_convert_fusion.1
  474.0 2.7 add_convert_fusion
  480.9 19.4 %collective-permute-done.47 = bf16[96,1536]{1,0:T(8,128)(2,1)S(1)} collective-permute-done((bf16[96,1536]{1,0:T(8,128)(2,1)S(1)}, bf16[96,1536]{1,0:T(8,128)(2,1)S(1)}, u32[]{:S(2)}, u32[]{:S(2)}) %collective-permute-start.47) | collective-permute-done | bytes 294944 | tf_op jit(solution)/shard_map/ppermute | solution.py:82
  500.2 2.5 collective-permute-start.58
  503.7 8.5 %collective-permute-done.51 = bf16[96,1536]{1,0:T(8,128)(2,1)S(1)} collective-permute-done((bf16[96,1536]{1,0:T(8,128)(2,1)S(1)}, bf16[96,1536]{1,0:T(8,128)(2,1)S(1)}, u32[]{:S(2)}, u32[]{:S(2)}) %collective-permute-start.51) | collective-permute-done | bytes 294944 | tf_op jit(solution)/shard_map/ppermute | solution.py:82
  516.3 5.1 collective-permute-done.62.refs_5_
  523.3 9.1 %text_grad.1 = f32[2,512,384]{2,1,0:T(8,128)} custom-call(s32[6]{0:T(128)} %get-tuple-element.132.slab_at, bf16[512,2048]{1,0:T(8,128)(2,1)} %fusion.7.cap_ref, bf16[2048,128]{1,0:T(8,128)(2,1)} %get-tuple-element.133.refs_0_, bf16[2048,128]{1,0:T(8,128)(2,1)} %collective-permute-done.55.refs_1_, bf16[2048,128]{1,0:T(8,128)(2,1)} %collective-permute-done.56.refs_2_, ...), custom_call_target="tpu_custom_call" | custom-call | flops 1610612736 | bytes 4194304 | tf_op jit(solution)/shard_map/text_grad/pallas_call | solution.py:214
  532.4 2.5 multiply_reduce_fusion.1
  540.8 8.7 %leave.1 = (f32[256,1536]{1,0:T(8,128)}, f32[48,384]{1,0:T(8,128)}, f32[8,1536]{1,0:T(8,128)}) custom-call(s32[3]{0:T(128)} %pad_add_fusion.1.scal, bf16[256,1536]{1,0:T(8,128)(2,1)} %get-tuple-element.86.x_ref, f32[256,1536]{1,0:T(8,128)} %get-tuple-element.104.grad_ref, bf16[128,1536]{1,0:T(8,128)(2,1)} %copy-done.42, bf16[128,1536]{1,0:T(8,128)(2,1)} %copy-done.65, ...), custom_call_target="tpu_custom_call" | custom-call | bytes 6291456 | tf_op jit(solution)/shard_map/leave/pallas_call | solution.py:214
  552.1 2.2 convert_add_fusion
  557.5 3.4 collective-permute-done.68
  576.4 3.6 collective-permute-done.54
  591.9 3.6 collective-permute-done.72
  596.0 3.1 collective-permute-done.73
  600.3 3.3 collective-permute-done.74
  609.9 3.0 multiply_subtract_fusion.2
  615.6 3.1 multiply_subtract_fusion.1
  623.0 7.3 %multiply_subtract_fusion = (f32[128,9216]{1,0:T(8,128)}, f32[128,9216]{1,0:T(8,128)}, f32[128,9216]{1,0:T(8,128)}) fusion(f32[128,9216]{1,0:T(8,128)S(1)} %bitcast.145, f32[128,9216]{1,0:T(8,128)S(1)} %bitcast.163, f32[128,9216]{1,0:T(8,128)S(1)} %copy-done.99, f32[]{:T(128)S(6)} %min.18, bf16[8,128]{1,0:T(8,128)(2,1)S(1)} %copy-done.86, ...), kind=kOutput, calls=%fused_computation.5 | convolution fusion | flops 37748736 | bytes 28461060 | tf_op jit(solution)/shard_map/dot_general | solution.py:71
  (493 shorter events, 181.6 us)
Async XLA Ops:
  2.1 24.7 %collective-permute-start.8 = (bf16[192,1536]{1,0:T(8,128)(2,1)S(1)}, bf16[192,1536]{1,0:T(8,128)(2,1)S(1)}, u32[]{:S(2)}, u32[]{:S(2)}) collective-permute-start(bf16[192,1536]{1,0:T(8,128)(2,1)S(1)} %pad_maximum_fusion.7.refs_0_), channel_id=1, source_target_pairs={{0,8},{8,16},{16,24},{24,28},{28,20},{20,12},{12,4},{4,0},{1,9},{9... | collective-permute-start | bytes 1769480 | tf_op jit(solution)/shard_map/ppermute | solution.py:82
  5.2 21.7 %collective-permute-start.5 = (bf16[192,1536]{1,0:T(8,128)(2,1)S(1)}, bf16[192,1536]{1,0:T(8,128)(2,1)S(1)}, u32[]{:S(2)}, u32[]{:S(2)}) collective-permute-start(bf16[192,1536]{1,0:T(8,128)(2,1)S(1)} %pad_maximum_fusion.7.refs_0_), channel_id=1, source_target_pairs={{0,4},{8,0},{16,8},{24,16},{28,24},{20,28},{12,20},{4,12},{1,5},{9... | collective-permute-start | bytes 1769480 | tf_op jit(solution)/shard_map/ppermute | solution.py:82
  11.3 21.0 %all-to-all-start.1 = ((bf16[8,256,128]{2,1,0:T(8,128)(2,1)}), bf16[8,256,128]{2,1,0:T(8,128)(2,1)}, u32[]{:S(2)}, u32[]{:S(2)}) async-start(bf16[8,256,128]{2,1,0:T(8,128)(2,1)} %caption_slabs.1), calls=%async_computation.1 | async-start | bytes 1048576 | tf_op jit(solution)/shard_map/all_to_all | solution.py:761
  24.8 10.6 %collective-permute-start = (f32[64,384]{1,0:T(8,128)S(1)}, f32[64,384]{1,0:T(8,128)}, u32[]{:S(2)}, u32[]{:S(2)}) collective-permute-start(f32[64,384]{1,0:T(8,128)S(1)} %pad_maximum_fusion.16), channel_id=1, source_target_pairs={{0,4},{4,0},{8,12},{12,8},{16,20},{20,16},{24,28},{28,24},{1,5},{5... | collective-permute-start | bytes 294920 | tf_op jit(solution)/shard_map/ppermute | solution.py:161
  34.4 9.9 %collective-permute-start.17 = (bf16[2048,128]{0,1:T(8,128)(2,1)}, bf16[2048,128]{0,1:T(8,128)(2,1)}, u32[]{:S(2)}, u32[]{:S(2)}) collective-permute-start(bf16[2048,128]{0,1:T(8,128)(2,1)} %copy.156), channel_id=1, source_target_pairs={{0,1},{1,0},{2,3},{3,2},{4,5},{5,4},{6,7},{7,6},{8,9},{9,8},{10,11... | collective-permute-start | bytes 1572872 | tf_op jit(solution)/shard_map/ppermute | solution.py:174
  42.3 16.8 %collective-permute-start.9 = (bf16[192,1536]{1,0:T(8,128)(2,1)S(1)}, bf16[192,1536]{1,0:T(8,128)(2,1)S(1)}, u32[]{:S(2)}, u32[]{:S(2)}) collective-permute-start(bf16[192,1536]{1,0:T(8,128)(2,1)S(1)} %collective-permute-done.8.refs_8_), channel_id=1, source_target_pairs={{0,8},{8,16},{16,24},{24,28},{28,20},{20,12},{12,4},{4,0},{1,9},{9... | collective-permute-start | bytes 1769480 | tf_op jit(solution)/shard_map/ppermute | solution.py:82
  43.5 16.7 %collective-permute-start.6 = (bf16[192,1536]{1,0:T(8,128)(2,1)S(1)}, bf16[192,1536]{1,0:T(8,128)(2,1)S(1)}, u32[]{:S(2)}, u32[]{:S(2)}) collective-permute-start(bf16[192,1536]{1,0:T(8,128)(2,1)S(1)} %collective-permute-done.5.refs_1_), channel_id=1, source_target_pairs={{0,4},{8,0},{16,8},{24,16},{28,24},{20,28},{12,20},{4,12},{1,5},{9... | collective-permute-start | bytes 1769480 | tf_op jit(solution)/shard_map/ppermute | solution.py:82
  46.7 55.1 %collective-permute-start.18 = (bf16[2048,256]{0,1:T(8,128)(2,1)}, bf16[2048,256]{0,1:T(8,128)(2,1)}, u32[]{:S(2)}, u32[]{:S(2)}) collective-permute-start(bf16[2048,256]{0,1:T(8,128)(2,1)} %pad_maximum_fusion.4), channel_id=1, source_target_pairs={{0,2},{2,0},{1,3},{3,1},{4,6},{6,4},{5,7},{7,5},{8,10},{10,8},{9,1... | collective-permute-start | bytes 3145736 | tf_op jit(solution)/shard_map/ppermute | solution.py:175
  51.7 9.4 %collective-permute-start.3 = (f32[48,384]{1,0:T(8,128)}, f32[48,384]{1,0:T(8,128)}, u32[]{:S(2)}, u32[]{:S(2)}) collective-permute-start(f32[48,384]{1,0:T(8,128)} %slice.331), channel_id=1, source_target_pairs={{0,1},{1,0},{2,3},{3,2},{4,5},{5,4},{6,7},{7,6},{8,9},{9,8},{10,11... | collective-permute-start | bytes 221192 | tf_op jit(solution)/shard_map/ppermute | solution.py:174
  56.7 52.9 %collective-permute-start.11 = (bf16[192,3072]{1,0:T(8,128)(2,1)}, bf16[192,3072]{1,0:T(8,128)(2,1)}, u32[]{:S(2)}, u32[]{:S(2)}) collective-permute-start(bf16[192,3072]{1,0:T(8,128)(2,1)} %pad_maximum_fusion.2.refs_0_), channel_id=1, source_target_pairs={{0,4},{8,0},{16,8},{24,16},{28,24},{20,28},{12,20},{4,12},{1,5},{9... | collective-permute-start | bytes 3538952 | tf_op jit(solution)/shard_map/ppermute | solution.py:82
  59.1 40.7 %collective-permute-start.10 = (bf16[192,1536]{1,0:T(8,128)(2,1)S(1)}, bf16[192,1536]{1,0:T(8,128)(2,1)S(1)}, u32[]{:S(2)}, u32[]{:S(2)}) collective-permute-start(bf16[192,1536]{1,0:T(8,128)(2,1)S(1)} %collective-permute-done.9.refs_7_), channel_id=1, source_target_pairs={{0,8},{8,16},{16,24},{24,28},{28,20},{20,12},{12,4},{4,0},{1,9},{9... | collective-permute-start | bytes 1769480 | tf_op jit(solution)/shard_map/ppermute | solution.py:82
  60.2 37.7 %collective-permute-start.7 = (bf16[192,1536]{1,0:T(8,128)(2,1)S(1)}, bf16[192,1536]{1,0:T(8,128)(2,1)S(1)}, u32[]{:S(2)}, u32[]{:S(2)}) collective-permute-start(bf16[192,1536]{1,0:T(8,128)(2,1)S(1)} %collective-permute-done.6.refs_2_), channel_id=1, source_target_pairs={{0,4},{8,0},{16,8},{24,16},{28,24},{20,28},{12,20},{4,12},{1,5},{9... | collective-permute-start | bytes 1769480 | tf_op jit(solution)/shard_map/ppermute | solution.py:82
  62.0 12.0 %collective-permute-start.4 = (f32[48,768]{1,0:T(8,128)S(1)}, f32[48,768]{1,0:T(8,128)S(1)}, u32[]{:S(2)}, u32[]{:S(2)}) collective-permute-start(f32[48,768]{1,0:T(8,128)S(1)} %pad_maximum_fusion.14), channel_id=1, source_target_pairs={{0,2},{2,0},{1,3},{3,1},{4,6},{6,4},{5,7},{7,5},{8,10},{10,8},{9,1... | collective-permute-start | bytes 442376 | tf_op jit(solution)/shard_map/ppermute | solution.py:175
  74.0 37.6 %collective-permute-start.12 = (bf16[192,3072]{1,0:T(8,128)(2,1)}, bf16[192,3072]{1,0:T(8,128)(2,1)}, u32[]{:S(2)}, u32[]{:S(2)}) collective-permute-start(bf16[192,3072]{1,0:T(8,128)(2,1)} %pad_maximum_fusion.2.refs_0_), channel_id=1, source_target_pairs={{0,8},{8,16},{16,24},{24,28},{28,20},{20,12},{12,4},{4,0},{1,9},{9... | collective-permute-start | bytes 3538952 | tf_op jit(solution)/shard_map/ppermute | solution.py:82
  98.7 20.2 %collective-permute-start.13 = (bf16[96,1536]{1,0:T(8,128)(2,1)}, bf16[96,1536]{1,0:T(8,128)(2,1)S(1)}, u32[]{:S(2)}, u32[]{:S(2)}) collective-permute-start(bf16[96,1536]{1,0:T(8,128)(2,1)} %slice.338), channel_id=1, source_target_pairs={{0,4},{8,0},{16,8},{24,16},{28,24},{20,28},{12,20},{4,12},{1,5},{9... | collective-permute-start | bytes 884744 | tf_op jit(solution)/shard_map/ppermute | solution.py:82
  100.6 18.3 %collective-permute-start.14 = (bf16[96,1536]{1,0:T(8,128)(2,1)}, bf16[96,1536]{1,0:T(8,128)(2,1)S(1)}, u32[]{:S(2)}, u32[]{:S(2)}) collective-permute-start(bf16[96,1536]{1,0:T(8,128)(2,1)} %slice.339), channel_id=1, source_target_pairs={{0,8},{8,16},{16,24},{24,28},{28,20},{20,12},{12,4},{4,0},{1,9},{9... | collective-permute-start | bytes 884744 | tf_op jit(solution)/shard_map/ppermute | solution.py:82
  108.2 17.1 %collective-permute-start.19 = (bf16[1024,128]{1,0:T(8,128)(2,1)S(1)}, bf16[1024,128]{1,0:T(8,128)(2,1)S(1)}, u32[]{:S(2)}, u32[]{:S(2)}) collective-permute-start(bf16[1024,128]{1,0:T(8,128)(2,1)S(1)} %get-tuple-element.263), channel_id=1, source_target_pairs={{8,16},{16,24},{24,28},{20,12},{12,4},{4,0},{9,17},{17,25},{25,29}... | collective-permute-start | bytes 786440 | tf_op jit(solution)/shard_map/ppermute | solution.py:82
  109.5 15.8 %collective-permute-start.20 = (bf16[1024,128]{1,0:T(8,128)(2,1)S(1)}, bf16[1024,128]{1,0:T(8,128)(2,1)S(1)}, u32[]{:S(2)}, u32[]{:S(2)}) collective-permute-start(bf16[1024,128]{1,0:T(8,128)(2,1)S(1)} %get-tuple-element.262), channel_id=1, source_target_pairs={{8,0},{16,8},{24,16},{20,28},{12,20},{4,12},{9,1},{17,9},{25,17},{... | collective-permute-start | bytes 786440 | tf_op jit(solution)/shard_map/ppermute | solution.py:82
  126.5 17.0 %collective-permute-start.21 = (bf16[2048,128]{1,0:T(8,128)(2,1)S(1)}, bf16[2048,128]{1,0:T(8,128)(2,1)S(1)}, u32[]{:S(2)}, u32[]{:S(2)}) collective-permute-start(bf16[2048,128]{1,0:T(8,128)(2,1)S(1)} %pad_maximum_fusion.9), channel_id=1, source_target_pairs={{0,8},{16,24},{24,28},{28,20},{12,4},{4,0},{1,9},{17,25},{25,29},{... | collective-permute-start | bytes 1572872 | tf_op jit(solution)/shard_map/ppermute | solution.py:82
  132.5 18.5 %collective-permute-start.24 = (bf16[2048,128]{1,0:T(8,128)(2,1)S(1)}, bf16[2048,128]{1,0:T(8,128)(2,1)S(1)}, u32[]{:S(2)}, u32[]{:S(2)}) collective-permute-start(bf16[2048,128]{1,0:T(8,128)(2,1)S(1)} %pad_maximum_fusion.10), channel_id=1, source_target_pairs={{0,4},{8,0},{16,8},{28,24},{20,28},{12,20},{1,5},{9,1},{17,9},{29,... | collective-permute-start | bytes 1572872 | tf_op jit(solution)/shard_map/ppermute | solution.py:82
  144.7 16.9 %collective-permute-start.22 = (bf16[2048,128]{1,0:T(8,128)(2,1)S(1)}, bf16[2048,128]{1,0:T(8,128)(2,1)}, u32[]{:S(2)}, u32[]{:S(2)}) collective-permute-start(bf16[2048,128]{1,0:T(8,128)(2,1)S(1)} %add_convert_fusion.14), channel_id=1, source_target_pairs={{0,8},{8,16},{24,28},{28,20},{20,12},{4,0},{1,9},{9,17},{25,29},{2... | collective-permute-start | bytes 1572872 | tf_op jit(solution)/shard_map/ppermute | solution.py:82
  148.4 31.4 %collective-permute-start.15 = (bf16[192,3072]{1,0:T(8,128)(2,1)}, bf16[192,3072]{1,0:T(8,128)(2,1)}, u32[]{:S(2)}, u32[]{:S(2)}) collective-permute-start(bf16[192,3072]{1,0:T(8,128)(2,1)} %collective-permute-done.11.refs_1_), channel_id=1, source_target_pairs={{0,4},{8,0},{16,8},{24,16},{28,24},{20,28},{12,20},{4,12},{1,5},{9... | collective-permute-start | bytes 3538952 | tf_op jit(solution)/shard_map/ppermute | solution.py:82
  149.4 40.0 %collective-permute-start.16 = (bf16[192,3072]{1,0:T(8,128)(2,1)}, bf16[192,3072]{1,0:T(8,128)(2,1)}, u32[]{:S(2)}, u32[]{:S(2)}) collective-permute-start(bf16[192,3072]{1,0:T(8,128)(2,1)} %collective-permute-done.12.refs_8_), channel_id=1, source_target_pairs={{0,8},{8,16},{16,24},{24,28},{28,20},{20,12},{12,4},{4,0},{1,9},{9... | collective-permute-start | bytes 3538952 | tf_op jit(solution)/shard_map/ppermute | solution.py:82
  163.2 34.0 %collective-permute-start.25 = (bf16[2048,128]{1,0:T(8,128)(2,1)S(1)}, bf16[2048,128]{1,0:T(8,128)(2,1)S(1)}, u32[]{:S(2)}, u32[]{:S(2)}) collective-permute-start(bf16[2048,128]{1,0:T(8,128)(2,1)S(1)} %get-tuple-element.257), channel_id=1, source_target_pairs={{0,4},{8,0},{24,16},{28,24},{20,28},{4,12},{1,5},{9,1},{25,17},{29... | collective-permute-start | bytes 1572872 | tf_op jit(solution)/shard_map/ppermute | solution.py:82
  167.3 34.2 %all-to-all-start = ((bf16[8,256,192]{1,2,0:T(8,128)(2,1)}), bf16[8,256,192]{1,2,0:T(8,128)(2,1)S(1)}, u32[]{:S(2)}, u32[]{:S(2)}) async-start(bf16[8,256,192]{1,2,0:T(8,128)(2,1)} %copy.139), calls=%async_computation | async-start | bytes 1572864 | tf_op jit(solution)/shard_map/all_to_all | solution.py:761
  179.8 43.9 %collective-permute-start.27 = (bf16[192,3072]{1,0:T(8,128)(2,1)}, bf16[192,3072]{1,0:T(8,128)(2,1)}, u32[]{:S(2)}, u32[]{:S(2)}) collective-permute-start(bf16[192,3072]{1,0:T(8,128)(2,1)} %collective-permute-done.15.refs_2_), channel_id=1, source_target_pairs={{0,4},{8,0},{16,8},{24,16},{28,24},{20,28},{12,20},{4,12},{1,5},{9... | collective-permute-start | bytes 3538952 | tf_op jit(solution)/shard_map/ppermute | solution.py:82
  189.5 37.1 %collective-permute-start.28 = (bf16[192,3072]{1,0:T(8,128)(2,1)}, bf16[192,3072]{1,0:T(8,128)(2,1)}, u32[]{:S(2)}, u32[]{:S(2)}) collective-permute-start(bf16[192,3072]{1,0:T(8,128)(2,1)} %collective-permute-done.16.refs_7_), channel_id=1, source_target_pairs={{0,8},{8,16},{16,24},{24,28},{28,20},{20,12},{12,4},{4,0},{1,9},{9... | collective-permute-start | bytes 3538952 | tf_op jit(solution)/shard_map/ppermute | solution.py:82
  189.5 45.7 %collective-permute-start.23 = (bf16[2048,128]{1,0:T(8,128)(2,1)S(1)}, bf16[2048,128]{1,0:T(8,128)(2,1)S(1)}, u32[]{:S(2)}, u32[]{:S(2)}) collective-permute-start(bf16[2048,128]{1,0:T(8,128)(2,1)S(1)} %get-tuple-element.256), channel_id=1, source_target_pairs={{0,8},{8,16},{16,24},{28,20},{20,12},{12,4},{1,9},{9,17},{17,25},{... | collective-permute-start | bytes 1572872 | tf_op jit(solution)/shard_map/ppermute | solution.py:82
  198.4 36.8 %collective-permute-start.26 = (bf16[2048,128]{1,0:T(8,128)(2,1)S(1)}, bf16[2048,128]{1,0:T(8,128)(2,1)S(1)}, u32[]{:S(2)}, u32[]{:S(2)}) collective-permute-start(bf16[2048,128]{1,0:T(8,128)(2,1)S(1)} %add_convert_fusion.11), channel_id=1, source_target_pairs={{0,4},{16,8},{24,16},{28,24},{12,20},{4,12},{1,5},{17,9},{25,17},{... | collective-permute-start | bytes 1572872 | tf_op jit(solution)/shard_map/ppermute | solution.py:82
  224.8 33.2 %collective-permute-start.29 = (bf16[96,3072]{1,0:T(8,128)(2,1)S(1)}, bf16[96,3072]{1,0:T(8,128)(2,1)}, u32[]{:S(2)}, u32[]{:S(2)}) collective-permute-start(bf16[96,3072]{1,0:T(8,128)(2,1)S(1)} %slice.351), channel_id=1, source_target_pairs={{0,4},{8,0},{16,8},{24,16},{28,24},{20,28},{12,20},{4,12},{1,5},{9... | collective-permute-start | bytes 1769480 | tf_op jit(solution)/shard_map/ppermute | solution.py:82
  227.7 30.3 %collective-permute-start.30 = (bf16[96,3072]{1,0:T(8,128)(2,1)S(1)}, bf16[96,3072]{1,0:T(8,128)(2,1)}, u32[]{:S(2)}, u32[]{:S(2)}) collective-permute-start(bf16[96,3072]{1,0:T(8,128)(2,1)S(1)} %slice.352), channel_id=1, source_target_pairs={{0,8},{8,16},{16,24},{24,28},{28,20},{20,12},{12,4},{4,0},{1,9},{9... | collective-permute-start | bytes 1769480 | tf_op jit(solution)/shard_map/ppermute | solution.py:82
  250.5 15.6 %all-to-all-start.2 = ((bf16[8,256,64]{1,2,0:T(8,128)(2,1)}), bf16[8,256,64]{1,2,0:T(8,128)(2,1)S(1)}, u32[]{:S(2)}, u32[]{:S(2)}) async-start(bf16[8,256,64]{1,2,0:T(8,128)(2,1)} %copy.143), calls=%async_computation.2 | async-start | bytes 524288 | tf_op jit(solution)/shard_map/all_to_all | solution.py:761
  275.9 11.2 %collective-permute-start.32 = (bf16[128,1536]{1,0:T(8,128)(2,1)S(1)}, bf16[128,1536]{1,0:T(8,128)(2,1)S(1)}, u32[]{:S(2)}, u32[]{:S(2)}) collective-permute-start(bf16[128,1536]{1,0:T(8,128)(2,1)S(1)} %add_convert_fusion.22), channel_id=1, source_target_pairs={{0,2},{2,0},{1,3},{3,1},{4,6},{6,4},{5,7},{7,5},{8,10},{10,8},{9,1... | collective-permute-start | bytes 1179656 | tf_op jit(solution)/shard_map/ppermute | solution.py:181
  315.6 11.5 %collective-permute-start.35 = (bf16[128,1536]{1,0:T(8,128)(2,1)S(1)}, bf16[128,1536]{1,0:T(8,128)(2,1)S(1)}, u32[]{:S(2)}, u32[]{:S(2)}) collective-permute-start(bf16[128,1536]{1,0:T(8,128)(2,1)S(1)} %add_convert_fusion.20), channel_id=1, source_target_pairs={{0,2},{2,0},{1,3},{3,1},{4,6},{6,4},{5,7},{7,5},{8,10},{10,8},{9,1... | collective-permute-start | bytes 1179656 | tf_op jit(solution)/shard_map/ppermute | solution.py:181
  319.6 17.6 %collective-permute-start.40 = (bf16[96,3072]{1,0:T(8,128)(2,1)}, bf16[96,3072]{1,0:T(8,128)(2,1)}, u32[]{:S(2)}, u32[]{:S(2)}) collective-permute-start(bf16[96,3072]{1,0:T(8,128)(2,1)} %get-tuple-element.291), channel_id=1, source_target_pairs={{0,8},{8,16},{16,24},{24,28},{28,20},{20,12},{12,4},{4,0},{1,9},{9... | collective-permute-start | bytes 1769480 | tf_op jit(solution)/shard_map/ppermute | solution.py:82
  319.6 17.6 %collective-permute-start.41 = (bf16[96,3072]{1,0:T(8,128)(2,1)}, bf16[96,3072]{1,0:T(8,128)(2,1)}, u32[]{:S(2)}, u32[]{:S(2)}) collective-permute-start(bf16[96,3072]{1,0:T(8,128)(2,1)} %get-tuple-element.290), channel_id=1, source_target_pairs={{0,4},{8,0},{16,8},{24,16},{28,24},{20,28},{12,20},{4,12},{1,5},{9... | collective-permute-start | bytes 1769480 | tf_op jit(solution)/shard_map/ppermute | solution.py:82
  339.6 37.1 %collective-permute-start.43 = (bf16[192,3072]{1,0:T(8,128)(2,1)}, bf16[192,3072]{1,0:T(8,128)(2,1)}, u32[]{:S(2)}, u32[]{:S(2)}) collective-permute-start(bf16[192,3072]{1,0:T(8,128)(2,1)} %pad_maximum_fusion.3), channel_id=1, source_target_pairs={{0,4},{8,0},{16,8},{24,16},{28,24},{20,28},{12,20},{4,12},{1,5},{9... | collective-permute-start | bytes 3538952 | tf_op jit(solution)/shard_map/ppermute | solution.py:82
  341.9 34.8 %collective-permute-start.42 = (bf16[192,3072]{1,0:T(8,128)(2,1)}, bf16[192,3072]{1,0:T(8,128)(2,1)}, u32[]{:S(2)}, u32[]{:S(2)}) collective-permute-start(bf16[192,3072]{1,0:T(8,128)(2,1)} %fusion.9), channel_id=1, source_target_pairs={{0,8},{8,16},{16,24},{24,28},{28,20},{20,12},{12,4},{4,0},{1,9},{9... | collective-permute-start | bytes 3538952 | tf_op jit(solution)/shard_map/ppermute | solution.py:82
  347.3 28.4 %all-to-all-start.3 = ((bf16[8,256,64]{1,2,0:T(8,128)(2,1)}), bf16[8,256,64]{1,2,0:T(8,128)(2,1)S(1)}, u32[]{:S(2)}, u32[]{:S(2)}) async-start(bf16[8,256,64]{1,2,0:T(8,128)(2,1)} %copy.148), calls=%async_computation.3 | async-start | bytes 524288 | tf_op jit(solution)/shard_map/all_to_all | solution.py:761
  351.8 46.5 %collective-permute-start.38 = (bf16[128,1536]{1,0:T(8,128)(2,1)S(1)}, bf16[128,1536]{1,0:T(8,128)(2,1)S(1)}, u32[]{:S(2)}, u32[]{:S(2)}) collective-permute-start(bf16[128,1536]{1,0:T(8,128)(2,1)S(1)} %add_convert_fusion.18), channel_id=1, source_target_pairs={{0,2},{2,0},{1,3},{3,1},{4,6},{6,4},{5,7},{7,5},{8,10},{10,8},{9,1... | collective-permute-start | bytes 1179656 | tf_op jit(solution)/shard_map/ppermute | solution.py:181
  379.5 77.5 %collective-permute-start.64 = (bf16[192,3072]{1,0:T(8,128)(2,1)}, bf16[192,3072]{1,0:T(8,128)(2,1)}, u32[]{:S(2)}, u32[]{:S(2)}) collective-permute-start(bf16[192,3072]{1,0:T(8,128)(2,1)} %add_convert_fusion.2), channel_id=1, source_target_pairs={{0,4},{8,0},{16,8},{24,16},{28,24},{20,28},{12,20},{4,12},{1,5},{9... | collective-permute-start | bytes 3538952 | tf_op jit(solution)/shard_map/ppermute | solution.py:82
  383.5 73.4 %collective-permute-start.63 = (bf16[192,3072]{1,0:T(8,128)(2,1)}, bf16[192,3072]{1,0:T(8,128)(2,1)}, u32[]{:S(2)}, u32[]{:S(2)}) collective-permute-start(bf16[192,3072]{1,0:T(8,128)(2,1)} %add_convert_fusion.3), channel_id=1, source_target_pairs={{0,8},{8,16},{16,24},{24,28},{28,20},{20,12},{12,4},{4,0},{1,9},{9... | collective-permute-start | bytes 3538952 | tf_op jit(solution)/shard_map/ppermute | solution.py:82
  396.2 27.8 %collective-permute-start.55 = (bf16[2048,128]{1,0:T(8,128)(2,1)}, bf16[2048,128]{1,0:T(8,128)(2,1)}, u32[]{:S(2)}, u32[]{:S(2)}) collective-permute-start(bf16[2048,128]{1,0:T(8,128)(2,1)} %get-tuple-element.133.refs_0_), channel_id=1, source_target_pairs={{0,4},{8,0},{16,8},{24,16},{28,24},{20,28},{12,20},{4,12},{1,5},{9... | collective-permute-start | bytes 1572872 | tf_op jit(solution)/shard_map/ppermute | solution.py:82
  397.6 28.5 %collective-permute-start.59 = (bf16[2048,128]{1,0:T(8,128)(2,1)}, bf16[2048,128]{1,0:T(8,128)(2,1)}, u32[]{:S(2)}, u32[]{:S(2)}) collective-permute-start(bf16[2048,128]{1,0:T(8,128)(2,1)} %get-tuple-element.133.refs_0_), channel_id=1, source_target_pairs={{0,8},{8,16},{16,24},{24,28},{28,20},{20,12},{12,4},{4,0},{1,9},{9... | collective-permute-start | bytes 1572872 | tf_op jit(solution)/shard_map/ppermute | solution.py:82
  398.4 30.6 %collective-permute-start.39 = (bf16[128,1536]{1,0:T(8,128)(2,1)S(1)}, bf16[128,1536]{1,0:T(8,128)(2,1)S(1)}, u32[]{:S(2)}, u32[]{:S(2)}) collective-permute-start(bf16[128,1536]{1,0:T(8,128)(2,1)S(1)} %add_convert_fusion.17.fm_ref), channel_id=1, source_target_pairs={{0,1},{1,0},{2,3},{3,2},{4,5},{5,4},{6,7},{7,6},{8,9},{9,8},{10,11... | collective-permute-start | bytes 1179656 | tf_op jit(solution)/shard_map/ppermute | solution.py:182
  420.0 41.8 %all-to-all-start.4 = ((bf16[8,256,192]{1,2,0:T(8,128)(2,1)}), bf16[8,256,192]{1,2,0:T(8,128)(2,1)S(1)}, u32[]{:S(2)}, u32[]{:S(2)}) async-start(bf16[8,256,192]{1,2,0:T(8,128)(2,1)} %copy.151), calls=%async_computation.4 | async-start | bytes 1572864 | tf_op jit(solution)/shard_map/all_to_all | solution.py:761
  424.0 27.0 %collective-permute-start.56 = (bf16[2048,128]{1,0:T(8,128)(2,1)}, bf16[2048,128]{1,0:T(8,128)(2,1)}, u32[]{:S(2)}, u32[]{:S(2)}) collective-permute-start(bf16[2048,128]{1,0:T(8,128)(2,1)} %collective-permute-done.55.refs_1_), channel_id=1, source_target_pairs={{0,4},{8,0},{16,8},{24,16},{28,24},{20,28},{12,20},{4,12},{1,5},{9... | collective-permute-start | bytes 1572872 | tf_op jit(solution)/shard_map/ppermute | solution.py:82
  426.1 25.0 %collective-permute-start.60 = (bf16[2048,128]{1,0:T(8,128)(2,1)}, bf16[2048,128]{1,0:T(8,128)(2,1)}, u32[]{:S(2)}, u32[]{:S(2)}) collective-permute-start(bf16[2048,128]{1,0:T(8,128)(2,1)} %collective-permute-done.59.refs_8_), channel_id=1, source_target_pairs={{0,8},{8,16},{16,24},{24,28},{28,20},{20,12},{12,4},{4,0},{1,9},{9... | collective-permute-start | bytes 1572872 | tf_op jit(solution)/shard_map/ppermute | solution.py:82
  451.1 27.7 %collective-permute-start.57 = (bf16[2048,128]{1,0:T(8,128)(2,1)}, bf16[2048,128]{1,0:T(8,128)(2,1)}, u32[]{:S(2)}, u32[]{:S(2)}) collective-permute-start(bf16[2048,128]{1,0:T(8,128)(2,1)} %collective-permute-done.56.refs_2_), channel_id=1, source_target_pairs={{0,4},{8,0},{16,8},{24,16},{28,24},{20,28},{12,20},{4,12},{1,5},{9... | collective-permute-start | bytes 1572872 | tf_op jit(solution)/shard_map/ppermute | solution.py:82
  451.1 28.8 %collective-permute-start.61 = (bf16[2048,128]{1,0:T(8,128)(2,1)}, bf16[2048,128]{1,0:T(8,128)(2,1)}, u32[]{:S(2)}, u32[]{:S(2)}) collective-permute-start(bf16[2048,128]{1,0:T(8,128)(2,1)} %collective-permute-done.60.refs_7_), channel_id=1, source_target_pairs={{0,8},{8,16},{16,24},{24,28},{28,20},{20,12},{12,4},{4,0},{1,9},{9... | collective-permute-start | bytes 1572872 | tf_op jit(solution)/shard_map/ppermute | solution.py:82
  459.7 92.4 %collective-permute-start.65 = (bf16[192,3072]{1,0:T(8,128)(2,1)}, bf16[192,3072]{1,0:T(8,128)(2,1)}, u32[]{:S(2)}, u32[]{:S(2)}) collective-permute-start(bf16[192,3072]{1,0:T(8,128)(2,1)} %add_convert_fusion.1), channel_id=1, source_target_pairs={{0,8},{8,16},{16,24},{24,28},{28,20},{20,12},{12,4},{4,0},{1,9},{9... | collective-permute-start | bytes 3538952 | tf_op jit(solution)/shard_map/ppermute | solution.py:82
  473.9 26.3 %collective-permute-start.47 = (bf16[96,1536]{1,0:T(8,128)(2,1)S(1)}, bf16[96,1536]{1,0:T(8,128)(2,1)S(1)}, u32[]{:S(2)}, u32[]{:S(2)}) collective-permute-start(bf16[96,1536]{1,0:T(8,128)(2,1)S(1)} %get-tuple-element.294), channel_id=1, source_target_pairs={{0,8},{8,16},{16,24},{24,28},{28,20},{20,12},{12,4},{4,0},{1,9},{9... | collective-permute-start | bytes 884744 | tf_op jit(solution)/shard_map/ppermute | solution.py:82
  476.7 75.4 %collective-permute-start.66 = (bf16[192,3072]{1,0:T(8,128)(2,1)}, bf16[192,3072]{1,0:T(8,128)(2,1)}, u32[]{:S(2)}, u32[]{:S(2)}) collective-permute-start(bf16[192,3072]{1,0:T(8,128)(2,1)} %add_convert_fusion), channel_id=1, source_target_pairs={{0,4},{8,0},{16,8},{24,16},{28,24},{20,28},{12,20},{4,12},{1,5},{9... | collective-permute-start | bytes 3538952 | tf_op jit(solution)/shard_map/ppermute | solution.py:82
  478.8 33.5 %collective-permute-start.44 = (bf16[128,1536]{1,0:T(8,128)(2,1)S(1)}, bf16[128,1536]{1,0:T(8,128)(2,1)S(1)}, u32[]{:S(2)}, u32[]{:S(2)}) collective-permute-start(bf16[128,1536]{1,0:T(8,128)(2,1)S(1)} %copy-done.100), channel_id=1, source_target_pairs={{0,1},{1,0},{2,3},{3,2},{4,5},{5,4},{6,7},{7,6},{8,9},{9,8},{10,11... | collective-permute-start | bytes 1179656 | tf_op jit(solution)/shard_map/ppermute | solution.py:180
  479.8 32.3 %collective-permute-start.51 = (bf16[96,1536]{1,0:T(8,128)(2,1)S(1)}, bf16[96,1536]{1,0:T(8,128)(2,1)S(1)}, u32[]{:S(2)}, u32[]{:S(2)}) collective-permute-start(bf16[96,1536]{1,0:T(8,128)(2,1)S(1)} %get-tuple-element.295), channel_id=1, source_target_pairs={{0,4},{8,0},{16,8},{24,16},{28,24},{20,28},{12,20},{4,12},{1,5},{9... | collective-permute-start | bytes 884744 | tf_op jit(solution)/shard_map/ppermute | solution.py:82
  500.2 15.1 %collective-permute-start.58 = (bf16[1024,128]{1,0:T(8,128)(2,1)S(1)}, bf16[1024,128]{1,0:T(8,128)(2,1)S(1)}, u32[]{:S(2)}, u32[]{:S(2)}) collective-permute-start(bf16[1024,128]{1,0:T(8,128)(2,1)S(1)} %slice.393), channel_id=1, source_target_pairs={{0,4},{8,0},{16,8},{24,16},{28,24},{20,28},{12,20},{4,12},{1,5},{9... | collective-permute-start | bytes 786440 | tf_op jit(solution)/shard_map/ppermute | solution.py:82
  512.4 22.5 %collective-permute-start.45 = (bf16[128,1536]{1,0:T(8,128)(2,1)S(1)}, bf16[128,1536]{1,0:T(8,128)(2,1)}, u32[]{:S(2)}, u32[]{:S(2)}) collective-permute-start(bf16[128,1536]{1,0:T(8,128)(2,1)S(1)} %add_convert_fusion.16), channel_id=1, source_target_pairs={{0,2},{2,0},{1,3},{3,1},{4,6},{6,4},{5,7},{7,5},{8,10},{10,8},{9,1... | collective-permute-start | bytes 1179656 | tf_op jit(solution)/shard_map/ppermute | solution.py:181
  515.3 20.8 %collective-permute-start.48 = (bf16[192,1536]{1,0:T(8,128)(2,1)}, bf16[192,1536]{1,0:T(8,128)(2,1)S(1)}, u32[]{:S(2)}, u32[]{:S(2)}) collective-permute-start(bf16[192,1536]{1,0:T(8,128)(2,1)} %fusion.21), channel_id=1, source_target_pairs={{0,8},{8,16},{16,24},{24,28},{28,20},{20,12},{12,4},{4,0},{1,9},{9... | collective-permute-start | bytes 1769480 | tf_op jit(solution)/shard_map/ppermute | solution.py:82
  521.4 15.8 %collective-permute-start.52 = (bf16[192,1536]{1,0:T(8,128)(2,1)S(1)}, bf16[192,1536]{1,0:T(8,128)(2,1)S(1)}, u32[]{:S(2)}, u32[]{:S(2)}) collective-permute-start(bf16[192,1536]{1,0:T(8,128)(2,1)S(1)} %pad_maximum_fusion.8), channel_id=1, source_target_pairs={{0,4},{8,0},{16,8},{24,16},{28,24},{20,28},{12,20},{4,12},{1,5},{9... | collective-permute-start | bytes 1769480 | tf_op jit(solution)/shard_map/ppermute | solution.py:82
  537.1 24.5 %collective-permute-start.49 = (bf16[192,1536]{1,0:T(8,128)(2,1)}, bf16[192,1536]{1,0:T(8,128)(2,1)}, u32[]{:S(2)}, u32[]{:S(2)}) collective-permute-start(bf16[192,1536]{1,0:T(8,128)(2,1)} %add_convert_fusion.7), channel_id=1, source_target_pairs={{0,8},{8,16},{16,24},{24,28},{28,20},{20,12},{12,4},{4,0},{1,9},{9... | collective-permute-start | bytes 1769480 | tf_op jit(solution)/shard_map/ppermute | solution.py:82
  538.1 26.7 %collective-permute-start.53 = (bf16[192,1536]{1,0:T(8,128)(2,1)}, bf16[192,1536]{1,0:T(8,128)(2,1)}, u32[]{:S(2)}, u32[]{:S(2)}) collective-permute-start(bf16[192,1536]{1,0:T(8,128)(2,1)} %add_convert_fusion.5), channel_id=1, source_target_pairs={{0,4},{8,0},{16,8},{24,16},{28,24},{20,28},{12,20},{4,12},{1,5},{9... | collective-permute-start | bytes 1769480 | tf_op jit(solution)/shard_map/ppermute | solution.py:82
  562.7 13.7 %collective-permute-start.50 = (bf16[192,1536]{1,0:T(8,128)(2,1)S(1)}, bf16[192,1536]{1,0:T(8,128)(2,1)}, u32[]{:S(2)}, u32[]{:S(2)}) collective-permute-start(bf16[192,1536]{1,0:T(8,128)(2,1)S(1)} %add_convert_fusion.6), channel_id=1, source_target_pairs={{0,8},{8,16},{16,24},{24,28},{28,20},{20,12},{12,4},{4,0},{1,9},{9... | collective-permute-start | bytes 1769480 | tf_op jit(solution)/shard_map/ppermute | solution.py:82
  566.0 14.0 %collective-permute-start.54 = (bf16[192,1536]{1,0:T(8,128)(2,1)S(1)}, bf16[192,1536]{1,0:T(8,128)(2,1)}, u32[]{:S(2)}, u32[]{:S(2)}) collective-permute-start(bf16[192,1536]{1,0:T(8,128)(2,1)S(1)} %add_convert_fusion.4), channel_id=1, source_target_pairs={{0,4},{8,0},{16,8},{24,16},{28,24},{20,28},{12,20},{4,12},{1,5},{9... | collective-permute-start | bytes 1769480 | tf_op jit(solution)/shard_map/ppermute | solution.py:82
  570.0 17.1 %collective-permute-start.75 = (bf16[48,384]{1,0:T(8,128)(2,1)}, bf16[48,384]{1,0:T(8,128)(2,1)}, u32[]{:S(2)}, u32[]{:S(2)}) collective-permute-start(bf16[48,384]{1,0:T(8,128)(2,1)} %slice.481), channel_id=1, source_target_pairs={{0,1},{1,0},{2,3},{3,2},{4,5},{5,4},{6,7},{7,6},{8,9},{9,8},{10,11... | collective-permute-start | bytes 110600 | tf_op jit(solution)/shard_map/ppermute | solution.py:174
  (124 other events, 896.3 us)

commit v4 on v3

--- a/solution.py
+++ b/solution.py
@@ -175,9 +175,10 @@
     return join(tp >= 2, pair, lax.ppermute(pair, "tp", Y_SWAP))
 
 
-def psum_tp(halves):
+def psum_tp(halves, held=()):
     mine, other = halves
     mine = (mine.astype(f32) + lax.ppermute(other, "tp", CORE_SWAP).astype(f32)).astype(bf16)
+    mine = once(mine, *held)
     mine = (mine.astype(f32) + lax.ppermute(mine, "tp", Y_SWAP).astype(f32)).astype(bf16)
     return (mine, lax.ppermute(mine, "tp", CORE_SWAP))
 
@@ -824,10 +825,34 @@
 
     cap_own = once(exchange(cap_own), *hop(attn_chunks, 1))
     caption_cols = gather_tp(cap_own.reshape(text_rows, cap_part), 1)
+    if ring.ring:
+        text_slabs = call(
+            text_heads_kernel, "text_heads", 1, [slab_head],
+            [(text_weight, whole(text_weight.shape))],
+            [((cap_cols, seq_size * 2 * HD), bf16, whole((cap_cols, seq_size * 2 * HD)))],
+            [pltpu.VMEM((heads, cap_cols, 2 * HD), bf16)],
+            moved=text_weight.size * 6,
+        )[0]
+        text_parts = dot(caption_cols, text_slabs, ((1,), (0,))).astype(bf16)
+
+        text_sum = ring.reduce(
+            lambda k: text_parts[:, 2 * k * HD : 2 * (k + 1) * HD], owners
+        )
+        next(text_sum)
+    else:
+        parts = jnp.einsum(
+            "rc,jchd->hrjd", caption_cols,
+            text_weight.astype(bf16).reshape(2, cap_cols, heads, HD), preferred_element_type=f32,
+        ).reshape(heads, text_rows, 2 * HD)
+        after = seq_size - heads - first_owner
+        parts = jnp.pad(parts.astype(bf16), ((first_owner, after), (0, 0), (0, 0)))
+        text_kv = lax.psum_scatter(parts, "seq", scatter_dimension=0, tiled=False)
+
     ffn_shard = jnp.concatenate([turned(updown_weight), down_weight.astype(bf16).T], axis=1)
-    ffn_chunks = ring.gather(once(ffn_shard, packed))
+    ffn_chunks = ring.gather(once(ffn_shard, packed, *([text_parts] if ring.ring else [])))
     ffn_ins = [(chunk, anywhere()) for chunk in ffn_chunks]
-    modulation = once(modulation, *hop(attn_chunks, 3), *hop(ffn_chunks, 1))
+    text_sent = text_sum.send(()) if ring.ring else ()
+    modulation = once(modulation, *hop(attn_chunks, 3), *hop(ffn_chunks, 1), *text_sent)
     segment_col = segment_ids[:, None]
     steps = here // ROWS
     segment_row = segment_ids.reshape(steps, 1, ROWS)
@@ -863,33 +888,7 @@
         [pltpu.VMEM((width, qkv_width), bf16), piece_sems],
         moved=width * qkv_width * 2, flops=2 * here * width * qkv_width,
     )[0]
-    if ring.ring:
-        text_slabs = call(
-            text_heads_kernel, "text_heads", 1, [slab_head],
-            [(text_weight, whole(text_weight.shape))],
-            [((cap_cols, seq_size * 2 * HD), bf16, whole((cap_cols, seq_size * 2 * HD)))],
-            [pltpu.VMEM((heads, cap_cols, 2 * HD), bf16)],
-            moved=text_weight.size * 6,
-        )[0]
-        text_parts = dot(caption_cols, text_slabs, ((1,), (0,))).astype(bf16)
-
-        text_sum = ring.reduce(
-            lambda k: text_parts[:, 2 * k * HD : 2 * (k + 1) * HD], owners
-        )
-        next(text_sum)
-        for held in ((slabs,), (), (), ()):
-            text_kv = text_sum.send(held)
-        text_kv = text_kv.astype(bf16)
-    else:
-        parts = jnp.einsum(
-            "rc,jchd->hrjd", caption_cols,
-            text_weight.astype(bf16).reshape(2, cap_cols, heads, HD), preferred_element_type=f32,
-        ).reshape(heads, text_rows, 2 * HD)
-        after = seq_size - heads - first_owner
-        parts = jnp.pad(parts.astype(bf16), ((first_owner, after), (0, 0), (0, 0)))
-        text_kv = lax.psum_scatter(parts, "seq", scatter_dimension=0, tiled=False)
-
-    qkv_head = once(exchange(slabs), *hop(ffn_chunks, 2)).reshape(count, 3 * HD)
+    qkv_head = exchange(slabs).reshape(count, 3 * HD)
 
     block_q = math.gcd(count, 512)
     block_k = math.gcd(count, 512)
@@ -910,6 +909,11 @@
         [pltpu.VMEM((count, HD), bf16), pltpu.VMEM((HD, count), bf16)],
         flops=4 * area, moved=count * HD * 20, exps=count * count,
     )
+    self_out = once(self_out, *hop(ffn_chunks, 2))
+    if ring.ring:
+        for held in ((slabs,), (qkv_head,), ()):
+            text_kv = text_sum.send(held)
+        text_kv = text_kv.astype(bf16)
     mixed_head, text_out, text_stat = call(
         text_kernel, "attend_text", blocks, [table, my_gate],
         q_ins

time: 644 us -> 621 us (0.964)
  waiting for transfers between devices: 207 us -> 172 us
  blocking collectives: 0 us -> 14.7 us
    ppermute x48, waiting for transfers between devices: 121 us -> 89 us  [hop(): return lax.ppermute(value, 'seq', pairs)]
    all_to_all x0 -> x1, blocking collectives: none -> 14.7 us  [exchange(): return lax.all_to_all(slabs, 'seq', 0, 0, tiled=True)]
    ppermute x48, starting transfers between devices: 69.5 us -> 76.4 us  [hop(): return lax.ppermute(value, 'seq', pairs)]
    all_to_all x5 -> x4, starting transfers between devices: 25.4 us -> 18.9 us  [exchange(): return lax.all_to_all(slabs, 'seq', 0, 0, tiled=True)]
    convert_element_type x16 -> x15, other arithmetic: 23 us -> 21.9 us  [plus(): return (part.astype(f32) + moved.astype(f32)).astype(bf16)]
    all_to_all x5 -> x4, waiting for transfers between devices: 36.9 us -> 37.3 us  [exchange(): return lax.all_to_all(slabs, 'seq', 0, 0, tiled=True)]
  transfers between devices with their start and end apart: 82 -> 81, of which waited for: 32 -> 31; matrix products, arithmetic and copies ran while one was open for 17% -> 17% of each run, Pallas kernels for 21% -> 21%
where the time goes in v4:
time: 621 us; the launch traced here: 609 us
  waiting for transfers between devices  172 us (28%)
  Pallas kernels  154 us (25%)
  starting transfers between devices  115 us (19%)
  other arithmetic  81.2 us (13%)
  local copies, waits for them, and re-layouts  43.2 us (7%)
  matrix products  18.8 us (3%)
  blocking collectives  14.7 us (2%)
  between operations  9.9 us (2%)
    pallas_call x16, Pallas kernels, call(): pl.pallas_call(kernel, out_shape=tuple((shape_of(shape, dtype) for shape,...  154 us
    ppermute x48, waiting for transfers between devices, hop(): return lax.ppermute(value, 'seq', pairs)  89 us
    ppermute x48, starting transfers between devices, hop(): return lax.ppermute(value, 'seq', pairs)  76.4 us
    all_to_all x4, waiting for transfers between devices, exchange(): return lax.all_to_all(slabs, 'seq', 0, 0, tiled=True)  37.3 us
    ppermute x11, waiting for transfers between devices, butterfly(): lax.ppermute(value, axis, [(i, i ^ step) for i in range(size)])  23 us
    convert_element_type x15, other arithmetic, plus(): return (part.astype(f32) + moved.astype(f32)).astype(bf16)  21.9 us
    all_to_all x4, starting transfers between devices, exchange(): return lax.all_to_all(slabs, 'seq', 0, 0, tiled=True)  18.9 us
    dot_general x7, matrix products, dot(): return lax.dot_general(a, b, (dims, ((), ())), preferred_element_type=f32)  18.8 us
  transfers between devices with their start and end apart: 81, of which 31 were waited for; matrix products, arithmetic and copies ran while one was open for 17% of the time, Pallas kernels for 21%

profile of v4, /device:TPU:0, one launch (start us, length us, event | category | flops | bytes accessed | tf_op | source)
XLA Modules:
  0.0 609.3 jit_solution(14044781965120160353)
XLA Ops:
  2.1 3.0 collective-permute-start.5
  5.8 5.5 caption_slabs.1
  11.4 6.2 %all-to-all-start = ((bf16[8,256,128]{2,1,0:T(8,128)(2,1)}), bf16[8,256,128]{2,1,0:T(8,128)(2,1)}, u32[]{:S(2)}, u32[]{:S(2)}) async-start(bf16[8,256,128]{2,1,0:T(8,128)(2,1)} %caption_slabs.1), calls=%async_computation | async-start | bytes 1048576 | tf_op jit(solution)/shard_map/all_to_all | solution.py:762
  18.9 5.2 modulation.1
  24.1 7.5 %all-to-all-done = bf16[8,256,128]{2,1,0:T(8,128)(2,1)} async-done(((bf16[8,256,128]{2,1,0:T(8,128)(2,1)}), bf16[8,256,128]{2,1,0:T(8,128)(2,1)}, u32[]{:S(2)}, u32[]{:S(2)}) %all-to-all-start) | async-done | bytes 524320 | tf_op jit(solution)/shard_map/all_to_all | solution.py:762
  37.1 2.6 collective-permute-done
  50.6 2.7 collective-permute-done.2
  55.5 3.8 text_heads.1
  65.5 4.7 collective-permute-done.12
  72.0 2.4 convolution_convert_fusion.3
  77.5 4.0 collective-permute-start.13
  88.6 2.5 collective-permute-start.20
  92.0 21.1 %collective-permute-done.13.refs_1_ = bf16[192,3072]{1,0:T(8,128)(2,1)} collective-permute-done((bf16[192,3072]{1,0:T(8,128)(2,1)S(1)}, bf16[192,3072]{1,0:T(8,128)(2,1)}, u32[]{:S(2)}, u32[]{:S(2)}) %collective-permute-start.13) | collective-permute-done | bytes 1179680 | tf_op jit(solution)/shard_map/ppermute | solution.py:82
  113.0 3.9 collective-permute-start.19
  117.7 7.3 %enter.1 = (bf16[256,1536]{1,0:T(8,128)(2,1)}, bf16[256,1536]{1,0:T(8,128)(2,1)}, f32[48,1536]{1,0:T(8,128)}, f32[8,1536]{1,0:T(8,128)}, bf16[256,1536]{1,0:T(8,128)(2,1)}) custom-call(s32[3]{0:T(128)} %pad_add_fusion.1.scal, bf16[256,1536]{1,0:T(8,128)(2,1)} %x_ref.1, bf16[256,1536]{1,0:T(8,128)(2,1)} %g_ref.1, f32[48,1536]{1,0:T(8,128)} %pad_maximum_fusion.13.mod_ref, ...), custom_call_target="tpu_custom_call" | custom-call | bytes 3932160 | tf_op jit(solution)/shard_map/enter/pallas_call | solution.py:215
  127.7 5.6 project.1
  135.6 5.2 all-to-all-start.1
  142.5 3.9 collective-permute-start.21
  149.9 9.1 %collective-permute-done.25.refs_2_ = bf16[192,3072]{1,0:T(8,128)(2,1)} collective-permute-done((bf16[192,3072]{1,0:T(8,128)(2,1)}, bf16[192,3072]{1,0:T(8,128)(2,1)}, u32[]{:S(2)}, u32[]{:S(2)}) %collective-permute-start.25) | collective-permute-done | bytes 1179680 | tf_op jit(solution)/shard_map/ppermute | solution.py:82
  159.0 6.2 %collective-permute-start.28 = (bf16[192,3072]{1,0:T(8,128)(2,1)}, bf16[192,3072]{1,0:T(8,128)(2,1)}, u32[]{:S(2)}, u32[]{:S(2)}) collective-permute-start(bf16[192,3072]{1,0:T(8,128)(2,1)} %collective-permute-done.26.refs_7_), channel_id=1, source_target_pairs={{0,8},{8,16},{16,24},{24,28},{28,20},{20,12},{12,4},{4,0},{1,9},{9... | collective-permute-start | bytes 3538952 | tf_op jit(solution)/shard_map/ppermute | solution.py:82
  166.6 7.5 %all-to-all-done.1 = bf16[8,256,192]{1,2,0:T(8,128)(2,1)S(1)} async-done(((bf16[8,256,192]{1,2,0:T(8,128)(2,1)}), bf16[8,256,192]{1,2,0:T(8,128)(2,1)S(1)}, u32[]{:S(2)}, u32[]{:S(2)}) %all-to-all-start.1) | async-done | bytes 786464 | tf_op jit(solution)/shard_map/all_to_all | solution.py:762
  179.6 2.3 add_convert_fusion.12
  181.9 4.0 collective-permute-start.23
  188.1 14.4 %attend.1 = (f32[64,2048]{1,0:T(8,128)}, f32[1,2048]{1,0:T(1,128)}) custom-call(s32[4,4]{1,0:T(4,128)} %pad_add_fusion.table, bf16[2048,192]{1,0:T(8,128)(2,1)} %bitcast.137, bf16[2048,192]{1,0:T(8,128)(2,1)} %bitcast.138, s32[1,2048]{1,0:T(1,128)} %bitcast.154, s32[2048,1]{1,0:T(8,128)} %copy.142.sk_ref), custom_call_target="tpu_custom_call" | custom-call | flops 1073741824 | bytes 2621440 | tf_op jit(solution)/shard_map/attend/pallas_call | solution.py:215
  203.7 4.2 collective-permute-start.29
  209.0 5.1 collective-permute-done.23
  216.2 11.3 %attend_text.1 = (bf16[2048,64]{1,0:T(8,128)(2,1)}, f32[64,2048]{1,0:T(8,128)}, f32[1,2048]{1,0:T(1,128)}) custom-call(s32[4,4]{1,0:T(4,128)} %pad_add_fusion.table, f32[1]{0:T(128)} %bitcast.14.gate, bf16[2048,192]{1,0:T(8,128)(2,1)} %bitcast.139, bf16[2048,128]{1,0:T(8,128)(2,1)} %add_convert_fusion.10.kv_ref, f32[64,2048]{1,0:T(8,128)} %get-tuple-element.97.self_ref, ...), custom_call_target="tpu_custom_call" | custom-call | flops 134217728 | bytes 2621440 | tf_op jit(solution)/shard_map/attend_text/pallas_call | solution.py:215
  228.7 14.7 %all_to_all.25 = bf16[8,256,64]{1,2,0:T(8,128)(2,1)S(1)} all-to-all(bf16[8,256,64]{1,2,0:T(8,128)(2,1)S(1)} %copy.143), channel_id=1, replica_groups=mesh['seq'=8,'tp'=4] {'seq'}, dimensions={0} | all-to-all | bytes 524288 | tf_op jit(solution)/shard_map/all_to_all | solution.py:762
  244.5 5.7 out.1
  254.9 9.6 %collective-permute-done.32 = bf16[128,1536]{1,0:T(8,128)(2,1)S(1)} collective-permute-done((bf16[128,1536]{1,0:T(8,128)(2,1)S(1)}, bf16[128,1536]{1,0:T(8,128)(2,1)S(1)}, u32[]{:S(2)}, u32[]{:S(2)}) %collective-permute-start.32) | collective-permute-done | bytes 393248 | tf_op jit(solution)/shard_map/ppermute | solution.py:182
  267.1 19.0 %ffn.1 = (f32[256,1536]{1,0:T(8,128)}, bf16[256,1536]{1,0:T(8,128)(2,1)}, bf16[256,1536]{1,0:T(8,128)(2,1)}, bf16[256,1024]{1,0:T(8,128)(2,1)}, bf16[256,2048]{1...) custom-call(s32[3]{0:T(128)} %pad_add_fusion.1.scal, ...), custom_call_target="tpu_custom_call" | custom-call | flops 4831838208 | bytes 9437184 | tf_op jit(solution)/shard_map/ffn/pallas_call | solution.py:215
  286.3 3.3 convolution_convert_fusion
  299.2 5.2 collective-permute-done.35
  306.7 7.8 %mid.1 = (f32[256,1536]{1,0:T(8,128)}, bf16[256,1536]{1,0:T(8,128)(2,1)}, bf16[8,256,64]{2,1,0:T(8,128)(2,1)}) custom-call(s32[3]{0:T(128)} %pad_add_fusion.1.scal, f32[256,1536]{1,0:T(8,128)} %get-tuple-element.105.mid_ref, bf16[256,1536]{1,0:T(8,128)(2,1)} %get-tuple-element.90.g_ref, bf16[128,1536]{1,0:T(8,128)(2,1)} %copy-done.19, ...), custom_call_target="tpu_custom_call" | custom-call | flops 301989888 | bytes 1179648 | tf_op jit(solution)/shard_map/mid/pallas_call | solution.py:215
  324.6 3.4 all-to-all-start.3
  330.7 22.3 %all-to-all-done.3 = bf16[8,256,64]{1,2,0:T(8,128)(2,1)S(1)} async-done(((bf16[8,256,64]{1,2,0:T(8,128)(2,1)}), bf16[8,256,64]{1,2,0:T(8,128)(2,1)S(1)}, u32[]{:S(2)}, u32[]{:S(2)}) %all-to-all-start.3) | async-done | bytes 262176 | tf_op jit(solution)/shard_map/all_to_all | solution.py:762
  354.1 2.8 add_convert_fusion.2
  358.2 2.7 add_convert_fusion.3
  361.6 12.0 %attend_text_back.1 = (bf16[2048,128]{1,0:T(8,128)(2,1)}, f32[64,2048]{1,0:T(8,128)}, f32[1,2048]{1,0:T(1,128)}) custom-call(s32[4,4]{1,0:T(4,128)} %pad_add_fusion.table, f32[1]{0:T(128)} %bitcast.14.gate, bf16[2048,192]{1,0:T(8,128)(2,1)} %bitcast.140, bf16[2048,64]{1,0:T(8,128)(2,1)} %bitcast.148, bf16[2048,128]{1,0:T(8,128)(2,1)} %add_convert_fusion.10.kv_ref, ...), custom_call_target="tpu_custom_call" | custom-call | flops 335544320 | bytes 2621440 | tf_op jit(solution)/shard_map/attend_text_back/pallas_call | solution.py:215
  375.8 19.2 %attend_back.1 = bf16[2048,192]{1,0:T(8,128)(2,1)} custom-call(s32[4,4]{1,0:T(4,128)} %pad_add_fusion.table, bf16[2048,192]{1,0:T(8,128)(2,1)} %bitcast.141, bf16[2048,64]{1,0:T(8,128)(2,1)} %bitcast.149, bf16[2048,192]{1,0:T(8,128)(2,1)} %bitcast.142, f32[64,2048]{1,0:T(8,128)} %get-tuple-element.97.self_ref, f32[1,2048]{1,0:T(1,128)} %get-tuple-element.124.stat_ref, ...), custom_call_target="tpu_custom_call" | custom-call | flops 2684354560 | bytes 2621440 | tf_op jit(solution)/shard_map/attend_back/pallas_call | solution.py:215
  395.0 2.3 copy.151
  397.3 4.0 all-to-all-start.4
  407.1 12.5 %side.1 = (f32[256,1536]{1,0:T(8,128)}, f32[32,1536]{1,0:T(8,128)}, f32[8,1536]{1,0:T(8,128)}) custom-call(s32[3]{0:T(128)} %pad_add_fusion.1.scal, f32[256,1536]{1,0:T(8,128)} %get-tuple-element.105.mid_ref, f32[256,1536]{1,0:T(8,128)} %get-tuple-element.108.grad_ref, bf16[256,1536]{1,0:T(8,128)(2,1)} %get-tuple-element.90.g_ref, ...), custom_call_target="tpu_custom_call" | custom-call | bytes 9437184 | tf_op jit(solution)/shard_map/side/pallas_call | solution.py:215
  419.6 8.9 %collective-permute-done.56.refs_2_ = bf16[2048,128]{1,0:T(8,128)(2,1)} collective-permute-done((bf16[2048,128]{1,0:T(8,128)(2,1)}, bf16[2048,128]{1,0:T(8,128)(2,1)}, u32[]{:S(2)}, u32[]{:S(2)}) %collective-permute-start.56) | collective-permute-done | bytes 524320 | tf_op jit(solution)/shard_map/ppermute | solution.py:82
  428.4 5.9 collective-permute-start.61
  434.4 2.7 add_convert_fusion.1
  440.4 7.3 %qkv_back.1 = (bf16[256,1152]{1,0:T(8,128)(2,1)}, bf16[128,1536]{1,0:T(8,128)(2,1)}, bf16[128,1536]{1,0:T(8,128)(2,1)}) custom-call(s32[3]{0:T(128)} %pad_add_fusion.1.scal, bf16[8,256,192]{2,1,0:T(8,128)(2,1)} %copy.152.slab_ref, bf16[192,1536]{1,0:T(8,128)(2,1)} %copy-done, bf16[192,1536]{1,0:T(8,128)(2,1)} %copy-done.4, bf16[192,1536]{1,0:T(8,128)(2,1)} %copy-done.7, ...), custom_call_target="tpu_custom_call" | custom-call | flops 905969664 | bytes 3538944 | tf_op jit(solution)/shard_map/qkv_back/pallas_call | solution.py:215
  447.7 2.3 convolution_convert_fusion.1
  451.3 2.7 add_convert_fusion
  458.2 19.4 %collective-permute-done.47 = bf16[96,1536]{1,0:T(8,128)(2,1)S(1)} collective-permute-done((bf16[96,1536]{1,0:T(8,128)(2,1)S(1)}, bf16[96,1536]{1,0:T(8,128)(2,1)S(1)}, u32[]{:S(2)}, u32[]{:S(2)}) %collective-permute-start.47) | collective-permute-done | bytes 294944 | tf_op jit(solution)/shard_map/ppermute | solution.py:82
  477.6 2.5 collective-permute-start.58
  481.0 8.5 %collective-permute-done.51 = bf16[96,1536]{1,0:T(8,128)(2,1)S(1)} collective-permute-done((bf16[96,1536]{1,0:T(8,128)(2,1)S(1)}, bf16[96,1536]{1,0:T(8,128)(2,1)S(1)}, u32[]{:S(2)}, u32[]{:S(2)}) %collective-permute-start.51) | collective-permute-done | bytes 294944 | tf_op jit(solution)/shard_map/ppermute | solution.py:82
  493.6 5.1 collective-permute-done.62.refs_5_
  500.6 9.1 %text_grad.1 = f32[2,512,384]{2,1,0:T(8,128)} custom-call(s32[6]{0:T(128)} %get-tuple-element.136.slab_at, bf16[512,2048]{1,0:T(8,128)(2,1)} %fusion.7.cap_ref, bf16[2048,128]{1,0:T(8,128)(2,1)} %get-tuple-element.137.refs_0_, bf16[2048,128]{1,0:T(8,128)(2,1)} %collective-permute-done.55.refs_1_, bf16[2048,128]{1,0:T(8,128)(2,1)} %collective-permute-done.56.refs_2_, ...), custom_call_target="tpu_custom_call" | custom-call | flops 1610612736 | bytes 4194304 | tf_op jit(solution)/shard_map/text_grad/pallas_call | solution.py:215
  509.7 2.5 multiply_reduce_fusion.1
  518.1 8.7 %leave.1 = (f32[256,1536]{1,0:T(8,128)}, f32[48,384]{1,0:T(8,128)}, f32[8,1536]{1,0:T(8,128)}) custom-call(s32[3]{0:T(128)} %pad_add_fusion.1.scal, bf16[256,1536]{1,0:T(8,128)(2,1)} %get-tuple-element.89.x_ref, f32[256,1536]{1,0:T(8,128)} %get-tuple-element.108.grad_ref, bf16[128,1536]{1,0:T(8,128)(2,1)} %copy-done.39, bf16[128,1536]{1,0:T(8,128)(2,1)} %copy-done.63, ...), custom_call_target="tpu_custom_call" | custom-call | bytes 6291456 | tf_op jit(solution)/shard_map/leave/pallas_call | solution.py:215
  534.8 3.4 collective-permute-done.68
  553.7 3.7 collective-permute-done.54
  569.3 3.6 collective-permute-done.72
  573.3 3.1 collective-permute-done.73
  577.6 3.3 collective-permute-done.74
  587.3 3.0 multiply_subtract_fusion.2
  593.0 3.1 multiply_subtract_fusion.1
  600.4 7.3 %multiply_subtract_fusion = (f32[128,9216]{1,0:T(8,128)}, f32[128,9216]{1,0:T(8,128)}, f32[128,9216]{1,0:T(8,128)}) fusion(f32[128,9216]{1,0:T(8,128)S(1)} %bitcast.145, f32[128,9216]{1,0:T(8,128)S(1)} %bitcast.163, f32[128,9216]{1,0:T(8,128)S(1)} %copy-done.98, f32[]{:T(128)S(6)} %min.18, bf16[8,128]{1,0:T(8,128)(2,1)S(1)} %copy-done.85, ...), kind=kOutput, calls=%fused_computation.5 | convolution fusion | flops 37748736 | bytes 28461060 | tf_op jit(solution)/shard_map/dot_general | solution.py:71
  (491 shorter events, 175.5 us)
Async XLA Ops:
  2.1 22.0 %collective-permute-start.5 = (bf16[192,1536]{1,0:T(8,128)(2,1)S(1)}, bf16[192,1536]{1,0:T(8,128)(2,1)S(1)}, u32[]{:S(2)}, u32[]{:S(2)}) collective-permute-start(bf16[192,1536]{1,0:T(8,128)(2,1)S(1)} %pad_maximum_fusion.7.refs_0_), channel_id=1, source_target_pairs={{0,4},{8,0},{16,8},{24,16},{28,24},{20,28},{12,20},{4,12},{1,5},{9... | collective-permute-start | bytes 1769480 | tf_op jit(solution)/shard_map/ppermute | solution.py:82
  5.1 19.0 %collective-permute-start.8 = (bf16[192,1536]{1,0:T(8,128)(2,1)S(1)}, bf16[192,1536]{1,0:T(8,128)(2,1)S(1)}, u32[]{:S(2)}, u32[]{:S(2)}) collective-permute-start(bf16[192,1536]{1,0:T(8,128)(2,1)S(1)} %pad_maximum_fusion.7.refs_0_), channel_id=1, source_target_pairs={{0,8},{8,16},{16,24},{24,28},{28,20},{20,12},{12,4},{4,0},{1,9},{9... | collective-permute-start | bytes 1769480 | tf_op jit(solution)/shard_map/ppermute | solution.py:82
  11.4 20.3 %all-to-all-start = ((bf16[8,256,128]{2,1,0:T(8,128)(2,1)}), bf16[8,256,128]{2,1,0:T(8,128)(2,1)}, u32[]{:S(2)}, u32[]{:S(2)}) async-start(bf16[8,256,128]{2,1,0:T(8,128)(2,1)} %caption_slabs.1), calls=%async_computation | async-start | bytes 1048576 | tf_op jit(solution)/shard_map/all_to_all | solution.py:762
  32.9 8.7 %collective-permute-start.11 = (bf16[2048,128]{0,1:T(8,128)(2,1)S(1)}, bf16[2048,128]{0,1:T(8,128)(2,1)}, u32[]{:S(2)}, u32[]{:S(2)}) collective-permute-start(bf16[2048,128]{0,1:T(8,128)(2,1)S(1)} %copy.156), channel_id=1, source_target_pairs={{0,1},{1,0},{2,3},{3,2},{4,5},{5,4},{6,7},{7,6},{8,9},{9,8},{10,11... | collective-permute-start | bytes 1572872 | tf_op jit(solution)/shard_map/ppermute | solution.py:174
  43.8 26.4 %collective-permute-start.12 = (bf16[2048,256]{0,1:T(8,128)(2,1)}, bf16[2048,256]{0,1:T(8,128)(2,1)}, u32[]{:S(2)}, u32[]{:S(2)}) collective-permute-start(bf16[2048,256]{0,1:T(8,128)(2,1)} %pad_maximum_fusion.4), channel_id=1, source_target_pairs={{0,2},{2,0},{1,3},{3,1},{4,6},{6,4},{5,7},{7,5},{8,10},{10,8},{9,1... | collective-permute-start | bytes 3145736 | tf_op jit(solution)/shard_map/ppermute | solution.py:175
  45.5 7.9 %collective-permute-start.2 = (f32[64,384]{1,0:T(8,128)S(1)}, f32[64,384]{1,0:T(8,128)}, u32[]{:S(2)}, u32[]{:S(2)}) collective-permute-start(f32[64,384]{1,0:T(8,128)S(1)} %add.372), channel_id=1, source_target_pairs={{0,16},{4,20},{8,24},{12,28},{16,0},{20,4},{24,8},{28,12},{1,17},{... | collective-permute-start | bytes 294920 | tf_op jit(solution)/shard_map/ppermute | solution.py:161
  46.7 16.8 %collective-permute-start.9 = (bf16[192,1536]{1,0:T(8,128)(2,1)S(1)}, bf16[192,1536]{1,0:T(8,128)(2,1)S(1)}, u32[]{:S(2)}, u32[]{:S(2)}) collective-permute-start(bf16[192,1536]{1,0:T(8,128)(2,1)S(1)} %collective-permute-done.8.refs_8_), channel_id=1, source_target_pairs={{0,8},{8,16},{16,24},{24,28},{28,20},{20,12},{12,4},{4,0},{1,9},{9... | collective-permute-start | bytes 1769480 | tf_op jit(solution)/shard_map/ppermute | solution.py:82
  47.5 16.0 %collective-permute-start.6 = (bf16[192,1536]{1,0:T(8,128)(2,1)S(1)}, bf16[192,1536]{1,0:T(8,128)(2,1)S(1)}, u32[]{:S(2)}, u32[]{:S(2)}) collective-permute-start(bf16[192,1536]{1,0:T(8,128)(2,1)S(1)} %collective-permute-done.5.refs_1_), channel_id=1, source_target_pairs={{0,4},{8,0},{16,8},{24,16},{28,24},{20,28},{12,20},{4,12},{1,5},{9... | collective-permute-start | bytes 1769480 | tf_op jit(solution)/shard_map/ppermute | solution.py:82
  62.2 15.3 %collective-permute-start.4 = (f32[48,768]{1,0:T(8,128)S(1)}, f32[48,768]{1,0:T(8,128)S(1)}, u32[]{:S(2)}, u32[]{:S(2)}) collective-permute-start(f32[48,768]{1,0:T(8,128)S(1)} %pad_maximum_fusion.14), channel_id=1, source_target_pairs={{0,2},{2,0},{1,3},{3,1},{4,6},{6,4},{5,7},{7,5},{8,10},{10,8},{9,1... | collective-permute-start | bytes 442376 | tf_op jit(solution)/shard_map/ppermute | solution.py:175
  63.5 18.8 %collective-permute-start.10 = (bf16[192,1536]{1,0:T(8,128)(2,1)S(1)}, bf16[192,1536]{1,0:T(8,128)(2,1)S(1)}, u32[]{:S(2)}, u32[]{:S(2)}) collective-permute-start(bf16[192,1536]{1,0:T(8,128)(2,1)S(1)} %collective-permute-done.9.refs_7_), channel_id=1, source_target_pairs={{0,8},{8,16},{16,24},{24,28},{28,20},{20,12},{12,4},{4,0},{1,9},{9... | collective-permute-start | bytes 1769480 | tf_op jit(solution)/shard_map/ppermute | solution.py:82
  63.5 18.7 %collective-permute-start.7 = (bf16[192,1536]{1,0:T(8,128)(2,1)S(1)}, bf16[192,1536]{1,0:T(8,128)(2,1)S(1)}, u32[]{:S(2)}, u32[]{:S(2)}) collective-permute-start(bf16[192,1536]{1,0:T(8,128)(2,1)S(1)} %collective-permute-done.6.refs_2_), channel_id=1, source_target_pairs={{0,4},{8,0},{16,8},{24,16},{28,24},{20,28},{12,20},{4,12},{1,5},{9... | collective-permute-start | bytes 1769480 | tf_op jit(solution)/shard_map/ppermute | solution.py:82
  74.6 11.4 %collective-permute-start.15 = (bf16[1024,128]{1,0:T(8,128)(2,1)S(1)}, bf16[1024,128]{1,0:T(8,128)(2,1)S(1)}, u32[]{:S(2)}, u32[]{:S(2)}) collective-permute-start(bf16[1024,128]{1,0:T(8,128)(2,1)S(1)} %get-tuple-element.267), channel_id=1, source_target_pairs={{8,16},{16,24},{24,28},{20,12},{12,4},{4,0},{9,17},{17,25},{25,29}... | collective-permute-start | bytes 786440 | tf_op jit(solution)/shard_map/ppermute | solution.py:82
  76.2 11.4 %collective-permute-start.16 = (bf16[1024,128]{1,0:T(8,128)(2,1)S(1)}, bf16[1024,128]{1,0:T(8,128)(2,1)S(1)}, u32[]{:S(2)}, u32[]{:S(2)}) collective-permute-start(bf16[1024,128]{1,0:T(8,128)(2,1)S(1)} %get-tuple-element.265), channel_id=1, source_target_pairs={{8,0},{16,8},{24,16},{20,28},{12,20},{4,12},{9,1},{17,9},{25,17},{... | collective-permute-start | bytes 786440 | tf_op jit(solution)/shard_map/ppermute | solution.py:82
  77.5 35.5 %collective-permute-start.13 = (bf16[192,3072]{1,0:T(8,128)(2,1)S(1)}, bf16[192,3072]{1,0:T(8,128)(2,1)}, u32[]{:S(2)}, u32[]{:S(2)}) collective-permute-start(bf16[192,3072]{1,0:T(8,128)(2,1)S(1)} %copy-done.46), channel_id=1, source_target_pairs={{0,4},{8,0},{16,8},{24,16},{28,24},{20,28},{12,20},{4,12},{1,5},{9... | collective-permute-start | bytes 3538952 | tf_op jit(solution)/shard_map/ppermute | solution.py:82
  82.2 35.5 %collective-permute-start.14 = (bf16[192,3072]{1,0:T(8,128)(2,1)S(1)}, bf16[192,3072]{1,0:T(8,128)(2,1)}, u32[]{:S(2)}, u32[]{:S(2)}) collective-permute-start(bf16[192,3072]{1,0:T(8,128)(2,1)S(1)} %copy-done.46), channel_id=1, source_target_pairs={{0,8},{8,16},{16,24},{24,28},{28,20},{20,12},{12,4},{4,0},{1,9},{9... | collective-permute-start | bytes 3538952 | tf_op jit(solution)/shard_map/ppermute | solution.py:82
  82.3 42.8 %collective-permute-start.17 = (bf16[96,1536]{1,0:T(8,128)(2,1)S(1)}, bf16[96,1536]{1,0:T(8,128)(2,1)S(1)}, u32[]{:S(2)}, u32[]{:S(2)}) collective-permute-start(bf16[96,1536]{1,0:T(8,128)(2,1)S(1)} %slice.344), channel_id=1, source_target_pairs={{0,4},{8,0},{16,8},{24,16},{28,24},{20,28},{12,20},{4,12},{1,5},{9... | collective-permute-start | bytes 884744 | tf_op jit(solution)/shard_map/ppermute | solution.py:82
  86.1 41.0 %collective-permute-start.18 = (bf16[96,1536]{1,0:T(8,128)(2,1)}, bf16[96,1536]{1,0:T(8,128)(2,1)S(1)}, u32[]{:S(2)}, u32[]{:S(2)}) collective-permute-start(bf16[96,1536]{1,0:T(8,128)(2,1)} %slice.345), channel_id=1, source_target_pairs={{0,8},{8,16},{16,24},{24,28},{28,20},{20,12},{12,4},{4,0},{1,9},{9... | collective-permute-start | bytes 884744 | tf_op jit(solution)/shard_map/ppermute | solution.py:82
  88.6 52.2 %collective-permute-start.20 = (bf16[2048,128]{1,0:T(8,128)(2,1)}, bf16[2048,128]{1,0:T(8,128)(2,1)}, u32[]{:S(2)}, u32[]{:S(2)}) collective-permute-start(bf16[2048,128]{1,0:T(8,128)(2,1)} %pad_maximum_fusion.10), channel_id=1, source_target_pairs={{0,4},{8,0},{16,8},{28,24},{20,28},{12,20},{1,5},{9,1},{17,9},{29,... | collective-permute-start | bytes 1572872 | tf_op jit(solution)/shard_map/ppermute | solution.py:82
  113.0 27.8 %collective-permute-start.19 = (bf16[2048,128]{1,0:T(8,128)(2,1)}, bf16[2048,128]{1,0:T(8,128)(2,1)S(1)}, u32[]{:S(2)}, u32[]{:S(2)}) collective-permute-start(bf16[2048,128]{1,0:T(8,128)(2,1)} %pad_maximum_fusion.9), channel_id=1, source_target_pairs={{0,8},{16,24},{24,28},{28,20},{12,4},{4,0},{1,9},{17,25},{25,29},{... | collective-permute-start | bytes 1572872 | tf_op jit(solution)/shard_map/ppermute | solution.py:82
  125.0 34.1 %collective-permute-start.25 = (bf16[192,3072]{1,0:T(8,128)(2,1)}, bf16[192,3072]{1,0:T(8,128)(2,1)}, u32[]{:S(2)}, u32[]{:S(2)}) collective-permute-start(bf16[192,3072]{1,0:T(8,128)(2,1)} %collective-permute-done.13.refs_1_), channel_id=1, source_target_pairs={{0,4},{8,0},{16,8},{24,16},{28,24},{20,28},{12,20},{4,12},{1,5},{9... | collective-permute-start | bytes 3538952 | tf_op jit(solution)/shard_map/ppermute | solution.py:82
  125.1 33.9 %collective-permute-start.26 = (bf16[192,3072]{1,0:T(8,128)(2,1)}, bf16[192,3072]{1,0:T(8,128)(2,1)}, u32[]{:S(2)}, u32[]{:S(2)}) collective-permute-start(bf16[192,3072]{1,0:T(8,128)(2,1)} %collective-permute-done.14.refs_8_), channel_id=1, source_target_pairs={{0,8},{8,16},{16,24},{24,28},{28,20},{20,12},{12,4},{4,0},{1,9},{9... | collective-permute-start | bytes 3538952 | tf_op jit(solution)/shard_map/ppermute | solution.py:82
  135.6 38.5 %all-to-all-start.1 = ((bf16[8,256,192]{1,2,0:T(8,128)(2,1)}), bf16[8,256,192]{1,2,0:T(8,128)(2,1)S(1)}, u32[]{:S(2)}, u32[]{:S(2)}) async-start(bf16[8,256,192]{1,2,0:T(8,128)(2,1)} %copy.140), calls=%async_computation.1 | async-start | bytes 1572864 | tf_op jit(solution)/shard_map/all_to_all | solution.py:762
  142.5 35.0 %collective-permute-start.21 = (bf16[2048,128]{1,0:T(8,128)(2,1)S(1)}, bf16[2048,128]{1,0:T(8,128)(2,1)S(1)}, u32[]{:S(2)}, u32[]{:S(2)}) collective-permute-start(bf16[2048,128]{1,0:T(8,128)(2,1)S(1)} %get-tuple-element.263), channel_id=1, source_target_pairs={{0,8},{8,16},{24,28},{28,20},{20,12},{4,0},{1,9},{9,17},{25,29},{2... | collective-permute-start | bytes 1572872 | tf_op jit(solution)/shard_map/ppermute | solution.py:82
  146.4 33.2 %collective-permute-start.22 = (bf16[2048,128]{1,0:T(8,128)(2,1)S(1)}, bf16[2048,128]{1,0:T(8,128)(2,1)S(1)}, u32[]{:S(2)}, u32[]{:S(2)}) collective-permute-start(bf16[2048,128]{1,0:T(8,128)(2,1)S(1)} %get-tuple-element.262), channel_id=1, source_target_pairs={{0,4},{8,0},{24,16},{28,24},{20,28},{4,12},{1,5},{9,1},{25,17},{29... | collective-permute-start | bytes 1572872 | tf_op jit(solution)/shard_map/ppermute | solution.py:82
  159.0 43.5 %collective-permute-start.27 = (bf16[192,3072]{1,0:T(8,128)(2,1)}, bf16[192,3072]{1,0:T(8,128)(2,1)}, u32[]{:S(2)}, u32[]{:S(2)}) collective-permute-start(bf16[192,3072]{1,0:T(8,128)(2,1)} %collective-permute-done.25.refs_2_), channel_id=1, source_target_pairs={{0,4},{8,0},{16,8},{24,16},{28,24},{20,28},{12,20},{4,12},{1,5},{9... | collective-permute-start | bytes 3538952 | tf_op jit(solution)/shard_map/ppermute | solution.py:82
  159.0 48.8 %collective-permute-start.28 = (bf16[192,3072]{1,0:T(8,128)(2,1)}, bf16[192,3072]{1,0:T(8,128)(2,1)}, u32[]{:S(2)}, u32[]{:S(2)}) collective-permute-start(bf16[192,3072]{1,0:T(8,128)(2,1)} %collective-permute-done.26.refs_7_), channel_id=1, source_target_pairs={{0,8},{8,16},{16,24},{24,28},{28,20},{20,12},{12,4},{4,0},{1,9},{9... | collective-permute-start | bytes 3538952 | tf_op jit(solution)/shard_map/ppermute | solution.py:82
  181.9 32.2 %collective-permute-start.23 = (bf16[2048,128]{1,0:T(8,128)(2,1)}, bf16[2048,128]{1,0:T(8,128)(2,1)S(1)}, u32[]{:S(2)}, u32[]{:S(2)}) collective-permute-start(bf16[2048,128]{1,0:T(8,128)(2,1)} %get-tuple-element.260), channel_id=1, source_target_pairs={{0,8},{8,16},{16,24},{28,20},{20,12},{12,4},{1,9},{9,17},{17,25},{... | collective-permute-start | bytes 1572872 | tf_op jit(solution)/shard_map/ppermute | solution.py:82
  186.0 28.2 %collective-permute-start.24 = (bf16[2048,128]{1,0:T(8,128)(2,1)S(1)}, bf16[2048,128]{1,0:T(8,128)(2,1)S(1)}, u32[]{:S(2)}, u32[]{:S(2)}) collective-permute-start(bf16[2048,128]{1,0:T(8,128)(2,1)S(1)} %get-tuple-element.261), channel_id=1, source_target_pairs={{0,4},{16,8},{24,16},{28,24},{12,20},{4,12},{1,5},{17,9},{25,17},{... | collective-permute-start | bytes 1572872 | tf_op jit(solution)/shard_map/ppermute | solution.py:82
  203.7 39.8 %collective-permute-start.29 = (bf16[96,3072]{1,0:T(8,128)(2,1)S(1)}, bf16[96,3072]{1,0:T(8,128)(2,1)S(1)}, u32[]{:S(2)}, u32[]{:S(2)}) collective-permute-start(bf16[96,3072]{1,0:T(8,128)(2,1)S(1)} %slice.351), channel_id=1, source_target_pairs={{0,4},{8,0},{16,8},{24,16},{28,24},{20,28},{12,20},{4,12},{1,5},{9... | collective-permute-start | bytes 1769480 | tf_op jit(solution)/shard_map/ppermute | solution.py:82
  209.0 34.5 %collective-permute-start.30 = (bf16[96,3072]{1,0:T(8,128)(2,1)S(1)}, bf16[96,3072]{1,0:T(8,128)(2,1)}, u32[]{:S(2)}, u32[]{:S(2)}) collective-permute-start(bf16[96,3072]{1,0:T(8,128)(2,1)S(1)} %slice.352), channel_id=1, source_target_pairs={{0,8},{8,16},{16,24},{24,28},{28,20},{20,12},{12,4},{4,0},{1,9},{9... | collective-permute-start | bytes 1769480 | tf_op jit(solution)/shard_map/ppermute | solution.py:82
  253.3 11.2 %collective-permute-start.32 = (bf16[128,1536]{1,0:T(8,128)(2,1)S(1)}, bf16[128,1536]{1,0:T(8,128)(2,1)S(1)}, u32[]{:S(2)}, u32[]{:S(2)}) collective-permute-start(bf16[128,1536]{1,0:T(8,128)(2,1)S(1)} %add_convert_fusion.22), channel_id=1, source_target_pairs={{0,2},{2,0},{1,3},{3,1},{4,6},{6,4},{5,7},{7,5},{8,10},{10,8},{9,1... | collective-permute-start | bytes 1179656 | tf_op jit(solution)/shard_map/ppermute | solution.py:182
  292.9 11.4 %collective-permute-start.35 = (bf16[128,1536]{1,0:T(8,128)(2,1)S(1)}, bf16[128,1536]{1,0:T(8,128)(2,1)S(1)}, u32[]{:S(2)}, u32[]{:S(2)}) collective-permute-start(bf16[128,1536]{1,0:T(8,128)(2,1)S(1)} %add_convert_fusion.20), channel_id=1, source_target_pairs={{0,2},{2,0},{1,3},{3,1},{4,6},{6,4},{5,7},{7,5},{8,10},{10,8},{9,1... | collective-permute-start | bytes 1179656 | tf_op jit(solution)/shard_map/ppermute | solution.py:182
  297.0 17.5 %collective-permute-start.40 = (bf16[96,3072]{1,0:T(8,128)(2,1)}, bf16[96,3072]{1,0:T(8,128)(2,1)}, u32[]{:S(2)}, u32[]{:S(2)}) collective-permute-start(bf16[96,3072]{1,0:T(8,128)(2,1)} %get-tuple-element.297), channel_id=1, source_target_pairs={{0,8},{8,16},{16,24},{24,28},{28,20},{20,12},{12,4},{4,0},{1,9},{9... | collective-permute-start | bytes 1769480 | tf_op jit(solution)/shard_map/ppermute | solution.py:82
  297.0 17.5 %collective-permute-start.41 = (bf16[96,3072]{1,0:T(8,128)(2,1)}, bf16[96,3072]{1,0:T(8,128)(2,1)}, u32[]{:S(2)}, u32[]{:S(2)}) collective-permute-start(bf16[96,3072]{1,0:T(8,128)(2,1)} %get-tuple-element.296), channel_id=1, source_target_pairs={{0,4},{8,0},{16,8},{24,16},{28,24},{20,28},{12,20},{4,12},{1,5},{9... | collective-permute-start | bytes 1769480 | tf_op jit(solution)/shard_map/ppermute | solution.py:82
  316.9 37.1 %collective-permute-start.43 = (bf16[192,3072]{1,0:T(8,128)(2,1)}, bf16[192,3072]{1,0:T(8,128)(2,1)}, u32[]{:S(2)}, u32[]{:S(2)}) collective-permute-start(bf16[192,3072]{1,0:T(8,128)(2,1)} %pad_maximum_fusion.3), channel_id=1, source_target_pairs={{0,4},{8,0},{16,8},{24,16},{28,24},{20,28},{12,20},{4,12},{1,5},{9... | collective-permute-start | bytes 3538952 | tf_op jit(solution)/shard_map/ppermute | solution.py:82
  319.3 34.8 %collective-permute-start.42 = (bf16[192,3072]{1,0:T(8,128)(2,1)}, bf16[192,3072]{1,0:T(8,128)(2,1)}, u32[]{:S(2)}, u32[]{:S(2)}) collective-permute-start(bf16[192,3072]{1,0:T(8,128)(2,1)} %fusion.9), channel_id=1, source_target_pairs={{0,8},{8,16},{16,24},{24,28},{28,20},{20,12},{12,4},{4,0},{1,9},{9... | collective-permute-start | bytes 3538952 | tf_op jit(solution)/shard_map/ppermute | solution.py:82
  324.6 28.5 %all-to-all-start.3 = ((bf16[8,256,64]{1,2,0:T(8,128)(2,1)}), bf16[8,256,64]{1,2,0:T(8,128)(2,1)S(1)}, u32[]{:S(2)}, u32[]{:S(2)}) async-start(bf16[8,256,64]{1,2,0:T(8,128)(2,1)} %copy.148), calls=%async_computation.3 | async-start | bytes 524288 | tf_op jit(solution)/shard_map/all_to_all | solution.py:762
  329.1 46.5 %collective-permute-start.38 = (bf16[128,1536]{1,0:T(8,128)(2,1)S(1)}, bf16[128,1536]{1,0:T(8,128)(2,1)S(1)}, u32[]{:S(2)}, u32[]{:S(2)}) collective-permute-start(bf16[128,1536]{1,0:T(8,128)(2,1)S(1)} %add_convert_fusion.18), channel_id=1, source_target_pairs={{0,2},{2,0},{1,3},{3,1},{4,6},{6,4},{5,7},{7,5},{8,10},{10,8},{9,1... | collective-permute-start | bytes 1179656 | tf_op jit(solution)/shard_map/ppermute | solution.py:182
  356.9 77.4 %collective-permute-start.64 = (bf16[192,3072]{1,0:T(8,128)(2,1)}, bf16[192,3072]{1,0:T(8,128)(2,1)}, u32[]{:S(2)}, u32[]{:S(2)}) collective-permute-start(bf16[192,3072]{1,0:T(8,128)(2,1)} %add_convert_fusion.2), channel_id=1, source_target_pairs={{0,4},{8,0},{16,8},{24,16},{28,24},{20,28},{12,20},{4,12},{1,5},{9... | collective-permute-start | bytes 3538952 | tf_op jit(solution)/shard_map/ppermute | solution.py:82
  360.9 73.4 %collective-permute-start.63 = (bf16[192,3072]{1,0:T(8,128)(2,1)}, bf16[192,3072]{1,0:T(8,128)(2,1)}, u32[]{:S(2)}, u32[]{:S(2)}) collective-permute-start(bf16[192,3072]{1,0:T(8,128)(2,1)} %add_convert_fusion.3), channel_id=1, source_target_pairs={{0,8},{8,16},{16,24},{24,28},{28,20},{20,12},{12,4},{4,0},{1,9},{9... | collective-permute-start | bytes 3538952 | tf_op jit(solution)/shard_map/ppermute | solution.py:82
  373.6 27.8 %collective-permute-start.55 = (bf16[2048,128]{1,0:T(8,128)(2,1)}, bf16[2048,128]{1,0:T(8,128)(2,1)}, u32[]{:S(2)}, u32[]{:S(2)}) collective-permute-start(bf16[2048,128]{1,0:T(8,128)(2,1)} %get-tuple-element.137.refs_0_), channel_id=1, source_target_pairs={{0,4},{8,0},{16,8},{24,16},{28,24},{20,28},{12,20},{4,12},{1,5},{9... | collective-permute-start | bytes 1572872 | tf_op jit(solution)/shard_map/ppermute | solution.py:82
  374.9 28.5 %collective-permute-start.59 = (bf16[2048,128]{1,0:T(8,128)(2,1)}, bf16[2048,128]{1,0:T(8,128)(2,1)}, u32[]{:S(2)}, u32[]{:S(2)}) collective-permute-start(bf16[2048,128]{1,0:T(8,128)(2,1)} %get-tuple-element.137.refs_0_), channel_id=1, source_target_pairs={{0,8},{8,16},{16,24},{24,28},{28,20},{20,12},{12,4},{4,0},{1,9},{9... | collective-permute-start | bytes 1572872 | tf_op jit(solution)/shard_map/ppermute | solution.py:82
  375.8 30.6 %collective-permute-start.39 = (bf16[128,1536]{1,0:T(8,128)(2,1)S(1)}, bf16[128,1536]{1,0:T(8,128)(2,1)S(1)}, u32[]{:S(2)}, u32[]{:S(2)}) collective-permute-start(bf16[128,1536]{1,0:T(8,128)(2,1)S(1)} %add_convert_fusion.17.fm_ref), channel_id=1, source_target_pairs={{0,1},{1,0},{2,3},{3,2},{4,5},{5,4},{6,7},{7,6},{8,9},{9,8},{10,11... | collective-permute-start | bytes 1179656 | tf_op jit(solution)/shard_map/ppermute | solution.py:183
  397.3 41.7 %all-to-all-start.4 = ((bf16[8,256,192]{1,2,0:T(8,128)(2,1)}), bf16[8,256,192]{1,2,0:T(8,128)(2,1)S(1)}, u32[]{:S(2)}, u32[]{:S(2)}) async-start(bf16[8,256,192]{1,2,0:T(8,128)(2,1)} %copy.151), calls=%async_computation.4 | async-start | bytes 1572864 | tf_op jit(solution)/shard_map/all_to_all | solution.py:762
  401.4 27.0 %collective-permute-start.56 = (bf16[2048,128]{1,0:T(8,128)(2,1)}, bf16[2048,128]{1,0:T(8,128)(2,1)}, u32[]{:S(2)}, u32[]{:S(2)}) collective-permute-start(bf16[2048,128]{1,0:T(8,128)(2,1)} %collective-permute-done.55.refs_1_), channel_id=1, source_target_pairs={{0,4},{8,0},{16,8},{24,16},{28,24},{20,28},{12,20},{4,12},{1,5},{9... | collective-permute-start | bytes 1572872 | tf_op jit(solution)/shard_map/ppermute | solution.py:82
  403.4 25.0 %collective-permute-start.60 = (bf16[2048,128]{1,0:T(8,128)(2,1)}, bf16[2048,128]{1,0:T(8,128)(2,1)}, u32[]{:S(2)}, u32[]{:S(2)}) collective-permute-start(bf16[2048,128]{1,0:T(8,128)(2,1)} %collective-permute-done.59.refs_8_), channel_id=1, source_target_pairs={{0,8},{8,16},{16,24},{24,28},{28,20},{20,12},{12,4},{4,0},{1,9},{9... | collective-permute-start | bytes 1572872 | tf_op jit(solution)/shard_map/ppermute | solution.py:82
  428.4 27.7 %collective-permute-start.57 = (bf16[2048,128]{1,0:T(8,128)(2,1)}, bf16[2048,128]{1,0:T(8,128)(2,1)}, u32[]{:S(2)}, u32[]{:S(2)}) collective-permute-start(bf16[2048,128]{1,0:T(8,128)(2,1)} %collective-permute-done.56.refs_2_), channel_id=1, source_target_pairs={{0,4},{8,0},{16,8},{24,16},{28,24},{20,28},{12,20},{4,12},{1,5},{9... | collective-permute-start | bytes 1572872 | tf_op jit(solution)/shard_map/ppermute | solution.py:82
  428.4 28.8 %collective-permute-start.61 = (bf16[2048,128]{1,0:T(8,128)(2,1)}, bf16[2048,128]{1,0:T(8,128)(2,1)}, u32[]{:S(2)}, u32[]{:S(2)}) collective-permute-start(bf16[2048,128]{1,0:T(8,128)(2,1)} %collective-permute-done.60.refs_7_), channel_id=1, source_target_pairs={{0,8},{8,16},{16,24},{24,28},{28,20},{20,12},{12,4},{4,0},{1,9},{9... | collective-permute-start | bytes 1572872 | tf_op jit(solution)/shard_map/ppermute | solution.py:82
  437.0 92.4 %collective-permute-start.65 = (bf16[192,3072]{1,0:T(8,128)(2,1)}, bf16[192,3072]{1,0:T(8,128)(2,1)}, u32[]{:S(2)}, u32[]{:S(2)}) collective-permute-start(bf16[192,3072]{1,0:T(8,128)(2,1)} %add_convert_fusion.1), channel_id=1, source_target_pairs={{0,8},{8,16},{16,24},{24,28},{28,20},{20,12},{12,4},{4,0},{1,9},{9... | collective-permute-start | bytes 3538952 | tf_op jit(solution)/shard_map/ppermute | solution.py:82
  451.2 26.3 %collective-permute-start.47 = (bf16[96,1536]{1,0:T(8,128)(2,1)S(1)}, bf16[96,1536]{1,0:T(8,128)(2,1)S(1)}, u32[]{:S(2)}, u32[]{:S(2)}) collective-permute-start(bf16[96,1536]{1,0:T(8,128)(2,1)S(1)} %get-tuple-element.300), channel_id=1, source_target_pairs={{0,8},{8,16},{16,24},{24,28},{28,20},{20,12},{12,4},{4,0},{1,9},{9... | collective-permute-start | bytes 884744 | tf_op jit(solution)/shard_map/ppermute | solution.py:82
  454.1 75.4 %collective-permute-start.66 = (bf16[192,3072]{1,0:T(8,128)(2,1)}, bf16[192,3072]{1,0:T(8,128)(2,1)}, u32[]{:S(2)}, u32[]{:S(2)}) collective-permute-start(bf16[192,3072]{1,0:T(8,128)(2,1)} %add_convert_fusion), channel_id=1, source_target_pairs={{0,4},{8,0},{16,8},{24,16},{28,24},{20,28},{12,20},{4,12},{1,5},{9... | collective-permute-start | bytes 3538952 | tf_op jit(solution)/shard_map/ppermute | solution.py:82
  456.1 33.5 %collective-permute-start.44 = (bf16[128,1536]{1,0:T(8,128)(2,1)S(1)}, bf16[128,1536]{1,0:T(8,128)(2,1)S(1)}, u32[]{:S(2)}, u32[]{:S(2)}) collective-permute-start(bf16[128,1536]{1,0:T(8,128)(2,1)S(1)} %copy-done.100), channel_id=1, source_target_pairs={{0,1},{1,0},{2,3},{3,2},{4,5},{5,4},{6,7},{7,6},{8,9},{9,8},{10,11... | collective-permute-start | bytes 1179656 | tf_op jit(solution)/shard_map/ppermute | solution.py:180
  457.2 32.3 %collective-permute-start.51 = (bf16[96,1536]{1,0:T(8,128)(2,1)S(1)}, bf16[96,1536]{1,0:T(8,128)(2,1)S(1)}, u32[]{:S(2)}, u32[]{:S(2)}) collective-permute-start(bf16[96,1536]{1,0:T(8,128)(2,1)S(1)} %get-tuple-element.301), channel_id=1, source_target_pairs={{0,4},{8,0},{16,8},{24,16},{28,24},{20,28},{12,20},{4,12},{1,5},{9... | collective-permute-start | bytes 884744 | tf_op jit(solution)/shard_map/ppermute | solution.py:82
  477.6 15.1 %collective-permute-start.58 = (bf16[1024,128]{1,0:T(8,128)(2,1)S(1)}, bf16[1024,128]{1,0:T(8,128)(2,1)S(1)}, u32[]{:S(2)}, u32[]{:S(2)}) collective-permute-start(bf16[1024,128]{1,0:T(8,128)(2,1)S(1)} %slice.393), channel_id=1, source_target_pairs={{0,4},{8,0},{16,8},{24,16},{28,24},{20,28},{12,20},{4,12},{1,5},{9... | collective-permute-start | bytes 786440 | tf_op jit(solution)/shard_map/ppermute | solution.py:82
  489.5 9.2 %collective-permute-start.62 = (bf16[1024,128]{1,0:T(8,128)(2,1)S(1)}, bf16[1024,128]{1,0:T(8,128)(2,1)S(1)}, u32[]{:S(2)}, u32[]{:S(2)}) collective-permute-start(bf16[1024,128]{1,0:T(8,128)(2,1)S(1)} %slice.394), channel_id=1, source_target_pairs={{0,8},{8,16},{16,24},{24,28},{28,20},{20,12},{12,4},{4,0},{1,9},{9... | collective-permute-start | bytes 786440 | tf_op jit(solution)/shard_map/ppermute | solution.py:82
  489.7 22.5 %collective-permute-start.45 = (bf16[128,1536]{1,0:T(8,128)(2,1)S(1)}, bf16[128,1536]{1,0:T(8,128)(2,1)}, u32[]{:S(2)}, u32[]{:S(2)}) collective-permute-start(bf16[128,1536]{1,0:T(8,128)(2,1)S(1)} %add_convert_fusion.16), channel_id=1, source_target_pairs={{0,2},{2,0},{1,3},{3,1},{4,6},{6,4},{5,7},{7,5},{8,10},{10,8},{9,1... | collective-permute-start | bytes 1179656 | tf_op jit(solution)/shard_map/ppermute | solution.py:182
  492.6 20.8 %collective-permute-start.48 = (bf16[192,1536]{1,0:T(8,128)(2,1)}, bf16[192,1536]{1,0:T(8,128)(2,1)S(1)}, u32[]{:S(2)}, u32[]{:S(2)}) collective-permute-start(bf16[192,1536]{1,0:T(8,128)(2,1)} %fusion.21), channel_id=1, source_target_pairs={{0,8},{8,16},{16,24},{24,28},{28,20},{20,12},{12,4},{4,0},{1,9},{9... | collective-permute-start | bytes 1769480 | tf_op jit(solution)/shard_map/ppermute | solution.py:82
  498.7 15.8 %collective-permute-start.52 = (bf16[192,1536]{1,0:T(8,128)(2,1)S(1)}, bf16[192,1536]{1,0:T(8,128)(2,1)S(1)}, u32[]{:S(2)}, u32[]{:S(2)}) collective-permute-start(bf16[192,1536]{1,0:T(8,128)(2,1)S(1)} %pad_maximum_fusion.8), channel_id=1, source_target_pairs={{0,4},{8,0},{16,8},{24,16},{28,24},{20,28},{12,20},{4,12},{1,5},{9... | collective-permute-start | bytes 1769480 | tf_op jit(solution)/shard_map/ppermute | solution.py:82
  514.4 24.5 %collective-permute-start.49 = (bf16[192,1536]{1,0:T(8,128)(2,1)}, bf16[192,1536]{1,0:T(8,128)(2,1)}, u32[]{:S(2)}, u32[]{:S(2)}) collective-permute-start(bf16[192,1536]{1,0:T(8,128)(2,1)} %add_convert_fusion.7), channel_id=1, source_target_pairs={{0,8},{8,16},{16,24},{24,28},{28,20},{20,12},{12,4},{4,0},{1,9},{9... | collective-permute-start | bytes 1769480 | tf_op jit(solution)/shard_map/ppermute | solution.py:82
  515.5 26.7 %collective-permute-start.53 = (bf16[192,1536]{1,0:T(8,128)(2,1)}, bf16[192,1536]{1,0:T(8,128)(2,1)}, u32[]{:S(2)}, u32[]{:S(2)}) collective-permute-start(bf16[192,1536]{1,0:T(8,128)(2,1)} %add_convert_fusion.5), channel_id=1, source_target_pairs={{0,4},{8,0},{16,8},{24,16},{28,24},{20,28},{12,20},{4,12},{1,5},{9... | collective-permute-start | bytes 1769480 | tf_op jit(solution)/shard_map/ppermute | solution.py:82
  538.2 7.1 %collective-permute-start.69 = (f32[64,384]{1,0:T(8,128)S(1)}, f32[64,384]{1,0:T(8,128)S(1)}, u32[]{:S(2)}, u32[]{:S(2)}) collective-permute-start(f32[64,384]{1,0:T(8,128)S(1)} %add.416), channel_id=1, source_target_pairs={{0,16},{4,20},{8,24},{12,28},{16,0},{20,4},{24,8},{28,12},{1,17},{... | collective-permute-start | bytes 294920 | tf_op jit(solution)/shard_map/ppermute | solution.py:161
  540.1 13.6 %collective-permute-start.50 = (bf16[192,1536]{1,0:T(8,128)(2,1)S(1)}, bf16[192,1536]{1,0:T(8,128)(2,1)}, u32[]{:S(2)}, u32[]{:S(2)}) collective-permute-start(bf16[192,1536]{1,0:T(8,128)(2,1)S(1)} %add_convert_fusion.6), channel_id=1, source_target_pairs={{0,8},{8,16},{16,24},{24,28},{28,20},{20,12},{12,4},{4,0},{1,9},{9... | collective-permute-start | bytes 1769480 | tf_op jit(solution)/shard_map/ppermute | solution.py:82
  543.4 14.0 %collective-permute-start.54 = (bf16[192,1536]{1,0:T(8,128)(2,1)S(1)}, bf16[192,1536]{1,0:T(8,128)(2,1)}, u32[]{:S(2)}, u32[]{:S(2)}) collective-permute-start(bf16[192,1536]{1,0:T(8,128)(2,1)S(1)} %add_convert_fusion.4), channel_id=1, source_target_pairs={{0,4},{8,0},{16,8},{24,16},{28,24},{20,28},{12,20},{4,12},{1,5},{9... | collective-permute-start | bytes 1769480 | tf_op jit(solution)/shard_map/ppermute | solution.py:82
  547.4 17.1 %collective-permute-start.75 = (bf16[48,384]{1,0:T(8,128)(2,1)}, bf16[48,384]{1,0:T(8,128)(2,1)}, u32[]{:S(2)}, u32[]{:S(2)}) collective-permute-start(bf16[48,384]{1,0:T(8,128)(2,1)} %slice.481), channel_id=1, source_target_pairs={{0,1},{1,0},{2,3},{3,2},{4,5},{5,4},{6,7},{7,6},{8,9},{9,8},{10,11... | collective-permute-start | bytes 110600 | tf_op jit(solution)/shard_map/ppermute | solution.py:174
  (123 other events, 779.6 us)

commit v5 on v4

--- a/solution.py
+++ b/solution.py
@@ -30,7 +30,7 @@
 score_scale = HD ** (-0.5)
 
 WIDE = 256
-ROWS = 64
+ROWS = 128
 
 CORE_SWAP = [(0, 1), (1, 0), (2, 3), (3, 2)]
 Y_SWAP = [(0, 2), (2, 0), (1, 3), (3, 1)]
@@ -183,10 +183,15 @@
     return (mine, lax.ppermute(mine, "tp", CORE_SWAP))
 
 
-def exact_dot(a, b):
-    return lax.dot_general(
-        a, b, (((1,), (0,)), ((), ())), precision=highest, preferred_element_type=f32
-    )
+def thirds(value):
+    high = value.astype(bf16).astype(f32)
+    rest = value - high
+    middle = rest.astype(bf16).astype(f32)
+    return jnp.concatenate([high, middle, rest - middle], axis=0).astype(bf16)
+
+
+def item_sum(by_item, value):
+    return dot(jnp.concatenate([by_item] * 3, axis=1).astype(bf16), thirds(value), ((1,), (0,)))
 
 
 def anywhere():
@@ -272,8 +277,8 @@
 
 
 def onehot_rows(segment_col):
-    items = lax.broadcasted_iota(jnp.int32, (segment_col.shape[0], ITEMS), 1)
-    return (segment_col == items).astype(f32)
+    items = lax.broadcasted_iota(jnp.int32, (segment_col.shape[0], 3 * ITEMS), 1) % ITEMS
+    return (segment_col == items).astype(f32).astype(bf16)
 
 
 def onehot_cols(segment_row):
@@ -282,7 +287,7 @@
 
 
 def modulate(onehot, mod_ref, block):
-    return exact_dot(onehot, mod_ref[block * ITEMS : (block + 1) * ITEMS, :])
+    return dot(onehot, thirds(mod_ref[block * ITEMS : (block + 1) * ITEMS, :]), ((1,), (0,)))
 
 
 def enter_kernel(scal, x_ref, g_ref, mod_ref, gain_ref, sc_ref,
@@ -344,7 +349,7 @@
         full_ref[:, at] = dot(value_ref[...], held[at, :], ((1,), (1,))).astype(bf16)
         return 0
 
-    lax.fori_loop(0, tiles, one, 0)
+    lax.fori_loop(0, tiles, one, 0, unroll=True)
 
 
 def out_kernel(scal, slab_ref, *refs, heads, first_owner, count, low, high):
@@ -422,7 +427,7 @@
         both_ref[:, at(units)] = (inner_grad * silu).astype(bf16)
         return 0
 
-    lax.fori_loop(0, units // WIDE, tile, 0)
+    lax.fori_loop(0, units // WIDE, tile, 0, unroll=True)
     times_turned(both_ref, held.at[:, 0 : 2 * units], full)
     split_halves(core, full, hm_ref, ho_ref)
     times_turned(inner_ref, held.at[:, 2 * units : 3 * units], full)
@@ -489,7 +494,7 @@
     normed, _ = rms_parts(x_mid)
 
     def add(block, value):
-        sums_ref[block * ITEMS : (block + 1) * ITEMS, :] += exact_dot(by_item, value)
+        sums_ref[block * ITEMS : (block + 1) * ITEMS, :] += item_sum(by_item, value)
 
     add(0, grad_ref[...] * attn * (1.0 - tanh_attn * tanh_attn))
     add(1, hgrad)
@@ -517,8 +522,8 @@
     absolute_store(
         size, ring, place, input_ref, grad_ref[...] + rms_back(normed, inverse, normed_grad)
     )
-    total[0:ITEMS, :] += exact_dot(by_item, hgrad)
-    total[ITEMS : 2 * ITEMS, :] += exact_dot(by_item, hgrad * normed * gainr_ref[0:1, :])
+    total[0:ITEMS, :] += item_sum(by_item, hgrad)
+    total[ITEMS : 2 * ITEMS, :] += item_sum(by_item, hgrad * normed * gainr_ref[0:1, :])
     total[6 * ITEMS : 6 * ITEMS + 1, :] += jnp.sum(
         hgrad * normed * (1.0 + scale), axis=0, keepdims=True
     )
@@ -973,14 +978,6 @@
     head_grad = once(head_grad, *ffn_sum.send((head_grad,)))
     half_block = pl.BlockSpec((ROWS, width), lambda i, *_: (i % (steps // 2), 0))
     sums_shape, one_gain = (4 * ITEMS, width), (8, width)
-    block_out, early_sums, early_gain = call(
-        functools.partial(side_kernel, **which), "side", steps, [scal],
-        [(x_mid, block), (mid_grad, block), (g_rel, block)]
-        + halves(attn, half_block) + halves(ffn_out, half_block) + halves(hgrad, half_block)
-        + mod_ins + row_ins,
-        [(tokens, f32, block), (sums_shape, f32, whole(sums_shape)), (one_gain, f32, whole(one_gain))],
-        moved=here * width * 24,
-    )
 
     g_ins = [(head_grad, rows_block(block_q, HD))]
     kv64 = pltpu.VMEM((text_rows, HD), bf16)
@@ -1041,8 +1038,17 @@
 
     attn_sum = ring.reduce_products([(hidden_attn, qkv_grads), (attn_grad, mixed)])
     next(attn_sum)
-    ffn_sum.send((dqkv,))
+    ffn_sent = ffn_sum.send((dqkv,))
     updown_rows, down_owned = ffn_sum.send(())
+    side_mid = once(x_mid, *ffn_sent)
+    block_out, early_sums, early_gain = call(
+        functools.partial(side_kernel, **which), "side", steps, [scal],
+        [(side_mid, block), (mid_grad, block), (g_rel, block)]
+        + halves(attn, half_block) + halves(ffn_out, half_block) + halves(hgrad, half_block)
+        + mod_ins + row_ins,
+        [(tokens, f32, block), (sums_shape, f32, whole(sums_shape)), (one_gain, f32, whole(one_gain))],
+        moved=here * width * 24,
+    )
     for _ in range(4):
         attn_grads = attn_sum.send(())
     qkv_rows, out_owned = attn_grads

time: 621 us -> 600 us (0.966)
  Pallas kernels: 154 us -> 135 us
    pallas_call x16, Pallas kernels: 154 us -> 135 us  [call(): pl.pallas_call(kernel, out_shape=tuple((shape_of(shape, dtype) for shape,...]
  transfers between devices with their start and end apart: 81 -> 81, of which waited for: 31 -> 32; matrix products, arithmetic and copies ran while one was open for 17% -> 18% of each run, Pallas kernels for 21% -> 20%
where the time goes in v5:
time: 600 us; the launch traced here: 588 us
  waiting for transfers between devices  166 us (28%)
  Pallas kernels  135 us (22%)
  starting transfers between devices  118 us (20%)
  other arithmetic  83.1 us (14%)
  local copies, waits for them, and re-layouts  43.7 us (7%)
  matrix products  18.8 us (3%)
  blocking collectives  13.6 us (2%)
  between operations  9.92 us (2%)
    pallas_call x16, Pallas kernels, call(): pl.pallas_call(kernel, out_shape=tuple((shape_of(shape, dtype) for shape,...  135 us
    ppermute x48, waiting for transfers between devices, hop(): return lax.ppermute(value, 'seq', pairs)  84 us
    ppermute x48, starting transfers between devices, hop(): return lax.ppermute(value, 'seq', pairs)  76.8 us
    all_to_all x4, waiting for transfers between devices, exchange(): return lax.all_to_all(slabs, 'seq', 0, 0, tiled=True)  37.1 us
    convert_element_type x15, other arithmetic, plus(): return (part.astype(f32) + moved.astype(f32)).astype(bf16)  21.8 us
    ppermute x11, waiting for transfers between devices, butterfly(): lax.ppermute(value, axis, [(i, i ^ step) for i in range(size)])  21 us
    dot_general x7, matrix products, dot(): return lax.dot_general(a, b, (dims, ((), ())), preferred_element_type=f32)  18.8 us
    all_to_all x4, starting transfers between devices, exchange(): return lax.all_to_all(slabs, 'seq', 0, 0, tiled=True)  18.5 us
  transfers between devices with their start and end apart: 81, of which 32 were waited for; matrix products, arithmetic and copies ran while one was open for 18% of the time, Pallas kernels for 20%

profile of v5, /device:TPU:0, one launch (start us, length us, event | category | flops | bytes accessed | tf_op | source)
XLA Modules:
  0.0 588.3 jit_solution(14484074942017339989)
XLA Ops:
  2.1 3.0 collective-permute-start.5
  5.8 5.5 caption_slabs.1
  11.4 6.2 %all-to-all-start = ((bf16[8,256,128]{2,1,0:T(8,128)(2,1)}), bf16[8,256,128]{2,1,0:T(8,128)(2,1)}, u32[]{:S(2)}, u32[]{:S(2)}) async-start(bf16[8,256,128]{2,1,0:T(8,128)(2,1)} %caption_slabs.1), calls=%async_computation | async-start | bytes 1048576 | tf_op jit(solution)/shard_map/all_to_all | solution.py:767
  18.9 5.2 modulation.1
  24.2 7.5 %all-to-all-done = bf16[8,256,128]{2,1,0:T(8,128)(2,1)} async-done(((bf16[8,256,128]{2,1,0:T(8,128)(2,1)}), bf16[8,256,128]{2,1,0:T(8,128)(2,1)}, u32[]{:S(2)}, u32[]{:S(2)}) %all-to-all-start) | async-done | bytes 524320 | tf_op jit(solution)/shard_map/all_to_all | solution.py:767
  37.1 2.6 collective-permute-done
  50.7 2.7 collective-permute-done.2
  55.5 3.8 text_heads.1
  65.5 4.7 collective-permute-done.12
  72.0 2.4 convolution_convert_fusion.3
  77.5 4.0 collective-permute-start.13
  88.6 2.5 collective-permute-start.20
  92.0 21.1 %collective-permute-done.13.refs_1_ = bf16[192,3072]{1,0:T(8,128)(2,1)} collective-permute-done((bf16[192,3072]{1,0:T(8,128)(2,1)S(1)}, bf16[192,3072]{1,0:T(8,128)(2,1)}, u32[]{:S(2)}, u32[]{:S(2)}) %collective-permute-start.13) | collective-permute-done | bytes 1179680 | tf_op jit(solution)/shard_map/ppermute | solution.py:82
  113.0 3.9 collective-permute-start.19
  117.7 4.6 enter.1
  125.4 5.6 project.1
  133.2 4.8 all-to-all-start.1
  139.7 3.9 collective-permute-start.21
  147.1 13.0 %collective-permute-done.25.refs_2_ = bf16[192,3072]{1,0:T(8,128)(2,1)} collective-permute-done((bf16[192,3072]{1,0:T(8,128)(2,1)}, bf16[192,3072]{1,0:T(8,128)(2,1)}, u32[]{:S(2)}, u32[]{:S(2)}) %collective-permute-start.25) | collective-permute-done | bytes 1179680 | tf_op jit(solution)/shard_map/ppermute | solution.py:82
  160.1 6.2 %collective-permute-start.28 = (bf16[192,3072]{1,0:T(8,128)(2,1)}, bf16[192,3072]{1,0:T(8,128)(2,1)}, u32[]{:S(2)}, u32[]{:S(2)}) collective-permute-start(bf16[192,3072]{1,0:T(8,128)(2,1)} %collective-permute-done.26.refs_7_), channel_id=1, source_target_pairs={{0,8},{8,16},{16,24},{24,28},{28,20},{20,12},{12,4},{4,0},{1,9},{9... | collective-permute-start | bytes 3538952 | tf_op jit(solution)/shard_map/ppermute | solution.py:82
  167.7 6.4 %all-to-all-done.1 = bf16[8,256,192]{1,2,0:T(8,128)(2,1)S(1)} async-done(((bf16[8,256,192]{1,2,0:T(8,128)(2,1)}), bf16[8,256,192]{1,2,0:T(8,128)(2,1)S(1)}, u32[]{:S(2)}, u32[]{:S(2)}) %all-to-all-start.1) | async-done | bytes 786464 | tf_op jit(solution)/shard_map/all_to_all | solution.py:767
  175.4 3.3 collective-permute-done.21
  179.6 2.3 add_convert_fusion.12
  181.9 3.4 collective-permute-start.23
  187.5 14.4 %attend.1 = (f32[64,2048]{1,0:T(8,128)}, f32[1,2048]{1,0:T(1,128)}) custom-call(s32[4,4]{1,0:T(4,128)} %pad_add_fusion.table, bf16[2048,192]{1,0:T(8,128)(2,1)} %bitcast.138, bf16[2048,192]{1,0:T(8,128)(2,1)} %bitcast.139, s32[1,2048]{1,0:T(1,128)} %bitcast.155, s32[2048,1]{1,0:T(8,128)} %copy.142.sk_ref), custom_call_target="tpu_custom_call" | custom-call | flops 1073741824 | bytes 2621440 | tf_op jit(solution)/shard_map/attend/pallas_call | solution.py:220
  203.1 2.5 collective-permute-start.29
  206.8 6.5 %collective-permute-done.23 = bf16[2048,128]{1,0:T(8,128)(2,1)S(1)} collective-permute-done((bf16[2048,128]{1,0:T(8,128)(2,1)}, bf16[2048,128]{1,0:T(8,128)(2,1)S(1)}, u32[]{:S(2)}, u32[]{:S(2)}) %collective-permute-start.23) | collective-permute-done | bytes 524320 | tf_op jit(solution)/shard_map/ppermute | solution.py:82
  215.3 11.3 %attend_text.1 = (bf16[2048,64]{1,0:T(8,128)(2,1)}, f32[64,2048]{1,0:T(8,128)}, f32[1,2048]{1,0:T(1,128)}) custom-call(s32[4,4]{1,0:T(4,128)} %pad_add_fusion.table, f32[1]{0:T(128)} %bitcast.14.gate, bf16[2048,192]{1,0:T(8,128)(2,1)} %bitcast.140, bf16[2048,128]{1,0:T(8,128)(2,1)} %add_convert_fusion.10.kv_ref, f32[64,2048]{1,0:T(8,128)} %get-tuple-element.98.self_ref, ...), custom_call_target="tpu_custom_call" | custom-call | flops 134217728 | bytes 2621440 | tf_op jit(solution)/shard_map/attend_text/pallas_call | solution.py:220
  227.8 13.6 %all_to_all.25 = bf16[8,256,64]{1,2,0:T(8,128)(2,1)S(1)} all-to-all(bf16[8,256,64]{1,2,0:T(8,128)(2,1)S(1)} %copy.143), channel_id=1, replica_groups=mesh['seq'=8,'tp'=4] {'seq'}, dimensions={0} | all-to-all | bytes 524288 | tf_op jit(solution)/shard_map/all_to_all | solution.py:767
  242.4 4.7 out.1
  251.8 9.6 %collective-permute-done.32 = bf16[128,1536]{1,0:T(8,128)(2,1)S(1)} collective-permute-done((bf16[128,1536]{1,0:T(8,128)(2,1)S(1)}, bf16[128,1536]{1,0:T(8,128)(2,1)S(1)}, u32[]{:S(2)}, u32[]{:S(2)}) %collective-permute-start.32) | collective-permute-done | bytes 393248 | tf_op jit(solution)/shard_map/ppermute | solution.py:182
  264.1 12.6 %ffn.1 = (f32[256,1536]{1,0:T(8,128)}, bf16[256,1536]{1,0:T(8,128)(2,1)}, bf16[256,1536]{1,0:T(8,128)(2,1)}, bf16[256,1024]{1,0:T(8,128)(2,1)}, bf16[256,2048]{1...) custom-call(s32[3]{0:T(128)} %pad_add_fusion.1.scal, ...), custom_call_target="tpu_custom_call" | custom-call | flops 4831838208 | bytes 9437184 | tf_op jit(solution)/shard_map/ffn/pallas_call | solution.py:220
  276.9 3.3 convolution_convert_fusion
  289.9 5.2 collective-permute-done.37
  297.7 5.7 mid.1
  308.8 2.2 fusion.9
  313.6 3.4 all-to-all-start.3
  319.5 23.2 %all-to-all-done.3 = bf16[8,256,64]{1,2,0:T(8,128)(2,1)S(1)} async-done(((bf16[8,256,64]{1,2,0:T(8,128)(2,1)}), bf16[8,256,64]{1,2,0:T(8,128)(2,1)S(1)}, u32[]{:S(2)}, u32[]{:S(2)}) %all-to-all-start.3) | async-done | bytes 262176 | tf_op jit(solution)/shard_map/all_to_all | solution.py:767
  343.7 2.8 add_convert_fusion.2
  348.1 2.7 add_convert_fusion.3
  351.2 12.0 %attend_text_back.1 = (bf16[2048,128]{1,0:T(8,128)(2,1)}, f32[64,2048]{1,0:T(8,128)}, f32[1,2048]{1,0:T(1,128)}) custom-call(s32[4,4]{1,0:T(4,128)} %pad_add_fusion.table, f32[1]{0:T(128)} %bitcast.14.gate, bf16[2048,192]{1,0:T(8,128)(2,1)} %bitcast.141, bf16[2048,64]{1,0:T(8,128)(2,1)} %bitcast.149, bf16[2048,128]{1,0:T(8,128)(2,1)} %add_convert_fusion.10.kv_ref, ...), custom_call_target="tpu_custom_call" | custom-call | flops 335544320 | bytes 2621440 | tf_op jit(solution)/shard_map/attend_text_back/pallas_call | solution.py:220
  367.0 19.2 %attend_back.1 = bf16[2048,192]{1,0:T(8,128)(2,1)} custom-call(s32[4,4]{1,0:T(4,128)} %pad_add_fusion.table, bf16[2048,192]{1,0:T(8,128)(2,1)} %bitcast.142, bf16[2048,64]{1,0:T(8,128)(2,1)} %bitcast.150, bf16[2048,192]{1,0:T(8,128)(2,1)} %bitcast.143, f32[64,2048]{1,0:T(8,128)} %get-tuple-element.98.self_ref, f32[1,2048]{1,0:T(1,128)} %get-tuple-element.119.stat_ref, ...), custom_call_target="tpu_custom_call" | custom-call | flops 2684354560 | bytes 2621440 | tf_op jit(solution)/shard_map/attend_back/pallas_call | solution.py:220
  388.4 4.1 all-to-all-start.4
  398.0 17.5 %collective-permute-done.58.refs_2_ = bf16[2048,128]{1,0:T(8,128)(2,1)} collective-permute-done((bf16[2048,128]{1,0:T(8,128)(2,1)}, bf16[2048,128]{1,0:T(8,128)(2,1)}, u32[]{:S(2)}, u32[]{:S(2)}) %collective-permute-start.58) | collective-permute-done | bytes 524320 | tf_op jit(solution)/shard_map/ppermute | solution.py:82
  415.6 6.0 %collective-permute-start.63 = (bf16[2048,128]{1,0:T(8,128)(2,1)}, bf16[2048,128]{1,0:T(8,128)(2,1)}, u32[]{:S(2)}, u32[]{:S(2)}) collective-permute-start(bf16[2048,128]{1,0:T(8,128)(2,1)} %collective-permute-done.62.refs_7_), channel_id=1, source_target_pairs={{0,8},{8,16},{16,24},{24,28},{28,20},{20,12},{12,4},{4,0},{1,9},{9... | collective-permute-start | bytes 1572872 | tf_op jit(solution)/shard_map/ppermute | solution.py:82
  421.6 2.7 add_convert_fusion
  425.8 6.2 %qkv_back.1 = (bf16[256,1152]{1,0:T(8,128)(2,1)}, bf16[128,1536]{1,0:T(8,128)(2,1)}, bf16[128,1536]{1,0:T(8,128)(2,1)}) custom-call(s32[3]{0:T(128)} %pad_add_fusion.1.scal, bf16[8,256,192]{2,1,0:T(8,128)(2,1)} %copy.152.slab_ref, bf16[192,1536]{1,0:T(8,128)(2,1)} %copy-done, bf16[192,1536]{1,0:T(8,128)(2,1)} %copy-done.4, bf16[192,1536]{1,0:T(8,128)(2,1)} %copy-done.7, ...), custom_call_target="tpu_custom_call" | custom-call | flops 905969664 | bytes 3538944 | tf_op jit(solution)/shard_map/qkv_back/pallas_call | solution.py:220
  432.0 2.3 convolution_convert_fusion.1
  437.7 2.7 add_convert_fusion.1
  442.4 8.3 %side.1 = (f32[256,1536]{1,0:T(8,128)}, f32[32,1536]{1,0:T(8,128)}, f32[8,1536]{1,0:T(8,128)}) custom-call(s32[3]{0:T(128)} %pad_add_fusion.1.scal, f32[256,1536]{1,0:T(8,128)} %get-tuple-element.125.mid_ref, f32[256,1536]{1,0:T(8,128)} %get-tuple-element.126.grad_ref, bf16[256,1536]{1,0:T(8,128)(2,1)} %get-tuple-element.91.g_ref, ...), custom_call_target="tpu_custom_call" | custom-call | bytes 9437184 | tf_op jit(solution)/shard_map/side/pallas_call | solution.py:220
  454.7 8.2 %collective-permute-done.53 = bf16[96,1536]{1,0:T(8,128)(2,1)S(1)} collective-permute-done((bf16[96,1536]{1,0:T(8,128)(2,1)S(1)}, bf16[96,1536]{1,0:T(8,128)(2,1)S(1)}, u32[]{:S(2)}, u32[]{:S(2)}) %collective-permute-start.53) | collective-permute-done | bytes 294944 | tf_op jit(solution)/shard_map/ppermute | solution.py:82
  463.0 2.9 collective-permute-start.64
  469.7 6.2 %collective-permute-done.64.refs_5_ = bf16[1024,128]{1,0:T(8,128)(2,1)S(1)} collective-permute-done((bf16[1024,128]{1,0:T(8,128)(2,1)S(1)}, bf16[1024,128]{1,0:T(8,128)(2,1)S(1)}, u32[]{:S(2)}, u32[]{:S(2)}) %collective-permute-start.64) | collective-permute-done | bytes 262176 | tf_op jit(solution)/shard_map/ppermute | solution.py:82
  478.4 9.1 %text_grad.1 = f32[2,512,384]{2,1,0:T(8,128)} custom-call(s32[6]{0:T(128)} %get-tuple-element.140.slab_at, bf16[512,2048]{1,0:T(8,128)(2,1)} %fusion.7.cap_ref, bf16[2048,128]{1,0:T(8,128)(2,1)} %get-tuple-element.141.refs_0_, bf16[2048,128]{1,0:T(8,128)(2,1)} %collective-permute-done.57.refs_1_, bf16[2048,128]{1,0:T(8,128)(2,1)} %collective-permute-done.58.refs_2_, ...), custom_call_target="tpu_custom_call" | custom-call | flops 1610612736 | bytes 4194304 | tf_op jit(solution)/shard_map/text_grad/pallas_call | solution.py:220
  487.5 2.5 multiply_reduce_fusion.1
  496.1 6.6 %leave.1 = (f32[256,1536]{1,0:T(8,128)}, f32[48,384]{1,0:T(8,128)}, f32[8,1536]{1,0:T(8,128)}) custom-call(s32[3]{0:T(128)} %pad_add_fusion.1.scal, bf16[256,1536]{1,0:T(8,128)(2,1)} %get-tuple-element.90.x_ref, f32[256,1536]{1,0:T(8,128)} %get-tuple-element.126.grad_ref, bf16[128,1536]{1,0:T(8,128)(2,1)} %copy-done.42, bf16[128,1536]{1,0:T(8,128)(2,1)} %copy-done.69, ...), custom_call_target="tpu_custom_call" | custom-call | bytes 6291456 | tf_op jit(solution)/shard_map/leave/pallas_call | solution.py:220
  511.9 3.6 collective-permute-done.68
  515.5 3.0 collective-permute-start.69
  534.0 2.4 collective-permute-done.56
  548.9 3.0 collective-permute-done.72
  552.2 3.3 collective-permute-done.73
  566.3 3.0 multiply_subtract_fusion.2
  572.0 3.1 multiply_subtract_fusion.1
  579.4 7.3 %multiply_subtract_fusion = (f32[128,9216]{1,0:T(8,128)}, f32[128,9216]{1,0:T(8,128)}, f32[128,9216]{1,0:T(8,128)}) fusion(f32[128,9216]{1,0:T(8,128)S(1)} %bitcast.146, f32[128,9216]{1,0:T(8,128)S(1)} %bitcast.166, f32[128,9216]{1,0:T(8,128)S(1)} %copy-done.103, f32[]{:T(128)S(6)} %min.18, bf16[8,128]{1,0:T(8,128)(2,1)S(1)} %copy-done.90, ...), kind=kOutput, calls=%fused_computation.5 | convolution fusion | flops 37748736 | bytes 28461060 | tf_op jit(solution)/shard_map/dot_general | solution.py:71
  (502 shorter events, 181.1 us)
Async XLA Ops:
  2.1 22.1 %collective-permute-start.5 = (bf16[192,1536]{1,0:T(8,128)(2,1)S(1)}, bf16[192,1536]{1,0:T(8,128)(2,1)S(1)}, u32[]{:S(2)}, u32[]{:S(2)}) collective-permute-start(bf16[192,1536]{1,0:T(8,128)(2,1)S(1)} %pad_maximum_fusion.7.refs_0_), channel_id=1, source_target_pairs={{0,4},{8,0},{16,8},{24,16},{28,24},{20,28},{12,20},{4,12},{1,5},{9... | collective-permute-start | bytes 1769480 | tf_op jit(solution)/shard_map/ppermute | solution.py:82
  5.1 19.1 %collective-permute-start.8 = (bf16[192,1536]{1,0:T(8,128)(2,1)S(1)}, bf16[192,1536]{1,0:T(8,128)(2,1)S(1)}, u32[]{:S(2)}, u32[]{:S(2)}) collective-permute-start(bf16[192,1536]{1,0:T(8,128)(2,1)S(1)} %pad_maximum_fusion.7.refs_0_), channel_id=1, source_target_pairs={{0,8},{8,16},{16,24},{24,28},{28,20},{20,12},{12,4},{4,0},{1,9},{9... | collective-permute-start | bytes 1769480 | tf_op jit(solution)/shard_map/ppermute | solution.py:82
  11.4 20.3 %all-to-all-start = ((bf16[8,256,128]{2,1,0:T(8,128)(2,1)}), bf16[8,256,128]{2,1,0:T(8,128)(2,1)}, u32[]{:S(2)}, u32[]{:S(2)}) async-start(bf16[8,256,128]{2,1,0:T(8,128)(2,1)} %caption_slabs.1), calls=%async_computation | async-start | bytes 1048576 | tf_op jit(solution)/shard_map/all_to_all | solution.py:767
  32.9 8.7 %collective-permute-start.11 = (bf16[2048,128]{0,1:T(8,128)(2,1)S(1)}, bf16[2048,128]{0,1:T(8,128)(2,1)}, u32[]{:S(2)}, u32[]{:S(2)}) collective-permute-start(bf16[2048,128]{0,1:T(8,128)(2,1)S(1)} %copy.156), channel_id=1, source_target_pairs={{0,1},{1,0},{2,3},{3,2},{4,5},{5,4},{6,7},{7,6},{8,9},{9,8},{10,11... | collective-permute-start | bytes 1572872 | tf_op jit(solution)/shard_map/ppermute | solution.py:174
  43.8 26.4 %collective-permute-start.12 = (bf16[2048,256]{0,1:T(8,128)(2,1)}, bf16[2048,256]{0,1:T(8,128)(2,1)}, u32[]{:S(2)}, u32[]{:S(2)}) collective-permute-start(bf16[2048,256]{0,1:T(8,128)(2,1)} %pad_maximum_fusion.4), channel_id=1, source_target_pairs={{0,2},{2,0},{1,3},{3,1},{4,6},{6,4},{5,7},{7,5},{8,10},{10,8},{9,1... | collective-permute-start | bytes 3145736 | tf_op jit(solution)/shard_map/ppermute | solution.py:175
  46.7 16.8 %collective-permute-start.9 = (bf16[192,1536]{1,0:T(8,128)(2,1)S(1)}, bf16[192,1536]{1,0:T(8,128)(2,1)S(1)}, u32[]{:S(2)}, u32[]{:S(2)}) collective-permute-start(bf16[192,1536]{1,0:T(8,128)(2,1)S(1)} %collective-permute-done.8.refs_8_), channel_id=1, source_target_pairs={{0,8},{8,16},{16,24},{24,28},{28,20},{20,12},{12,4},{4,0},{1,9},{9... | collective-permute-start | bytes 1769480 | tf_op jit(solution)/shard_map/ppermute | solution.py:82
  47.5 16.0 %collective-permute-start.6 = (bf16[192,1536]{1,0:T(8,128)(2,1)S(1)}, bf16[192,1536]{1,0:T(8,128)(2,1)S(1)}, u32[]{:S(2)}, u32[]{:S(2)}) collective-permute-start(bf16[192,1536]{1,0:T(8,128)(2,1)S(1)} %collective-permute-done.5.refs_1_), channel_id=1, source_target_pairs={{0,4},{8,0},{16,8},{24,16},{28,24},{20,28},{12,20},{4,12},{1,5},{9... | collective-permute-start | bytes 1769480 | tf_op jit(solution)/shard_map/ppermute | solution.py:82
  62.2 15.3 %collective-permute-start.4 = (f32[48,768]{1,0:T(8,128)S(1)}, f32[48,768]{1,0:T(8,128)S(1)}, u32[]{:S(2)}, u32[]{:S(2)}) collective-permute-start(f32[48,768]{1,0:T(8,128)S(1)} %pad_maximum_fusion.14), channel_id=1, source_target_pairs={{0,2},{2,0},{1,3},{3,1},{4,6},{6,4},{5,7},{7,5},{8,10},{10,8},{9,1... | collective-permute-start | bytes 442376 | tf_op jit(solution)/shard_map/ppermute | solution.py:175
  63.5 18.8 %collective-permute-start.10 = (bf16[192,1536]{1,0:T(8,128)(2,1)S(1)}, bf16[192,1536]{1,0:T(8,128)(2,1)S(1)}, u32[]{:S(2)}, u32[]{:S(2)}) collective-permute-start(bf16[192,1536]{1,0:T(8,128)(2,1)S(1)} %collective-permute-done.9.refs_7_), channel_id=1, source_target_pairs={{0,8},{8,16},{16,24},{24,28},{28,20},{20,12},{12,4},{4,0},{1,9},{9... | collective-permute-start | bytes 1769480 | tf_op jit(solution)/shard_map/ppermute | solution.py:82
  63.5 18.7 %collective-permute-start.7 = (bf16[192,1536]{1,0:T(8,128)(2,1)S(1)}, bf16[192,1536]{1,0:T(8,128)(2,1)S(1)}, u32[]{:S(2)}, u32[]{:S(2)}) collective-permute-start(bf16[192,1536]{1,0:T(8,128)(2,1)S(1)} %collective-permute-done.6.refs_2_), channel_id=1, source_target_pairs={{0,4},{8,0},{16,8},{24,16},{28,24},{20,28},{12,20},{4,12},{1,5},{9... | collective-permute-start | bytes 1769480 | tf_op jit(solution)/shard_map/ppermute | solution.py:82
  74.6 11.4 %collective-permute-start.15 = (bf16[1024,128]{1,0:T(8,128)(2,1)S(1)}, bf16[1024,128]{1,0:T(8,128)(2,1)S(1)}, u32[]{:S(2)}, u32[]{:S(2)}) collective-permute-start(bf16[1024,128]{1,0:T(8,128)(2,1)S(1)} %get-tuple-element.269), channel_id=1, source_target_pairs={{8,16},{16,24},{24,28},{20,12},{12,4},{4,0},{9,17},{17,25},{25,29}... | collective-permute-start | bytes 786440 | tf_op jit(solution)/shard_map/ppermute | solution.py:82
  76.2 11.4 %collective-permute-start.16 = (bf16[1024,128]{1,0:T(8,128)(2,1)S(1)}, bf16[1024,128]{1,0:T(8,128)(2,1)S(1)}, u32[]{:S(2)}, u32[]{:S(2)}) collective-permute-start(bf16[1024,128]{1,0:T(8,128)(2,1)S(1)} %get-tuple-element.267), channel_id=1, source_target_pairs={{8,0},{16,8},{24,16},{20,28},{12,20},{4,12},{9,1},{17,9},{25,17},{... | collective-permute-start | bytes 786440 | tf_op jit(solution)/shard_map/ppermute | solution.py:82
  77.5 35.5 %collective-permute-start.13 = (bf16[192,3072]{1,0:T(8,128)(2,1)S(1)}, bf16[192,3072]{1,0:T(8,128)(2,1)}, u32[]{:S(2)}, u32[]{:S(2)}) collective-permute-start(bf16[192,3072]{1,0:T(8,128)(2,1)S(1)} %copy-done.53), channel_id=1, source_target_pairs={{0,4},{8,0},{16,8},{24,16},{28,24},{20,28},{12,20},{4,12},{1,5},{9... | collective-permute-start | bytes 3538952 | tf_op jit(solution)/shard_map/ppermute | solution.py:82
  82.2 35.5 %collective-permute-start.14 = (bf16[192,3072]{1,0:T(8,128)(2,1)S(1)}, bf16[192,3072]{1,0:T(8,128)(2,1)}, u32[]{:S(2)}, u32[]{:S(2)}) collective-permute-start(bf16[192,3072]{1,0:T(8,128)(2,1)S(1)} %copy-done.53), channel_id=1, source_target_pairs={{0,8},{8,16},{16,24},{24,28},{28,20},{20,12},{12,4},{4,0},{1,9},{9... | collective-permute-start | bytes 3538952 | tf_op jit(solution)/shard_map/ppermute | solution.py:82
  82.3 40.1 %collective-permute-start.17 = (bf16[96,1536]{1,0:T(8,128)(2,1)S(1)}, bf16[96,1536]{1,0:T(8,128)(2,1)S(1)}, u32[]{:S(2)}, u32[]{:S(2)}) collective-permute-start(bf16[96,1536]{1,0:T(8,128)(2,1)S(1)} %slice.344), channel_id=1, source_target_pairs={{0,4},{8,0},{16,8},{24,16},{28,24},{20,28},{12,20},{4,12},{1,5},{9... | collective-permute-start | bytes 884744 | tf_op jit(solution)/shard_map/ppermute | solution.py:82
  86.1 38.6 %collective-permute-start.18 = (bf16[96,1536]{1,0:T(8,128)(2,1)}, bf16[96,1536]{1,0:T(8,128)(2,1)S(1)}, u32[]{:S(2)}, u32[]{:S(2)}) collective-permute-start(bf16[96,1536]{1,0:T(8,128)(2,1)} %slice.345), channel_id=1, source_target_pairs={{0,8},{8,16},{16,24},{24,28},{28,20},{20,12},{12,4},{4,0},{1,9},{9... | collective-permute-start | bytes 884744 | tf_op jit(solution)/shard_map/ppermute | solution.py:82
  88.6 49.4 %collective-permute-start.20 = (bf16[2048,128]{1,0:T(8,128)(2,1)}, bf16[2048,128]{1,0:T(8,128)(2,1)}, u32[]{:S(2)}, u32[]{:S(2)}) collective-permute-start(bf16[2048,128]{1,0:T(8,128)(2,1)} %pad_maximum_fusion.10), channel_id=1, source_target_pairs={{0,4},{8,0},{16,8},{28,24},{20,28},{12,20},{1,5},{9,1},{17,9},{29,... | collective-permute-start | bytes 1572872 | tf_op jit(solution)/shard_map/ppermute | solution.py:82
  113.0 25.0 %collective-permute-start.19 = (bf16[2048,128]{1,0:T(8,128)(2,1)}, bf16[2048,128]{1,0:T(8,128)(2,1)S(1)}, u32[]{:S(2)}, u32[]{:S(2)}) collective-permute-start(bf16[2048,128]{1,0:T(8,128)(2,1)} %pad_maximum_fusion.9), channel_id=1, source_target_pairs={{0,8},{16,24},{24,28},{28,20},{12,4},{4,0},{1,9},{17,25},{25,29},{... | collective-permute-start | bytes 1572872 | tf_op jit(solution)/shard_map/ppermute | solution.py:82
  122.3 37.8 %collective-permute-start.25 = (bf16[192,3072]{1,0:T(8,128)(2,1)}, bf16[192,3072]{1,0:T(8,128)(2,1)}, u32[]{:S(2)}, u32[]{:S(2)}) collective-permute-start(bf16[192,3072]{1,0:T(8,128)(2,1)} %collective-permute-done.13.refs_1_), channel_id=1, source_target_pairs={{0,4},{8,0},{16,8},{24,16},{28,24},{20,28},{12,20},{4,12},{1,5},{9... | collective-permute-start | bytes 3538952 | tf_op jit(solution)/shard_map/ppermute | solution.py:82
  122.4 37.7 %collective-permute-start.26 = (bf16[192,3072]{1,0:T(8,128)(2,1)}, bf16[192,3072]{1,0:T(8,128)(2,1)}, u32[]{:S(2)}, u32[]{:S(2)}) collective-permute-start(bf16[192,3072]{1,0:T(8,128)(2,1)} %collective-permute-done.14.refs_8_), channel_id=1, source_target_pairs={{0,8},{8,16},{16,24},{24,28},{28,20},{20,12},{12,4},{4,0},{1,9},{9... | collective-permute-start | bytes 3538952 | tf_op jit(solution)/shard_map/ppermute | solution.py:82
  133.2 40.9 %all-to-all-start.1 = ((bf16[8,256,192]{1,2,0:T(8,128)(2,1)}), bf16[8,256,192]{1,2,0:T(8,128)(2,1)S(1)}, u32[]{:S(2)}, u32[]{:S(2)}) async-start(bf16[8,256,192]{1,2,0:T(8,128)(2,1)} %copy.140), calls=%async_computation.1 | async-start | bytes 1572864 | tf_op jit(solution)/shard_map/all_to_all | solution.py:767
  139.7 39.0 %collective-permute-start.21 = (bf16[2048,128]{1,0:T(8,128)(2,1)S(1)}, bf16[2048,128]{1,0:T(8,128)(2,1)S(1)}, u32[]{:S(2)}, u32[]{:S(2)}) collective-permute-start(bf16[2048,128]{1,0:T(8,128)(2,1)S(1)} %get-tuple-element.265), channel_id=1, source_target_pairs={{0,8},{8,16},{24,28},{28,20},{20,12},{4,0},{1,9},{9,17},{25,29},{2... | collective-permute-start | bytes 1572872 | tf_op jit(solution)/shard_map/ppermute | solution.py:82
  143.6 36.0 %collective-permute-start.22 = (bf16[2048,128]{1,0:T(8,128)(2,1)S(1)}, bf16[2048,128]{1,0:T(8,128)(2,1)S(1)}, u32[]{:S(2)}, u32[]{:S(2)}) collective-permute-start(bf16[2048,128]{1,0:T(8,128)(2,1)S(1)} %get-tuple-element.264), channel_id=1, source_target_pairs={{0,4},{8,0},{24,16},{28,24},{20,28},{4,12},{1,5},{9,1},{25,17},{29... | collective-permute-start | bytes 1572872 | tf_op jit(solution)/shard_map/ppermute | solution.py:82
  160.1 41.9 %collective-permute-start.27 = (bf16[192,3072]{1,0:T(8,128)(2,1)}, bf16[192,3072]{1,0:T(8,128)(2,1)}, u32[]{:S(2)}, u32[]{:S(2)}) collective-permute-start(bf16[192,3072]{1,0:T(8,128)(2,1)} %collective-permute-done.25.refs_2_), channel_id=1, source_target_pairs={{0,4},{8,0},{16,8},{24,16},{28,24},{20,28},{12,20},{4,12},{1,5},{9... | collective-permute-start | bytes 3538952 | tf_op jit(solution)/shard_map/ppermute | solution.py:82
  160.1 45.5 %collective-permute-start.28 = (bf16[192,3072]{1,0:T(8,128)(2,1)}, bf16[192,3072]{1,0:T(8,128)(2,1)}, u32[]{:S(2)}, u32[]{:S(2)}) collective-permute-start(bf16[192,3072]{1,0:T(8,128)(2,1)} %collective-permute-done.26.refs_7_), channel_id=1, source_target_pairs={{0,8},{8,16},{16,24},{24,28},{28,20},{20,12},{12,4},{4,0},{1,9},{9... | collective-permute-start | bytes 3538952 | tf_op jit(solution)/shard_map/ppermute | solution.py:82
  181.9 31.3 %collective-permute-start.23 = (bf16[2048,128]{1,0:T(8,128)(2,1)}, bf16[2048,128]{1,0:T(8,128)(2,1)S(1)}, u32[]{:S(2)}, u32[]{:S(2)}) collective-permute-start(bf16[2048,128]{1,0:T(8,128)(2,1)} %get-tuple-element.262), channel_id=1, source_target_pairs={{0,8},{8,16},{16,24},{28,20},{20,12},{12,4},{1,9},{9,17},{17,25},{... | collective-permute-start | bytes 1572872 | tf_op jit(solution)/shard_map/ppermute | solution.py:82
  185.3 27.9 %collective-permute-start.24 = (bf16[2048,128]{1,0:T(8,128)(2,1)S(1)}, bf16[2048,128]{1,0:T(8,128)(2,1)S(1)}, u32[]{:S(2)}, u32[]{:S(2)}) collective-permute-start(bf16[2048,128]{1,0:T(8,128)(2,1)S(1)} %get-tuple-element.263), channel_id=1, source_target_pairs={{0,4},{16,8},{24,16},{28,24},{12,20},{4,12},{1,5},{17,9},{25,17},{... | collective-permute-start | bytes 1572872 | tf_op jit(solution)/shard_map/ppermute | solution.py:82
  203.1 38.3 %collective-permute-start.29 = (bf16[96,3072]{1,0:T(8,128)(2,1)S(1)}, bf16[96,3072]{1,0:T(8,128)(2,1)S(1)}, u32[]{:S(2)}, u32[]{:S(2)}) collective-permute-start(bf16[96,3072]{1,0:T(8,128)(2,1)S(1)} %slice.351), channel_id=1, source_target_pairs={{0,4},{8,0},{16,8},{24,16},{28,24},{20,28},{12,20},{4,12},{1,5},{9... | collective-permute-start | bytes 1769480 | tf_op jit(solution)/shard_map/ppermute | solution.py:82
  206.7 34.7 %collective-permute-start.30 = (bf16[96,3072]{1,0:T(8,128)(2,1)S(1)}, bf16[96,3072]{1,0:T(8,128)(2,1)}, u32[]{:S(2)}, u32[]{:S(2)}) collective-permute-start(bf16[96,3072]{1,0:T(8,128)(2,1)S(1)} %slice.352), channel_id=1, source_target_pairs={{0,8},{8,16},{16,24},{24,28},{28,20},{20,12},{12,4},{4,0},{1,9},{9... | collective-permute-start | bytes 1769480 | tf_op jit(solution)/shard_map/ppermute | solution.py:82
  250.2 11.2 %collective-permute-start.32 = (bf16[128,1536]{1,0:T(8,128)(2,1)S(1)}, bf16[128,1536]{1,0:T(8,128)(2,1)S(1)}, u32[]{:S(2)}, u32[]{:S(2)}) collective-permute-start(bf16[128,1536]{1,0:T(8,128)(2,1)S(1)} %add_convert_fusion.22), channel_id=1, source_target_pairs={{0,2},{2,0},{1,3},{3,1},{4,6},{6,4},{5,7},{7,5},{8,10},{10,8},{9,1... | collective-permute-start | bytes 1179656 | tf_op jit(solution)/shard_map/ppermute | solution.py:182
  283.6 11.5 %collective-permute-start.37 = (bf16[128,1536]{1,0:T(8,128)(2,1)S(1)}, bf16[128,1536]{1,0:T(8,128)(2,1)S(1)}, u32[]{:S(2)}, u32[]{:S(2)}) collective-permute-start(bf16[128,1536]{1,0:T(8,128)(2,1)S(1)} %add_convert_fusion.20), channel_id=1, source_target_pairs={{0,2},{2,0},{1,3},{3,1},{4,6},{6,4},{5,7},{7,5},{8,10},{10,8},{9,1... | collective-permute-start | bytes 1179656 | tf_op jit(solution)/shard_map/ppermute | solution.py:182
  287.7 15.7 %collective-permute-start.34 = (bf16[96,3072]{1,0:T(8,128)(2,1)}, bf16[96,3072]{1,0:T(8,128)(2,1)}, u32[]{:S(2)}, u32[]{:S(2)}) collective-permute-start(bf16[96,3072]{1,0:T(8,128)(2,1)} %get-tuple-element.299), channel_id=1, source_target_pairs={{0,8},{8,16},{16,24},{24,28},{28,20},{20,12},{12,4},{4,0},{1,9},{9... | collective-permute-start | bytes 1769480 | tf_op jit(solution)/shard_map/ppermute | solution.py:82
  287.7 15.8 %collective-permute-start.35 = (bf16[96,3072]{1,0:T(8,128)(2,1)}, bf16[96,3072]{1,0:T(8,128)(2,1)}, u32[]{:S(2)}, u32[]{:S(2)}) collective-permute-start(bf16[96,3072]{1,0:T(8,128)(2,1)} %get-tuple-element.298), channel_id=1, source_target_pairs={{0,4},{8,0},{16,8},{24,16},{28,24},{20,28},{12,20},{4,12},{1,5},{9... | collective-permute-start | bytes 1769480 | tf_op jit(solution)/shard_map/ppermute | solution.py:82
  305.8 37.8 %collective-permute-start.40 = (bf16[192,3072]{1,0:T(8,128)(2,1)}, bf16[192,3072]{1,0:T(8,128)(2,1)}, u32[]{:S(2)}, u32[]{:S(2)}) collective-permute-start(bf16[192,3072]{1,0:T(8,128)(2,1)} %pad_maximum_fusion.3), channel_id=1, source_target_pairs={{0,4},{8,0},{16,8},{24,16},{28,24},{20,28},{12,20},{4,12},{1,5},{9... | collective-permute-start | bytes 3538952 | tf_op jit(solution)/shard_map/ppermute | solution.py:82
  311.0 32.6 %collective-permute-start.39 = (bf16[192,3072]{1,0:T(8,128)(2,1)}, bf16[192,3072]{1,0:T(8,128)(2,1)}, u32[]{:S(2)}, u32[]{:S(2)}) collective-permute-start(bf16[192,3072]{1,0:T(8,128)(2,1)} %fusion.9), channel_id=1, source_target_pairs={{0,8},{8,16},{16,24},{24,28},{28,20},{20,12},{12,4},{4,0},{1,9},{9... | collective-permute-start | bytes 3538952 | tf_op jit(solution)/shard_map/ppermute | solution.py:82
  313.6 29.1 %all-to-all-start.3 = ((bf16[8,256,64]{1,2,0:T(8,128)(2,1)}), bf16[8,256,64]{1,2,0:T(8,128)(2,1)S(1)}, u32[]{:S(2)}, u32[]{:S(2)}) async-start(bf16[8,256,64]{1,2,0:T(8,128)(2,1)} %copy.147), calls=%async_computation.3 | async-start | bytes 524288 | tf_op jit(solution)/shard_map/all_to_all | solution.py:767
  318.5 46.7 %collective-permute-start.43 = (bf16[128,1536]{1,0:T(8,128)(2,1)S(1)}, bf16[128,1536]{1,0:T(8,128)(2,1)S(1)}, u32[]{:S(2)}, u32[]{:S(2)}) collective-permute-start(bf16[128,1536]{1,0:T(8,128)(2,1)S(1)} %copy-done.105), channel_id=1, source_target_pairs={{0,1},{1,0},{2,3},{3,2},{4,5},{5,4},{6,7},{7,6},{8,9},{9,8},{10,11... | collective-permute-start | bytes 1179656 | tf_op jit(solution)/shard_map/ppermute | solution.py:180
  346.5 75.0 %collective-permute-start.42 = (bf16[192,3072]{1,0:T(8,128)(2,1)}, bf16[192,3072]{1,0:T(8,128)(2,1)}, u32[]{:S(2)}, u32[]{:S(2)}) collective-permute-start(bf16[192,3072]{1,0:T(8,128)(2,1)} %add_convert_fusion.2), channel_id=1, source_target_pairs={{0,4},{8,0},{16,8},{24,16},{28,24},{20,28},{12,20},{4,12},{1,5},{9... | collective-permute-start | bytes 3538952 | tf_op jit(solution)/shard_map/ppermute | solution.py:82
  350.8 70.7 %collective-permute-start.41 = (bf16[192,3072]{1,0:T(8,128)(2,1)}, bf16[192,3072]{1,0:T(8,128)(2,1)}, u32[]{:S(2)}, u32[]{:S(2)}) collective-permute-start(bf16[192,3072]{1,0:T(8,128)(2,1)} %add_convert_fusion.3), channel_id=1, source_target_pairs={{0,8},{8,16},{16,24},{24,28},{28,20},{20,12},{12,4},{4,0},{1,9},{9... | collective-permute-start | bytes 3538952 | tf_op jit(solution)/shard_map/ppermute | solution.py:82
  363.2 30.3 %collective-permute-start.57 = (bf16[2048,128]{1,0:T(8,128)(2,1)}, bf16[2048,128]{1,0:T(8,128)(2,1)}, u32[]{:S(2)}, u32[]{:S(2)}) collective-permute-start(bf16[2048,128]{1,0:T(8,128)(2,1)} %get-tuple-element.141.refs_0_), channel_id=1, source_target_pairs={{0,4},{8,0},{16,8},{24,16},{28,24},{20,28},{12,20},{4,12},{1,5},{9... | collective-permute-start | bytes 1572872 | tf_op jit(solution)/shard_map/ppermute | solution.py:82
  364.8 30.7 %collective-permute-start.61 = (bf16[2048,128]{1,0:T(8,128)(2,1)}, bf16[2048,128]{1,0:T(8,128)(2,1)}, u32[]{:S(2)}, u32[]{:S(2)}) collective-permute-start(bf16[2048,128]{1,0:T(8,128)(2,1)} %get-tuple-element.141.refs_0_), channel_id=1, source_target_pairs={{0,8},{8,16},{16,24},{24,28},{28,20},{20,12},{12,4},{4,0},{1,9},{9... | collective-permute-start | bytes 1572872 | tf_op jit(solution)/shard_map/ppermute | solution.py:82
  365.4 30.2 %collective-permute-start.44 = (bf16[128,1536]{1,0:T(8,128)(2,1)S(1)}, bf16[128,1536]{1,0:T(8,128)(2,1)}, u32[]{:S(2)}, u32[]{:S(2)}) collective-permute-start(bf16[128,1536]{1,0:T(8,128)(2,1)S(1)} %add_convert_fusion.18), channel_id=1, source_target_pairs={{0,2},{2,0},{1,3},{3,1},{4,6},{6,4},{5,7},{7,5},{8,10},{10,8},{9,1... | collective-permute-start | bytes 1179656 | tf_op jit(solution)/shard_map/ppermute | solution.py:182
  388.4 36.1 %all-to-all-start.4 = ((bf16[8,256,192]{1,2,0:T(8,128)(2,1)}), bf16[8,256,192]{1,2,0:T(8,128)(2,1)S(1)}, u32[]{:S(2)}, u32[]{:S(2)}) async-start(bf16[8,256,192]{1,2,0:T(8,128)(2,1)} %copy.151), calls=%async_computation.4 | async-start | bytes 1572864 | tf_op jit(solution)/shard_map/all_to_all | solution.py:767
  393.5 22.1 %collective-permute-start.58 = (bf16[2048,128]{1,0:T(8,128)(2,1)}, bf16[2048,128]{1,0:T(8,128)(2,1)}, u32[]{:S(2)}, u32[]{:S(2)}) collective-permute-start(bf16[2048,128]{1,0:T(8,128)(2,1)} %collective-permute-done.57.refs_1_), channel_id=1, source_target_pairs={{0,4},{8,0},{16,8},{24,16},{28,24},{20,28},{12,20},{4,12},{1,5},{9... | collective-permute-start | bytes 1572872 | tf_op jit(solution)/shard_map/ppermute | solution.py:82
  395.5 20.1 %collective-permute-start.62 = (bf16[2048,128]{1,0:T(8,128)(2,1)}, bf16[2048,128]{1,0:T(8,128)(2,1)}, u32[]{:S(2)}, u32[]{:S(2)}) collective-permute-start(bf16[2048,128]{1,0:T(8,128)(2,1)} %collective-permute-done.61.refs_8_), channel_id=1, source_target_pairs={{0,8},{8,16},{16,24},{24,28},{28,20},{20,12},{12,4},{4,0},{1,9},{9... | collective-permute-start | bytes 1572872 | tf_op jit(solution)/shard_map/ppermute | solution.py:82
  396.7 43.7 %collective-permute-start.45 = (bf16[128,1536]{1,0:T(8,128)(2,1)S(1)}, bf16[128,1536]{1,0:T(8,128)(2,1)}, u32[]{:S(2)}, u32[]{:S(2)}) collective-permute-start(bf16[128,1536]{1,0:T(8,128)(2,1)S(1)} %add_convert_fusion.17.fm_ref), channel_id=1, source_target_pairs={{0,1},{1,0},{2,3},{3,2},{4,5},{5,4},{6,7},{7,6},{8,9},{9,8},{10,11... | collective-permute-start | bytes 1179656 | tf_op jit(solution)/shard_map/ppermute | solution.py:183
  415.6 35.2 %collective-permute-start.59 = (bf16[2048,128]{1,0:T(8,128)(2,1)}, bf16[2048,128]{1,0:T(8,128)(2,1)}, u32[]{:S(2)}, u32[]{:S(2)}) collective-permute-start(bf16[2048,128]{1,0:T(8,128)(2,1)} %collective-permute-done.58.refs_2_), channel_id=1, source_target_pairs={{0,4},{8,0},{16,8},{24,16},{28,24},{20,28},{12,20},{4,12},{1,5},{9... | collective-permute-start | bytes 1572872 | tf_op jit(solution)/shard_map/ppermute | solution.py:82
  415.6 36.3 %collective-permute-start.63 = (bf16[2048,128]{1,0:T(8,128)(2,1)}, bf16[2048,128]{1,0:T(8,128)(2,1)}, u32[]{:S(2)}, u32[]{:S(2)}) collective-permute-start(bf16[2048,128]{1,0:T(8,128)(2,1)} %collective-permute-done.62.refs_7_), channel_id=1, source_target_pairs={{0,8},{8,16},{16,24},{24,28},{28,20},{20,12},{12,4},{4,0},{1,9},{9... | collective-permute-start | bytes 1572872 | tf_op jit(solution)/shard_map/ppermute | solution.py:82
  424.2 82.2 %collective-permute-start.66 = (bf16[192,3072]{1,0:T(8,128)(2,1)}, bf16[192,3072]{1,0:T(8,128)(2,1)}, u32[]{:S(2)}, u32[]{:S(2)}) collective-permute-start(bf16[192,3072]{1,0:T(8,128)(2,1)} %add_convert_fusion), channel_id=1, source_target_pairs={{0,4},{8,0},{16,8},{24,16},{28,24},{20,28},{12,20},{4,12},{1,5},{9... | collective-permute-start | bytes 3538952 | tf_op jit(solution)/shard_map/ppermute | solution.py:82
  435.6 17.3 %collective-permute-start.49 = (bf16[96,1536]{1,0:T(8,128)(2,1)S(1)}, bf16[96,1536]{1,0:T(8,128)(2,1)S(1)}, u32[]{:S(2)}, u32[]{:S(2)}) collective-permute-start(bf16[96,1536]{1,0:T(8,128)(2,1)S(1)} %get-tuple-element.302), channel_id=1, source_target_pairs={{0,8},{8,16},{16,24},{24,28},{28,20},{20,12},{12,4},{4,0},{1,9},{9... | collective-permute-start | bytes 884744 | tf_op jit(solution)/shard_map/ppermute | solution.py:82
  440.4 66.0 %collective-permute-start.65 = (bf16[192,3072]{1,0:T(8,128)(2,1)}, bf16[192,3072]{1,0:T(8,128)(2,1)}, u32[]{:S(2)}, u32[]{:S(2)}) collective-permute-start(bf16[192,3072]{1,0:T(8,128)(2,1)} %add_convert_fusion.1), channel_id=1, source_target_pairs={{0,8},{8,16},{16,24},{24,28},{28,20},{20,12},{12,4},{4,0},{1,9},{9... | collective-permute-start | bytes 3538952 | tf_op jit(solution)/shard_map/ppermute | solution.py:82
  450.8 15.1 %collective-permute-start.46 = (bf16[128,1536]{1,0:T(8,128)(2,1)S(1)}, bf16[128,1536]{1,0:T(8,128)(2,1)S(1)}, u32[]{:S(2)}, u32[]{:S(2)}) collective-permute-start(bf16[128,1536]{1,0:T(8,128)(2,1)S(1)} %copy-done.106), channel_id=1, source_target_pairs={{0,1},{1,0},{2,3},{3,2},{4,5},{5,4},{6,7},{7,6},{8,9},{9,8},{10,11... | collective-permute-start | bytes 1179656 | tf_op jit(solution)/shard_map/ppermute | solution.py:180
  451.9 11.1 %collective-permute-start.53 = (bf16[96,1536]{1,0:T(8,128)(2,1)S(1)}, bf16[96,1536]{1,0:T(8,128)(2,1)S(1)}, u32[]{:S(2)}, u32[]{:S(2)}) collective-permute-start(bf16[96,1536]{1,0:T(8,128)(2,1)S(1)} %get-tuple-element.303), channel_id=1, source_target_pairs={{0,4},{8,0},{16,8},{24,16},{28,24},{20,28},{12,20},{4,12},{1,5},{9... | collective-permute-start | bytes 884744 | tf_op jit(solution)/shard_map/ppermute | solution.py:82
  452.9 14.9 %collective-permute-start.60 = (bf16[1024,128]{1,0:T(8,128)(2,1)S(1)}, bf16[1024,128]{1,0:T(8,128)(2,1)S(1)}, u32[]{:S(2)}, u32[]{:S(2)}) collective-permute-start(bf16[1024,128]{1,0:T(8,128)(2,1)S(1)} %slice.397), channel_id=1, source_target_pairs={{0,4},{8,0},{16,8},{24,16},{28,24},{20,28},{12,20},{4,12},{1,5},{9... | collective-permute-start | bytes 786440 | tf_op jit(solution)/shard_map/ppermute | solution.py:82
  463.0 13.0 %collective-permute-start.64 = (bf16[1024,128]{1,0:T(8,128)(2,1)S(1)}, bf16[1024,128]{1,0:T(8,128)(2,1)S(1)}, u32[]{:S(2)}, u32[]{:S(2)}) collective-permute-start(bf16[1024,128]{1,0:T(8,128)(2,1)S(1)} %slice.398), channel_id=1, source_target_pairs={{0,8},{8,16},{16,24},{24,28},{28,20},{20,12},{12,4},{4,0},{1,9},{9... | collective-permute-start | bytes 786440 | tf_op jit(solution)/shard_map/ppermute | solution.py:82
  466.1 23.9 %collective-permute-start.47 = (bf16[128,1536]{1,0:T(8,128)(2,1)S(1)}, bf16[128,1536]{1,0:T(8,128)(2,1)}, u32[]{:S(2)}, u32[]{:S(2)}) collective-permute-start(bf16[128,1536]{1,0:T(8,128)(2,1)S(1)} %add_convert_fusion.16), channel_id=1, source_target_pairs={{0,2},{2,0},{1,3},{3,1},{4,6},{6,4},{5,7},{7,5},{8,10},{10,8},{9,1... | collective-permute-start | bytes 1179656 | tf_op jit(solution)/shard_map/ppermute | solution.py:182
  467.8 23.4 %collective-permute-start.50 = (bf16[192,1536]{1,0:T(8,128)(2,1)}, bf16[192,1536]{1,0:T(8,128)(2,1)S(1)}, u32[]{:S(2)}, u32[]{:S(2)}) collective-permute-start(bf16[192,1536]{1,0:T(8,128)(2,1)} %fusion.21), channel_id=1, source_target_pairs={{0,8},{8,16},{16,24},{24,28},{28,20},{20,12},{12,4},{4,0},{1,9},{9... | collective-permute-start | bytes 1769480 | tf_op jit(solution)/shard_map/ppermute | solution.py:82
  476.6 16.2 %collective-permute-start.54 = (bf16[192,1536]{1,0:T(8,128)(2,1)}, bf16[192,1536]{1,0:T(8,128)(2,1)S(1)}, u32[]{:S(2)}, u32[]{:S(2)}) collective-permute-start(bf16[192,1536]{1,0:T(8,128)(2,1)} %pad_maximum_fusion.8), channel_id=1, source_target_pairs={{0,4},{8,0},{16,8},{24,16},{28,24},{20,28},{12,20},{4,12},{1,5},{9... | collective-permute-start | bytes 1769480 | tf_op jit(solution)/shard_map/ppermute | solution.py:82
  492.1 26.4 %collective-permute-start.51 = (bf16[192,1536]{1,0:T(8,128)(2,1)}, bf16[192,1536]{1,0:T(8,128)(2,1)}, u32[]{:S(2)}, u32[]{:S(2)}) collective-permute-start(bf16[192,1536]{1,0:T(8,128)(2,1)} %add_convert_fusion.7), channel_id=1, source_target_pairs={{0,8},{8,16},{16,24},{24,28},{28,20},{20,12},{12,4},{4,0},{1,9},{9... | collective-permute-start | bytes 1769480 | tf_op jit(solution)/shard_map/ppermute | solution.py:82
  493.8 28.0 %collective-permute-start.55 = (bf16[192,1536]{1,0:T(8,128)(2,1)}, bf16[192,1536]{1,0:T(8,128)(2,1)}, u32[]{:S(2)}, u32[]{:S(2)}) collective-permute-start(bf16[192,1536]{1,0:T(8,128)(2,1)} %add_convert_fusion.5), channel_id=1, source_target_pairs={{0,4},{8,0},{16,8},{24,16},{28,24},{20,28},{12,20},{4,12},{1,5},{9... | collective-permute-start | bytes 1769480 | tf_op jit(solution)/shard_map/ppermute | solution.py:82
  515.5 8.4 %collective-permute-start.69 = (f32[64,384]{1,0:T(8,128)S(1)}, f32[64,384]{1,0:T(8,128)S(1)}, u32[]{:S(2)}, u32[]{:S(2)}) collective-permute-start(f32[64,384]{1,0:T(8,128)S(1)} %add.416), channel_id=1, source_target_pairs={{0,16},{4,20},{8,24},{12,28},{16,0},{20,4},{24,8},{28,12},{1,17},{... | collective-permute-start | bytes 294920 | tf_op jit(solution)/shard_map/ppermute | solution.py:161
  519.8 14.2 %collective-permute-start.52 = (bf16[192,1536]{1,0:T(8,128)(2,1)S(1)}, bf16[192,1536]{1,0:T(8,128)(2,1)}, u32[]{:S(2)}, u32[]{:S(2)}) collective-permute-start(bf16[192,1536]{1,0:T(8,128)(2,1)S(1)} %add_convert_fusion.6), channel_id=1, source_target_pairs={{0,8},{8,16},{16,24},{24,28},{28,20},{20,12},{12,4},{4,0},{1,9},{9... | collective-permute-start | bytes 1769480 | tf_op jit(solution)/shard_map/ppermute | solution.py:82
  523.0 13.4 %collective-permute-start.56 = (bf16[192,1536]{1,0:T(8,128)(2,1)S(1)}, bf16[192,1536]{1,0:T(8,128)(2,1)}, u32[]{:S(2)}, u32[]{:S(2)}) collective-permute-start(bf16[192,1536]{1,0:T(8,128)(2,1)S(1)} %add_convert_fusion.4), channel_id=1, source_target_pairs={{0,4},{8,0},{16,8},{24,16},{28,24},{20,28},{12,20},{4,12},{1,5},{9... | collective-permute-start | bytes 1769480 | tf_op jit(solution)/shard_map/ppermute | solution.py:82
  526.0 17.5 %collective-permute-start.75 = (bf16[48,384]{1,0:T(8,128)(2,1)}, bf16[48,384]{1,0:T(8,128)(2,1)}, u32[]{:S(2)}, u32[]{:S(2)}) collective-permute-start(bf16[48,384]{1,0:T(8,128)(2,1)} %slice.481), channel_id=1, source_target_pairs={{0,1},{1,0},{2,3},{3,2},{4,5},{5,4},{6,7},{7,6},{8,9},{9,8},{10,11... | collective-permute-start | bytes 110600 | tf_op jit(solution)/shard_map/ppermute | solution.py:174
  (129 other events, 855.1 us)

commit v6 on v5

--- a/solution.py
+++ b/solution.py
@@ -570,7 +570,7 @@
         out_ref[:, at] = jnp.transpose(source_ref[at, low : low + HD].astype(f32)).astype(bf16)
         return 0
 
-    lax.fori_loop(0, source_ref.shape[0] // block, one, 0)
+    lax.fori_loop(0, source_ref.shape[0] // block, one, 0, unroll=source_ref.shape[0] <= 2048)
 
 
 def self_kernel(table, q_ref, all_ref, sq_ref, sk_ref, out_ref, stat_ref, k_ref, vt_ref, *, block_k):
@@ -895,8 +895,9 @@
     )[0]
     qkv_head = exchange(slabs).reshape(count, 3 * HD)
 
-    block_q = math.gcd(count, 512)
-    block_k = math.gcd(count, 512)
+    most = 1024 if count <= 4096 else 512
+    block_q = math.gcd(count, most)
+    block_k = math.gcd(count, most)
     table = attention_table(segments, block_q, block_k)
     tanh_cross = jnp.tanh(cross_gates)
     my_gate = jnp.sum(jnp.where(jnp.arange(heads) == my_head, tanh_cross, 0.0)).reshape(1)

time: 600 us -> 597 us (level)
  Pallas kernels: 135 us -> 128 us
    pallas_call x16, Pallas kernels: 135 us -> 128 us  [call(): pl.pallas_call(kernel, out_shape=tuple((shape_of(shape, dtype) for shape,...]
  transfers between devices with their start and end apart: 81 -> 81, of which waited for: 32 -> 33; matrix products, arithmetic and copies ran while one was open for 18% -> 18% of each run, Pallas kernels for 20% -> 19%
where the time goes in v6:
time: 597 us; the launch traced here: 586 us
  waiting for transfers between devices  171 us (29%)
  Pallas kernels  128 us (21%)
  starting transfers between devices  118 us (20%)
  other arithmetic  82.4 us (14%)
  local copies, waits for them, and re-layouts  43.7 us (7%)
  matrix products  18.8 us (3%)
  blocking collectives  13.8 us (2%)
  between operations  9.66 us (2%)
    pallas_call x16, Pallas kernels, call(): pl.pallas_call(kernel, out_shape=tuple((shape_of(shape, dtype) for shape,...  128 us
    ppermute x48, waiting for transfers between devices, hop(): return lax.ppermute(value, 'seq', pairs)  88.7 us
    ppermute x48, starting transfers between devices, hop(): return lax.ppermute(value, 'seq', pairs)  76.8 us
    all_to_all x4, waiting for transfers between devices, exchange(): return lax.all_to_all(slabs, 'seq', 0, 0, tiled=True)  37 us
    ppermute x11, waiting for transfers between devices, butterfly(): lax.ppermute(value, axis, [(i, i ^ step) for i in range(size)])  21.1 us
    convert_element_type x15, other arithmetic, plus(): return (part.astype(f32) + moved.astype(f32)).astype(bf16)  21.1 us
    dot_general x7, matrix products, dot(): return lax.dot_general(a, b, (dims, ((), ())), preferred_element_type=f32)  18.8 us
    all_to_all x4, starting transfers between devices, exchange(): return lax.all_to_all(slabs, 'seq', 0, 0, tiled=True)  18.5 us
  transfers between devices with their start and end apart: 81, of which 33 were waited for; matrix products, arithmetic and copies ran while one was open for 18% of the time, Pallas kernels for 19%

profile of v6, /device:TPU:0, one launch (start us, length us, event | category | flops | bytes accessed | tf_op | source)
XLA Modules:
  0.0 585.8 jit_solution(3170940340562621435)
XLA Ops:
  2.1 3.0 collective-permute-start.5
  5.8 5.5 caption_slabs.1
  11.4 6.2 %all-to-all-start = ((bf16[8,256,128]{2,1,0:T(8,128)(2,1)}), bf16[8,256,128]{2,1,0:T(8,128)(2,1)}, u32[]{:S(2)}, u32[]{:S(2)}) async-start(bf16[8,256,128]{2,1,0:T(8,128)(2,1)} %caption_slabs.1), calls=%async_computation | async-start | bytes 1048576 | tf_op jit(solution)/shard_map/all_to_all | solution.py:767
  18.9 5.2 modulation.1
  24.2 7.5 %all-to-all-done = bf16[8,256,128]{2,1,0:T(8,128)(2,1)} async-done(((bf16[8,256,128]{2,1,0:T(8,128)(2,1)}), bf16[8,256,128]{2,1,0:T(8,128)(2,1)}, u32[]{:S(2)}, u32[]{:S(2)}) %all-to-all-start) | async-done | bytes 524320 | tf_op jit(solution)/shard_map/all_to_all | solution.py:767
  37.1 2.6 collective-permute-done
  50.6 2.7 collective-permute-done.2
  55.5 3.8 text_heads.1
  65.5 4.7 collective-permute-done.12
  72.0 2.4 convolution_convert_fusion.3
  77.5 4.0 collective-permute-start.13
  88.6 2.5 collective-permute-start.20
  92.0 21.1 %collective-permute-done.13.refs_1_ = bf16[192,3072]{1,0:T(8,128)(2,1)} collective-permute-done((bf16[192,3072]{1,0:T(8,128)(2,1)S(1)}, bf16[192,3072]{1,0:T(8,128)(2,1)}, u32[]{:S(2)}, u32[]{:S(2)}) %collective-permute-start.13) | collective-permute-done | bytes 1179680 | tf_op jit(solution)/shard_map/ppermute | solution.py:82
  113.0 3.9 collective-permute-start.19
  117.7 4.6 enter.1
  122.4 2.4 collective-permute-start.26
  125.5 5.6 project.1
  133.3 4.8 all-to-all-start.1
  139.8 3.9 collective-permute-start.21
  147.3 12.8 %collective-permute-done.25.refs_2_ = bf16[192,3072]{1,0:T(8,128)(2,1)} collective-permute-done((bf16[192,3072]{1,0:T(8,128)(2,1)}, bf16[192,3072]{1,0:T(8,128)(2,1)}, u32[]{:S(2)}, u32[]{:S(2)}) %collective-permute-start.25) | collective-permute-done | bytes 1179680 | tf_op jit(solution)/shard_map/ppermute | solution.py:82
  160.1 6.2 %collective-permute-start.28 = (bf16[192,3072]{1,0:T(8,128)(2,1)}, bf16[192,3072]{1,0:T(8,128)(2,1)}, u32[]{:S(2)}, u32[]{:S(2)}) collective-permute-start(bf16[192,3072]{1,0:T(8,128)(2,1)} %collective-permute-done.26.refs_7_), channel_id=1, source_target_pairs={{0,8},{8,16},{16,24},{24,28},{28,20},{20,12},{12,4},{4,0},{1,9},{9... | collective-permute-start | bytes 3538952 | tf_op jit(solution)/shard_map/ppermute | solution.py:82
  167.7 6.4 %all-to-all-done.1 = bf16[8,256,192]{1,2,0:T(8,128)(2,1)S(1)} async-done(((bf16[8,256,192]{1,2,0:T(8,128)(2,1)}), bf16[8,256,192]{1,2,0:T(8,128)(2,1)S(1)}, u32[]{:S(2)}, u32[]{:S(2)}) %all-to-all-start.1) | async-done | bytes 786464 | tf_op jit(solution)/shard_map/all_to_all | solution.py:767
  175.4 3.3 collective-permute-done.21
  181.1 3.4 collective-permute-start.23
  186.7 10.8 %attend.1 = (f32[64,2048]{1,0:T(8,128)}, f32[1,2048]{1,0:T(1,128)}) custom-call(s32[4,2]{1,0:T(4,128)} %pad_add_fusion.table, bf16[2048,192]{1,0:T(8,128)(2,1)} %bitcast.138, bf16[2048,192]{1,0:T(8,128)(2,1)} %bitcast.139, s32[1,2048]{1,0:T(1,128)} %bitcast.155, s32[2048,1]{1,0:T(8,128)} %copy.142.sk_ref), custom_call_target="tpu_custom_call" | custom-call | flops 1073741824 | bytes 2621440 | tf_op jit(solution)/shard_map/attend/pallas_call | solution.py:220
  197.5 4.5 collective-permute-done.27.refs_3_
  206.5 6.9 %collective-permute-done.23 = bf16[2048,128]{1,0:T(8,128)(2,1)S(1)} collective-permute-done((bf16[2048,128]{1,0:T(8,128)(2,1)S(1)}, bf16[2048,128]{1,0:T(8,128)(2,1)S(1)}, u32[]{:S(2)}, u32[]{:S(2)}) %collective-permute-start.23) | collective-permute-done | bytes 524320 | tf_op jit(solution)/shard_map/ppermute | solution.py:82
  215.6 10.2 %attend_text.1 = (bf16[2048,64]{1,0:T(8,128)(2,1)}, f32[64,2048]{1,0:T(8,128)}, f32[1,2048]{1,0:T(1,128)}) custom-call(s32[4,2]{1,0:T(4,128)} %pad_add_fusion.table, f32[1]{0:T(128)} %bitcast.14.gate, bf16[2048,192]{1,0:T(8,128)(2,1)} %bitcast.140, bf16[2048,128]{1,0:T(8,128)(2,1)} %add_convert_fusion.10.kv_ref, f32[64,2048]{1,0:T(8,128)} %get-tuple-element.98.self_ref, ...), custom_call_target="tpu_custom_call" | custom-call | flops 134217728 | bytes 2621440 | tf_op jit(solution)/shard_map/attend_text/pallas_call | solution.py:220
  227.0 13.8 %all_to_all.25 = bf16[8,256,64]{1,2,0:T(8,128)(2,1)S(1)} all-to-all(bf16[8,256,64]{1,2,0:T(8,128)(2,1)S(1)} %copy.143), channel_id=1, replica_groups=mesh['seq'=8,'tp'=4] {'seq'}, dimensions={0} | all-to-all | bytes 524288 | tf_op jit(solution)/shard_map/all_to_all | solution.py:767
  241.8 4.7 out.1
  251.2 9.6 %collective-permute-done.32 = bf16[128,1536]{1,0:T(8,128)(2,1)S(1)} collective-permute-done((bf16[128,1536]{1,0:T(8,128)(2,1)S(1)}, bf16[128,1536]{1,0:T(8,128)(2,1)S(1)}, u32[]{:S(2)}, u32[]{:S(2)}) %collective-permute-start.32) | collective-permute-done | bytes 393248 | tf_op jit(solution)/shard_map/ppermute | solution.py:182
  263.4 12.6 %ffn.1 = (f32[256,1536]{1,0:T(8,128)}, bf16[256,1536]{1,0:T(8,128)(2,1)}, bf16[256,1536]{1,0:T(8,128)(2,1)}, bf16[256,1024]{1,0:T(8,128)(2,1)}, bf16[256,2048]{1...) custom-call(s32[3]{0:T(128)} %pad_add_fusion.1.scal, ...), custom_call_target="tpu_custom_call" | custom-call | flops 4831838208 | bytes 9437184 | tf_op jit(solution)/shard_map/ffn/pallas_call | solution.py:220
  276.2 3.3 convolution_convert_fusion
  289.2 5.1 collective-permute-done.37
  297.0 5.7 mid.1
  308.1 2.2 fusion.9
  312.9 3.4 all-to-all-start.3
  318.8 23.2 %all-to-all-done.3 = bf16[8,256,64]{1,2,0:T(8,128)(2,1)S(1)} async-done(((bf16[8,256,64]{1,2,0:T(8,128)(2,1)}), bf16[8,256,64]{1,2,0:T(8,128)(2,1)S(1)}, u32[]{:S(2)}, u32[]{:S(2)}) %all-to-all-start.3) | async-done | bytes 262176 | tf_op jit(solution)/shard_map/all_to_all | solution.py:767
  343.0 2.8 add_convert_fusion.2
  347.4 2.7 add_convert_fusion.3
  350.5 12.6 %attend_text_back.1 = (bf16[2048,128]{1,0:T(8,128)(2,1)}, f32[64,2048]{1,0:T(8,128)}, f32[1,2048]{1,0:T(1,128)}) custom-call(s32[4,2]{1,0:T(4,128)} %pad_add_fusion.table, f32[1]{0:T(128)} %bitcast.14.gate, bf16[2048,192]{1,0:T(8,128)(2,1)} %bitcast.141, bf16[2048,64]{1,0:T(8,128)(2,1)} %bitcast.149, bf16[2048,128]{1,0:T(8,128)(2,1)} %add_convert_fusion.10.kv_ref, ...), custom_call_target="tpu_custom_call" | custom-call | flops 335544320 | bytes 2621440 | tf_op jit(solution)/shard_map/attend_text_back/pallas_call | solution.py:220
  366.8 16.8 %attend_back.1 = bf16[2048,192]{1,0:T(8,128)(2,1)} custom-call(s32[4,2]{1,0:T(4,128)} %pad_add_fusion.table, bf16[2048,192]{1,0:T(8,128)(2,1)} %bitcast.142, bf16[2048,64]{1,0:T(8,128)(2,1)} %bitcast.150, bf16[2048,192]{1,0:T(8,128)(2,1)} %bitcast.143, f32[64,2048]{1,0:T(8,128)} %get-tuple-element.98.self_ref, f32[1,2048]{1,0:T(1,128)} %get-tuple-element.119.stat_ref, ...), custom_call_target="tpu_custom_call" | custom-call | flops 2684354560 | bytes 2621440 | tf_op jit(solution)/shard_map/attend_back/pallas_call | solution.py:220
  385.9 4.1 all-to-all-start.4
  395.6 17.5 %collective-permute-done.58.refs_2_ = bf16[2048,128]{1,0:T(8,128)(2,1)} collective-permute-done((bf16[2048,128]{1,0:T(8,128)(2,1)}, bf16[2048,128]{1,0:T(8,128)(2,1)}, u32[]{:S(2)}, u32[]{:S(2)}) %collective-permute-start.58) | collective-permute-done | bytes 524320 | tf_op jit(solution)/shard_map/ppermute | solution.py:82
  413.1 6.5 %collective-permute-start.63 = (bf16[2048,128]{1,0:T(8,128)(2,1)}, bf16[2048,128]{1,0:T(8,128)(2,1)}, u32[]{:S(2)}, u32[]{:S(2)}) collective-permute-start(bf16[2048,128]{1,0:T(8,128)(2,1)} %collective-permute-done.62.refs_7_), channel_id=1, source_target_pairs={{0,8},{8,16},{16,24},{24,28},{28,20},{20,12},{12,4},{4,0},{1,9},{9... | collective-permute-start | bytes 1572872 | tf_op jit(solution)/shard_map/ppermute | solution.py:82
  419.6 2.7 add_convert_fusion
  423.6 6.2 %qkv_back.1 = (bf16[256,1152]{1,0:T(8,128)(2,1)}, bf16[128,1536]{1,0:T(8,128)(2,1)}, bf16[128,1536]{1,0:T(8,128)(2,1)}) custom-call(s32[3]{0:T(128)} %pad_add_fusion.1.scal, bf16[8,256,192]{2,1,0:T(8,128)(2,1)} %copy.152.slab_ref, bf16[192,1536]{1,0:T(8,128)(2,1)} %copy-done, bf16[192,1536]{1,0:T(8,128)(2,1)} %copy-done.4, bf16[192,1536]{1,0:T(8,128)(2,1)} %copy-done.7, ...), custom_call_target="tpu_custom_call" | custom-call | flops 905969664 | bytes 3538944 | tf_op jit(solution)/shard_map/qkv_back/pallas_call | solution.py:220
  429.8 2.3 convolution_convert_fusion.1
  435.5 2.7 add_convert_fusion.1
  440.2 8.3 %side.1 = (f32[256,1536]{1,0:T(8,128)}, f32[32,1536]{1,0:T(8,128)}, f32[8,1536]{1,0:T(8,128)}) custom-call(s32[3]{0:T(128)} %pad_add_fusion.1.scal, f32[256,1536]{1,0:T(8,128)} %get-tuple-element.125.mid_ref, f32[256,1536]{1,0:T(8,128)} %get-tuple-element.126.grad_ref, bf16[256,1536]{1,0:T(8,128)(2,1)} %get-tuple-element.91.g_ref, ...), custom_call_target="tpu_custom_call" | custom-call | bytes 9437184 | tf_op jit(solution)/shard_map/side/pallas_call | solution.py:220
  452.5 7.7 %collective-permute-done.53 = bf16[96,1536]{1,0:T(8,128)(2,1)S(1)} collective-permute-done((bf16[96,1536]{1,0:T(8,128)(2,1)S(1)}, bf16[96,1536]{1,0:T(8,128)(2,1)S(1)}, u32[]{:S(2)}, u32[]{:S(2)}) %collective-permute-start.53) | collective-permute-done | bytes 294944 | tf_op jit(solution)/shard_map/ppermute | solution.py:82
  460.2 2.9 collective-permute-start.64
  467.3 6.5 %collective-permute-done.64.refs_5_ = bf16[1024,128]{1,0:T(8,128)(2,1)S(1)} collective-permute-done((bf16[1024,128]{1,0:T(8,128)(2,1)S(1)}, bf16[1024,128]{1,0:T(8,128)(2,1)S(1)}, u32[]{:S(2)}, u32[]{:S(2)}) %collective-permute-start.64) | collective-permute-done | bytes 262176 | tf_op jit(solution)/shard_map/ppermute | solution.py:82
  476.2 9.1 %text_grad.1 = f32[2,512,384]{2,1,0:T(8,128)} custom-call(s32[6]{0:T(128)} %get-tuple-element.140.slab_at, bf16[512,2048]{1,0:T(8,128)(2,1)} %fusion.7.cap_ref, bf16[2048,128]{1,0:T(8,128)(2,1)} %get-tuple-element.141.refs_0_, bf16[2048,128]{1,0:T(8,128)(2,1)} %collective-permute-done.57.refs_1_, bf16[2048,128]{1,0:T(8,128)(2,1)} %collective-permute-done.58.refs_2_, ...), custom_call_target="tpu_custom_call" | custom-call | flops 1610612736 | bytes 4194304 | tf_op jit(solution)/shard_map/text_grad/pallas_call | solution.py:220
  485.3 2.5 multiply_reduce_fusion.1
  493.9 6.6 %leave.1 = (f32[256,1536]{1,0:T(8,128)}, f32[48,384]{1,0:T(8,128)}, f32[8,1536]{1,0:T(8,128)}) custom-call(s32[3]{0:T(128)} %pad_add_fusion.1.scal, bf16[256,1536]{1,0:T(8,128)(2,1)} %get-tuple-element.90.x_ref, f32[256,1536]{1,0:T(8,128)} %get-tuple-element.126.grad_ref, bf16[128,1536]{1,0:T(8,128)(2,1)} %copy-done.42, bf16[128,1536]{1,0:T(8,128)(2,1)} %copy-done.69, ...), custom_call_target="tpu_custom_call" | custom-call | bytes 6291456 | tf_op jit(solution)/shard_map/leave/pallas_call | solution.py:220
  509.7 3.6 collective-permute-done.68
  513.3 3.0 collective-permute-start.69
  531.7 2.4 collective-permute-done.56
  546.6 3.0 collective-permute-done.72
  549.9 3.3 collective-permute-done.73
  564.0 3.0 multiply_subtract_fusion.2
  569.7 3.1 multiply_subtract_fusion.1
  577.1 7.3 %multiply_subtract_fusion = (f32[128,9216]{1,0:T(8,128)}, f32[128,9216]{1,0:T(8,128)}, f32[128,9216]{1,0:T(8,128)}) fusion(f32[128,9216]{1,0:T(8,128)S(1)} %bitcast.146, f32[128,9216]{1,0:T(8,128)S(1)} %bitcast.166, f32[128,9216]{1,0:T(8,128)S(1)} %copy-done.103, f32[]{:T(128)S(6)} %min.18, bf16[8,128]{1,0:T(8,128)(2,1)S(1)} %copy-done.90, ...), kind=kOutput, calls=%fused_computation.5 | convolution fusion | flops 37748736 | bytes 28461060 | tf_op jit(solution)/shard_map/dot_general | solution.py:71
  (500 shorter events, 182.6 us)
Async XLA Ops:
  2.1 22.1 %collective-permute-start.5 = (bf16[192,1536]{1,0:T(8,128)(2,1)S(1)}, bf16[192,1536]{1,0:T(8,128)(2,1)S(1)}, u32[]{:S(2)}, u32[]{:S(2)}) collective-permute-start(bf16[192,1536]{1,0:T(8,128)(2,1)S(1)} %pad_maximum_fusion.7.refs_0_), channel_id=1, source_target_pairs={{0,4},{8,0},{16,8},{24,16},{28,24},{20,28},{12,20},{4,12},{1,5},{9... | collective-permute-start | bytes 1769480 | tf_op jit(solution)/shard_map/ppermute | solution.py:82
  5.1 19.1 %collective-permute-start.8 = (bf16[192,1536]{1,0:T(8,128)(2,1)S(1)}, bf16[192,1536]{1,0:T(8,128)(2,1)S(1)}, u32[]{:S(2)}, u32[]{:S(2)}) collective-permute-start(bf16[192,1536]{1,0:T(8,128)(2,1)S(1)} %pad_maximum_fusion.7.refs_0_), channel_id=1, source_target_pairs={{0,8},{8,16},{16,24},{24,28},{28,20},{20,12},{12,4},{4,0},{1,9},{9... | collective-permute-start | bytes 1769480 | tf_op jit(solution)/shard_map/ppermute | solution.py:82
  11.4 20.3 %all-to-all-start = ((bf16[8,256,128]{2,1,0:T(8,128)(2,1)}), bf16[8,256,128]{2,1,0:T(8,128)(2,1)}, u32[]{:S(2)}, u32[]{:S(2)}) async-start(bf16[8,256,128]{2,1,0:T(8,128)(2,1)} %caption_slabs.1), calls=%async_computation | async-start | bytes 1048576 | tf_op jit(solution)/shard_map/all_to_all | solution.py:767
  32.9 8.7 %collective-permute-start.11 = (bf16[2048,128]{0,1:T(8,128)(2,1)S(1)}, bf16[2048,128]{0,1:T(8,128)(2,1)}, u32[]{:S(2)}, u32[]{:S(2)}) collective-permute-start(bf16[2048,128]{0,1:T(8,128)(2,1)S(1)} %copy.156), channel_id=1, source_target_pairs={{0,1},{1,0},{2,3},{3,2},{4,5},{5,4},{6,7},{7,6},{8,9},{9,8},{10,11... | collective-permute-start | bytes 1572872 | tf_op jit(solution)/shard_map/ppermute | solution.py:174
  43.8 26.4 %collective-permute-start.12 = (bf16[2048,256]{0,1:T(8,128)(2,1)}, bf16[2048,256]{0,1:T(8,128)(2,1)}, u32[]{:S(2)}, u32[]{:S(2)}) collective-permute-start(bf16[2048,256]{0,1:T(8,128)(2,1)} %pad_maximum_fusion.4), channel_id=1, source_target_pairs={{0,2},{2,0},{1,3},{3,1},{4,6},{6,4},{5,7},{7,5},{8,10},{10,8},{9,1... | collective-permute-start | bytes 3145736 | tf_op jit(solution)/shard_map/ppermute | solution.py:175
  46.7 16.8 %collective-permute-start.9 = (bf16[192,1536]{1,0:T(8,128)(2,1)S(1)}, bf16[192,1536]{1,0:T(8,128)(2,1)S(1)}, u32[]{:S(2)}, u32[]{:S(2)}) collective-permute-start(bf16[192,1536]{1,0:T(8,128)(2,1)S(1)} %collective-permute-done.8.refs_8_), channel_id=1, source_target_pairs={{0,8},{8,16},{16,24},{24,28},{28,20},{20,12},{12,4},{4,0},{1,9},{9... | collective-permute-start | bytes 1769480 | tf_op jit(solution)/shard_map/ppermute | solution.py:82
  47.5 16.0 %collective-permute-start.6 = (bf16[192,1536]{1,0:T(8,128)(2,1)S(1)}, bf16[192,1536]{1,0:T(8,128)(2,1)S(1)}, u32[]{:S(2)}, u32[]{:S(2)}) collective-permute-start(bf16[192,1536]{1,0:T(8,128)(2,1)S(1)} %collective-permute-done.5.refs_1_), channel_id=1, source_target_pairs={{0,4},{8,0},{16,8},{24,16},{28,24},{20,28},{12,20},{4,12},{1,5},{9... | collective-permute-start | bytes 1769480 | tf_op jit(solution)/shard_map/ppermute | solution.py:82
  62.2 15.3 %collective-permute-start.4 = (f32[48,768]{1,0:T(8,128)S(1)}, f32[48,768]{1,0:T(8,128)S(1)}, u32[]{:S(2)}, u32[]{:S(2)}) collective-permute-start(f32[48,768]{1,0:T(8,128)S(1)} %pad_maximum_fusion.14), channel_id=1, source_target_pairs={{0,2},{2,0},{1,3},{3,1},{4,6},{6,4},{5,7},{7,5},{8,10},{10,8},{9,1... | collective-permute-start | bytes 442376 | tf_op jit(solution)/shard_map/ppermute | solution.py:175
  63.5 18.8 %collective-permute-start.10 = (bf16[192,1536]{1,0:T(8,128)(2,1)S(1)}, bf16[192,1536]{1,0:T(8,128)(2,1)S(1)}, u32[]{:S(2)}, u32[]{:S(2)}) collective-permute-start(bf16[192,1536]{1,0:T(8,128)(2,1)S(1)} %collective-permute-done.9.refs_7_), channel_id=1, source_target_pairs={{0,8},{8,16},{16,24},{24,28},{28,20},{20,12},{12,4},{4,0},{1,9},{9... | collective-permute-start | bytes 1769480 | tf_op jit(solution)/shard_map/ppermute | solution.py:82
  63.5 18.7 %collective-permute-start.7 = (bf16[192,1536]{1,0:T(8,128)(2,1)S(1)}, bf16[192,1536]{1,0:T(8,128)(2,1)S(1)}, u32[]{:S(2)}, u32[]{:S(2)}) collective-permute-start(bf16[192,1536]{1,0:T(8,128)(2,1)S(1)} %collective-permute-done.6.refs_2_), channel_id=1, source_target_pairs={{0,4},{8,0},{16,8},{24,16},{28,24},{20,28},{12,20},{4,12},{1,5},{9... | collective-permute-start | bytes 1769480 | tf_op jit(solution)/shard_map/ppermute | solution.py:82
  74.6 11.4 %collective-permute-start.15 = (bf16[1024,128]{1,0:T(8,128)(2,1)S(1)}, bf16[1024,128]{1,0:T(8,128)(2,1)S(1)}, u32[]{:S(2)}, u32[]{:S(2)}) collective-permute-start(bf16[1024,128]{1,0:T(8,128)(2,1)S(1)} %get-tuple-element.269), channel_id=1, source_target_pairs={{8,16},{16,24},{24,28},{20,12},{12,4},{4,0},{9,17},{17,25},{25,29}... | collective-permute-start | bytes 786440 | tf_op jit(solution)/shard_map/ppermute | solution.py:82
  76.2 11.4 %collective-permute-start.16 = (bf16[1024,128]{1,0:T(8,128)(2,1)S(1)}, bf16[1024,128]{1,0:T(8,128)(2,1)S(1)}, u32[]{:S(2)}, u32[]{:S(2)}) collective-permute-start(bf16[1024,128]{1,0:T(8,128)(2,1)S(1)} %get-tuple-element.267), channel_id=1, source_target_pairs={{8,0},{16,8},{24,16},{20,28},{12,20},{4,12},{9,1},{17,9},{25,17},{... | collective-permute-start | bytes 786440 | tf_op jit(solution)/shard_map/ppermute | solution.py:82
  77.5 35.5 %collective-permute-start.13 = (bf16[192,3072]{1,0:T(8,128)(2,1)S(1)}, bf16[192,3072]{1,0:T(8,128)(2,1)}, u32[]{:S(2)}, u32[]{:S(2)}) collective-permute-start(bf16[192,3072]{1,0:T(8,128)(2,1)S(1)} %copy-done.53), channel_id=1, source_target_pairs={{0,4},{8,0},{16,8},{24,16},{28,24},{20,28},{12,20},{4,12},{1,5},{9... | collective-permute-start | bytes 3538952 | tf_op jit(solution)/shard_map/ppermute | solution.py:82
  82.2 35.5 %collective-permute-start.14 = (bf16[192,3072]{1,0:T(8,128)(2,1)S(1)}, bf16[192,3072]{1,0:T(8,128)(2,1)}, u32[]{:S(2)}, u32[]{:S(2)}) collective-permute-start(bf16[192,3072]{1,0:T(8,128)(2,1)S(1)} %copy-done.53), channel_id=1, source_target_pairs={{0,8},{8,16},{16,24},{24,28},{28,20},{20,12},{12,4},{4,0},{1,9},{9... | collective-permute-start | bytes 3538952 | tf_op jit(solution)/shard_map/ppermute | solution.py:82
  82.3 40.1 %collective-permute-start.17 = (bf16[96,1536]{1,0:T(8,128)(2,1)S(1)}, bf16[96,1536]{1,0:T(8,128)(2,1)S(1)}, u32[]{:S(2)}, u32[]{:S(2)}) collective-permute-start(bf16[96,1536]{1,0:T(8,128)(2,1)S(1)} %slice.344), channel_id=1, source_target_pairs={{0,4},{8,0},{16,8},{24,16},{28,24},{20,28},{12,20},{4,12},{1,5},{9... | collective-permute-start | bytes 884744 | tf_op jit(solution)/shard_map/ppermute | solution.py:82
  86.1 38.7 %collective-permute-start.18 = (bf16[96,1536]{1,0:T(8,128)(2,1)}, bf16[96,1536]{1,0:T(8,128)(2,1)S(1)}, u32[]{:S(2)}, u32[]{:S(2)}) collective-permute-start(bf16[96,1536]{1,0:T(8,128)(2,1)} %slice.345), channel_id=1, source_target_pairs={{0,8},{8,16},{16,24},{24,28},{28,20},{20,12},{12,4},{4,0},{1,9},{9... | collective-permute-start | bytes 884744 | tf_op jit(solution)/shard_map/ppermute | solution.py:82
  88.6 49.5 %collective-permute-start.20 = (bf16[2048,128]{1,0:T(8,128)(2,1)}, bf16[2048,128]{1,0:T(8,128)(2,1)}, u32[]{:S(2)}, u32[]{:S(2)}) collective-permute-start(bf16[2048,128]{1,0:T(8,128)(2,1)} %pad_maximum_fusion.10), channel_id=1, source_target_pairs={{0,4},{8,0},{16,8},{28,24},{20,28},{12,20},{1,5},{9,1},{17,9},{29,... | collective-permute-start | bytes 1572872 | tf_op jit(solution)/shard_map/ppermute | solution.py:82
  113.0 25.1 %collective-permute-start.19 = (bf16[2048,128]{1,0:T(8,128)(2,1)}, bf16[2048,128]{1,0:T(8,128)(2,1)S(1)}, u32[]{:S(2)}, u32[]{:S(2)}) collective-permute-start(bf16[2048,128]{1,0:T(8,128)(2,1)} %pad_maximum_fusion.9), channel_id=1, source_target_pairs={{0,8},{16,24},{24,28},{28,20},{12,4},{4,0},{1,9},{17,25},{25,29},{... | collective-permute-start | bytes 1572872 | tf_op jit(solution)/shard_map/ppermute | solution.py:82
  122.3 37.8 %collective-permute-start.25 = (bf16[192,3072]{1,0:T(8,128)(2,1)}, bf16[192,3072]{1,0:T(8,128)(2,1)}, u32[]{:S(2)}, u32[]{:S(2)}) collective-permute-start(bf16[192,3072]{1,0:T(8,128)(2,1)} %collective-permute-done.13.refs_1_), channel_id=1, source_target_pairs={{0,4},{8,0},{16,8},{24,16},{28,24},{20,28},{12,20},{4,12},{1,5},{9... | collective-permute-start | bytes 3538952 | tf_op jit(solution)/shard_map/ppermute | solution.py:82
  122.4 37.7 %collective-permute-start.26 = (bf16[192,3072]{1,0:T(8,128)(2,1)}, bf16[192,3072]{1,0:T(8,128)(2,1)}, u32[]{:S(2)}, u32[]{:S(2)}) collective-permute-start(bf16[192,3072]{1,0:T(8,128)(2,1)} %collective-permute-done.14.refs_8_), channel_id=1, source_target_pairs={{0,8},{8,16},{16,24},{24,28},{28,20},{20,12},{12,4},{4,0},{1,9},{9... | collective-permute-start | bytes 3538952 | tf_op jit(solution)/shard_map/ppermute | solution.py:82
  133.3 40.7 %all-to-all-start.1 = ((bf16[8,256,192]{1,2,0:T(8,128)(2,1)}), bf16[8,256,192]{1,2,0:T(8,128)(2,1)S(1)}, u32[]{:S(2)}, u32[]{:S(2)}) async-start(bf16[8,256,192]{1,2,0:T(8,128)(2,1)} %copy.140), calls=%async_computation.1 | async-start | bytes 1572864 | tf_op jit(solution)/shard_map/all_to_all | solution.py:767
  139.8 38.8 %collective-permute-start.21 = (bf16[2048,128]{1,0:T(8,128)(2,1)S(1)}, bf16[2048,128]{1,0:T(8,128)(2,1)S(1)}, u32[]{:S(2)}, u32[]{:S(2)}) collective-permute-start(bf16[2048,128]{1,0:T(8,128)(2,1)S(1)} %get-tuple-element.265), channel_id=1, source_target_pairs={{0,8},{8,16},{24,28},{28,20},{20,12},{4,0},{1,9},{9,17},{25,29},{2... | collective-permute-start | bytes 1572872 | tf_op jit(solution)/shard_map/ppermute | solution.py:82
  143.7 35.9 %collective-permute-start.22 = (bf16[2048,128]{1,0:T(8,128)(2,1)S(1)}, bf16[2048,128]{1,0:T(8,128)(2,1)S(1)}, u32[]{:S(2)}, u32[]{:S(2)}) collective-permute-start(bf16[2048,128]{1,0:T(8,128)(2,1)S(1)} %get-tuple-element.264), channel_id=1, source_target_pairs={{0,4},{8,0},{24,16},{28,24},{20,28},{4,12},{1,5},{9,1},{25,17},{29... | collective-permute-start | bytes 1572872 | tf_op jit(solution)/shard_map/ppermute | solution.py:82
  160.1 41.9 %collective-permute-start.27 = (bf16[192,3072]{1,0:T(8,128)(2,1)}, bf16[192,3072]{1,0:T(8,128)(2,1)}, u32[]{:S(2)}, u32[]{:S(2)}) collective-permute-start(bf16[192,3072]{1,0:T(8,128)(2,1)} %collective-permute-done.25.refs_2_), channel_id=1, source_target_pairs={{0,4},{8,0},{16,8},{24,16},{28,24},{20,28},{12,20},{4,12},{1,5},{9... | collective-permute-start | bytes 3538952 | tf_op jit(solution)/shard_map/ppermute | solution.py:82
  160.1 43.1 %collective-permute-start.28 = (bf16[192,3072]{1,0:T(8,128)(2,1)}, bf16[192,3072]{1,0:T(8,128)(2,1)}, u32[]{:S(2)}, u32[]{:S(2)}) collective-permute-start(bf16[192,3072]{1,0:T(8,128)(2,1)} %collective-permute-done.26.refs_7_), channel_id=1, source_target_pairs={{0,8},{8,16},{16,24},{24,28},{28,20},{20,12},{12,4},{4,0},{1,9},{9... | collective-permute-start | bytes 3538952 | tf_op jit(solution)/shard_map/ppermute | solution.py:82
  181.1 32.3 %collective-permute-start.23 = (bf16[2048,128]{1,0:T(8,128)(2,1)S(1)}, bf16[2048,128]{1,0:T(8,128)(2,1)S(1)}, u32[]{:S(2)}, u32[]{:S(2)}) collective-permute-start(bf16[2048,128]{1,0:T(8,128)(2,1)S(1)} %get-tuple-element.262), channel_id=1, source_target_pairs={{0,8},{8,16},{16,24},{28,20},{20,12},{12,4},{1,9},{9,17},{17,25},{... | collective-permute-start | bytes 1572872 | tf_op jit(solution)/shard_map/ppermute | solution.py:82
  184.5 28.9 %collective-permute-start.24 = (bf16[2048,128]{1,0:T(8,128)(2,1)S(1)}, bf16[2048,128]{1,0:T(8,128)(2,1)S(1)}, u32[]{:S(2)}, u32[]{:S(2)}) collective-permute-start(bf16[2048,128]{1,0:T(8,128)(2,1)S(1)} %get-tuple-element.263), channel_id=1, source_target_pairs={{0,4},{16,8},{24,16},{28,24},{12,20},{4,12},{1,5},{17,9},{25,17},{... | collective-permute-start | bytes 1572872 | tf_op jit(solution)/shard_map/ppermute | solution.py:82
  203.1 37.7 %collective-permute-start.29 = (bf16[96,3072]{1,0:T(8,128)(2,1)S(1)}, bf16[96,3072]{1,0:T(8,128)(2,1)}, u32[]{:S(2)}, u32[]{:S(2)}) collective-permute-start(bf16[96,3072]{1,0:T(8,128)(2,1)S(1)} %slice.351), channel_id=1, source_target_pairs={{0,4},{8,0},{16,8},{24,16},{28,24},{20,28},{12,20},{4,12},{1,5},{9... | collective-permute-start | bytes 1769480 | tf_op jit(solution)/shard_map/ppermute | solution.py:82
  204.3 36.5 %collective-permute-start.30 = (bf16[96,3072]{1,0:T(8,128)(2,1)S(1)}, bf16[96,3072]{1,0:T(8,128)(2,1)}, u32[]{:S(2)}, u32[]{:S(2)}) collective-permute-start(bf16[96,3072]{1,0:T(8,128)(2,1)S(1)} %slice.352), channel_id=1, source_target_pairs={{0,8},{8,16},{16,24},{24,28},{28,20},{20,12},{12,4},{4,0},{1,9},{9... | collective-permute-start | bytes 1769480 | tf_op jit(solution)/shard_map/ppermute | solution.py:82
  249.6 11.2 %collective-permute-start.32 = (bf16[128,1536]{1,0:T(8,128)(2,1)S(1)}, bf16[128,1536]{1,0:T(8,128)(2,1)S(1)}, u32[]{:S(2)}, u32[]{:S(2)}) collective-permute-start(bf16[128,1536]{1,0:T(8,128)(2,1)S(1)} %add_convert_fusion.22), channel_id=1, source_target_pairs={{0,2},{2,0},{1,3},{3,1},{4,6},{6,4},{5,7},{7,5},{8,10},{10,8},{9,1... | collective-permute-start | bytes 1179656 | tf_op jit(solution)/shard_map/ppermute | solution.py:182
  282.9 11.5 %collective-permute-start.37 = (bf16[128,1536]{1,0:T(8,128)(2,1)S(1)}, bf16[128,1536]{1,0:T(8,128)(2,1)S(1)}, u32[]{:S(2)}, u32[]{:S(2)}) collective-permute-start(bf16[128,1536]{1,0:T(8,128)(2,1)S(1)} %add_convert_fusion.20), channel_id=1, source_target_pairs={{0,2},{2,0},{1,3},{3,1},{4,6},{6,4},{5,7},{7,5},{8,10},{10,8},{9,1... | collective-permute-start | bytes 1179656 | tf_op jit(solution)/shard_map/ppermute | solution.py:182
  287.0 15.7 %collective-permute-start.34 = (bf16[96,3072]{1,0:T(8,128)(2,1)}, bf16[96,3072]{1,0:T(8,128)(2,1)}, u32[]{:S(2)}, u32[]{:S(2)}) collective-permute-start(bf16[96,3072]{1,0:T(8,128)(2,1)} %get-tuple-element.299), channel_id=1, source_target_pairs={{0,8},{8,16},{16,24},{24,28},{28,20},{20,12},{12,4},{4,0},{1,9},{9... | collective-permute-start | bytes 1769480 | tf_op jit(solution)/shard_map/ppermute | solution.py:82
  287.0 15.8 %collective-permute-start.35 = (bf16[96,3072]{1,0:T(8,128)(2,1)}, bf16[96,3072]{1,0:T(8,128)(2,1)}, u32[]{:S(2)}, u32[]{:S(2)}) collective-permute-start(bf16[96,3072]{1,0:T(8,128)(2,1)} %get-tuple-element.298), channel_id=1, source_target_pairs={{0,4},{8,0},{16,8},{24,16},{28,24},{20,28},{12,20},{4,12},{1,5},{9... | collective-permute-start | bytes 1769480 | tf_op jit(solution)/shard_map/ppermute | solution.py:82
  305.2 37.8 %collective-permute-start.40 = (bf16[192,3072]{1,0:T(8,128)(2,1)}, bf16[192,3072]{1,0:T(8,128)(2,1)}, u32[]{:S(2)}, u32[]{:S(2)}) collective-permute-start(bf16[192,3072]{1,0:T(8,128)(2,1)} %pad_maximum_fusion.3), channel_id=1, source_target_pairs={{0,4},{8,0},{16,8},{24,16},{28,24},{20,28},{12,20},{4,12},{1,5},{9... | collective-permute-start | bytes 3538952 | tf_op jit(solution)/shard_map/ppermute | solution.py:82
  310.3 32.7 %collective-permute-start.39 = (bf16[192,3072]{1,0:T(8,128)(2,1)}, bf16[192,3072]{1,0:T(8,128)(2,1)}, u32[]{:S(2)}, u32[]{:S(2)}) collective-permute-start(bf16[192,3072]{1,0:T(8,128)(2,1)} %fusion.9), channel_id=1, source_target_pairs={{0,8},{8,16},{16,24},{24,28},{28,20},{20,12},{12,4},{4,0},{1,9},{9... | collective-permute-start | bytes 3538952 | tf_op jit(solution)/shard_map/ppermute | solution.py:82
  312.9 29.1 %all-to-all-start.3 = ((bf16[8,256,64]{1,2,0:T(8,128)(2,1)}), bf16[8,256,64]{1,2,0:T(8,128)(2,1)S(1)}, u32[]{:S(2)}, u32[]{:S(2)}) async-start(bf16[8,256,64]{1,2,0:T(8,128)(2,1)} %copy.147), calls=%async_computation.3 | async-start | bytes 524288 | tf_op jit(solution)/shard_map/all_to_all | solution.py:767
  317.8 47.3 %collective-permute-start.43 = (bf16[128,1536]{1,0:T(8,128)(2,1)S(1)}, bf16[128,1536]{1,0:T(8,128)(2,1)S(1)}, u32[]{:S(2)}, u32[]{:S(2)}) collective-permute-start(bf16[128,1536]{1,0:T(8,128)(2,1)S(1)} %copy-done.104), channel_id=1, source_target_pairs={{0,1},{1,0},{2,3},{3,2},{4,5},{5,4},{6,7},{7,6},{8,9},{9,8},{10,11... | collective-permute-start | bytes 1179656 | tf_op jit(solution)/shard_map/ppermute | solution.py:180
  345.8 73.7 %collective-permute-start.42 = (bf16[192,3072]{1,0:T(8,128)(2,1)}, bf16[192,3072]{1,0:T(8,128)(2,1)}, u32[]{:S(2)}, u32[]{:S(2)}) collective-permute-start(bf16[192,3072]{1,0:T(8,128)(2,1)} %add_convert_fusion.2), channel_id=1, source_target_pairs={{0,4},{8,0},{16,8},{24,16},{28,24},{20,28},{12,20},{4,12},{1,5},{9... | collective-permute-start | bytes 3538952 | tf_op jit(solution)/shard_map/ppermute | solution.py:82
  350.1 69.4 %collective-permute-start.41 = (bf16[192,3072]{1,0:T(8,128)(2,1)}, bf16[192,3072]{1,0:T(8,128)(2,1)}, u32[]{:S(2)}, u32[]{:S(2)}) collective-permute-start(bf16[192,3072]{1,0:T(8,128)(2,1)} %add_convert_fusion.3), channel_id=1, source_target_pairs={{0,8},{8,16},{16,24},{24,28},{28,20},{20,12},{12,4},{4,0},{1,9},{9... | collective-permute-start | bytes 3538952 | tf_op jit(solution)/shard_map/ppermute | solution.py:82
  363.1 27.9 %collective-permute-start.57 = (bf16[2048,128]{1,0:T(8,128)(2,1)}, bf16[2048,128]{1,0:T(8,128)(2,1)}, u32[]{:S(2)}, u32[]{:S(2)}) collective-permute-start(bf16[2048,128]{1,0:T(8,128)(2,1)} %get-tuple-element.141.refs_0_), channel_id=1, source_target_pairs={{0,4},{8,0},{16,8},{24,16},{28,24},{20,28},{12,20},{4,12},{1,5},{9... | collective-permute-start | bytes 1572872 | tf_op jit(solution)/shard_map/ppermute | solution.py:82
  364.7 28.3 %collective-permute-start.61 = (bf16[2048,128]{1,0:T(8,128)(2,1)}, bf16[2048,128]{1,0:T(8,128)(2,1)}, u32[]{:S(2)}, u32[]{:S(2)}) collective-permute-start(bf16[2048,128]{1,0:T(8,128)(2,1)} %get-tuple-element.141.refs_0_), channel_id=1, source_target_pairs={{0,8},{8,16},{16,24},{24,28},{28,20},{20,12},{12,4},{4,0},{1,9},{9... | collective-permute-start | bytes 1572872 | tf_op jit(solution)/shard_map/ppermute | solution.py:82
  365.2 27.9 %collective-permute-start.44 = (bf16[128,1536]{1,0:T(8,128)(2,1)S(1)}, bf16[128,1536]{1,0:T(8,128)(2,1)}, u32[]{:S(2)}, u32[]{:S(2)}) collective-permute-start(bf16[128,1536]{1,0:T(8,128)(2,1)S(1)} %add_convert_fusion.18), channel_id=1, source_target_pairs={{0,2},{2,0},{1,3},{3,1},{4,6},{6,4},{5,7},{7,5},{8,10},{10,8},{9,1... | collective-permute-start | bytes 1179656 | tf_op jit(solution)/shard_map/ppermute | solution.py:182
  385.9 36.4 %all-to-all-start.4 = ((bf16[8,256,192]{1,2,0:T(8,128)(2,1)}), bf16[8,256,192]{1,2,0:T(8,128)(2,1)S(1)}, u32[]{:S(2)}, u32[]{:S(2)}) async-start(bf16[8,256,192]{1,2,0:T(8,128)(2,1)} %copy.151), calls=%async_computation.4 | async-start | bytes 1572864 | tf_op jit(solution)/shard_map/all_to_all | solution.py:767
  391.0 22.1 %collective-permute-start.58 = (bf16[2048,128]{1,0:T(8,128)(2,1)}, bf16[2048,128]{1,0:T(8,128)(2,1)}, u32[]{:S(2)}, u32[]{:S(2)}) collective-permute-start(bf16[2048,128]{1,0:T(8,128)(2,1)} %collective-permute-done.57.refs_1_), channel_id=1, source_target_pairs={{0,4},{8,0},{16,8},{24,16},{28,24},{20,28},{12,20},{4,12},{1,5},{9... | collective-permute-start | bytes 1572872 | tf_op jit(solution)/shard_map/ppermute | solution.py:82
  393.0 20.1 %collective-permute-start.62 = (bf16[2048,128]{1,0:T(8,128)(2,1)}, bf16[2048,128]{1,0:T(8,128)(2,1)}, u32[]{:S(2)}, u32[]{:S(2)}) collective-permute-start(bf16[2048,128]{1,0:T(8,128)(2,1)} %collective-permute-done.61.refs_8_), channel_id=1, source_target_pairs={{0,8},{8,16},{16,24},{24,28},{28,20},{20,12},{12,4},{4,0},{1,9},{9... | collective-permute-start | bytes 1572872 | tf_op jit(solution)/shard_map/ppermute | solution.py:82
  394.2 44.0 %collective-permute-start.45 = (bf16[128,1536]{1,0:T(8,128)(2,1)S(1)}, bf16[128,1536]{1,0:T(8,128)(2,1)}, u32[]{:S(2)}, u32[]{:S(2)}) collective-permute-start(bf16[128,1536]{1,0:T(8,128)(2,1)S(1)} %add_convert_fusion.17.fm_ref), channel_id=1, source_target_pairs={{0,1},{1,0},{2,3},{3,2},{4,5},{5,4},{6,7},{7,6},{8,9},{9,8},{10,11... | collective-permute-start | bytes 1179656 | tf_op jit(solution)/shard_map/ppermute | solution.py:183
  413.1 35.5 %collective-permute-start.59 = (bf16[2048,128]{1,0:T(8,128)(2,1)}, bf16[2048,128]{1,0:T(8,128)(2,1)}, u32[]{:S(2)}, u32[]{:S(2)}) collective-permute-start(bf16[2048,128]{1,0:T(8,128)(2,1)} %collective-permute-done.58.refs_2_), channel_id=1, source_target_pairs={{0,4},{8,0},{16,8},{24,16},{28,24},{20,28},{12,20},{4,12},{1,5},{9... | collective-permute-start | bytes 1572872 | tf_op jit(solution)/shard_map/ppermute | solution.py:82
  413.1 36.6 %collective-permute-start.63 = (bf16[2048,128]{1,0:T(8,128)(2,1)}, bf16[2048,128]{1,0:T(8,128)(2,1)}, u32[]{:S(2)}, u32[]{:S(2)}) collective-permute-start(bf16[2048,128]{1,0:T(8,128)(2,1)} %collective-permute-done.62.refs_7_), channel_id=1, source_target_pairs={{0,8},{8,16},{16,24},{24,28},{28,20},{20,12},{12,4},{4,0},{1,9},{9... | collective-permute-start | bytes 1572872 | tf_op jit(solution)/shard_map/ppermute | solution.py:82
  422.2 81.9 %collective-permute-start.66 = (bf16[192,3072]{1,0:T(8,128)(2,1)}, bf16[192,3072]{1,0:T(8,128)(2,1)}, u32[]{:S(2)}, u32[]{:S(2)}) collective-permute-start(bf16[192,3072]{1,0:T(8,128)(2,1)} %add_convert_fusion), channel_id=1, source_target_pairs={{0,4},{8,0},{16,8},{24,16},{28,24},{20,28},{12,20},{4,12},{1,5},{9... | collective-permute-start | bytes 3538952 | tf_op jit(solution)/shard_map/ppermute | solution.py:82
  433.4 17.3 %collective-permute-start.49 = (bf16[96,1536]{1,0:T(8,128)(2,1)S(1)}, bf16[96,1536]{1,0:T(8,128)(2,1)S(1)}, u32[]{:S(2)}, u32[]{:S(2)}) collective-permute-start(bf16[96,1536]{1,0:T(8,128)(2,1)S(1)} %get-tuple-element.302), channel_id=1, source_target_pairs={{0,8},{8,16},{16,24},{24,28},{28,20},{20,12},{12,4},{4,0},{1,9},{9... | collective-permute-start | bytes 884744 | tf_op jit(solution)/shard_map/ppermute | solution.py:82
  438.2 66.0 %collective-permute-start.65 = (bf16[192,3072]{1,0:T(8,128)(2,1)}, bf16[192,3072]{1,0:T(8,128)(2,1)}, u32[]{:S(2)}, u32[]{:S(2)}) collective-permute-start(bf16[192,3072]{1,0:T(8,128)(2,1)} %add_convert_fusion.1), channel_id=1, source_target_pairs={{0,8},{8,16},{16,24},{24,28},{28,20},{20,12},{12,4},{4,0},{1,9},{9... | collective-permute-start | bytes 3538952 | tf_op jit(solution)/shard_map/ppermute | solution.py:82
  448.6 14.6 %collective-permute-start.46 = (bf16[128,1536]{1,0:T(8,128)(2,1)S(1)}, bf16[128,1536]{1,0:T(8,128)(2,1)S(1)}, u32[]{:S(2)}, u32[]{:S(2)}) collective-permute-start(bf16[128,1536]{1,0:T(8,128)(2,1)S(1)} %copy-done.105), channel_id=1, source_target_pairs={{0,1},{1,0},{2,3},{3,2},{4,5},{5,4},{6,7},{7,6},{8,9},{9,8},{10,11... | collective-permute-start | bytes 1179656 | tf_op jit(solution)/shard_map/ppermute | solution.py:180
  449.7 10.5 %collective-permute-start.53 = (bf16[96,1536]{1,0:T(8,128)(2,1)S(1)}, bf16[96,1536]{1,0:T(8,128)(2,1)S(1)}, u32[]{:S(2)}, u32[]{:S(2)}) collective-permute-start(bf16[96,1536]{1,0:T(8,128)(2,1)S(1)} %get-tuple-element.303), channel_id=1, source_target_pairs={{0,4},{8,0},{16,8},{24,16},{28,24},{20,28},{12,20},{4,12},{1,5},{9... | collective-permute-start | bytes 884744 | tf_op jit(solution)/shard_map/ppermute | solution.py:82
  450.7 14.6 %collective-permute-start.60 = (bf16[1024,128]{1,0:T(8,128)(2,1)S(1)}, bf16[1024,128]{1,0:T(8,128)(2,1)S(1)}, u32[]{:S(2)}, u32[]{:S(2)}) collective-permute-start(bf16[1024,128]{1,0:T(8,128)(2,1)S(1)} %slice.397), channel_id=1, source_target_pairs={{0,4},{8,0},{16,8},{24,16},{28,24},{20,28},{12,20},{4,12},{1,5},{9... | collective-permute-start | bytes 786440 | tf_op jit(solution)/shard_map/ppermute | solution.py:82
  460.2 13.6 %collective-permute-start.64 = (bf16[1024,128]{1,0:T(8,128)(2,1)S(1)}, bf16[1024,128]{1,0:T(8,128)(2,1)S(1)}, u32[]{:S(2)}, u32[]{:S(2)}) collective-permute-start(bf16[1024,128]{1,0:T(8,128)(2,1)S(1)} %slice.398), channel_id=1, source_target_pairs={{0,8},{8,16},{16,24},{24,28},{28,20},{20,12},{12,4},{4,0},{1,9},{9... | collective-permute-start | bytes 786440 | tf_op jit(solution)/shard_map/ppermute | solution.py:82
  463.3 24.5 %collective-permute-start.47 = (bf16[128,1536]{1,0:T(8,128)(2,1)S(1)}, bf16[128,1536]{1,0:T(8,128)(2,1)}, u32[]{:S(2)}, u32[]{:S(2)}) collective-permute-start(bf16[128,1536]{1,0:T(8,128)(2,1)S(1)} %add_convert_fusion.16), channel_id=1, source_target_pairs={{0,2},{2,0},{1,3},{3,1},{4,6},{6,4},{5,7},{7,5},{8,10},{10,8},{9,1... | collective-permute-start | bytes 1179656 | tf_op jit(solution)/shard_map/ppermute | solution.py:182
  465.3 23.7 %collective-permute-start.50 = (bf16[192,1536]{1,0:T(8,128)(2,1)}, bf16[192,1536]{1,0:T(8,128)(2,1)S(1)}, u32[]{:S(2)}, u32[]{:S(2)}) collective-permute-start(bf16[192,1536]{1,0:T(8,128)(2,1)} %fusion.21), channel_id=1, source_target_pairs={{0,8},{8,16},{16,24},{24,28},{28,20},{20,12},{12,4},{4,0},{1,9},{9... | collective-permute-start | bytes 1769480 | tf_op jit(solution)/shard_map/ppermute | solution.py:82
  474.4 16.2 %collective-permute-start.54 = (bf16[192,1536]{1,0:T(8,128)(2,1)}, bf16[192,1536]{1,0:T(8,128)(2,1)S(1)}, u32[]{:S(2)}, u32[]{:S(2)}) collective-permute-start(bf16[192,1536]{1,0:T(8,128)(2,1)} %pad_maximum_fusion.8), channel_id=1, source_target_pairs={{0,4},{8,0},{16,8},{24,16},{28,24},{20,28},{12,20},{4,12},{1,5},{9... | collective-permute-start | bytes 1769480 | tf_op jit(solution)/shard_map/ppermute | solution.py:82
  490.0 26.3 %collective-permute-start.51 = (bf16[192,1536]{1,0:T(8,128)(2,1)}, bf16[192,1536]{1,0:T(8,128)(2,1)}, u32[]{:S(2)}, u32[]{:S(2)}) collective-permute-start(bf16[192,1536]{1,0:T(8,128)(2,1)} %add_convert_fusion.7), channel_id=1, source_target_pairs={{0,8},{8,16},{16,24},{24,28},{28,20},{20,12},{12,4},{4,0},{1,9},{9... | collective-permute-start | bytes 1769480 | tf_op jit(solution)/shard_map/ppermute | solution.py:82
  491.6 27.9 %collective-permute-start.55 = (bf16[192,1536]{1,0:T(8,128)(2,1)}, bf16[192,1536]{1,0:T(8,128)(2,1)}, u32[]{:S(2)}, u32[]{:S(2)}) collective-permute-start(bf16[192,1536]{1,0:T(8,128)(2,1)} %add_convert_fusion.5), channel_id=1, source_target_pairs={{0,4},{8,0},{16,8},{24,16},{28,24},{20,28},{12,20},{4,12},{1,5},{9... | collective-permute-start | bytes 1769480 | tf_op jit(solution)/shard_map/ppermute | solution.py:82
  513.3 8.4 %collective-permute-start.69 = (f32[64,384]{1,0:T(8,128)S(1)}, f32[64,384]{1,0:T(8,128)S(1)}, u32[]{:S(2)}, u32[]{:S(2)}) collective-permute-start(f32[64,384]{1,0:T(8,128)S(1)} %add.416), channel_id=1, source_target_pairs={{0,16},{4,20},{8,24},{12,28},{16,0},{20,4},{24,8},{28,12},{1,17},{... | collective-permute-start | bytes 294920 | tf_op jit(solution)/shard_map/ppermute | solution.py:161
  517.5 14.2 %collective-permute-start.52 = (bf16[192,1536]{1,0:T(8,128)(2,1)S(1)}, bf16[192,1536]{1,0:T(8,128)(2,1)}, u32[]{:S(2)}, u32[]{:S(2)}) collective-permute-start(bf16[192,1536]{1,0:T(8,128)(2,1)S(1)} %add_convert_fusion.6), channel_id=1, source_target_pairs={{0,8},{8,16},{16,24},{24,28},{28,20},{20,12},{12,4},{4,0},{1,9},{9... | collective-permute-start | bytes 1769480 | tf_op jit(solution)/shard_map/ppermute | solution.py:82
  520.7 13.4 %collective-permute-start.56 = (bf16[192,1536]{1,0:T(8,128)(2,1)S(1)}, bf16[192,1536]{1,0:T(8,128)(2,1)}, u32[]{:S(2)}, u32[]{:S(2)}) collective-permute-start(bf16[192,1536]{1,0:T(8,128)(2,1)S(1)} %add_convert_fusion.4), channel_id=1, source_target_pairs={{0,4},{8,0},{16,8},{24,16},{28,24},{20,28},{12,20},{4,12},{1,5},{9... | collective-permute-start | bytes 1769480 | tf_op jit(solution)/shard_map/ppermute | solution.py:82
  523.7 17.5 %collective-permute-start.75 = (bf16[48,384]{1,0:T(8,128)(2,1)}, bf16[48,384]{1,0:T(8,128)(2,1)}, u32[]{:S(2)}, u32[]{:S(2)}) collective-permute-start(bf16[48,384]{1,0:T(8,128)(2,1)} %slice.481), channel_id=1, source_target_pairs={{0,1},{1,0},{2,3},{3,2},{4,5},{5,4},{6,7},{7,6},{8,9},{9,8},{10,11... | collective-permute-start | bytes 110600 | tf_op jit(solution)/shard_map/ppermute | solution.py:174
  (128 other events, 847.4 us)
